TPU v7x, 32 devices: a whole 2x2x4 slice. The times are simulated.
32 devices in a mesh: row: 4 (over y, x), col: 8 (over z, core).
Axes of the slice: x: 2, y: 2, z: 4, core: 2. Of those that a mesh axis runs over, the one named last changes fastest.
Arguments:
- vectors: float32 [32768, 128], P(('row', 'col')), may hold values from -6 to 6
- diagonal: float32 [32768], P(('row', 'col')), may hold values from 0.25 to 4
- source_basis: float32 [128, 256, 64], P(('row', 'col')), may hold values from -0.375 to 0.375
- transfer: float32 [7, 128, 64, 128], P(None, ('row', 'col')), may hold values from -0.5 to 0.5
- target_basis: float32 [128, 256, 64], P(('row', 'col')), may hold values from -0.75 to 0.75
Outputs:
- forward_image: float32 [32768, 128], P(('row', 'col'))
- adjoint: float32 [32768, 128], P(('row', 'col'))
All inputs are finite; a program needn't handle non-finite values.
Results may differ from a plain program's by a relative error of at most 0.00017.
Values sent between devices are 32-bit elements; how exact they have to be, the bound alone decides.
No kernel may reach another device: no remote copies, remote signals or barrier semaphores. Data moves between devices by JAX's collectives and lax.ppermute only.
A program may use at most 64 MiB of HBM per device.

v0:
```python
import jax
import jax.numpy as jnp
from jax import lax
from jax.sharding import PartitionSpec as P

LEAF = 256
RANK = 64
VECS = 128
LEAF_DEV = 4


def partner_2(block, axis, bit):
    count = lax.axis_size(axis)
    route = []
    for low in range(count):
        high = low | 1 << bit
        if high != low and high < count:
            route += [(low, high), (high, low)]
    return lax.ppermute(block, axis, route)


def forward_level(coeffs, blocks, level_index):
    node_count = coeffs.shape[0]
    low_span = 2**level_index
    high_span = node_count // (2 * low_span)
    parted = coeffs.reshape(high_span, 2, low_span, RANK, coeffs.shape[-1])
    stacked = jnp.concatenate([parted[:, 0], parted[:, 1]], axis=2)
    shaped = blocks.reshape(high_span, 2, low_span, RANK, 2 * RANK)
    updated = jnp.einsum("aebij,abjv->aebiv", shaped, stacked, precision=lax.Precision.HIGHEST)
    return updated.reshape(node_count, RANK, coeffs.shape[-1])


def reverse_level(coeffs, blocks, level_index):
    node_count = coeffs.shape[0]
    low_span = 2**level_index
    high_span = node_count // (2 * low_span)
    parted = coeffs.reshape(high_span, 2, low_span, RANK, coeffs.shape[-1])
    shaped = blocks.reshape(high_span, 2, low_span, RANK, 2 * RANK)
    product = jnp.einsum("aebij,aebiv->abjv", shaped, parted, precision=lax.Precision.HIGHEST)
    halves = product.reshape(high_span, low_span, 2, RANK, coeffs.shape[-1]).transpose(
        0, 2, 1, 3, 4
    )
    return halves.reshape(node_count, RANK, coeffs.shape[-1])


def join_pair(owned, partner, is_upper, blocks):
    lower_half = jnp.where(is_upper, partner, owned)
    upper_half = jnp.where(is_upper, owned, partner)
    stacked = jnp.concatenate([lower_half, upper_half], axis=1)
    return jnp.einsum("nij,njv->niv", blocks, stacked, precision=lax.Precision.HIGHEST)


def split_parent(coeffs, blocks, is_upper):
    product = jnp.einsum("nij,niv->njv", blocks, coeffs, precision=lax.Precision.HIGHEST)
    kept_half = jnp.where(is_upper, product[:, RANK:], product[:, :RANK])
    sent_half = jnp.where(is_upper, product[:, :RANK], product[:, RANK:])
    return (kept_half, sent_half)


def send_fwd_col(merged):
    return lax.all_to_all(merged, "col", split_axis=0, concat_axis=0, tiled=True)


def send_fwd_row(merged):
    return lax.all_to_all(merged, "row", split_axis=0, concat_axis=0, tiled=True)


def send_back_col(merged):
    return lax.all_to_all(merged, "col", split_axis=0, concat_axis=0, tiled=True)


def send_back_row(merged):
    return lax.all_to_all(merged, "row", split_axis=0, concat_axis=0, tiled=True)


def regroup_section(tensor, local_labels, axis_labels, wanted, sender):
    bit_count = len(wanted)
    chosen = [local_labels.index(one_label) for one_label in wanted]
    leftover = [
        position for position in range(len(local_labels)) if local_labels[position] not in wanted
    ]
    axes_order = chosen + leftover + list(range(len(local_labels), tensor.ndim))
    permuted = jnp.transpose(tensor, axes_order)
    merged = permuted.reshape((2**bit_count,) + permuted.shape[bit_count:])
    arrived = sender(merged)
    parted = arrived.reshape((2,) * len(axis_labels) + arrived.shape[1:])
    new_local = list(axis_labels) + [local_labels[position] for position in leftover]
    return (parted, new_local, list(wanted))


def finish_local(tensor, local_labels, final_labels, lead_shape):
    chosen = [local_labels.index(one_label) for one_label in final_labels]
    axes_order = chosen + list(range(len(local_labels), tensor.ndim))
    permuted = jnp.transpose(tensor, axes_order)
    return permuted.reshape(lead_shape + permuted.shape[len(local_labels) :])


def to_target(leaf_image, local_bits, col_bits, row_bits, leaf_bits):
    all_levels = local_bits + col_bits + row_bits
    local_labels = [("t", level_index) for level_index in range(local_bits - 1, -1, -1)]
    local_labels = local_labels + [("r", bit_pos) for bit_pos in range(leaf_bits)]
    col_labels = [
        ("t", level_index) for level_index in range(local_bits + col_bits - 1, local_bits - 1, -1)
    ]
    row_labels = [
        ("t", level_index) for level_index in range(all_levels - 1, local_bits + col_bits - 1, -1)
    ]
    tensor = leaf_image.reshape((2,) * (local_bits + leaf_bits) + leaf_image.shape[2:])
    wanted = [("r", bit_pos) for bit_pos in range(col_bits)]
    tensor, local_labels, col_labels = regroup_section(
        tensor, local_labels, col_labels, wanted, send_fwd_col
    )
    wanted = [("t", level_index) for level_index in range(row_bits)]
    tensor, local_labels, row_labels = regroup_section(
        tensor, local_labels, row_labels, wanted, send_fwd_row
    )
    wanted = [("t", level_index) for level_index in range(row_bits, row_bits + col_bits)]
    tensor, local_labels, col_labels = regroup_section(
        tensor, local_labels, col_labels, wanted, send_fwd_col
    )
    final_labels = [("t", level_index) for level_index in range(row_bits + col_bits, all_levels)]
    final_labels = final_labels + [("r", bit_pos) for bit_pos in range(leaf_bits)]
    return finish_local(tensor, local_labels, final_labels, (2 ** (local_bits + leaf_bits),))


def to_butterfly(ordered, local_bits, col_bits, row_bits, leaf_bits):
    all_levels = local_bits + col_bits + row_bits
    row_labels = [("t", level_index) for level_index in range(row_bits)]
    col_labels = [("t", level_index) for level_index in range(row_bits, row_bits + col_bits)]
    local_labels = [("t", level_index) for level_index in range(row_bits + col_bits, all_levels)]
    local_labels = local_labels + [("r", bit_pos) for bit_pos in range(leaf_bits)]
    tensor = ordered.reshape((2,) * (local_bits + leaf_bits) + ordered.shape[1:])
    wanted = [("r", bit_pos) for bit_pos in range(col_bits)]
    tensor, local_labels, col_labels = regroup_section(
        tensor, local_labels, col_labels, wanted, send_back_col
    )
    wanted = [
        ("t", level_index) for level_index in range(all_levels - 1, local_bits + col_bits - 1, -1)
    ]
    tensor, local_labels, row_labels = regroup_section(
        tensor, local_labels, row_labels, wanted, send_back_row
    )
    wanted = [
        ("t", level_index) for level_index in range(local_bits + col_bits - 1, local_bits - 1, -1)
    ]
    tensor, local_labels, col_labels = regroup_section(
        tensor, local_labels, col_labels, wanted, send_back_col
    )
    final_labels = [("t", level_index) for level_index in range(local_bits - 1, -1, -1)]
    final_labels = final_labels + [("r", bit_pos) for bit_pos in range(leaf_bits)]
    return finish_local(tensor, local_labels, final_labels, (2**local_bits, 2**leaf_bits))


def body(vectors, diagonal, source_basis, transfer, target_basis):
    col_bits = lax.axis_size("col").bit_length() - 1
    row_bits = lax.axis_size("row").bit_length() - 1
    local_bits = LEAF_DEV.bit_length() - 1
    leaf_bits = LEAF.bit_length() - 1
    col_place = lax.axis_index("col")
    row_place = lax.axis_index("row")
    leaf_rows = vectors.reshape(LEAF_DEV, LEAF, VECS)
    coeffs = jnp.einsum("ksr,ksv->krv", source_basis, leaf_rows, precision=lax.Precision.HIGHEST)
    for level_index in range(local_bits):
        coeffs = forward_level(coeffs, transfer[level_index], level_index)
    for bit_pos in range(col_bits):
        partner = partner_2(coeffs, "col", bit_pos)
        is_upper = col_place // 2**bit_pos % 2 == 1
        coeffs = join_pair(coeffs, partner, is_upper, transfer[local_bits + bit_pos])
    for bit_pos in range(row_bits):
        partner = partner_2(coeffs, "row", bit_pos)
        is_upper = row_place // 2**bit_pos % 2 == 1
        coeffs = join_pair(coeffs, partner, is_upper, transfer[local_bits + col_bits + bit_pos])
    leaf_image = jnp.einsum("ksr,krv->ksv", target_basis, coeffs, precision=lax.Precision.HIGHEST)
    forward_image = to_target(leaf_image, local_bits, col_bits, row_bits, leaf_bits)
    diagonal_leaf = to_butterfly(diagonal, local_bits, col_bits, row_bits, leaf_bits)
    weighted_leaf = diagonal_leaf[:, :, None] * leaf_image
    adjoint_coeffs = jnp.einsum(
        "ksr,ksv->krv", target_basis, weighted_leaf, precision=lax.Precision.HIGHEST
    )
    for bit_pos in range(row_bits - 1, -1, -1):
        is_upper = row_place // 2**bit_pos % 2 == 1
        kept_half, sent_half = split_parent(
            adjoint_coeffs, transfer[local_bits + col_bits + bit_pos], is_upper
        )
        adjoint_coeffs = kept_half + partner_2(sent_half, "row", bit_pos)
    for bit_pos in range(col_bits - 1, -1, -1):
        is_upper = col_place // 2**bit_pos % 2 == 1
        kept_half, sent_half = split_parent(
            adjoint_coeffs, transfer[local_bits + bit_pos], is_upper
        )
        adjoint_coeffs = kept_half + partner_2(sent_half, "col", bit_pos)
    for level_index in range(local_bits - 1, -1, -1):
        adjoint_coeffs = reverse_level(adjoint_coeffs, transfer[level_index], level_index)
    adjoint = jnp.einsum(
        "ksr,krv->ksv", source_basis, adjoint_coeffs, precision=lax.Precision.HIGHEST
    )
    return (forward_image, adjoint.reshape(LEAF_DEV * LEAF, VECS))


def solution(mesh):
    placed = (
        P(("row", "col"), None),
        P(("row", "col")),
        P(("row", "col"), None, None),
        P(None, ("row", "col"), None, None),
        P(("row", "col"), None, None),
    )
    return jax.shard_map(
        body,
        mesh=mesh,
        in_specs=placed,
        out_specs=(P(("row", "col"), None), P(("row", "col"), None)),
        check_vma=False,
    )
```

profile of v0, /device:TPU:0, one launch (start us, length us, event | category | flops | bytes accessed | tf_op | source)
XLA Modules:
  0.0 130.8 jit_solution(5200367692783381859)
XLA Ops:
  0.7 1.0 copy-done
  1.7 1.4 %fusion.74 = f32[4,64,128]{2,1,0:T(8,128)S(1)} fusion(f32[4,256,64]{1,2,0:T(8,128)} %param.7, f32[4,256,128]{2,1,0:T(8,128)S(1)} %bitcast.149), kind=kOutput, calls=%fused_computation.109 | convolution fusion | flops 100663296 | bytes 917504 | tf_op jit(solution)/shard_map/ksr,ksv->krv/dot_general | solution.py:162
  3.1 0.3 convolution_bitcast_fusion.12
  3.4 0.3 convolution_bitcast_fusion.11
  3.7 0.6 collective-permute-start
  4.3 1.0 collective-permute-done
  5.3 0.3 convolution_bitcast_fusion.10
  5.6 3.0 %collective-permute-start.1 = (f32[4,64,128]{2,1,0:T(8,128)S(1)}, f32[4,64,128]{2,1,0:T(8,128)S(1)}, u32[]{:S(2)}, u32[]{:S(2)}) collective-permute-start(f32[4,64,128]{2,1,0:T(8,128)S(1)} %convolution_bitcast_fusion.10), channel_id=1, source_target_pairs={{0,2},{2,0},{1,3},{3,1},{4,6},{6,4},{5,7},{7,5},{8,10},{10,8},{9,1... | collective-permute-start | bytes 393224 | tf_op jit(solution)/shard_map/ppermute | solution.py:19
  8.6 3.8 %collective-permute-done.1 = f32[4,64,128]{2,1,0:T(8,128)S(1)} collective-permute-done((f32[4,64,128]{2,1,0:T(8,128)S(1)}, f32[4,64,128]{2,1,0:T(8,128)S(1)}, u32[]{:S(2)}, u32[]{:S(2)}) %collective-permute-start.1) | collective-permute-done | bytes 131104 | tf_op jit(solution)/shard_map/ppermute | solution.py:19
  12.5 0.3 convolution_bitcast_fusion.9
  12.8 2.8 %collective-permute-start.2 = (f32[4,64,128]{2,1,0:T(8,128)S(1)}, f32[4,64,128]{2,1,0:T(8,128)S(1)}, u32[]{:S(2)}, u32[]{:S(2)}) collective-permute-start(f32[4,64,128]{2,1,0:T(8,128)S(1)} %convolution_bitcast_fusion.9), channel_id=1, source_target_pairs={{0,4},{4,0},{1,5},{5,1},{2,6},{6,2},{3,7},{7,3},{8,12},{12,8},{9,1... | collective-permute-start | bytes 393224 | tf_op jit(solution)/shard_map/ppermute | solution.py:19
  15.6 5.9 %collective-permute-done.2 = f32[4,64,128]{2,1,0:T(8,128)S(1)} collective-permute-done((f32[4,64,128]{2,1,0:T(8,128)S(1)}, f32[4,64,128]{2,1,0:T(8,128)S(1)}, u32[]{:S(2)}, u32[]{:S(2)}) %collective-permute-start.2) | collective-permute-done | bytes 131104 | tf_op jit(solution)/shard_map/ppermute | solution.py:19
  21.6 0.3 convolution_bitcast_fusion.8
  21.9 1.4 %collective-permute-start.3 = (f32[4,64,128]{2,1,0:T(8,128)S(1)}, f32[4,64,128]{2,1,0:T(8,128)S(1)}, u32[]{:S(2)}, u32[]{:S(2)}) collective-permute-start(f32[4,64,128]{2,1,0:T(8,128)S(1)} %convolution_bitcast_fusion.8), channel_id=1, source_target_pairs={{0,8},{8,0},{16,24},{24,16},{1,9},{9,1},{17,25},{25,17},{2,10},{10... | collective-permute-start | bytes 393224 | tf_op jit(solution)/shard_map/ppermute | solution.py:19
  23.4 3.6 %collective-permute-done.3 = f32[4,64,128]{2,1,0:T(8,128)S(1)} collective-permute-done((f32[4,64,128]{2,1,0:T(8,128)S(1)}, f32[4,64,128]{2,1,0:T(8,128)S(1)}, u32[]{:S(2)}, u32[]{:S(2)}) %collective-permute-start.3) | collective-permute-done | bytes 131104 | tf_op jit(solution)/shard_map/ppermute | solution.py:19
  27.0 0.3 convolution_bitcast_fusion.7
  27.3 1.5 %collective-permute-start.4 = (f32[4,64,128]{2,1,0:T(8,128)S(1)}, f32[4,64,128]{2,1,0:T(8,128)S(1)}, u32[]{:S(2)}, u32[]{:S(2)}) collective-permute-start(f32[4,64,128]{2,1,0:T(8,128)S(1)} %convolution_bitcast_fusion.7), channel_id=1, source_target_pairs={{0,16},{16,0},{8,24},{24,8},{1,17},{17,1},{9,25},{25,9},{2,18},{18... | collective-permute-start | bytes 393224 | tf_op jit(solution)/shard_map/ppermute | solution.py:19
  28.8 0.4 reshape.113
  29.3 0.3 reshape.128
  29.6 10.4 %all_to_all.30 = f32[8,1,128]{2,1,0:T(1,128)S(1)} all-to-all(f32[8,1,128]{2,1,0:T(1,128)S(1)} %reshape.128), channel_id=1, replica_groups=mesh['row'=4,'col'=8] {'col'}, dimensions={0} | all-to-all | bytes 8192 | tf_op jit(solution)/shard_map/all_to_all | solution.py:69
  40.0 0.5 broadcast.10
  40.5 0.7 reduce
  41.2 0.4 reshape.129
  41.6 0.3 reshape.130
  42.0 7.2 %all_to_all.31 = f32[4,1,256]{2,1,0:T(1,128)S(1)} all-to-all(f32[4,1,256]{2,1,0:T(1,128)S(1)} %reshape.130), channel_id=1, replica_groups=mesh['row'=4,'col'=8] {'row'}, dimensions={0} | all-to-all | bytes 8192 | tf_op jit(solution)/shard_map/all_to_all | solution.py:73
  49.2 0.7 reduce.1
  49.9 0.4 reshape.131
  50.4 0.9 reshape.132
  51.3 3.3 %all-to-all-start.5 = ((f32[8,1,128]{2,1,0:T(1,128)}), f32[8,1,128]{2,1,0:T(1,128)S(1)}, u32[]{:S(2)}, u32[]{:S(2)}) async-start(f32[8,1,128]{2,1,0:T(1,128)} %reshape.132), calls=%async_computation.5 | async-start | bytes 8192 | tf_op jit(solution)/shard_map/all_to_all | solution.py:69
  54.6 5.4 %all-to-all-done.5 = f32[8,1,128]{2,1,0:T(1,128)S(1)} async-done(((f32[8,1,128]{2,1,0:T(1,128)}), f32[8,1,128]{2,1,0:T(1,128)S(1)}, u32[]{:S(2)}, u32[]{:S(2)}) %all-to-all-start.5) | async-done | bytes 4128 | tf_op jit(solution)/shard_map/all_to_all | solution.py:69
  60.0 0.7 reduce.2
  60.7 0.4 reshape.133
  61.2 0.3 mul.10
  61.5 0.3 fusion.14
  61.9 0.6 copy-done.2
  62.5 0.6 convolution_bitcast_fusion.1
  63.1 0.7 fusion
  63.8 0.6 convolution_bitcast_fusion.6
  64.4 0.6 collective-permute-start.5
  65.1 4.6 %collective-permute-done.5 = f32[4,64,128]{2,1,0:T(8,128)S(1)} collective-permute-done((f32[4,64,128]{2,1,0:T(8,128)S(1)}, f32[4,64,128]{2,1,0:T(8,128)S(1)}, u32[]{:S(2)}, u32[]{:S(2)}) %collective-permute-start.5) | collective-permute-done | bytes 131104 | tf_op jit(solution)/shard_map/ppermute | solution.py:19
  69.7 0.6 convolution_bitcast_fusion.5
  70.3 0.6 collective-permute-start.6
  71.0 0.2 copy.39
  71.2 1.0 copy.40
  72.1 3.5 %all-to-all-start = ((f32[8,2,2,2,2,2,2,2,128]{8,7,6,5,4,3,2,1,0:T(2,128)}), f32[8,2,2,2,2,2,2,2,128]{8,7,6,5,4,3,2,1,0:T(2,128)S(1)}, u32[]{:S(2)}, u32[]{:S(2)}) async-start(f32[8,2,2,2,2,2,2,2,128]{8,7,6,5,4,3,2,1,0:T(2,128)} %copy.40), calls=%async_computation | async-start | bytes 1048576 | tf_op jit(solution)/shard_map/all_to_all | solution.py:61
  75.7 0.6 convolution_bitcast_fusion.4
  76.3 2.9 %collective-permute-start.7 = (f32[4,64,128]{2,1,0:T(8,128)S(1)}, f32[4,64,128]{2,1,0:T(8,128)S(1)}, u32[]{:S(2)}, u32[]{:S(2)}) collective-permute-start(f32[4,64,128]{2,1,0:T(8,128)S(1)} %slice_select_fusion.2), channel_id=1, source_target_pairs={{0,4},{4,0},{1,5},{5,1},{2,6},{6,2},{3,7},{7,3},{8,12},{12,8},{9,1... | collective-permute-start | bytes 393224 | tf_op jit(solution)/shard_map/ppermute | solution.py:19
  79.2 17.3 %collective-permute-done.7 = f32[4,64,128]{2,1,0:T(8,128)S(1)} collective-permute-done((f32[4,64,128]{2,1,0:T(8,128)S(1)}, f32[4,64,128]{2,1,0:T(8,128)S(1)}, u32[]{:S(2)}, u32[]{:S(2)}) %collective-permute-start.7) | collective-permute-done | bytes 131104 | tf_op jit(solution)/shard_map/ppermute | solution.py:19
  96.5 0.6 convolution_bitcast_fusion.3
  97.2 1.0 copy.41
  98.2 3.5 %all-to-all-start.1 = ((f32[4,2,2,2,2,2,2,2,2,128]{9,8,7,6,5,4,3,2,1,0:T(2,128)}), f32[4,2,2,2,2,2,2,2,2,128]{9,8,7,6,5,4,3,2,1,0:T(2,128)S(1)}, u32[]{:S(2)}, u32[]{:S(2)}) async-start(f32[4,2,2,2,2,2,2,2,2,128]{9,8,7,6,5,4,3,2,1,0:T(2,128)} %bitcast.37), calls=%async_computation.1 | async-start | bytes 1048576 | tf_op jit(solution)/shard_map/all_to_all | solution.py:65
  101.7 0.5 collective-permute-done.8
  102.2 0.6 convolution_bitcast_fusion.2
  102.9 6.8 %all-to-all-done.1 = f32[4,2,2,2,2,2,2,2,2,128]{9,8,7,6,5,4,3,2,1,0:T(2,128)S(1)} async-done(((f32[4,2,2,2,2,2,2,2,2,128]{9,8,7,6,5,4,3,2,1,0:T(2,128)}), f32[4,2,2,2,2,2,2,2,2,128]{9,8,7,6,5,4,3,2,1,0:T(2,128)S(1)}, u32[]{:S(2)}, u32[]{:S(2)}) %all-to-all-start.1) | async-done | bytes 524320 | tf_op jit(solution)/shard_map/all_to_all | solution.py:65
  109.6 0.4 copy.42
  110.0 1.1 copy.43
  111.1 3.5 %all-to-all-start.2 = ((f32[8,2,2,2,2,2,2,2,128]{8,7,6,5,4,3,2,1,0:T(2,128)}), f32[8,2,2,2,2,2,2,2,128]{8,7,6,5,4,3,2,1,0:T(2,128)S(1)}, u32[]{:S(2)}, u32[]{:S(2)}) async-start(f32[8,2,2,2,2,2,2,2,128]{8,7,6,5,4,3,2,1,0:T(2,128)} %copy.43), calls=%async_computation.2 | async-start | bytes 1048576 | tf_op jit(solution)/shard_map/all_to_all | solution.py:61
  114.7 0.4 fusion.75
  115.1 0.4 fusion.33
  115.4 0.6 copy-done.3
  116.0 0.6 convolution_bitcast_fusion
  116.6 1.0 copy.54
  117.6 12.2 %all-to-all-done.2 = f32[8,2,2,2,2,2,2,2,128]{8,7,6,5,4,3,2,1,0:T(2,128)S(1)} async-done(((f32[8,2,2,2,2,2,2,2,128]{8,7,6,5,4,3,2,1,0:T(2,128)}), f32[8,2,2,2,2,2,2,2,128]{8,7,6,5,4,3,2,1,0:T(2,128)S(1)}, u32[]{:S(2)}, u32[]{:S(2)}) %all-to-all-start.2) | async-done | bytes 524320 | tf_op jit(solution)/shard_map/all_to_all | solution.py:61
  129.9 1.0 copy.44
  (32 shorter events, 0.5 us)
Async XLA Ops:
  0.6 1.0 copy-start
  0.6 2.5 %copy-start.1 = (f32[7,4,64,128]{3,2,1,0:T(8,128)S(1)}, f32[7,4,64,128]{3,2,1,0:T(8,128)}, u32[]{:S(2)}) copy-start(f32[7,4,64,128]{3,2,1,0:T(8,128)} %param.8) | copy-start | bytes 2752516
  3.7 1.5 %collective-permute-start = (f32[4,64,128]{2,1,0:T(8,128)S(1)}, f32[4,64,128]{2,1,0:T(8,128)S(1)}, u32[]{:S(2)}, u32[]{:S(2)}) collective-permute-start(f32[4,64,128]{2,1,0:T(8,128)S(1)} %bitcast.168), channel_id=1, source_target_pairs={{0,1},{1,0},{2,3},{3,2},{4,5},{5,4},{6,7},{7,6},{8,9},{9,8},{10,11... | collective-permute-start | bytes 393224 | tf_op jit(solution)/shard_map/ppermute | solution.py:19
  5.6 6.8 %collective-permute-start.1 = (f32[4,64,128]{2,1,0:T(8,128)S(1)}, f32[4,64,128]{2,1,0:T(8,128)S(1)}, u32[]{:S(2)}, u32[]{:S(2)}) collective-permute-start(f32[4,64,128]{2,1,0:T(8,128)S(1)} %convolution_bitcast_fusion.10), channel_id=1, source_target_pairs={{0,2},{2,0},{1,3},{3,1},{4,6},{6,4},{5,7},{7,5},{8,10},{10,8},{9,1... | collective-permute-start | bytes 393224 | tf_op jit(solution)/shard_map/ppermute | solution.py:19
  12.8 8.7 %collective-permute-start.2 = (f32[4,64,128]{2,1,0:T(8,128)S(1)}, f32[4,64,128]{2,1,0:T(8,128)S(1)}, u32[]{:S(2)}, u32[]{:S(2)}) collective-permute-start(f32[4,64,128]{2,1,0:T(8,128)S(1)} %convolution_bitcast_fusion.9), channel_id=1, source_target_pairs={{0,4},{4,0},{1,5},{5,1},{2,6},{6,2},{3,7},{7,3},{8,12},{12,8},{9,1... | collective-permute-start | bytes 393224 | tf_op jit(solution)/shard_map/ppermute | solution.py:19
  21.9 5.0 %collective-permute-start.3 = (f32[4,64,128]{2,1,0:T(8,128)S(1)}, f32[4,64,128]{2,1,0:T(8,128)S(1)}, u32[]{:S(2)}, u32[]{:S(2)}) collective-permute-start(f32[4,64,128]{2,1,0:T(8,128)S(1)} %convolution_bitcast_fusion.8), channel_id=1, source_target_pairs={{0,8},{8,0},{16,24},{24,16},{1,9},{9,1},{17,25},{25,17},{2,10},{10... | collective-permute-start | bytes 393224 | tf_op jit(solution)/shard_map/ppermute | solution.py:19
  27.0 1.8 %copy-start.4 = (f32[1024]{0:T(1024)S(1)}, f32[1024]{0:T(1024)}, u32[]{:S(2)}) copy-start(f32[1024]{0:T(1024)} %param.6) | copy-start | bytes 12292
  27.3 34.1 %collective-permute-start.4 = (f32[4,64,128]{2,1,0:T(8,128)S(1)}, f32[4,64,128]{2,1,0:T(8,128)S(1)}, u32[]{:S(2)}, u32[]{:S(2)}) collective-permute-start(f32[4,64,128]{2,1,0:T(8,128)S(1)} %convolution_bitcast_fusion.7), channel_id=1, source_target_pairs={{0,16},{16,0},{8,24},{24,8},{1,17},{17,1},{9,25},{25,9},{2,18},{18... | collective-permute-start | bytes 393224 | tf_op jit(solution)/shard_map/ppermute | solution.py:19
  51.3 8.8 %all-to-all-start.5 = ((f32[8,1,128]{2,1,0:T(1,128)}), f32[8,1,128]{2,1,0:T(1,128)S(1)}, u32[]{:S(2)}, u32[]{:S(2)}) async-start(f32[8,1,128]{2,1,0:T(1,128)} %reshape.132), calls=%async_computation.5 | async-start | bytes 8192 | tf_op jit(solution)/shard_map/all_to_all | solution.py:69
  61.5 1.0 copy-start.2
  64.4 5.3 %collective-permute-start.5 = (f32[4,64,128]{2,1,0:T(8,128)S(1)}, f32[4,64,128]{2,1,0:T(8,128)S(1)}, u32[]{:S(2)}, u32[]{:S(2)}) collective-permute-start(f32[4,64,128]{2,1,0:T(8,128)S(1)} %slice_select_fusion.4), channel_id=1, source_target_pairs={{0,16},{16,0},{8,24},{24,8},{1,17},{17,1},{9,25},{25,9},{2,18},{18... | collective-permute-start | bytes 393224 | tf_op jit(solution)/shard_map/ppermute | solution.py:19
  70.3 5.3 %collective-permute-start.6 = (f32[4,64,128]{2,1,0:T(8,128)S(1)}, f32[4,64,128]{2,1,0:T(8,128)S(1)}, u32[]{:S(2)}, u32[]{:S(2)}) collective-permute-start(f32[4,64,128]{2,1,0:T(8,128)S(1)} %slice_select_fusion.3), channel_id=1, source_target_pairs={{0,8},{8,0},{16,24},{24,16},{1,9},{9,1},{17,25},{25,17},{2,10},{10... | collective-permute-start | bytes 393224 | tf_op jit(solution)/shard_map/ppermute | solution.py:19
  72.1 25.1 %all-to-all-start = ((f32[8,2,2,2,2,2,2,2,128]{8,7,6,5,4,3,2,1,0:T(2,128)}), f32[8,2,2,2,2,2,2,2,128]{8,7,6,5,4,3,2,1,0:T(2,128)S(1)}, u32[]{:S(2)}, u32[]{:S(2)}) async-start(f32[8,2,2,2,2,2,2,2,128]{8,7,6,5,4,3,2,1,0:T(2,128)} %copy.40), calls=%async_computation | async-start | bytes 1048576 | tf_op jit(solution)/shard_map/all_to_all | solution.py:61
  76.3 20.2 %collective-permute-start.7 = (f32[4,64,128]{2,1,0:T(8,128)S(1)}, f32[4,64,128]{2,1,0:T(8,128)S(1)}, u32[]{:S(2)}, u32[]{:S(2)}) collective-permute-start(f32[4,64,128]{2,1,0:T(8,128)S(1)} %slice_select_fusion.2), channel_id=1, source_target_pairs={{0,4},{4,0},{1,5},{5,1},{2,6},{6,2},{3,7},{7,3},{8,12},{12,8},{9,1... | collective-permute-start | bytes 393224 | tf_op jit(solution)/shard_map/ppermute | solution.py:19
  97.1 5.0 %collective-permute-start.8 = (f32[4,64,128]{2,1,0:T(8,128)S(1)}, f32[4,64,128]{2,1,0:T(8,128)S(1)}, u32[]{:S(2)}, u32[]{:S(2)}) collective-permute-start(f32[4,64,128]{2,1,0:T(8,128)S(1)} %slice_select_fusion.1), channel_id=1, source_target_pairs={{0,2},{2,0},{1,3},{3,1},{4,6},{6,4},{5,7},{7,5},{8,10},{10,8},{9,1... | collective-permute-start | bytes 393224 | tf_op jit(solution)/shard_map/ppermute | solution.py:19
  98.2 11.5 %all-to-all-start.1 = ((f32[4,2,2,2,2,2,2,2,2,128]{9,8,7,6,5,4,3,2,1,0:T(2,128)}), f32[4,2,2,2,2,2,2,2,2,128]{9,8,7,6,5,4,3,2,1,0:T(2,128)S(1)}, u32[]{:S(2)}, u32[]{:S(2)}) async-start(f32[4,2,2,2,2,2,2,2,2,128]{9,8,7,6,5,4,3,2,1,0:T(2,128)} %bitcast.37), calls=%async_computation.1 | async-start | bytes 1048576 | tf_op jit(solution)/shard_map/all_to_all | solution.py:65
  102.8 11.8 %collective-permute-start.9 = (f32[4,64,128]{2,1,0:T(8,128)S(1)}, f32[4,64,128]{2,1,0:T(8,128)S(1)}, u32[]{:S(2)}, u32[]{:S(2)}) collective-permute-start(f32[4,64,128]{2,1,0:T(8,128)S(1)} %slice_select_fusion), channel_id=1, source_target_pairs={{0,1},{1,0},{2,3},{3,2},{4,5},{5,4},{6,7},{7,6},{8,9},{9,8},{10,11... | collective-permute-start | bytes 393224 | tf_op jit(solution)/shard_map/ppermute | solution.py:19
  111.1 18.8 %all-to-all-start.2 = ((f32[8,2,2,2,2,2,2,2,128]{8,7,6,5,4,3,2,1,0:T(2,128)}), f32[8,2,2,2,2,2,2,2,128]{8,7,6,5,4,3,2,1,0:T(2,128)S(1)}, u32[]{:S(2)}, u32[]{:S(2)}) async-start(f32[8,2,2,2,2,2,2,2,128]{8,7,6,5,4,3,2,1,0:T(2,128)} %copy.43), calls=%async_computation.2 | async-start | bytes 1048576 | tf_op jit(solution)/shard_map/all_to_all | solution.py:61
  115.0 1.0 copy-start.3
where the time goes:
time: 131 us
  waiting for transfers between devices  61.2 us (47%)
  starting transfers between devices  27.4 us (21%)
  blocking collectives  17.7 us (14%)
  local copies, waits for them, and re-layouts  11.9 us (9%)
  matrix products  9.35 us (7%)
  other arithmetic  2.2 us (2%)
    ppermute x10, waiting for transfers between devices, partner_2(): return lax.ppermute(block, axis, route)  36.8 us
    ppermute x10, starting transfers between devices, partner_2(): return lax.ppermute(block, axis, route)  13.6 us
    all_to_all x2, waiting for transfers between devices, send_fwd_col(): lax.all_to_all(merged, 'col', split_axis=0, concat_axis=0, tiled=True)  12.2 us
    all_to_all x1, blocking collectives, send_back_col(): lax.all_to_all(merged, 'col', split_axis=0, concat_axis=0, tiled=True)  10.4 us
    all_to_all x1, blocking collectives, send_back_row(): lax.all_to_all(merged, 'row', split_axis=0, concat_axis=0, tiled=True)  7.24 us
    all_to_all x2, starting transfers between devices, send_fwd_col(): lax.all_to_all(merged, 'col', split_axis=0, concat_axis=0, tiled=True)  6.99 us
    all_to_all x1, waiting for transfers between devices, send_fwd_row(): lax.all_to_all(merged, 'row', split_axis=0, concat_axis=0, tiled=True)  6.76 us
    all_to_all x1, waiting for transfers between devices, send_back_col(): lax.all_to_all(merged, 'col', split_axis=0, concat_axis=0, tiled=True)  5.41 us
  transfers between devices with their start and end apart: 14, of which 10 were waited for; matrix products, arithmetic and copies ran while one was open for 11% of the time, Pallas kernels for 0%

commit v1 on v0

v1 whole, which is shorter than its diff:
```python
import jax
import jax.numpy as jnp
from jax import lax
from jax.sharding import PartitionSpec as P

HIGHEST = lax.Precision.HIGHEST
BOTH = ("row", "col")


def reverse_bits(value, bits):
    out = 0
    for i in range(bits):
        out = out | ((value >> i) & 1) << (bits - 1 - i)
    return out


def pair_exchange(block, axis, bit):
    count = lax.axis_size(axis)
    return lax.ppermute(block, axis, [(i, i ^ (1 << bit)) for i in range(count)])


class Reversal:
    def __init__(self, local_bits):
        self.rows = lax.axis_size("row")
        self.cols = lax.axis_size("col")
        self.bits = (self.rows * self.cols).bit_length() - 1
        self.local_bits = local_bits
        self.count = 2**local_bits
        place = lax.axis_index("row") * self.cols + lax.axis_index("col")
        self.top = place >> (self.bits - local_bits)

    def route(self, k):
        low = self.bits - self.local_bits
        return [
            (d, ((d >> low) ^ k) << low | reverse_bits(d & (2**low - 1), low))
            for d in range(2**self.bits)
        ]

    def slot(self, k):
        return reverse_bits(self.top ^ k, self.local_bits)

    def send(self, blocks, k):
        picked = lax.dynamic_index_in_dim(blocks, self.slot(k), 0, keepdims=False)
        return lax.ppermute(picked, BOTH, self.route(k))

    def place(self, arrived):
        out = jnp.zeros((self.count,) + arrived[0].shape, arrived[0].dtype)
        for k, block in enumerate(arrived):
            out = lax.dynamic_update_index_in_dim(out, block, self.slot(k), 0)
        return out


def local_forward(coeffs, blocks, level):
    count, rank, vecs = coeffs.shape
    low = 2**level
    parted = coeffs.reshape(count // (2 * low), 2, low, rank, vecs)
    stacked = jnp.concatenate([parted[:, 0], parted[:, 1]], axis=2)
    shaped = blocks.reshape(count // (2 * low), 2, low, rank, 2 * rank)
    out = jnp.einsum("aebij,abjv->aebiv", shaped, stacked, precision=HIGHEST)
    return out.reshape(count, rank, vecs)


def local_reverse(coeffs, blocks, level):
    count, rank, vecs = coeffs.shape
    low = 2**level
    parted = coeffs.reshape(count // (2 * low), 2, low, rank, vecs)
    shaped = blocks.reshape(count // (2 * low), 2, low, rank, 2 * rank)
    out = jnp.einsum("aebij,aebiv->abjv", shaped, parted, precision=HIGHEST)
    halves = out.reshape(count // (2 * low), low, 2, rank, vecs).transpose(0, 2, 1, 3, 4)
    return halves.reshape(count, rank, vecs)


def body(vectors, diagonal, source_basis, transfer, target_basis):
    leaves, leaf, rank = source_basis.shape
    vecs = vectors.shape[-1]
    local_bits = leaves.bit_length() - 1
    col_bits = lax.axis_size("col").bit_length() - 1
    row_bits = lax.axis_size("row").bit_length() - 1
    steps = [("col", bit) for bit in range(col_bits)] + [("row", bit) for bit in range(row_bits)]
    uppers = [lax.axis_index(axis) >> bit & 1 == 1 for axis, bit in steps]
    levels = [transfer[local_bits + i] for i in range(len(steps))]
    reversal = Reversal(local_bits)

    diag_blocks = diagonal.reshape(leaves, leaf)
    weights = reversal.place([reversal.send(diag_blocks, k) for k in range(leaves)])
    gram = jnp.einsum(
        "ksr,kst->krt", target_basis * weights[:, :, None], target_basis, precision=HIGHEST
    )
    top = levels[-1]
    fold = jnp.einsum("krt,ktj->krj", gram, top, precision=HIGHEST)
    fold = jnp.einsum("kri,krj->kij", top, fold, precision=HIGHEST)
    kept = jnp.where(uppers[-1], fold[:, rank:], fold[:, :rank])
    sent = jnp.where(uppers[-1], fold[:, :rank], fold[:, rank:])
    fold = kept + pair_exchange(sent, *steps[-1])

    coeffs = jnp.einsum(
        "ksr,ksv->krv", source_basis, vectors.reshape(leaves, leaf, vecs), precision=HIGHEST
    )
    for level in range(local_bits):
        coeffs = local_forward(coeffs, transfer[level], level)

    def stacked_pair(coeffs, i):
        partner = pair_exchange(coeffs, *steps[i])
        lower = jnp.where(uppers[i], partner, coeffs)
        upper = jnp.where(uppers[i], coeffs, partner)
        return jnp.concatenate([lower, upper], axis=1)

    for i in range(len(steps) - 1):
        stacked = stacked_pair(coeffs, i)
        coeffs = jnp.einsum("nij,njv->niv", levels[i], stacked, precision=HIGHEST)
    stacked = stacked_pair(coeffs, len(steps) - 1)
    back = jnp.einsum("nij,njv->niv", fold, stacked, precision=HIGHEST)
    coeffs = jnp.einsum("nij,njv->niv", top, stacked, precision=HIGHEST)

    image = jnp.einsum("ksr,krv->ksv", target_basis, coeffs, precision=HIGHEST)
    forward_image = reversal.place([reversal.send(image, k) for k in range(leaves)])

    for i in range(len(steps) - 2, -1, -1):
        product = jnp.einsum("nij,niv->njv", levels[i], back, precision=HIGHEST)
        kept = jnp.where(uppers[i], product[:, rank:], product[:, :rank])
        sent = jnp.where(uppers[i], product[:, :rank], product[:, rank:])
        back = kept + pair_exchange(sent, *steps[i])
    for level in range(local_bits - 1, -1, -1):
        back = local_reverse(back, transfer[level], level)
    adjoint = jnp.einsum("ksr,krv->ksv", source_basis, back, precision=HIGHEST)
    return forward_image.reshape(leaves * leaf, vecs), adjoint.reshape(leaves * leaf, vecs)


def solution(mesh):
    placed = (
        P(BOTH, None),
        P(BOTH),
        P(BOTH, None, None),
        P(None, BOTH, None, None),
        P(BOTH, None, None),
    )
    return jax.shard_map(
        body, mesh=mesh, in_specs=placed, out_specs=(P(BOTH, None), P(BOTH, None)), check_vma=False
    )
```

time: 131 us -> 80.8 us (0.62)
  waiting for transfers between devices: 61.2 us -> 37.8 us
  blocking collectives: 17.7 us -> 0 us
  local copies, waits for them, and re-layouts: 11.9 us -> 3.93 us
  other arithmetic: 2.2 us -> 0.21 us
    all_to_all x4 -> x0, waiting for transfers between devices: 24.4 us -> none  [the longest x2 12.2 us: send_fwd_col(): lax.all_to_all(merged, 'col', split_axis=0, concat_axis=0, tiled=True)]
    all_to_all x2 -> x0, blocking collectives: 17.7 us -> none  [the longest x1 10.4 us: send_back_col(): lax.all_to_all(merged, 'col', split_axis=0, concat_axis=0, tiled=True)]
    ppermute x10 -> x18, starting transfers between devices: 13.6 us -> 27.9 us  [the longest x10 18.8 us: pair_exchange(): return lax.ppermute(block, axis, [(i, i ^ 1 << bit) for i in range(count)])]
    all_to_all x4 -> x0, starting transfers between devices: 13.8 us -> none  [the longest x2 6.99 us: send_fwd_col(): lax.all_to_all(merged, 'col', split_axis=0, concat_axis=0, tiled=True)]
    reshape x7 -> x1, local copies, waits for them, and re-layouts: 3.45 us -> 0.01 us  [body(): diag_blocks = diagonal.reshape(leaves, leaf)]
    unnamed x16 -> x12, local copies, waits for them, and re-layouts: 5.03 us -> 2.28 us
    all_to_all x3 -> x0, other arithmetic: 1.98 us -> none  [the longest x2 1.32 us: send_back_col(): lax.all_to_all(merged, 'col', split_axis=0, concat_axis=0, tiled=True)]
    transpose x4 -> x1, local copies, waits for them, and re-layouts: 1.39 us -> 0.01 us  [local_forward(): out = jnp.einsum('aebij,abjv->aebiv', shaped, stacked, precision=HIGHEST)]
  transfers between devices with their start and end apart: 14 -> 18, of which waited for: 10 -> 9; matrix products, arithmetic and copies ran while one was open for 11% -> 6% of each run, Pallas kernels for 0% -> 0%
where the time goes in v1:
time: 80.8 us; the launch traced here: 80.5 us
  waiting for transfers between devices  37.8 us (47%)
  starting transfers between devices  27.9 us (35%)
  matrix products  9.66 us (12%)
  local copies, waits for them, and re-layouts  3.93 us (5%)
  between operations  1.05 us (1%)
    ppermute x10, waiting for transfers between devices, pair_exchange(): return lax.ppermute(block, axis, [(i, i ^ 1 << bit) for i in range(count)])  34.3 us
    ppermute x10, starting transfers between devices, pair_exchange(): return lax.ppermute(block, axis, [(i, i ^ 1 << bit) for i in range(count)])  18.8 us
    ppermute x8, starting transfers between devices, send(): return lax.ppermute(picked, BOTH, self.route(k))  9.1 us
    ppermute x8, waiting for transfers between devices, send(): return lax.ppermute(picked, BOTH, self.route(k))  3.41 us
    dot_general x4, matrix products, body(): product = jnp.einsum('nij,niv->njv', levels[i], back, precision=HIGHEST)  2.38 us
    unnamed x12, local copies, waits for them, and re-layouts  2.28 us
  transfers between devices with their start and end apart: 18, of which 9 were waited for; matrix products, arithmetic and copies ran while one was open for 6% of the time, Pallas kernels for 0%

profile of v1, /device:TPU:0, one launch (start us, length us, event | category | flops | bytes accessed | tf_op | source)
XLA Modules:
  0.0 80.5 jit_solution(3853115678069073149)
XLA Ops:
  0.6 0.0 copy-start
  0.7 1.0 %copy-done = f32[1024,128]{1,0:T(8,128)S(1)} copy-done((f32[1024,128]{1,0:T(8,128)S(1)}, f32[1024,128]{1,0:T(8,128)}, u32[]{:S(2)}) %copy-start) | copy-done | bytes 524312
  1.7 1.4 %fusion.77 = f32[4,64,128]{2,1,0:T(8,128)S(1)} fusion(f32[4,256,64]{1,2,0:T(8,128)} %param.7, f32[4,256,128]{2,1,0:T(8,128)S(1)} %bitcast.152), kind=kOutput, calls=%fused_computation.124 | convolution fusion | flops 100663296 | bytes 917504 | tf_op jit(solution)/shard_map/ksr,ksv->krv/dot_general | solution.py:96
  3.1 0.3 convolution_bitcast_fusion.11
  3.4 0.3 convolution_bitcast_fusion.10
  3.7 0.6 collective-permute-start
  4.3 0.7 copy-done.5
  5.0 2.6 %collective-permute-start.11 = (f32[256]{0:T(256)S(1)}, f32[256]{0:T(256)S(1)}, u32[]{:S(2)}, u32[]{:S(2)}) collective-permute-start(f32[256]{0:T(256)S(1)} %bitcast.166), channel_id=1, source_target_pairs={{0,16},{1,20},{2,18},{3,22},{4,17},{5,21},{6,19},{7,23},{8,24},{9,... | collective-permute-start | bytes 3080 | tf_op jit(solution)/shard_map/ppermute | solution.py:44
  7.6 0.6 collective-permute-start.9
  8.3 1.5 %collective-permute-start.12 = (f32[256]{0:T(256)S(1)}, f32[256]{0:T(256)S(1)}, u32[]{:S(2)}, u32[]{:S(2)}) collective-permute-start(f32[256]{0:T(256)S(1)} %bitcast.165), channel_id=1, source_target_pairs={{0,24},{1,28},{2,26},{3,30},{4,25},{5,29},{6,27},{7,31},{8,16},{9,... | collective-permute-start | bytes 3080 | tf_op jit(solution)/shard_map/ppermute | solution.py:44
  9.7 0.1 collective-permute-start.10
  9.9 0.0 collective-permute-done.9
  9.9 3.4 %collective-permute-done.10 = f32[256]{0:T(256)S(1)} collective-permute-done((f32[256]{0:T(256)S(1)}, f32[256]{0:T(256)S(1)}, u32[]{:S(2)}, u32[]{:S(2)}) %collective-permute-start.10) | collective-permute-done | bytes 1056 | tf_op jit(solution)/shard_map/ppermute | solution.py:44
  13.4 0.0 collective-permute-done.11
  13.4 0.0 collective-permute-done.12
  13.4 0.0 collective-permute-done
  13.5 0.0 copy-start.2
  13.5 0.3 convolution_bitcast_fusion.9
  13.8 1.6 %collective-permute-start.1 = (f32[4,64,128]{2,1,0:T(8,128)S(1)}, f32[4,64,128]{2,1,0:T(8,128)S(1)}, u32[]{:S(2)}, u32[]{:S(2)}) collective-permute-start(f32[4,64,128]{2,1,0:T(8,128)S(1)} %convolution_bitcast_fusion.9), channel_id=1, source_target_pairs={{0,2},{1,3},{2,0},{3,1},{4,6},{5,7},{6,4},{7,5},{8,10},{9,11},{10,... | collective-permute-start | bytes 393224 | tf_op jit(solution)/shard_map/ppermute | solution.py:19
  15.5 0.4 fusion
  15.9 3.0 %collective-permute-done.1 = f32[4,64,128]{2,1,0:T(8,128)S(1)} collective-permute-done((f32[4,64,128]{2,1,0:T(8,128)S(1)}, f32[4,64,128]{2,1,0:T(8,128)S(1)}, u32[]{:S(2)}, u32[]{:S(2)}) %collective-permute-start.1) | collective-permute-done | bytes 131104 | tf_op jit(solution)/shard_map/ppermute | solution.py:19
  18.9 0.3 convolution_bitcast_fusion.8
  19.3 7.1 %collective-permute-start.2 = (f32[4,64,128]{2,1,0:T(8,128)S(1)}, f32[4,64,128]{2,1,0:T(8,128)S(1)}, u32[]{:S(2)}, u32[]{:S(2)}) collective-permute-start(f32[4,64,128]{2,1,0:T(8,128)S(1)} %convolution_bitcast_fusion.8), channel_id=1, source_target_pairs={{0,4},{1,5},{2,6},{3,7},{4,0},{5,1},{6,2},{7,3},{8,12},{9,13},{10,... | collective-permute-start | bytes 393224 | tf_op jit(solution)/shard_map/ppermute | solution.py:19
  26.3 0.3 fusion.23
  26.6 6.4 %collective-permute-done.2 = f32[4,64,128]{2,1,0:T(8,128)S(1)} collective-permute-done((f32[4,64,128]{2,1,0:T(8,128)S(1)}, f32[4,64,128]{2,1,0:T(8,128)S(1)}, u32[]{:S(2)}, u32[]{:S(2)}) %collective-permute-start.2) | collective-permute-done | bytes 131104 | tf_op jit(solution)/shard_map/ppermute | solution.py:19
  33.0 0.3 convolution_bitcast_fusion.7
  33.3 1.6 %collective-permute-start.3 = (f32[4,64,128]{2,1,0:T(8,128)S(1)}, f32[4,64,128]{2,1,0:T(8,128)S(1)}, u32[]{:S(2)}, u32[]{:S(2)}) collective-permute-start(f32[4,64,128]{2,1,0:T(8,128)S(1)} %convolution_bitcast_fusion.7), channel_id=1, source_target_pairs={{0,8},{8,0},{16,24},{24,16},{1,9},{9,1},{17,25},{25,17},{2,10},{10... | collective-permute-start | bytes 393224 | tf_op jit(solution)/shard_map/ppermute | solution.py:19
  34.9 0.6 convolution_bitcast_fusion.5
  35.5 3.6 %collective-permute-done.3 = f32[4,64,128]{2,1,0:T(8,128)S(1)} collective-permute-done((f32[4,64,128]{2,1,0:T(8,128)S(1)}, f32[4,64,128]{2,1,0:T(8,128)S(1)}, u32[]{:S(2)}, u32[]{:S(2)}) %collective-permute-start.3) | collective-permute-done | bytes 131104 | tf_op jit(solution)/shard_map/ppermute | solution.py:19
  39.2 0.3 convolution_bitcast_fusion.6
  39.5 1.6 %collective-permute-start.4 = (f32[4,64,128]{2,1,0:T(8,128)S(1)}, f32[4,64,128]{2,1,0:T(8,128)S(1)}, u32[]{:S(2)}, u32[]{:S(2)}) collective-permute-start(f32[4,64,128]{2,1,0:T(8,128)S(1)} %convolution_bitcast_fusion.6), channel_id=1, source_target_pairs={{0,16},{8,24},{16,0},{24,8},{1,17},{9,25},{17,1},{25,9},{2,18},{10... | collective-permute-start | bytes 393224 | tf_op jit(solution)/shard_map/ppermute | solution.py:19
  41.1 0.6 collective-permute-start.13
  41.7 4.2 %collective-permute-done.4 = f32[4,64,128]{2,1,0:T(8,128)S(1)} collective-permute-done((f32[4,64,128]{2,1,0:T(8,128)S(1)}, f32[4,64,128]{2,1,0:T(8,128)S(1)}, u32[]{:S(2)}, u32[]{:S(2)}) %collective-permute-start.4) | collective-permute-done | bytes 131104 | tf_op jit(solution)/shard_map/ppermute | solution.py:19
  45.9 0.3 fusion.15
  46.2 1.0 %collective-permute-done.13 = f32[4,64,128]{2,1,0:T(8,128)S(1)} collective-permute-done((f32[4,64,128]{2,1,0:T(8,128)S(1)}, f32[4,64,128]{2,1,0:T(8,128)S(1)}, u32[]{:S(2)}, u32[]{:S(2)}) %collective-permute-start.13) | collective-permute-done | bytes 131104 | tf_op jit(solution)/shard_map/ppermute | solution.py:19
  47.3 0.4 fusion.14
  47.6 0.6 convolution_bitcast_fusion.4
  48.3 1.1 %collective-permute-start.14 = (f32[4,64,128]{2,1,0:T(8,128)S(1)}, f32[4,64,128]{2,1,0:T(8,128)S(1)}, u32[]{:S(2)}, u32[]{:S(2)}) collective-permute-start(f32[4,64,128]{2,1,0:T(8,128)S(1)} %slice_select_fusion.3), channel_id=1, source_target_pairs={{0,8},{8,0},{16,24},{24,16},{1,9},{9,1},{17,25},{25,17},{2,10},{10... | collective-permute-start | bytes 393224 | tf_op jit(solution)/shard_map/ppermute | solution.py:19
  49.4 0.6 fusion.78
  50.1 2.0 %collective-permute-start.8 = (f32[256,128]{0,1:T(8,128)S(1)}, f32[256,128]{0,1:T(8,128)S(1)}, u32[]{:S(2)}, u32[]{:S(2)}) collective-permute-start(f32[256,128]{0,1:T(8,128)S(1)} %get-tuple-element.4), channel_id=1, source_target_pairs={{0,24},{1,28},{2,26},{3,30},{4,25},{5,29},{6,27},{7,31},{8,16},{9,... | collective-permute-start | bytes 393224 | tf_op jit(solution)/shard_map/ppermute | solution.py:44
  52.1 0.5 collective-permute-start.7
  52.6 1.1 %collective-permute-start.6 = (f32[256,128]{0,1:T(8,128)S(1)}, f32[256,128]{0,1:T(8,128)S(1)}, u32[]{:S(2)}, u32[]{:S(2)}) collective-permute-start(f32[256,128]{0,1:T(8,128)S(1)} %get-tuple-element.6), channel_id=1, source_target_pairs={{0,8},{1,12},{2,10},{3,14},{4,9},{5,13},{6,11},{7,15},{8,0},{9,4},... | collective-permute-start | bytes 393224 | tf_op jit(solution)/shard_map/ppermute | solution.py:44
  53.6 0.7 collective-permute-start.5
  54.3 0.0 collective-permute-done.14
  54.3 0.6 convolution_bitcast_fusion.3
  54.9 4.6 %collective-permute-start.15 = (f32[4,64,128]{2,1,0:T(8,128)S(1)}, f32[4,64,128]{2,1,0:T(8,128)S(1)}, u32[]{:S(2)}, u32[]{:S(2)}) collective-permute-start(f32[4,64,128]{2,1,0:T(8,128)S(1)} %slice_select_fusion.2), channel_id=1, source_target_pairs={{0,4},{1,5},{2,6},{3,7},{4,0},{5,1},{6,2},{7,3},{8,12},{9,13},{10,... | collective-permute-start | bytes 393224 | tf_op jit(solution)/shard_map/ppermute | solution.py:19
  59.6 10.2 %collective-permute-done.15 = f32[4,64,128]{2,1,0:T(8,128)S(1)} collective-permute-done((f32[4,64,128]{2,1,0:T(8,128)S(1)}, f32[4,64,128]{2,1,0:T(8,128)S(1)}, u32[]{:S(2)}, u32[]{:S(2)}) %collective-permute-start.15) | collective-permute-done | bytes 131104 | tf_op jit(solution)/shard_map/ppermute | solution.py:19
  69.8 0.6 convolution_bitcast_fusion.2
  70.4 0.1 collective-permute-start.16
  70.5 0.0 collective-permute-done.6
  70.5 4.9 %collective-permute-done.16 = f32[4,64,128]{2,1,0:T(8,128)S(1)} collective-permute-done((f32[4,64,128]{2,1,0:T(8,128)S(1)}, f32[4,64,128]{2,1,0:T(8,128)S(1)}, u32[]{:S(2)}, u32[]{:S(2)}) %collective-permute-start.16) | collective-permute-done | bytes 131104 | tf_op jit(solution)/shard_map/ppermute | solution.py:19
  75.5 0.6 convolution_bitcast_fusion.1
  76.1 0.1 collective-permute-start.17
  76.2 0.0 collective-permute-done.8
  76.2 0.1 copy.18
  76.3 0.2 copy.17
  76.5 0.0 copy-start.4
  76.5 1.0 %collective-permute-done.17 = f32[4,64,128]{2,1,0:T(8,128)S(1)} collective-permute-done((f32[4,64,128]{2,1,0:T(8,128)S(1)}, f32[4,64,128]{2,1,0:T(8,128)S(1)}, u32[]{:S(2)}, u32[]{:S(2)}) %collective-permute-start.17) | collective-permute-done | bytes 131104 | tf_op jit(solution)/shard_map/ppermute | solution.py:19
  77.5 0.4 fusion.79
  77.9 0.0 copy-start.3
  77.9 0.4 fusion.20
  78.3 0.5 copy-done.3
  78.9 0.6 convolution_bitcast_fusion
  79.5 1.0 %copy.22 = f32[4,256,128]{2,1,0:T(8,128)} copy(f32[4,256,128]{1,2,0:T(8,128)S(1)} %convolution_bitcast_fusion) | data formatting | bytes 1048576 | tf_op jit(solution)/shard_map/ksr,krv->ksv/dot_general | solution.py:125
  (35 shorter events, 0.6 us)
Async XLA Ops:
  0.6 1.0 %copy-start = (f32[1024,128]{1,0:T(8,128)S(1)}, f32[1024,128]{1,0:T(8,128)}, u32[]{:S(2)}) copy-start(f32[1024,128]{1,0:T(8,128)} %param.5) | copy-start | bytes 1572868
  0.6 2.5 %copy-start.1 = (f32[7,4,64,128]{3,2,1,0:T(8,128)S(1)}, f32[7,4,64,128]{3,2,1,0:T(8,128)}, u32[]{:S(2)}) copy-start(f32[7,4,64,128]{3,2,1,0:T(8,128)} %param.8) | copy-start | bytes 2752516
  3.7 9.7 %collective-permute-start = (f32[4,64,128]{2,1,0:T(8,128)S(1)}, f32[4,64,128]{2,1,0:T(8,128)S(1)}, u32[]{:S(2)}, u32[]{:S(2)}) collective-permute-start(f32[4,64,128]{2,1,0:T(8,128)S(1)} %bitcast.160), channel_id=1, source_target_pairs={{0,1},{1,0},{2,3},{3,2},{4,5},{5,4},{6,7},{7,6},{8,9},{9,8},{10,11... | collective-permute-start | bytes 393224 | tf_op jit(solution)/shard_map/ppermute | solution.py:19
  4.3 0.7 copy-start.5
  5.0 8.4 %collective-permute-start.11 = (f32[256]{0:T(256)S(1)}, f32[256]{0:T(256)S(1)}, u32[]{:S(2)}, u32[]{:S(2)}) collective-permute-start(f32[256]{0:T(256)S(1)} %bitcast.166), channel_id=1, source_target_pairs={{0,16},{1,20},{2,18},{3,22},{4,17},{5,21},{6,19},{7,23},{8,24},{9,... | collective-permute-start | bytes 3080 | tf_op jit(solution)/shard_map/ppermute | solution.py:44
  7.6 2.3 %collective-permute-start.9 = (f32[256]{0:T(256)S(1)}, f32[256]{0:T(256)S(1)}, u32[]{:S(2)}, u32[]{:S(2)}) collective-permute-start(f32[256]{0:T(256)S(1)} %bitcast.170), channel_id=1, source_target_pairs={{0,0},{1,4},{2,2},{3,6},{4,1},{5,5},{6,3},{7,7},{8,8},{9,12},{10,1... | collective-permute-start | bytes 3080 | tf_op jit(solution)/shard_map/ppermute | solution.py:44
  8.3 5.1 %collective-permute-start.12 = (f32[256]{0:T(256)S(1)}, f32[256]{0:T(256)S(1)}, u32[]{:S(2)}, u32[]{:S(2)}) collective-permute-start(f32[256]{0:T(256)S(1)} %bitcast.165), channel_id=1, source_target_pairs={{0,24},{1,28},{2,26},{3,30},{4,25},{5,29},{6,27},{7,31},{8,16},{9,... | collective-permute-start | bytes 3080 | tf_op jit(solution)/shard_map/ppermute | solution.py:44
  9.7 3.6 %collective-permute-start.10 = (f32[256]{0:T(256)S(1)}, f32[256]{0:T(256)S(1)}, u32[]{:S(2)}, u32[]{:S(2)}) collective-permute-start(f32[256]{0:T(256)S(1)} %bitcast.169), channel_id=1, source_target_pairs={{0,8},{1,12},{2,10},{3,14},{4,9},{5,13},{6,11},{7,15},{8,0},{9,4},... | collective-permute-start | bytes 3080 | tf_op jit(solution)/shard_map/ppermute | solution.py:44
  13.5 2.0 %copy-start.2 = (f32[4,256,64]{1,2,0:T(8,128)S(1)}, f32[4,256,64]{1,2,0:T(8,128)}, u32[]{:S(2)}) copy-start(f32[4,256,64]{1,2,0:T(8,128)} %param.9) | copy-start | bytes 786436
  13.8 5.0 %collective-permute-start.1 = (f32[4,64,128]{2,1,0:T(8,128)S(1)}, f32[4,64,128]{2,1,0:T(8,128)S(1)}, u32[]{:S(2)}, u32[]{:S(2)}) collective-permute-start(f32[4,64,128]{2,1,0:T(8,128)S(1)} %convolution_bitcast_fusion.9), channel_id=1, source_target_pairs={{0,2},{1,3},{2,0},{3,1},{4,6},{5,7},{6,4},{7,5},{8,10},{9,11},{10,... | collective-permute-start | bytes 393224 | tf_op jit(solution)/shard_map/ppermute | solution.py:19
  19.3 13.7 %collective-permute-start.2 = (f32[4,64,128]{2,1,0:T(8,128)S(1)}, f32[4,64,128]{2,1,0:T(8,128)S(1)}, u32[]{:S(2)}, u32[]{:S(2)}) collective-permute-start(f32[4,64,128]{2,1,0:T(8,128)S(1)} %convolution_bitcast_fusion.8), channel_id=1, source_target_pairs={{0,4},{1,5},{2,6},{3,7},{4,0},{5,1},{6,2},{7,3},{8,12},{9,13},{10,... | collective-permute-start | bytes 393224 | tf_op jit(solution)/shard_map/ppermute | solution.py:19
  33.3 5.8 %collective-permute-start.3 = (f32[4,64,128]{2,1,0:T(8,128)S(1)}, f32[4,64,128]{2,1,0:T(8,128)S(1)}, u32[]{:S(2)}, u32[]{:S(2)}) collective-permute-start(f32[4,64,128]{2,1,0:T(8,128)S(1)} %convolution_bitcast_fusion.7), channel_id=1, source_target_pairs={{0,8},{8,0},{16,24},{24,16},{1,9},{9,1},{17,25},{25,17},{2,10},{10... | collective-permute-start | bytes 393224 | tf_op jit(solution)/shard_map/ppermute | solution.py:19
  39.5 6.3 %collective-permute-start.4 = (f32[4,64,128]{2,1,0:T(8,128)S(1)}, f32[4,64,128]{2,1,0:T(8,128)S(1)}, u32[]{:S(2)}, u32[]{:S(2)}) collective-permute-start(f32[4,64,128]{2,1,0:T(8,128)S(1)} %convolution_bitcast_fusion.6), channel_id=1, source_target_pairs={{0,16},{8,24},{16,0},{24,8},{1,17},{9,25},{17,1},{25,9},{2,18},{10... | collective-permute-start | bytes 393224 | tf_op jit(solution)/shard_map/ppermute | solution.py:19
  41.1 6.1 %collective-permute-start.13 = (f32[4,64,128]{2,1,0:T(8,128)S(1)}, f32[4,64,128]{2,1,0:T(8,128)S(1)}, u32[]{:S(2)}, u32[]{:S(2)}) collective-permute-start(f32[4,64,128]{2,1,0:T(8,128)S(1)} %slice_select_fusion.4), channel_id=1, source_target_pairs={{0,16},{8,24},{16,0},{24,8},{1,17},{9,25},{17,1},{25,9},{2,18},{10... | collective-permute-start | bytes 393224 | tf_op jit(solution)/shard_map/ppermute | solution.py:19
  48.3 6.0 %collective-permute-start.14 = (f32[4,64,128]{2,1,0:T(8,128)S(1)}, f32[4,64,128]{2,1,0:T(8,128)S(1)}, u32[]{:S(2)}, u32[]{:S(2)}) collective-permute-start(f32[4,64,128]{2,1,0:T(8,128)S(1)} %slice_select_fusion.3), channel_id=1, source_target_pairs={{0,8},{8,0},{16,24},{24,16},{1,9},{9,1},{17,25},{25,17},{2,10},{10... | collective-permute-start | bytes 393224 | tf_op jit(solution)/shard_map/ppermute | solution.py:19
  50.1 26.1 %collective-permute-start.8 = (f32[256,128]{0,1:T(8,128)S(1)}, f32[256,128]{0,1:T(8,128)S(1)}, u32[]{:S(2)}, u32[]{:S(2)}) collective-permute-start(f32[256,128]{0,1:T(8,128)S(1)} %get-tuple-element.4), channel_id=1, source_target_pairs={{0,24},{1,28},{2,26},{3,30},{4,25},{5,29},{6,27},{7,31},{8,16},{9,... | collective-permute-start | bytes 393224 | tf_op jit(solution)/shard_map/ppermute | solution.py:44
  52.1 24.1 %collective-permute-start.7 = (f32[256,128]{0,1:T(8,128)S(1)}, f32[256,128]{0,1:T(8,128)S(1)}, u32[]{:S(2)}, u32[]{:S(2)}) collective-permute-start(f32[256,128]{0,1:T(8,128)S(1)} %get-tuple-element.5), channel_id=1, source_target_pairs={{0,16},{1,20},{2,18},{3,22},{4,17},{5,21},{6,19},{7,23},{8,24},{9,... | collective-permute-start | bytes 393224 | tf_op jit(solution)/shard_map/ppermute | solution.py:44
  52.6 17.9 %collective-permute-start.6 = (f32[256,128]{0,1:T(8,128)S(1)}, f32[256,128]{0,1:T(8,128)S(1)}, u32[]{:S(2)}, u32[]{:S(2)}) collective-permute-start(f32[256,128]{0,1:T(8,128)S(1)} %get-tuple-element.6), channel_id=1, source_target_pairs={{0,8},{1,12},{2,10},{3,14},{4,9},{5,13},{6,11},{7,15},{8,0},{9,4},... | collective-permute-start | bytes 393224 | tf_op jit(solution)/shard_map/ppermute | solution.py:44
  53.6 5.9 %collective-permute-start.5 = (f32[256,128]{0,1:T(8,128)S(1)}, f32[256,128]{0,1:T(8,128)S(1)}, u32[]{:S(2)}, u32[]{:S(2)}) collective-permute-start(f32[256,128]{0,1:T(8,128)S(1)} %get-tuple-element.7), channel_id=1, source_target_pairs={{0,0},{1,4},{2,2},{3,6},{4,1},{5,5},{6,3},{7,7},{8,8},{9,12},{10,1... | collective-permute-start | bytes 393224 | tf_op jit(solution)/shard_map/ppermute | solution.py:44
  54.9 14.9 %collective-permute-start.15 = (f32[4,64,128]{2,1,0:T(8,128)S(1)}, f32[4,64,128]{2,1,0:T(8,128)S(1)}, u32[]{:S(2)}, u32[]{:S(2)}) collective-permute-start(f32[4,64,128]{2,1,0:T(8,128)S(1)} %slice_select_fusion.2), channel_id=1, source_target_pairs={{0,4},{1,5},{2,6},{3,7},{4,0},{5,1},{6,2},{7,3},{8,12},{9,13},{10,... | collective-permute-start | bytes 393224 | tf_op jit(solution)/shard_map/ppermute | solution.py:19
  70.4 5.0 %collective-permute-start.16 = (f32[4,64,128]{2,1,0:T(8,128)S(1)}, f32[4,64,128]{2,1,0:T(8,128)S(1)}, u32[]{:S(2)}, u32[]{:S(2)}) collective-permute-start(f32[4,64,128]{2,1,0:T(8,128)S(1)} %slice_select_fusion.1), channel_id=1, source_target_pairs={{0,2},{1,3},{2,0},{3,1},{4,6},{5,7},{6,4},{7,5},{8,10},{9,11},{10,... | collective-permute-start | bytes 393224 | tf_op jit(solution)/shard_map/ppermute | solution.py:19
  76.1 1.4 %collective-permute-start.17 = (f32[4,64,128]{2,1,0:T(8,128)S(1)}, f32[4,64,128]{2,1,0:T(8,128)S(1)}, u32[]{:S(2)}, u32[]{:S(2)}) collective-permute-start(f32[4,64,128]{2,1,0:T(8,128)S(1)} %slice_select_fusion), channel_id=1, source_target_pairs={{0,1},{1,0},{2,3},{3,2},{4,5},{5,4},{6,7},{7,6},{8,9},{9,8},{10,11... | collective-permute-start | bytes 393224 | tf_op jit(solution)/shard_map/ppermute | solution.py:19
  76.5 1.8 %copy-start.4 = (f32[4,256,128]{2,1,0:T(8,128)}, f32[4,256,128]{2,1,0:T(8,128)S(1)}, u32[]{:S(2)}) copy-start(f32[4,256,128]{2,1,0:T(8,128)S(1)} %constant_dynamic-update-slice_fusion) | copy-start | bytes 1572868
  77.9 1.0 %copy-start.3 = (f32[4,256,64]{1,2,0:T(8,128)S(1)}, f32[4,256,64]{1,2,0:T(8,128)}, u32[]{:S(2)}) copy-start(f32[4,256,64]{1,2,0:T(8,128)} %param.7) | copy-start | bytes 786436

commit v2 on v1

v2 whole, which is shorter than its diff:
```python
import jax
import jax.numpy as jnp
from jax import lax
from jax.sharding import PartitionSpec as P

HIGHEST = lax.Precision.HIGHEST
BOTH = ("row", "col")


def reverse_bits(value, bits):
    out = 0
    for i in range(bits):
        out = out | ((value >> i) & 1) << (bits - 1 - i)
    return out


class Places:
    def __init__(self, slot_bits):
        self.devices = lax.axis_size("row") * lax.axis_size("col")
        self.slot_bits = slot_bits
        self.low_bits = self.devices.bit_length() - 1 - slot_bits
        self.place = lax.axis_index("row") * lax.axis_size("col") + lax.axis_index("col")
        self.top = self.place >> self.low_bits

    def permute(self, block, route):
        return lax.ppermute(block, BOTH, [(d, route(d)) for d in range(self.devices)])

    def partner(self, block, bit):
        return self.permute(block, lambda d: d ^ (1 << bit))

    def upper(self, bit):
        return (self.place >> bit) & 1 == 1

    def reverse_low(self, block):
        low = self.low_bits
        return self.permute(
            block, lambda d: (d >> low) << low | reverse_bits(d & (2**low - 1), low)
        )

    def slot(self, k):
        return reverse_bits(self.top ^ k, self.slot_bits)

    def swap(self, blocks):
        out = blocks
        for k in range(1, 2**self.slot_bits):
            picked = lax.dynamic_index_in_dim(blocks, self.slot(k), 0, keepdims=False)
            moved = self.permute(picked, lambda d: d ^ (k << self.low_bits))
            out = lax.dynamic_update_index_in_dim(out, moved, self.slot(k), 0)
        return out


def local_forward(coeffs, blocks, bit):
    count, rank, vecs = coeffs.shape
    low = 2**bit
    parted = coeffs.reshape(count // (2 * low), 2, low, rank, vecs)
    stacked = jnp.concatenate([parted[:, 0], parted[:, 1]], axis=2)
    shaped = blocks.reshape(count // (2 * low), 2, low, rank, 2 * rank)
    out = jnp.einsum("aebij,abjv->aebiv", shaped, stacked, precision=HIGHEST)
    return out.reshape(count, rank, vecs)


def local_reverse(coeffs, blocks, bit):
    count, rank, vecs = coeffs.shape
    low = 2**bit
    parted = coeffs.reshape(count // (2 * low), 2, low, rank, vecs)
    shaped = blocks.reshape(count // (2 * low), 2, low, rank, 2 * rank)
    out = jnp.einsum("aebij,aebiv->abjv", shaped, parted, precision=HIGHEST)
    halves = out.reshape(count // (2 * low), low, 2, rank, vecs).transpose(0, 2, 1, 3, 4)
    return halves.reshape(count, rank, vecs)


def body(vectors, diagonal, source_basis, transfer, target_basis):
    leaves, leaf, rank = source_basis.shape
    vecs = vectors.shape[-1]
    slot_bits = leaves.bit_length() - 1
    places = Places(slot_bits)
    pair_bits = range(places.low_bits)
    pair_levels = [transfer[slot_bits + bit] for bit in pair_bits]

    basis_t = jnp.swapaxes(target_basis, 1, 2)
    tops = [transfer[slot_bits + places.low_bits + j] for j in range(slot_bits)]
    moving = jnp.concatenate(
        [t.reshape(leaves, -1) for t in tops] + [basis_t.reshape(leaves, -1)], axis=1
    ).reshape(leaves, -1, 128)
    moved = places.swap(moving).reshape(leaves, -1)
    size = rank * 2 * rank
    tops = [
        moved[:, j * size : (j + 1) * size].reshape(leaves, rank, 2 * rank)
        for j in range(slot_bits)
    ]
    basis_t = moved[:, slot_bits * size :].reshape(leaves, rank, leaf)
    weights = places.reverse_low(diagonal).reshape(leaves, leaf)
    gram = jnp.einsum(
        "krs,kts->krt", basis_t * weights[:, None, :], basis_t, precision=HIGHEST
    )
    image_basis_t = places.reverse_low(basis_t)
    wide = jnp.eye(leaves * rank, dtype=jnp.float32).reshape(leaves, rank, leaves * rank)
    for j in range(slot_bits):
        wide = local_forward(wide, tops[j], slot_bits - 1 - j)
    middle = jnp.einsum("krt,kti->kri", gram, wide, precision=HIGHEST)
    middle = jnp.einsum("krj,kri->ji", wide, middle, precision=HIGHEST)

    coeffs = jnp.einsum(
        "ksr,ksv->krv", source_basis, vectors.reshape(leaves, leaf, vecs), precision=HIGHEST
    )
    for level in range(slot_bits):
        coeffs = local_forward(coeffs, transfer[level], level)
    for bit in pair_bits:
        other = places.partner(coeffs, bit)
        lower = jnp.where(places.upper(bit), other, coeffs)
        upper = jnp.where(places.upper(bit), coeffs, other)
        stacked = jnp.concatenate([lower, upper], axis=1)
        coeffs = jnp.einsum("nij,njv->niv", pair_levels[bit], stacked, precision=HIGHEST)

    stacked = places.swap(coeffs).reshape(leaves * rank, vecs)
    back = jnp.einsum("ij,jv->iv", middle, stacked, precision=HIGHEST)
    back = places.swap(back.reshape(leaves, rank, vecs))
    coeffs = jnp.einsum("krj,jv->krv", wide, stacked, precision=HIGHEST)
    image_coeffs = places.reverse_low(coeffs)
    forward_image = jnp.einsum(
        "krs,krv->ksv", image_basis_t, image_coeffs, precision=HIGHEST
    )

    for bit in reversed(pair_bits):
        product = jnp.einsum("nij,niv->njv", pair_levels[bit], back, precision=HIGHEST)
        kept = jnp.where(places.upper(bit), product[:, rank:], product[:, :rank])
        sent = jnp.where(places.upper(bit), product[:, :rank], product[:, rank:])
        back = kept + places.partner(sent, bit)
    for level in range(slot_bits - 1, -1, -1):
        back = local_reverse(back, transfer[level], level)
    adjoint = jnp.einsum("ksr,krv->ksv", source_basis, back, precision=HIGHEST)
    return forward_image.reshape(leaves * leaf, vecs), adjoint.reshape(leaves * leaf, vecs)


def solution(mesh):
    placed = (
        P(BOTH, None),
        P(BOTH),
        P(BOTH, None, None),
        P(None, BOTH, None, None),
        P(BOTH, None, None),
    )
    return jax.shard_map(
        body, mesh=mesh, in_specs=placed, out_specs=(P(BOTH, None), P(BOTH, None)), check_vma=False
    )
```

time: 80.8 us -> 69.8 us (0.86)
  waiting for transfers between devices: 37.8 us -> 31 us
  starting transfers between devices: 27.9 us -> 23.2 us
    ppermute x18, waiting for transfers between devices: 37.8 us -> 31 us  [permute(): lax.ppermute(block, BOTH, [(d, route(d)) for d in range(self.devices)])]
    ppermute x18, starting transfers between devices: 27.9 us -> 23.2 us  [permute(): lax.ppermute(block, BOTH, [(d, route(d)) for d in range(self.devices)])]
    unnamed x12 -> x17, local copies, waits for them, and re-layouts: 2.28 us -> 0.71 us
    slice x1, local copies, waits for them, and re-layouts: 0.02 us -> 1.2 us  [body(): coeffs = local_forward(coeffs, transfer[level], level)]
    dot_general x1, matrix products: 1.4 us -> 0.45 us  [body(): jnp.einsum('ksr,ksv->krv', source_basis, vectors.reshape(leaves, leaf, ve...]
    dot_general x14 -> x12, matrix products: 6.32 us -> 7.15 us  [the longest x1 1.83 us: body(): jnp.einsum('krs,krv->ksv', image_basis_t, image_coeffs, precision=HIGHEST)]
  transfers between devices with their start and end apart: 18 -> 18, of which waited for: 9 -> 9; matrix products, arithmetic and copies ran while one was open for 6% -> 12% of each run, Pallas kernels for 0% -> 0%
where the time goes in v2:
time: 69.8 us; the launch traced here: 69.6 us
  waiting for transfers between devices  31 us (44%)
  starting transfers between devices  23.2 us (33%)
  matrix products  10.3 us (15%)
  local copies, waits for them, and re-layouts  3.56 us (5%)
  between operations  1.2 us (2%)
    ppermute x18, waiting for transfers between devices, permute(): lax.ppermute(block, BOTH, [(d, route(d)) for d in range(self.devices)])  31 us
    ppermute x18, starting transfers between devices, permute(): lax.ppermute(block, BOTH, [(d, route(d)) for d in range(self.devices)])  23.2 us
    dot_general x1, matrix products, body(): jnp.einsum('krs,krv->ksv', image_basis_t, image_coeffs, precision=HIGHEST)  1.83 us
    dot_general x3, matrix products, body(): jnp.einsum('nij,niv->njv', pair_levels[bit], back, precision=HIGHEST)  1.78 us
  transfers between devices with their start and end apart: 18, of which 9 were waited for; matrix products, arithmetic and copies ran while one was open for 12% of the time, Pallas kernels for 0%

profile of v2, /device:TPU:0, one launch (start us, length us, event | category | flops | bytes accessed | tf_op | source)
XLA Modules:
  0.0 69.6 jit_solution(4261155656895576521)
XLA Ops:
  0.6 0.0 copy-start
  0.7 1.2 %fusion.59 = (f32[1,4,64,128]{3,2,1,0:T(8,128)S(1)}, f32[1,4,64,128]{3,2,1,0:T(8,128)S(1)}, f32[1,4,64,128]{3,2,1,0:T(8,128)S(1)}, f32[1,4,64,128]{3,2,1,0:T(8,128)S(1)}) fusion(f32[7,4,64,128]{3,2,1,0:T(8,128)} %param.8), kind=kLoop, calls=%fused_computation.121 | loop fusion | bytes 1048576 | tf_op jit(solution)/shard_map/slice | solution.py:107
  1.9 0.0 copy-done.3
  1.9 0.2 copy.35
  2.1 0.2 copy_bitcast_fusion.3
  2.3 0.1 maximum_bitcast_fusion
  2.4 0.0 copy-start.2
  2.5 0.0 copy-start.4
  2.5 3.0 %collective-permute-start = (f32[256,128]{1,0:T(8,128)S(1)}, f32[256,128]{1,0:T(8,128)S(1)}, u32[]{:S(2)}, u32[]{:S(2)}) collective-permute-start(f32[256,128]{1,0:T(8,128)S(1)} %dynamic-slice_bitcast_fusion.2), channel_id=1, source_target_pairs={{0,8},{1,9},{2,10},{3,11},{4,12},{5,13},{6,14},{7,15},{8,0},{9,1},... | collective-permute-start | bytes 393224 | tf_op jit(solution)/shard_map/ppermute | solution.py:26
  5.5 0.7 collective-permute-start.11
  6.2 0.5 fusion.60
  6.7 0.3 convolution_bitcast_fusion.9
  7.0 0.3 convolution_bitcast_fusion.8
  7.3 4.0 %collective-permute-start.4 = (f32[4,64,128]{2,1,0:T(8,128)S(1)}, f32[4,64,128]{2,1,0:T(8,128)S(1)}, u32[]{:S(2)}, u32[]{:S(2)}) collective-permute-start(f32[4,64,128]{2,1,0:T(8,128)S(1)} %bitcast.255), channel_id=1, source_target_pairs={{0,1},{1,0},{2,3},{3,2},{4,5},{5,4},{6,7},{7,6},{8,9},{9,8},{10,11... | collective-permute-start | bytes 393224 | tf_op jit(solution)/shard_map/ppermute | solution.py:26
  11.3 0.1 fusion.19
  11.4 0.0 copy-start.1
  11.5 0.0 collective-permute-done.11
  11.5 1.6 %collective-permute-start.1 = (f32[256,128]{1,0:T(8,128)S(1)}, f32[256,128]{1,0:T(8,128)S(1)}, u32[]{:S(2)}, u32[]{:S(2)}) collective-permute-start(f32[256,128]{1,0:T(8,128)S(1)} %get-tuple-element.9), channel_id=1, source_target_pairs={{0,16},{1,17},{2,18},{3,19},{4,20},{5,21},{6,22},{7,23},{8,24},{9,... | collective-permute-start | bytes 393224 | tf_op jit(solution)/shard_map/ppermute | solution.py:26
  13.1 0.6 collective-permute-start.2
  13.7 0.3 convolution_bitcast_fusion.7
  14.1 1.6 %collective-permute-start.5 = (f32[4,64,128]{2,1,0:T(8,128)S(1)}, f32[4,64,128]{2,1,0:T(8,128)S(1)}, u32[]{:S(2)}, u32[]{:S(2)}) collective-permute-start(f32[4,64,128]{2,1,0:T(8,128)S(1)} %convolution_bitcast_fusion.7), channel_id=1, source_target_pairs={{0,2},{1,3},{2,0},{3,1},{4,6},{5,7},{6,4},{7,5},{8,10},{9,11},{10,... | collective-permute-start | bytes 393224 | tf_op jit(solution)/shard_map/ppermute | solution.py:26
  15.7 4.1 %collective-permute-done.1 = f32[256,128]{1,0:T(8,128)S(1)} collective-permute-done((f32[256,128]{1,0:T(8,128)S(1)}, f32[256,128]{1,0:T(8,128)S(1)}, u32[]{:S(2)}, u32[]{:S(2)}) %collective-permute-start.1) | collective-permute-done | bytes 131104 | tf_op jit(solution)/shard_map/ppermute | solution.py:26
  19.8 0.0 collective-permute-done.2
  19.9 0.3 copy.59
  20.3 0.4 fusion.3
  20.8 0.3 convolution_bitcast_fusion.6
  21.1 1.6 %collective-permute-start.6 = (f32[4,64,128]{2,1,0:T(8,128)S(1)}, f32[4,64,128]{2,1,0:T(8,128)S(1)}, u32[]{:S(2)}, u32[]{:S(2)}) collective-permute-start(f32[4,64,128]{2,1,0:T(8,128)S(1)} %convolution_bitcast_fusion.6), channel_id=1, source_target_pairs={{0,4},{1,5},{2,6},{3,7},{4,0},{5,1},{6,2},{7,3},{8,12},{9,13},{10,... | collective-permute-start | bytes 393224 | tf_op jit(solution)/shard_map/ppermute | solution.py:26
  22.8 0.4 fusion.1
  23.2 0.4 fusion.6
  23.6 0.2 dot_general.108
  23.8 0.4 convolution_bitcast_fusion.2
  24.2 4.4 %collective-permute-done.6 = f32[4,64,128]{2,1,0:T(8,128)S(1)} collective-permute-done((f32[4,64,128]{2,1,0:T(8,128)S(1)}, f32[4,64,128]{2,1,0:T(8,128)S(1)}, u32[]{:S(2)}, u32[]{:S(2)}) %collective-permute-start.6) | collective-permute-done | bytes 131104 | tf_op jit(solution)/shard_map/ppermute | solution.py:26
  28.6 0.3 fusion.15
  29.0 0.7 %collective-permute-start.7 = (f32[64,128]{1,0:T(8,128)S(1)}, f32[64,128]{1,0:T(8,128)S(1)}, u32[]{:S(2)}, u32[]{:S(2)}) collective-permute-start(f32[64,128]{1,0:T(8,128)S(1)} %get-tuple-element.24), channel_id=1, source_target_pairs={{0,8},{1,9},{2,10},{3,11},{4,12},{5,13},{6,14},{7,15},{8,0},{9,1},... | collective-permute-start | bytes 98312 | tf_op jit(solution)/shard_map/ppermute | solution.py:26
  29.7 1.0 %convolution_bitcast_fusion.1 = f32[4,64,256]{2,1,0:T(8,128)S(1)} fusion(f32[4,64,256,1]{2,1,0,3:T(8,128)S(1)} %convolution_bitcast_fusion.2, f32[4,64,4,64]{1,0,3,2:T(4,128)S(1)} %dot_general.108), kind=kOutput, calls=%fused_computation.1 | convolution fusion | flops 201326592 | bytes 786432 | tf_op jit(solution)/shard_map/krj,kri->ji/dot_general | solution.py:101
  30.7 2.5 %collective-permute-start.8 = (f32[64,128]{1,0:T(8,128)S(1)}, f32[64,128]{1,0:T(8,128)S(1)}, u32[]{:S(2)}, u32[]{:S(2)}) collective-permute-start(f32[64,128]{1,0:T(8,128)S(1)} %get-tuple-element.23), channel_id=1, source_target_pairs={{0,16},{1,17},{2,18},{3,19},{4,20},{5,21},{6,22},{7,23},{8,24},{9,... | collective-permute-start | bytes 98312 | tf_op jit(solution)/shard_map/ppermute | solution.py:26
  33.2 0.9 %collective-permute-start.9 = (f32[64,128]{1,0:T(8,128)S(1)}, f32[64,128]{1,0:T(8,128)S(1)}, u32[]{:S(2)}, u32[]{:S(2)}) collective-permute-start(f32[64,128]{1,0:T(8,128)S(1)} %get-tuple-element.22), channel_id=1, source_target_pairs={{0,24},{1,25},{2,26},{3,27},{4,28},{5,29},{6,30},{7,31},{8,16},{9,... | collective-permute-start | bytes 98312 | tf_op jit(solution)/shard_map/ppermute | solution.py:26
  34.1 0.0 collective-permute-done.7
  34.1 1.0 %collective-permute-done.8 = f32[64,128]{1,0:T(8,128)S(1)} collective-permute-done((f32[64,128]{1,0:T(8,128)S(1)}, f32[64,128]{1,0:T(8,128)S(1)}, u32[]{:S(2)}, u32[]{:S(2)}) %collective-permute-start.8) | collective-permute-done | bytes 32800 | tf_op jit(solution)/shard_map/ppermute | solution.py:26
  35.1 2.9 %collective-permute-done.9 = f32[64,128]{1,0:T(8,128)S(1)} collective-permute-done((f32[64,128]{1,0:T(8,128)S(1)}, f32[64,128]{1,0:T(8,128)S(1)}, u32[]{:S(2)}, u32[]{:S(2)}) %collective-permute-start.9) | collective-permute-done | bytes 32800 | tf_op jit(solution)/shard_map/ppermute | solution.py:26
  38.0 0.4 fusion.63
  38.4 1.5 %collective-permute-start.12 = (f32[64,128]{1,0:T(8,128)S(1)}, f32[64,128]{1,0:T(8,128)S(1)}, u32[]{:S(2)}, u32[]{:S(2)}) collective-permute-start(f32[64,128]{1,0:T(8,128)S(1)} %dynamic-slice_bitcast_fusion.5), channel_id=1, source_target_pairs={{0,8},{1,9},{2,10},{3,11},{4,12},{5,13},{6,14},{7,15},{8,0},{9,1},... | collective-permute-start | bytes 98312 | tf_op jit(solution)/shard_map/ppermute | solution.py:26
  39.8 2.5 %collective-permute-done.12 = f32[64,128]{1,0:T(8,128)S(1)} collective-permute-done((f32[64,128]{1,0:T(8,128)S(1)}, f32[64,128]{1,0:T(8,128)S(1)}, u32[]{:S(2)}, u32[]{:S(2)}) %collective-permute-start.12) | collective-permute-done | bytes 32800 | tf_op jit(solution)/shard_map/ppermute | solution.py:26
  42.4 0.1 collective-permute-start.13
  42.5 2.8 %collective-permute-start.14 = (f32[64,128]{1,0:T(8,128)S(1)}, f32[64,128]{1,0:T(8,128)S(1)}, u32[]{:S(2)}, u32[]{:S(2)}) collective-permute-start(f32[64,128]{1,0:T(8,128)S(1)} %get-tuple-element.19), channel_id=1, source_target_pairs={{0,24},{1,25},{2,26},{3,27},{4,28},{5,29},{6,30},{7,31},{8,16},{9,... | collective-permute-start | bytes 98312 | tf_op jit(solution)/shard_map/ppermute | solution.py:26
  45.3 1.0 %collective-permute-done.13 = f32[64,128]{1,0:T(8,128)S(1)} collective-permute-done((f32[64,128]{1,0:T(8,128)S(1)}, f32[64,128]{1,0:T(8,128)S(1)}, u32[]{:S(2)}, u32[]{:S(2)}) %collective-permute-start.13) | collective-permute-done | bytes 32800 | tf_op jit(solution)/shard_map/ppermute | solution.py:26
  46.4 1.0 %collective-permute-done.14 = f32[64,128]{1,0:T(8,128)S(1)} collective-permute-done((f32[64,128]{1,0:T(8,128)S(1)}, f32[64,128]{1,0:T(8,128)S(1)}, u32[]{:S(2)}, u32[]{:S(2)}) %collective-permute-start.14) | collective-permute-done | bytes 32800 | tf_op jit(solution)/shard_map/ppermute | solution.py:26
  47.3 0.6 convolution_bitcast_fusion.5
  48.0 0.1 collective-permute-start.15
  48.0 0.1 copy.61
  48.1 0.7 collective-permute-start.3
  48.8 9.0 %collective-permute-done.15 = f32[4,64,128]{2,1,0:T(8,128)S(1)} collective-permute-done((f32[4,64,128]{2,1,0:T(8,128)S(1)}, f32[4,64,128]{2,1,0:T(8,128)S(1)}, u32[]{:S(2)}, u32[]{:S(2)}) %collective-permute-start.15) | collective-permute-done | bytes 131104 | tf_op jit(solution)/shard_map/ppermute | solution.py:26
  57.8 0.6 convolution_bitcast_fusion.4
  58.4 0.1 collective-permute-start.16
  58.5 0.4 fusion.61
  58.9 0.7 collective-permute-start.10
  59.5 5.1 %collective-permute-done.16 = f32[4,64,128]{2,1,0:T(8,128)S(1)} collective-permute-done((f32[4,64,128]{2,1,0:T(8,128)S(1)}, f32[4,64,128]{2,1,0:T(8,128)S(1)}, u32[]{:S(2)}, u32[]{:S(2)}) %collective-permute-start.16) | collective-permute-done | bytes 131104 | tf_op jit(solution)/shard_map/ppermute | solution.py:26
  64.6 0.6 convolution_bitcast_fusion.3
  65.2 0.1 collective-permute-start.17
  65.3 1.8 %fusion.62 = f32[4,256,128]{2,1,0:T(8,128)} fusion(f32[4,64,256]{2,1,0:T(8,128)S(1)} %collective-permute-done.3, f32[4,64,128]{2,1,0:T(8,128)S(1)} %collective-permute-done.10), kind=kOutput, calls=%fused_computation.124 | convolution fusion | flops 100663296 | bytes 917504 | tf_op jit(solution)/shard_map/krs,krv->ksv/dot_general | solution.py:120
  67.2 0.4 fusion.64
  67.6 0.4 fusion.24
  68.0 0.6 convolution_bitcast_fusion
  68.6 1.0 %copy.21 = f32[4,256,128]{2,1,0:T(8,128)} copy(f32[4,256,128]{1,2,0:T(8,128)S(1)} %convolution_bitcast_fusion) | data formatting | bytes 1048576 | tf_op jit(solution)/shard_map/ksr,krv->ksv/dot_general | solution.py:131
  (43 shorter events, 0.5 us)
Async XLA Ops:
  0.6 5.6 %copy-start = (f32[1024,128]{1,0:T(8,128)S(1)}, f32[1024,128]{1,0:T(8,128)}, u32[]{:S(2)}) copy-start(f32[1024,128]{1,0:T(8,128)} %param.5) | copy-start | bytes 1572868
  0.7 1.3 %copy-start.3 = (f32[4,256,64]{1,2,0:T(8,128)S(1)}, f32[4,256,64]{1,2,0:T(8,128)}, u32[]{:S(2)}) copy-start(f32[4,256,64]{1,2,0:T(8,128)} %param.9) | copy-start | bytes 786436
  2.4 3.8 %copy-start.2 = (f32[4,256,64]{1,2,0:T(8,128)S(1)}, f32[4,256,64]{1,2,0:T(8,128)}, u32[]{:S(2)}) copy-start(f32[4,256,64]{1,2,0:T(8,128)} %param.7) | copy-start | bytes 786436
  2.5 3.1 %copy-start.4 = (f32[1024]{0:T(1024)S(1)}, f32[1024]{0:T(1024)}, u32[]{:S(2)}) copy-start(f32[1024]{0:T(1024)} %param.6) | copy-start | bytes 12292
  2.5 9.0 %collective-permute-start = (f32[256,128]{1,0:T(8,128)S(1)}, f32[256,128]{1,0:T(8,128)S(1)}, u32[]{:S(2)}, u32[]{:S(2)}) collective-permute-start(f32[256,128]{1,0:T(8,128)S(1)} %dynamic-slice_bitcast_fusion.2), channel_id=1, source_target_pairs={{0,8},{1,9},{2,10},{3,11},{4,12},{5,13},{6,14},{7,15},{8,0},{9,1},... | collective-permute-start | bytes 393224 | tf_op jit(solution)/shard_map/ppermute | solution.py:26
  5.5 5.9 %collective-permute-start.11 = (f32[1024]{0:T(1024)S(1)}, f32[1024]{0:T(1024)S(1)}, u32[]{:S(2)}, u32[]{:S(2)}) collective-permute-start(f32[1024]{0:T(1024)S(1)} %copy-done.4), channel_id=1, source_target_pairs={{0,0},{1,4},{2,2},{3,6},{4,1},{5,5},{6,3},{7,7},{8,8},{9,12},{10,1... | collective-permute-start | bytes 12296 | tf_op jit(solution)/shard_map/ppermute | solution.py:26
  7.3 6.4 %collective-permute-start.4 = (f32[4,64,128]{2,1,0:T(8,128)S(1)}, f32[4,64,128]{2,1,0:T(8,128)S(1)}, u32[]{:S(2)}, u32[]{:S(2)}) collective-permute-start(f32[4,64,128]{2,1,0:T(8,128)S(1)} %bitcast.255), channel_id=1, source_target_pairs={{0,1},{1,0},{2,3},{3,2},{4,5},{5,4},{6,7},{7,6},{8,9},{9,8},{10,11... | collective-permute-start | bytes 393224 | tf_op jit(solution)/shard_map/ppermute | solution.py:26
  11.4 2.3 %copy-start.1 = (f32[7,4,64,128]{3,2,1,0:T(8,128)S(1)}, f32[7,4,64,128]{3,2,1,0:T(8,128)}, u32[]{:S(2)}) copy-start(f32[7,4,64,128]{3,2,1,0:T(8,128)} %param.8) | copy-start | bytes 2752516
  11.5 8.3 %collective-permute-start.1 = (f32[256,128]{1,0:T(8,128)S(1)}, f32[256,128]{1,0:T(8,128)S(1)}, u32[]{:S(2)}, u32[]{:S(2)}) collective-permute-start(f32[256,128]{1,0:T(8,128)S(1)} %get-tuple-element.9), channel_id=1, source_target_pairs={{0,16},{1,17},{2,18},{3,19},{4,20},{5,21},{6,22},{7,23},{8,24},{9,... | collective-permute-start | bytes 393224 | tf_op jit(solution)/shard_map/ppermute | solution.py:26
  13.1 6.7 %collective-permute-start.2 = (f32[256,128]{1,0:T(8,128)S(1)}, f32[256,128]{1,0:T(8,128)S(1)}, u32[]{:S(2)}, u32[]{:S(2)}) collective-permute-start(f32[256,128]{1,0:T(8,128)S(1)} %get-tuple-element.8), channel_id=1, source_target_pairs={{0,24},{1,25},{2,26},{3,27},{4,28},{5,29},{6,30},{7,31},{8,16},{9,... | collective-permute-start | bytes 393224 | tf_op jit(solution)/shard_map/ppermute | solution.py:26
  14.1 6.7 %collective-permute-start.5 = (f32[4,64,128]{2,1,0:T(8,128)S(1)}, f32[4,64,128]{2,1,0:T(8,128)S(1)}, u32[]{:S(2)}, u32[]{:S(2)}) collective-permute-start(f32[4,64,128]{2,1,0:T(8,128)S(1)} %convolution_bitcast_fusion.7), channel_id=1, source_target_pairs={{0,2},{1,3},{2,0},{3,1},{4,6},{5,7},{6,4},{7,5},{8,10},{9,11},{10,... | collective-permute-start | bytes 393224 | tf_op jit(solution)/shard_map/ppermute | solution.py:26
  21.1 7.4 %collective-permute-start.6 = (f32[4,64,128]{2,1,0:T(8,128)S(1)}, f32[4,64,128]{2,1,0:T(8,128)S(1)}, u32[]{:S(2)}, u32[]{:S(2)}) collective-permute-start(f32[4,64,128]{2,1,0:T(8,128)S(1)} %convolution_bitcast_fusion.6), channel_id=1, source_target_pairs={{0,4},{1,5},{2,6},{3,7},{4,0},{5,1},{6,2},{7,3},{8,12},{9,13},{10,... | collective-permute-start | bytes 393224 | tf_op jit(solution)/shard_map/ppermute | solution.py:26
  29.0 5.1 %collective-permute-start.7 = (f32[64,128]{1,0:T(8,128)S(1)}, f32[64,128]{1,0:T(8,128)S(1)}, u32[]{:S(2)}, u32[]{:S(2)}) collective-permute-start(f32[64,128]{1,0:T(8,128)S(1)} %get-tuple-element.24), channel_id=1, source_target_pairs={{0,8},{1,9},{2,10},{3,11},{4,12},{5,13},{6,14},{7,15},{8,0},{9,1},... | collective-permute-start | bytes 98312 | tf_op jit(solution)/shard_map/ppermute | solution.py:26
  30.7 4.4 %collective-permute-start.8 = (f32[64,128]{1,0:T(8,128)S(1)}, f32[64,128]{1,0:T(8,128)S(1)}, u32[]{:S(2)}, u32[]{:S(2)}) collective-permute-start(f32[64,128]{1,0:T(8,128)S(1)} %get-tuple-element.23), channel_id=1, source_target_pairs={{0,16},{1,17},{2,18},{3,19},{4,20},{5,21},{6,22},{7,23},{8,24},{9,... | collective-permute-start | bytes 98312 | tf_op jit(solution)/shard_map/ppermute | solution.py:26
  33.2 4.8 %collective-permute-start.9 = (f32[64,128]{1,0:T(8,128)S(1)}, f32[64,128]{1,0:T(8,128)S(1)}, u32[]{:S(2)}, u32[]{:S(2)}) collective-permute-start(f32[64,128]{1,0:T(8,128)S(1)} %get-tuple-element.22), channel_id=1, source_target_pairs={{0,24},{1,25},{2,26},{3,27},{4,28},{5,29},{6,30},{7,31},{8,16},{9,... | collective-permute-start | bytes 98312 | tf_op jit(solution)/shard_map/ppermute | solution.py:26
  38.4 4.0 %collective-permute-start.12 = (f32[64,128]{1,0:T(8,128)S(1)}, f32[64,128]{1,0:T(8,128)S(1)}, u32[]{:S(2)}, u32[]{:S(2)}) collective-permute-start(f32[64,128]{1,0:T(8,128)S(1)} %dynamic-slice_bitcast_fusion.5), channel_id=1, source_target_pairs={{0,8},{1,9},{2,10},{3,11},{4,12},{5,13},{6,14},{7,15},{8,0},{9,1},... | collective-permute-start | bytes 98312 | tf_op jit(solution)/shard_map/ppermute | solution.py:26
  42.4 4.0 %collective-permute-start.13 = (f32[64,128]{1,0:T(8,128)S(1)}, f32[64,128]{1,0:T(8,128)S(1)}, u32[]{:S(2)}, u32[]{:S(2)}) collective-permute-start(f32[64,128]{1,0:T(8,128)S(1)} %get-tuple-element.20), channel_id=1, source_target_pairs={{0,16},{1,17},{2,18},{3,19},{4,20},{5,21},{6,22},{7,23},{8,24},{9,... | collective-permute-start | bytes 98312 | tf_op jit(solution)/shard_map/ppermute | solution.py:26
  42.5 4.8 %collective-permute-start.14 = (f32[64,128]{1,0:T(8,128)S(1)}, f32[64,128]{1,0:T(8,128)S(1)}, u32[]{:S(2)}, u32[]{:S(2)}) collective-permute-start(f32[64,128]{1,0:T(8,128)S(1)} %get-tuple-element.19), channel_id=1, source_target_pairs={{0,24},{1,25},{2,26},{3,27},{4,28},{5,29},{6,30},{7,31},{8,16},{9,... | collective-permute-start | bytes 98312 | tf_op jit(solution)/shard_map/ppermute | solution.py:26
  48.0 9.8 %collective-permute-start.15 = (f32[4,64,128]{2,1,0:T(8,128)S(1)}, f32[4,64,128]{2,1,0:T(8,128)S(1)}, u32[]{:S(2)}, u32[]{:S(2)}) collective-permute-start(f32[4,64,128]{2,1,0:T(8,128)S(1)} %slice_select_fusion.2), channel_id=1, source_target_pairs={{0,4},{1,5},{2,6},{3,7},{4,0},{5,1},{6,2},{7,3},{8,12},{9,13},{10,... | collective-permute-start | bytes 393224 | tf_op jit(solution)/shard_map/ppermute | solution.py:26
  48.1 17.2 %collective-permute-start.3 = (f32[4,64,256]{2,1,0:T(8,128)S(1)}, f32[4,64,256]{2,1,0:T(8,128)S(1)}, u32[]{:S(2)}, u32[]{:S(2)}) collective-permute-start(f32[4,64,256]{2,1,0:T(8,128)S(1)} %bitcast.261), channel_id=1, source_target_pairs={{0,0},{1,4},{2,2},{3,6},{4,1},{5,5},{6,3},{7,7},{8,8},{9,12},{10,1... | collective-permute-start | bytes 786440 | tf_op jit(solution)/shard_map/ppermute | solution.py:26
  58.4 6.2 %collective-permute-start.16 = (f32[4,64,128]{2,1,0:T(8,128)S(1)}, f32[4,64,128]{2,1,0:T(8,128)S(1)}, u32[]{:S(2)}, u32[]{:S(2)}) collective-permute-start(f32[4,64,128]{2,1,0:T(8,128)S(1)} %slice_select_fusion.1), channel_id=1, source_target_pairs={{0,2},{1,3},{2,0},{3,1},{4,6},{5,7},{6,4},{7,5},{8,10},{9,11},{10,... | collective-permute-start | bytes 393224 | tf_op jit(solution)/shard_map/ppermute | solution.py:26
  58.9 6.4 %collective-permute-start.10 = (f32[4,64,128]{2,1,0:T(8,128)S(1)}, f32[4,64,128]{2,1,0:T(8,128)S(1)}, u32[]{:S(2)}, u32[]{:S(2)}) collective-permute-start(f32[4,64,128]{2,1,0:T(8,128)S(1)} %fusion.61), channel_id=1, source_target_pairs={{0,0},{1,4},{2,2},{3,6},{4,1},{5,5},{6,3},{7,7},{8,8},{9,12},{10,1... | collective-permute-start | bytes 393224 | tf_op jit(solution)/shard_map/ppermute | solution.py:26
  65.2 1.9 %collective-permute-start.17 = (f32[4,64,128]{2,1,0:T(8,128)S(1)}, f32[4,64,128]{2,1,0:T(8,128)S(1)}, u32[]{:S(2)}, u32[]{:S(2)}) collective-permute-start(f32[4,64,128]{2,1,0:T(8,128)S(1)} %slice_select_fusion), channel_id=1, source_target_pairs={{0,1},{1,0},{2,3},{3,2},{4,5},{5,4},{6,7},{7,6},{8,9},{9,8},{10,11... | collective-permute-start | bytes 393224 | tf_op jit(solution)/shard_map/ppermute | solution.py:26

commit v3 on v2

v3 whole, which is shorter than its diff:
```python
import jax
import jax.numpy as jnp
from jax import lax
from jax.sharding import PartitionSpec as P


PRECISION = lax.Precision.HIGH
BOTH = ("row", "col")


def reverse_bits(value, bits):
    out = 0
    for i in range(bits):
        out = out | ((value >> i) & 1) << (bits - 1 - i)
    return out


class Places:
    def __init__(self, slot_bits):
        self.devices = lax.axis_size("row") * lax.axis_size("col")
        self.slot_bits = slot_bits
        self.low_bits = self.devices.bit_length() - 1 - slot_bits
        self.place = lax.axis_index("row") * lax.axis_size("col") + lax.axis_index("col")
        self.top = self.place >> self.low_bits

    def permute(self, block, route):
        return lax.ppermute(block, BOTH, [(d, route(d)) for d in range(self.devices)])

    def partner(self, block, bit):
        return self.permute(block, lambda d: d ^ (1 << bit))

    def upper(self, bit):
        return (self.place >> bit) & 1 == 1

    def reverse_low(self, block):
        low = self.low_bits
        return self.permute(
            block, lambda d: (d >> low) << low | reverse_bits(d & (2**low - 1), low)
        )

    def slot(self, k):
        return reverse_bits(self.top ^ k, self.slot_bits)

    def across(self, block, k):
        return self.permute(block, lambda d: d ^ (k << self.low_bits))

    def gather(self, blocks):
        picked = [
            lax.dynamic_index_in_dim(blocks, self.slot(k), 0, keepdims=False)
            for k in range(2**self.slot_bits)
        ]
        return [b if k == 0 else self.across(b, k) for k, b in enumerate(picked)]

    def scatter(self, blocks):
        arrived = [b if k == 0 else self.across(b, k) for k, b in enumerate(blocks)]
        return self.in_order(arrived)

    def in_order(self, arrived):
        out = jnp.zeros((len(arrived),) + arrived[0].shape, arrived[0].dtype)
        for k, block in enumerate(arrived):
            out = lax.dynamic_update_index_in_dim(out, block, self.slot(k), 0)
        return out


def local_forward(coeffs, blocks, bit):
    count, rank, vecs = coeffs.shape
    low = 2**bit
    parted = coeffs.reshape(count // (2 * low), 2, low, rank, vecs)
    stacked = jnp.concatenate([parted[:, 0], parted[:, 1]], axis=2)
    shaped = blocks.reshape(count // (2 * low), 2, low, rank, 2 * rank)
    out = jnp.einsum("aebij,abjv->aebiv", shaped, stacked, precision=PRECISION)
    return out.reshape(count, rank, vecs)


def local_reverse(coeffs, blocks, bit):
    count, rank, vecs = coeffs.shape
    low = 2**bit
    parted = coeffs.reshape(count // (2 * low), 2, low, rank, vecs)
    shaped = blocks.reshape(count // (2 * low), 2, low, rank, 2 * rank)
    out = jnp.einsum("aebij,aebiv->abjv", shaped, parted, precision=PRECISION)
    halves = out.reshape(count // (2 * low), low, 2, rank, vecs).transpose(0, 2, 1, 3, 4)
    return halves.reshape(count, rank, vecs)


def body(vectors, diagonal, source_basis, transfer, target_basis):
    leaves, leaf, rank = source_basis.shape
    vecs = vectors.shape[-1]
    slot_bits = leaves.bit_length() - 1
    places = Places(slot_bits)
    pair_bits = range(places.low_bits)
    pair_levels = [transfer[slot_bits + bit] for bit in pair_bits]

    basis_t = jnp.swapaxes(target_basis, 1, 2)
    tops = [transfer[slot_bits + places.low_bits + j] for j in range(slot_bits)]
    halves = [basis_t[:, :, j : j + vecs] for j in range(0, leaf, vecs)]
    moving = jnp.concatenate(tops + halves, axis=1)
    moved = places.gather(moving)
    moved = places.in_order(moved)
    parts = [moved[:, j : j + rank] for j in range(0, moved.shape[1], rank)]
    tops = parts[:slot_bits]
    basis_t = jnp.concatenate(parts[slot_bits:], axis=2)
    weights = places.reverse_low(diagonal).reshape(leaves, leaf)
    order = jnp.stack([places.slot(k) for k in range(leaves)])
    chosen = jnp.arange(leaves)[:, None] == order[None, :]
    wide = chosen[:, None, :, None] & jnp.eye(rank, dtype=bool)[None, :, None, :]
    wide = wide.astype(jnp.float32).reshape(leaves, rank, leaves * rank)
    gram = jnp.einsum("krs,kts->krt", basis_t * weights[:, None, :], basis_t, precision=PRECISION)
    for j in range(slot_bits):
        wide = local_forward(wide, tops[j], slot_bits - 1 - j)
    middle = jnp.einsum("krt,kti->kri", gram, wide, precision=PRECISION)
    middle = jnp.einsum("krj,kri->ji", wide, middle, precision=PRECISION)

    coeffs = jnp.einsum(
        "ksr,ksv->krv", source_basis, vectors.reshape(leaves, leaf, vecs), precision=PRECISION
    )
    for level in range(slot_bits):
        coeffs = local_forward(coeffs, transfer[level], level)
    for bit in pair_bits:
        other = places.partner(coeffs, bit)
        lower = jnp.where(places.upper(bit), other, coeffs)
        upper = jnp.where(places.upper(bit), coeffs, other)
        stacked = jnp.concatenate([lower, upper], axis=1)
        coeffs = jnp.einsum("nij,njv->niv", pair_levels[bit], stacked, precision=PRECISION)

    stacked = jnp.concatenate(places.gather(coeffs), axis=0)
    back = jnp.einsum("ij,jv->iv", middle, stacked, precision=PRECISION)
    back = places.scatter(list(back.reshape(leaves, rank, vecs)))
    coeffs = jnp.einsum("krj,jv->krv", wide, stacked, precision=PRECISION)
    forward_image = jnp.einsum("krs,krv->ksv", basis_t, coeffs, precision=PRECISION)
    forward_image = places.reverse_low(forward_image)

    for bit in reversed(pair_bits):
        product = jnp.einsum("nij,niv->njv", pair_levels[bit], back, precision=PRECISION)
        kept = jnp.where(places.upper(bit), product[:, rank:], product[:, :rank])
        sent = jnp.where(places.upper(bit), product[:, :rank], product[:, rank:])
        back = kept + places.partner(sent, bit)
    for level in range(slot_bits - 1, -1, -1):
        back = local_reverse(back, transfer[level], level)
    adjoint = jnp.einsum("ksr,krv->ksv", source_basis, back, precision=PRECISION)
    return forward_image.reshape(leaves * leaf, vecs), adjoint.reshape(leaves * leaf, vecs)


def solution(mesh):
    placed = (
        P(BOTH, None),
        P(BOTH),
        P(BOTH, None, None),
        P(None, BOTH, None, None),
        P(BOTH, None, None),
    )

    return jax.shard_map(
        body, mesh=mesh, in_specs=placed, out_specs=(P(BOTH, None), P(BOTH, None)), check_vma=False
    )
```

time: 69.8 us -> 74.6 us (1.069)
  the two profiles are of different devices: /device:TPU:0 before, /device:TPU:1 now
where the time goes in v3:
time: 74.6 us; the launch traced here: 74.4 us
  waiting for transfers between devices  36.8 us (49%)
  starting transfers between devices  25.8 us (35%)
  matrix products  6.12 us (8%)
  local copies, waits for them, and re-layouts  4.2 us (6%)
  between operations  1.2 us (2%)
    ppermute x17, waiting for transfers between devices, permute(): lax.ppermute(block, BOTH, [(d, route(d)) for d in range(self.devices)])  36.8 us
    ppermute x17, starting transfers between devices, permute(): lax.ppermute(block, BOTH, [(d, route(d)) for d in range(self.devices)])  25.8 us
  transfers between devices with their start and end apart: 17, of which 10 were waited for; matrix products, arithmetic and copies ran while one was open for 8% of the time, Pallas kernels for 0%

profile of v3, /device:TPU:1, one launch (start us, length us, event | category | flops | bytes accessed | tf_op | source)
XLA Modules:
  0.0 74.4 jit_solution(8240684723540854682)
XLA Ops:
  0.6 0.0 copy-start
  0.7 1.2 %fusion.66 = (f32[1,4,64,128]{3,2,1,0:T(8,128)S(1)}, f32[1,4,64,128]{3,2,1,0:T(8,128)S(1)}, f32[4,64,128]{2,1,0:T(8,128)S(1)}, f32[4,64,128]{2,1,0:T(8,128)S(1)}) fusion(f32[7,4,64,128]{3,2,1,0:T(8,128)} %param.8), kind=kLoop, calls=%fused_computation.121 | loop fusion | bytes 1048576 | tf_op jit(solution)/shard_map/slice | solution.py:117
  1.9 0.0 copy-done.3
  2.1 0.0 copy-start.2
  2.1 0.0 copy-start.4
  2.1 2.1 %collective-permute-start = (f32[256,128]{1,0:T(8,128)S(1)}, f32[256,128]{1,0:T(8,128)S(1)}, u32[]{:S(2)}, u32[]{:S(2)}) collective-permute-start(f32[256,128]{1,0:T(8,128)S(1)} %get-tuple-element.12), channel_id=1, source_target_pairs={{0,8},{1,9},{2,10},{3,11},{4,12},{5,13},{6,14},{7,15},{8,0},{9,1},... | collective-permute-start | bytes 393224 | tf_op jit(solution)/shard_map/ppermute | solution.py:27
  4.2 1.2 %collective-permute-start.1 = (f32[256,128]{1,0:T(8,128)S(1)}, f32[256,128]{1,0:T(8,128)S(1)}, u32[]{:S(2)}, u32[]{:S(2)}) collective-permute-start(f32[256,128]{1,0:T(8,128)S(1)} %get-tuple-element.11), channel_id=1, source_target_pairs={{0,16},{1,17},{2,18},{3,19},{4,20},{5,21},{6,22},{7,23},{8,24},{9,... | collective-permute-start | bytes 393224 | tf_op jit(solution)/shard_map/ppermute | solution.py:27
  5.5 0.0 collective-permute-start.2
  5.5 5.8 %collective-permute-start.10 = (f32[1024]{0:T(1024)S(1)}, f32[1024]{0:T(1024)S(1)}, u32[]{:S(2)}, u32[]{:S(2)}) collective-permute-start(f32[1024]{0:T(1024)S(1)} %copy-done.4), channel_id=1, source_target_pairs={{0,0},{1,4},{2,2},{3,6},{4,1},{5,5},{6,3},{7,7},{8,8},{9,12},{10,1... | collective-permute-start | bytes 12296 | tf_op jit(solution)/shard_map/ppermute | solution.py:27
  11.3 0.3 fusion.70
  11.6 0.2 convolution_bitcast_fusion.8
  11.8 0.2 convolution_bitcast_fusion.7
  12.1 0.1 collective-permute-start.3
  12.2 0.1 pad_add_fusion
  12.3 0.1 and.53
  12.3 0.1 and.54
  12.5 0.1 and.57
  12.6 0.0 collective-permute-done.10
  12.7 0.0 collective-permute-done.1
  12.8 0.0 copy-start.1
  12.8 0.3 fusion.2
  13.1 0.3 collective-permute-done.3
  13.5 0.5 copy-done.1
  14.0 0.2 convolution_bitcast_fusion.6
  14.3 1.4 %collective-permute-start.4 = (f32[4,64,128]{2,1,0:T(8,128)S(1)}, f32[4,64,128]{2,1,0:T(8,128)S(1)}, u32[]{:S(2)}, u32[]{:S(2)}) collective-permute-start(f32[4,64,128]{2,1,0:T(8,128)S(1)} %convolution_bitcast_fusion.6), channel_id=1, source_target_pairs={{0,2},{1,3},{2,0},{3,1},{4,6},{5,7},{6,4},{7,5},{8,10},{9,11},{10,... | collective-permute-start | bytes 393224 | tf_op jit(solution)/shard_map/ppermute | solution.py:27
  15.6 0.3 fusion.5
  15.9 0.3 fusion
  16.1 2.7 %collective-permute-done.4 = f32[4,64,128]{2,1,0:T(8,128)S(1)} collective-permute-done((f32[4,64,128]{2,1,0:T(8,128)S(1)}, f32[4,64,128]{2,1,0:T(8,128)S(1)}, u32[]{:S(2)}, u32[]{:S(2)}) %collective-permute-start.4) | collective-permute-done | bytes 131104 | tf_op jit(solution)/shard_map/ppermute | solution.py:27
  18.9 0.2 convolution_bitcast_fusion.5
  19.2 0.1 collective-permute-start.5
  19.2 0.3 fusion.71
  19.5 7.8 %collective-permute-done.5 = f32[4,64,128]{2,1,0:T(8,128)S(1)} collective-permute-done((f32[4,64,128]{2,1,0:T(8,128)S(1)}, f32[4,64,128]{2,1,0:T(8,128)S(1)}, u32[]{:S(2)}, u32[]{:S(2)}) %collective-permute-start.5) | collective-permute-done | bytes 131104 | tf_op jit(solution)/shard_map/ppermute | solution.py:27
  27.4 0.2 fusion.14
  27.6 1.3 %collective-permute-start.6 = (f32[64,128]{1,0:T(8,128)S(1)}, f32[64,128]{1,0:T(8,128)S(1)}, u32[]{:S(2)}, u32[]{:S(2)}) collective-permute-start(f32[64,128]{1,0:T(8,128)S(1)} %get-tuple-element.30), channel_id=1, source_target_pairs={{0,8},{1,9},{2,10},{3,11},{4,12},{5,13},{6,14},{7,15},{8,0},{9,1},... | collective-permute-start | bytes 98312 | tf_op jit(solution)/shard_map/ppermute | solution.py:27
  28.9 1.2 %collective-permute-start.7 = (f32[64,128]{1,0:T(8,128)S(1)}, f32[64,128]{1,0:T(8,128)S(1)}, u32[]{:S(2)}, u32[]{:S(2)}) collective-permute-start(f32[64,128]{1,0:T(8,128)S(1)} %get-tuple-element.29), channel_id=1, source_target_pairs={{0,16},{1,17},{2,18},{3,19},{4,20},{5,21},{6,22},{7,23},{8,24},{9,... | collective-permute-start | bytes 98312 | tf_op jit(solution)/shard_map/ppermute | solution.py:27
  30.2 0.2 collective-permute-start.8
  30.4 0.4 convolution_bitcast_fusion.1
  30.7 0.0 collective-permute-done.6
  30.8 0.9 %collective-permute-done.7 = f32[64,128]{1,0:T(8,128)S(1)} collective-permute-done((f32[64,128]{1,0:T(8,128)S(1)}, f32[64,128]{1,0:T(8,128)S(1)}, u32[]{:S(2)}, u32[]{:S(2)}) %collective-permute-start.7) | collective-permute-done | bytes 32800 | tf_op jit(solution)/shard_map/ppermute | solution.py:27
  31.7 2.2 %collective-permute-done.8 = f32[64,128]{1,0:T(8,128)S(1)} collective-permute-done((f32[64,128]{1,0:T(8,128)S(1)}, f32[64,128]{1,0:T(8,128)S(1)}, u32[]{:S(2)}, u32[]{:S(2)}) %collective-permute-start.8) | collective-permute-done | bytes 32800 | tf_op jit(solution)/shard_map/ppermute | solution.py:27
  33.8 0.3 fusion.51
  34.1 0.3 collective-permute-start.11
  34.5 0.3 collective-permute-start.12
  34.8 2.2 %collective-permute-start.13 = (f32[64,128]{1,0:T(8,128)S(1)}, f32[64,128]{1,0:T(8,128)S(1)}, u32[]{:S(2)}, u32[]{:S(2)}) collective-permute-start(f32[64,128]{1,0:T(8,128)S(1)} %get-tuple-element.24), channel_id=1, source_target_pairs={{0,24},{1,25},{2,26},{3,27},{4,28},{5,29},{6,30},{7,31},{8,16},{9,... | collective-permute-start | bytes 98312 | tf_op jit(solution)/shard_map/ppermute | solution.py:27
  37.0 0.0 collective-permute-done.11
  37.0 0.3 collective-permute-done.12
  37.3 1.1 %collective-permute-done.13 = f32[64,128]{1,0:T(8,128)S(1)} collective-permute-done((f32[64,128]{1,0:T(8,128)S(1)}, f32[64,128]{1,0:T(8,128)S(1)}, u32[]{:S(2)}, u32[]{:S(2)}) %collective-permute-start.13) | collective-permute-done | bytes 32800 | tf_op jit(solution)/shard_map/ppermute | solution.py:27
  38.4 0.4 convolution_bitcast_fusion.4
  38.9 0.1 collective-permute-start.14
  38.9 4.7 %collective-permute-done.14 = f32[4,64,128]{2,1,0:T(8,128)S(1)} collective-permute-done((f32[4,64,128]{2,1,0:T(8,128)S(1)}, f32[4,64,128]{2,1,0:T(8,128)S(1)}, u32[]{:S(2)}, u32[]{:S(2)}) %collective-permute-start.14) | collective-permute-done | bytes 131104 | tf_op jit(solution)/shard_map/ppermute | solution.py:27
  43.6 0.4 convolution_bitcast_fusion.3
  44.1 0.1 collective-permute-start.15
  44.1 0.3 fusion.25
  44.4 4.1 %collective-permute-done.15 = f32[4,64,128]{2,1,0:T(8,128)S(1)} collective-permute-done((f32[4,64,128]{2,1,0:T(8,128)S(1)}, f32[4,64,128]{2,1,0:T(8,128)S(1)}, u32[]{:S(2)}, u32[]{:S(2)}) %collective-permute-start.15) | collective-permute-done | bytes 131104 | tf_op jit(solution)/shard_map/ppermute | solution.py:27
  48.6 0.4 convolution_bitcast_fusion.2
  49.0 7.6 %collective-permute-start.16 = (f32[4,64,128]{2,1,0:T(8,128)S(1)}, f32[4,64,128]{2,1,0:T(8,128)S(1)}, u32[]{:S(2)}, u32[]{:S(2)}) collective-permute-start(f32[4,64,128]{2,1,0:T(8,128)S(1)} %slice_select_fusion), channel_id=1, source_target_pairs={{0,1},{1,0},{2,3},{3,2},{4,5},{5,4},{6,7},{7,6},{8,9},{9,8},{10,11... | collective-permute-start | bytes 393224 | tf_op jit(solution)/shard_map/ppermute | solution.py:27
  56.5 0.6 fusion.18
  57.1 2.0 %collective-permute-start.9 = (f32[4,256,128]{2,1,0:T(8,128)S(1)}, f32[4,256,128]{2,1,0:T(8,128)S(1)}, u32[]{:S(2)}, u32[]{:S(2)}) collective-permute-start(f32[4,256,128]{2,1,0:T(8,128)S(1)} %fusion.18), channel_id=1, source_target_pairs={{0,0},{1,4},{2,2},{3,6},{4,1},{5,5},{6,3},{7,7},{8,8},{9,12},{10,1... | collective-permute-start | bytes 1572872 | tf_op jit(solution)/shard_map/ppermute | solution.py:27
  59.2 0.3 fusion.72
  59.4 0.3 fusion.23
  59.7 0.4 convolution_bitcast_fusion
  60.2 1.0 %copy.21 = f32[4,256,128]{2,1,0:T(8,128)} copy(f32[4,256,128]{1,2,0:T(8,128)S(1)} %convolution_bitcast_fusion) | data formatting | bytes 1048576 | tf_op jit(solution)/shard_map/ksr,krv->ksv/dot_general | solution.py:139
  61.1 12.5 %collective-permute-done.9 = f32[4,256,128]{2,1,0:T(8,128)S(1)} collective-permute-done((f32[4,256,128]{2,1,0:T(8,128)S(1)}, f32[4,256,128]{2,1,0:T(8,128)S(1)}, u32[]{:S(2)}, u32[]{:S(2)}) %collective-permute-start.9) | collective-permute-done | bytes 524320 | tf_op jit(solution)/shard_map/ppermute | solution.py:27
  73.6 0.8 %copy.48 = f32[1024,128]{1,0:T(8,128)} copy(f32[1024,128]{1,0:T(8,128)S(1)} %bitcast.205) | data formatting | bytes 1048576
  (40 shorter events, 0.6 us)
Async XLA Ops:
  0.6 10.7 %copy-start = (f32[1024,128]{1,0:T(8,128)S(1)}, f32[1024,128]{1,0:T(8,128)}, u32[]{:S(2)}) copy-start(f32[1024,128]{1,0:T(8,128)} %param.5) | copy-start | bytes 1572868
  0.7 1.3 %copy-start.3 = (f32[4,256,64]{1,2,0:T(8,128)S(1)}, f32[4,256,64]{1,2,0:T(8,128)}, u32[]{:S(2)}) copy-start(f32[4,256,64]{1,2,0:T(8,128)} %param.9) | copy-start | bytes 786436
  2.1 9.2 %copy-start.2 = (f32[4,256,64]{1,2,0:T(8,128)S(1)}, f32[4,256,64]{1,2,0:T(8,128)}, u32[]{:S(2)}) copy-start(f32[4,256,64]{1,2,0:T(8,128)} %param.7) | copy-start | bytes 786436
  2.1 3.4 %copy-start.4 = (f32[1024]{0:T(1024)S(1)}, f32[1024]{0:T(1024)}, u32[]{:S(2)}) copy-start(f32[1024]{0:T(1024)} %param.6) | copy-start | bytes 12292
  2.1 10.5 %collective-permute-start = (f32[256,128]{1,0:T(8,128)S(1)}, f32[256,128]{1,0:T(8,128)S(1)}, u32[]{:S(2)}, u32[]{:S(2)}) collective-permute-start(f32[256,128]{1,0:T(8,128)S(1)} %get-tuple-element.12), channel_id=1, source_target_pairs={{0,8},{1,9},{2,10},{3,11},{4,12},{5,13},{6,14},{7,15},{8,0},{9,1},... | collective-permute-start | bytes 393224 | tf_op jit(solution)/shard_map/ppermute | solution.py:27
  4.2 8.5 %collective-permute-start.1 = (f32[256,128]{1,0:T(8,128)S(1)}, f32[256,128]{1,0:T(8,128)S(1)}, u32[]{:S(2)}, u32[]{:S(2)}) collective-permute-start(f32[256,128]{1,0:T(8,128)S(1)} %get-tuple-element.11), channel_id=1, source_target_pairs={{0,16},{1,17},{2,18},{3,19},{4,20},{5,21},{6,22},{7,23},{8,24},{9,... | collective-permute-start | bytes 393224 | tf_op jit(solution)/shard_map/ppermute | solution.py:27
  5.5 7.3 %collective-permute-start.2 = (f32[256,128]{1,0:T(8,128)S(1)}, f32[256,128]{1,0:T(8,128)S(1)}, u32[]{:S(2)}, u32[]{:S(2)}) collective-permute-start(f32[256,128]{1,0:T(8,128)S(1)} %get-tuple-element.10), channel_id=1, source_target_pairs={{0,24},{1,25},{2,26},{3,27},{4,28},{5,29},{6,30},{7,31},{8,16},{9,... | collective-permute-start | bytes 393224 | tf_op jit(solution)/shard_map/ppermute | solution.py:27
  5.5 7.1 %collective-permute-start.10 = (f32[1024]{0:T(1024)S(1)}, f32[1024]{0:T(1024)S(1)}, u32[]{:S(2)}, u32[]{:S(2)}) collective-permute-start(f32[1024]{0:T(1024)S(1)} %copy-done.4), channel_id=1, source_target_pairs={{0,0},{1,4},{2,2},{3,6},{4,1},{5,5},{6,3},{7,7},{8,8},{9,12},{10,1... | collective-permute-start | bytes 12296 | tf_op jit(solution)/shard_map/ppermute | solution.py:27
  12.1 1.4 %collective-permute-start.3 = (f32[4,64,128]{2,1,0:T(8,128)S(1)}, f32[4,64,128]{2,1,0:T(8,128)S(1)}, u32[]{:S(2)}, u32[]{:S(2)}) collective-permute-start(f32[4,64,128]{2,1,0:T(8,128)S(1)} %bitcast.203), channel_id=1, source_target_pairs={{0,1},{1,0},{2,3},{3,2},{4,5},{5,4},{6,7},{7,6},{8,9},{9,8},{10,11... | collective-permute-start | bytes 393224 | tf_op jit(solution)/shard_map/ppermute | solution.py:27
  12.8 1.2 %copy-start.1 = (f32[7,4,64,128]{3,2,1,0:T(8,128)S(1)}, f32[7,4,64,128]{3,2,1,0:T(8,128)}, u32[]{:S(2)}) copy-start(f32[7,4,64,128]{3,2,1,0:T(8,128)} %param.8) | copy-start | bytes 2752516
  14.3 4.6 %collective-permute-start.4 = (f32[4,64,128]{2,1,0:T(8,128)S(1)}, f32[4,64,128]{2,1,0:T(8,128)S(1)}, u32[]{:S(2)}, u32[]{:S(2)}) collective-permute-start(f32[4,64,128]{2,1,0:T(8,128)S(1)} %convolution_bitcast_fusion.6), channel_id=1, source_target_pairs={{0,2},{1,3},{2,0},{3,1},{4,6},{5,7},{6,4},{7,5},{8,10},{9,11},{10,... | collective-permute-start | bytes 393224 | tf_op jit(solution)/shard_map/ppermute | solution.py:27
  19.2 8.2 %collective-permute-start.5 = (f32[4,64,128]{2,1,0:T(8,128)S(1)}, f32[4,64,128]{2,1,0:T(8,128)S(1)}, u32[]{:S(2)}, u32[]{:S(2)}) collective-permute-start(f32[4,64,128]{2,1,0:T(8,128)S(1)} %convolution_bitcast_fusion.5), channel_id=1, source_target_pairs={{0,4},{1,5},{2,6},{3,7},{4,0},{5,1},{6,2},{7,3},{8,12},{9,13},{10,... | collective-permute-start | bytes 393224 | tf_op jit(solution)/shard_map/ppermute | solution.py:27
  27.6 3.1 %collective-permute-start.6 = (f32[64,128]{1,0:T(8,128)S(1)}, f32[64,128]{1,0:T(8,128)S(1)}, u32[]{:S(2)}, u32[]{:S(2)}) collective-permute-start(f32[64,128]{1,0:T(8,128)S(1)} %get-tuple-element.30), channel_id=1, source_target_pairs={{0,8},{1,9},{2,10},{3,11},{4,12},{5,13},{6,14},{7,15},{8,0},{9,1},... | collective-permute-start | bytes 98312 | tf_op jit(solution)/shard_map/ppermute | solution.py:27
  28.9 2.8 %collective-permute-start.7 = (f32[64,128]{1,0:T(8,128)S(1)}, f32[64,128]{1,0:T(8,128)S(1)}, u32[]{:S(2)}, u32[]{:S(2)}) collective-permute-start(f32[64,128]{1,0:T(8,128)S(1)} %get-tuple-element.29), channel_id=1, source_target_pairs={{0,16},{1,17},{2,18},{3,19},{4,20},{5,21},{6,22},{7,23},{8,24},{9,... | collective-permute-start | bytes 98312 | tf_op jit(solution)/shard_map/ppermute | solution.py:27
  30.2 3.7 %collective-permute-start.8 = (f32[64,128]{1,0:T(8,128)S(1)}, f32[64,128]{1,0:T(8,128)S(1)}, u32[]{:S(2)}, u32[]{:S(2)}) collective-permute-start(f32[64,128]{1,0:T(8,128)S(1)} %get-tuple-element.28), channel_id=1, source_target_pairs={{0,24},{1,25},{2,26},{3,27},{4,28},{5,29},{6,30},{7,31},{8,16},{9,... | collective-permute-start | bytes 98312 | tf_op jit(solution)/shard_map/ppermute | solution.py:27
  34.1 2.8 %collective-permute-start.11 = (f32[64,128]{1,0:T(8,128)S(1)}, f32[64,128]{1,0:T(8,128)S(1)}, u32[]{:S(2)}, u32[]{:S(2)}) collective-permute-start(f32[64,128]{1,0:T(8,128)S(1)} %get-tuple-element.26), channel_id=1, source_target_pairs={{0,8},{1,9},{2,10},{3,11},{4,12},{5,13},{6,14},{7,15},{8,0},{9,1},... | collective-permute-start | bytes 98312 | tf_op jit(solution)/shard_map/ppermute | solution.py:27
  34.5 2.8 %collective-permute-start.12 = (f32[64,128]{1,0:T(8,128)S(1)}, f32[64,128]{1,0:T(8,128)S(1)}, u32[]{:S(2)}, u32[]{:S(2)}) collective-permute-start(f32[64,128]{1,0:T(8,128)S(1)} %get-tuple-element.25), channel_id=1, source_target_pairs={{0,16},{1,17},{2,18},{3,19},{4,20},{5,21},{6,22},{7,23},{8,24},{9,... | collective-permute-start | bytes 98312 | tf_op jit(solution)/shard_map/ppermute | solution.py:27
  34.8 3.7 %collective-permute-start.13 = (f32[64,128]{1,0:T(8,128)S(1)}, f32[64,128]{1,0:T(8,128)S(1)}, u32[]{:S(2)}, u32[]{:S(2)}) collective-permute-start(f32[64,128]{1,0:T(8,128)S(1)} %get-tuple-element.24), channel_id=1, source_target_pairs={{0,24},{1,25},{2,26},{3,27},{4,28},{5,29},{6,30},{7,31},{8,16},{9,... | collective-permute-start | bytes 98312 | tf_op jit(solution)/shard_map/ppermute | solution.py:27
  38.9 4.8 %collective-permute-start.14 = (f32[4,64,128]{2,1,0:T(8,128)S(1)}, f32[4,64,128]{2,1,0:T(8,128)S(1)}, u32[]{:S(2)}, u32[]{:S(2)}) collective-permute-start(f32[4,64,128]{2,1,0:T(8,128)S(1)} %slice_select_fusion.2), channel_id=1, source_target_pairs={{0,4},{1,5},{2,6},{3,7},{4,0},{5,1},{6,2},{7,3},{8,12},{9,13},{10,... | collective-permute-start | bytes 393224 | tf_op jit(solution)/shard_map/ppermute | solution.py:27
  44.1 4.5 %collective-permute-start.15 = (f32[4,64,128]{2,1,0:T(8,128)S(1)}, f32[4,64,128]{2,1,0:T(8,128)S(1)}, u32[]{:S(2)}, u32[]{:S(2)}) collective-permute-start(f32[4,64,128]{2,1,0:T(8,128)S(1)} %slice_select_fusion.1), channel_id=1, source_target_pairs={{0,2},{1,3},{2,0},{3,1},{4,6},{5,7},{6,4},{7,5},{8,10},{9,11},{10,... | collective-permute-start | bytes 393224 | tf_op jit(solution)/shard_map/ppermute | solution.py:27
  49.0 10.1 %collective-permute-start.16 = (f32[4,64,128]{2,1,0:T(8,128)S(1)}, f32[4,64,128]{2,1,0:T(8,128)S(1)}, u32[]{:S(2)}, u32[]{:S(2)}) collective-permute-start(f32[4,64,128]{2,1,0:T(8,128)S(1)} %slice_select_fusion), channel_id=1, source_target_pairs={{0,1},{1,0},{2,3},{3,2},{4,5},{5,4},{6,7},{7,6},{8,9},{9,8},{10,11... | collective-permute-start | bytes 393224 | tf_op jit(solution)/shard_map/ppermute | solution.py:27
  57.1 16.5 %collective-permute-start.9 = (f32[4,256,128]{2,1,0:T(8,128)S(1)}, f32[4,256,128]{2,1,0:T(8,128)S(1)}, u32[]{:S(2)}, u32[]{:S(2)}) collective-permute-start(f32[4,256,128]{2,1,0:T(8,128)S(1)} %fusion.18), channel_id=1, source_target_pairs={{0,0},{1,4},{2,2},{3,6},{4,1},{5,5},{6,3},{7,7},{8,8},{9,12},{10,1... | collective-permute-start | bytes 1572872 | tf_op jit(solution)/shard_map/ppermute | solution.py:27

commit v4 on v3

--- a/solution.py
+++ b/solution.py
@@ -4,7 +4,7 @@
 from jax.sharding import PartitionSpec as P
 
 
-PRECISION = lax.Precision.HIGH
+PRECISION = lax.Precision.HIGHEST
 BOTH = ("row", "col")
 
 
@@ -126,8 +126,11 @@
     back = jnp.einsum("ij,jv->iv", middle, stacked, precision=PRECISION)
     back = places.scatter(list(back.reshape(leaves, rank, vecs)))
     coeffs = jnp.einsum("krj,jv->krv", wide, stacked, precision=PRECISION)
-    forward_image = jnp.einsum("krs,krv->ksv", basis_t, coeffs, precision=PRECISION)
-    forward_image = places.reverse_low(forward_image)
+    image_coeffs = places.reverse_low(coeffs)
+    image_basis = places.reverse_low(basis_t)
+    forward_image = jnp.einsum(
+        "krs,krv->ksv", image_basis, image_coeffs, precision=PRECISION
+    )
 
     for bit in reversed(pair_bits):
         product = jnp.einsum("nij,niv->njv", pair_levels[bit], back, precision=PRECISION)

time: 74.6 us -> 65.9 us (0.88)
  the two profiles are of different devices: /device:TPU:1 before, /device:TPU:0 now
where the time goes in v4:
time: 65.9 us; the launch traced here: 65.7 us
  waiting for transfers between devices  28.9 us (44%)
  starting transfers between devices  21.8 us (33%)
  matrix products  9.9 us (15%)
  local copies, waits for them, and re-layouts  3.6 us (5%)
  between operations  1.2 us (2%)
    ppermute x18, waiting for transfers between devices, permute(): lax.ppermute(block, BOTH, [(d, route(d)) for d in range(self.devices)])  28.9 us
    ppermute x18, starting transfers between devices, permute(): lax.ppermute(block, BOTH, [(d, route(d)) for d in range(self.devices)])  21.8 us
    dot_general x1, matrix products, body(): jnp.einsum('krs,krv->ksv', image_basis, image_coeffs, precision=PRECISION)  1.84 us
    dot_general x3, matrix products, body(): jnp.einsum('nij,niv->njv', pair_levels[bit], back, precision=PRECISION)  1.78 us
  transfers between devices with their start and end apart: 18, of which 9 were waited for; matrix products, arithmetic and copies ran while one was open for 11% of the time, Pallas kernels for 0%

profile of v4, /device:TPU:0, one launch (start us, length us, event | category | flops | bytes accessed | tf_op | source)
XLA Modules:
  0.0 65.7 jit_solution(17672834894633947282)
XLA Ops:
  0.6 0.0 copy-start
  0.7 1.2 %fusion.63 = (f32[1,4,64,128]{3,2,1,0:T(8,128)S(1)}, f32[1,4,64,128]{3,2,1,0:T(8,128)S(1)}, f32[4,64,128]{2,1,0:T(8,128)S(1)}, f32[4,64,128]{2,1,0:T(8,128)S(1)}) fusion(f32[7,4,64,128]{3,2,1,0:T(8,128)} %param.8), kind=kLoop, calls=%fused_computation.118 | loop fusion | bytes 1048576 | tf_op jit(solution)/shard_map/slice | solution.py:117
  1.9 0.0 copy-done.3
  2.1 0.0 copy-start.2
  2.1 0.0 copy-start.4
  2.1 3.0 %collective-permute-start = (f32[256,128]{1,0:T(8,128)S(1)}, f32[256,128]{1,0:T(8,128)S(1)}, u32[]{:S(2)}, u32[]{:S(2)}) collective-permute-start(f32[256,128]{1,0:T(8,128)S(1)} %get-tuple-element.12), channel_id=1, source_target_pairs={{0,8},{1,9},{2,10},{3,11},{4,12},{5,13},{6,14},{7,15},{8,0},{9,1},... | collective-permute-start | bytes 393224 | tf_op jit(solution)/shard_map/ppermute | solution.py:27
  5.2 1.5 %collective-permute-start.1 = (f32[256,128]{1,0:T(8,128)S(1)}, f32[256,128]{1,0:T(8,128)S(1)}, u32[]{:S(2)}, u32[]{:S(2)}) collective-permute-start(f32[256,128]{1,0:T(8,128)S(1)} %get-tuple-element.11), channel_id=1, source_target_pairs={{0,16},{1,17},{2,18},{3,19},{4,20},{5,21},{6,22},{7,23},{8,24},{9,... | collective-permute-start | bytes 393224 | tf_op jit(solution)/shard_map/ppermute | solution.py:27
  6.7 0.0 collective-permute-start.2
  6.7 0.7 collective-permute-start.11
  7.4 0.5 fusion.67
  7.9 0.3 convolution_bitcast_fusion.8
  8.2 0.3 convolution_bitcast_fusion.7
  8.4 4.5 %collective-permute-start.4 = (f32[4,64,128]{2,1,0:T(8,128)S(1)}, f32[4,64,128]{2,1,0:T(8,128)S(1)}, u32[]{:S(2)}, u32[]{:S(2)}) collective-permute-start(f32[4,64,128]{2,1,0:T(8,128)S(1)} %bitcast.205), channel_id=1, source_target_pairs={{0,1},{1,0},{2,3},{3,2},{4,5},{5,4},{6,7},{7,6},{8,9},{9,8},{10,11... | collective-permute-start | bytes 393224 | tf_op jit(solution)/shard_map/ppermute | solution.py:27
  12.9 0.1 pad_add_fusion
  13.0 0.1 and.53
  13.1 0.1 and.54
  13.2 0.1 and.57
  13.4 0.0 collective-permute-done.11
  13.5 0.0 collective-permute-done.1
  13.5 0.0 collective-permute-done.2
  13.6 0.0 copy-start.1
  13.6 0.4 fusion.2
  14.1 0.0 collective-permute-done.4
  14.1 0.7 %copy-done.1 = f32[7,4,64,128]{3,2,1,0:T(8,128)S(1)} copy-done((f32[7,4,64,128]{3,2,1,0:T(8,128)S(1)}, f32[7,4,64,128]{3,2,1,0:T(8,128)}, u32[]{:S(2)}) %copy-start.1) | copy-done | bytes 917528
  14.8 0.3 convolution_bitcast_fusion.6
  15.1 1.6 %collective-permute-start.5 = (f32[4,64,128]{2,1,0:T(8,128)S(1)}, f32[4,64,128]{2,1,0:T(8,128)S(1)}, u32[]{:S(2)}, u32[]{:S(2)}) collective-permute-start(f32[4,64,128]{2,1,0:T(8,128)S(1)} %convolution_bitcast_fusion.6), channel_id=1, source_target_pairs={{0,2},{1,3},{2,0},{3,1},{4,6},{5,7},{6,4},{7,5},{8,10},{9,11},{10,... | collective-permute-start | bytes 393224 | tf_op jit(solution)/shard_map/ppermute | solution.py:27
  16.8 0.4 fusion.5
  17.2 0.4 fusion
  17.6 3.1 %collective-permute-done.5 = f32[4,64,128]{2,1,0:T(8,128)S(1)} collective-permute-done((f32[4,64,128]{2,1,0:T(8,128)S(1)}, f32[4,64,128]{2,1,0:T(8,128)S(1)}, u32[]{:S(2)}, u32[]{:S(2)}) %collective-permute-start.5) | collective-permute-done | bytes 131104 | tf_op jit(solution)/shard_map/ppermute | solution.py:27
  20.6 0.3 convolution_bitcast_fusion.5
  21.0 1.7 %collective-permute-start.6 = (f32[4,64,128]{2,1,0:T(8,128)S(1)}, f32[4,64,128]{2,1,0:T(8,128)S(1)}, u32[]{:S(2)}, u32[]{:S(2)}) collective-permute-start(f32[4,64,128]{2,1,0:T(8,128)S(1)} %convolution_bitcast_fusion.5), channel_id=1, source_target_pairs={{0,4},{1,5},{2,6},{3,7},{4,0},{5,1},{6,2},{7,3},{8,12},{9,13},{10,... | collective-permute-start | bytes 393224 | tf_op jit(solution)/shard_map/ppermute | solution.py:27
  22.7 0.4 fusion.69
  23.1 6.2 %collective-permute-done.6 = f32[4,64,128]{2,1,0:T(8,128)S(1)} collective-permute-done((f32[4,64,128]{2,1,0:T(8,128)S(1)}, f32[4,64,128]{2,1,0:T(8,128)S(1)}, u32[]{:S(2)}, u32[]{:S(2)}) %collective-permute-start.6) | collective-permute-done | bytes 131104 | tf_op jit(solution)/shard_map/ppermute | solution.py:27
  29.4 0.3 fusion.14
  29.7 1.6 %collective-permute-start.7 = (f32[64,128]{1,0:T(8,128)S(1)}, f32[64,128]{1,0:T(8,128)S(1)}, u32[]{:S(2)}, u32[]{:S(2)}) collective-permute-start(f32[64,128]{1,0:T(8,128)S(1)} %get-tuple-element.30), channel_id=1, source_target_pairs={{0,8},{1,9},{2,10},{3,11},{4,12},{5,13},{6,14},{7,15},{8,0},{9,1},... | collective-permute-start | bytes 98312 | tf_op jit(solution)/shard_map/ppermute | solution.py:27
  31.3 1.5 %collective-permute-start.8 = (f32[64,128]{1,0:T(8,128)S(1)}, f32[64,128]{1,0:T(8,128)S(1)}, u32[]{:S(2)}, u32[]{:S(2)}) collective-permute-start(f32[64,128]{1,0:T(8,128)S(1)} %get-tuple-element.29), channel_id=1, source_target_pairs={{0,16},{1,17},{2,18},{3,19},{4,20},{5,21},{6,22},{7,23},{8,24},{9,... | collective-permute-start | bytes 98312 | tf_op jit(solution)/shard_map/ppermute | solution.py:27
  32.8 0.5 collective-permute-start.9
  33.3 0.6 convolution_bitcast_fusion.1
  33.9 1.5 %collective-permute-done.8 = f32[64,128]{1,0:T(8,128)S(1)} collective-permute-done((f32[64,128]{1,0:T(8,128)S(1)}, f32[64,128]{1,0:T(8,128)S(1)}, u32[]{:S(2)}, u32[]{:S(2)}) %collective-permute-start.8) | collective-permute-done | bytes 32800 | tf_op jit(solution)/shard_map/ppermute | solution.py:27
  35.4 2.2 %collective-permute-done.9 = f32[64,128]{1,0:T(8,128)S(1)} collective-permute-done((f32[64,128]{1,0:T(8,128)S(1)}, f32[64,128]{1,0:T(8,128)S(1)}, u32[]{:S(2)}, u32[]{:S(2)}) %collective-permute-start.9) | collective-permute-done | bytes 32800 | tf_op jit(solution)/shard_map/ppermute | solution.py:27
  37.6 0.4 fusion.50
  38.0 0.6 collective-permute-start.12
  38.6 0.6 collective-permute-start.13
  39.2 2.4 %collective-permute-start.14 = (f32[64,128]{1,0:T(8,128)S(1)}, f32[64,128]{1,0:T(8,128)S(1)}, u32[]{:S(2)}, u32[]{:S(2)}) collective-permute-start(f32[64,128]{1,0:T(8,128)S(1)} %get-tuple-element.24), channel_id=1, source_target_pairs={{0,24},{1,25},{2,26},{3,27},{4,28},{5,29},{6,30},{7,31},{8,16},{9,... | collective-permute-start | bytes 98312 | tf_op jit(solution)/shard_map/ppermute | solution.py:27
  41.7 0.3 collective-permute-done.12
  42.0 0.6 collective-permute-done.13
  42.6 1.4 %collective-permute-done.14 = f32[64,128]{1,0:T(8,128)S(1)} collective-permute-done((f32[64,128]{1,0:T(8,128)S(1)}, f32[64,128]{1,0:T(8,128)S(1)}, u32[]{:S(2)}, u32[]{:S(2)}) %collective-permute-start.14) | collective-permute-done | bytes 32800 | tf_op jit(solution)/shard_map/ppermute | solution.py:27
  44.0 0.6 convolution_bitcast_fusion.4
  44.7 0.1 collective-permute-start.15
  44.8 0.7 %collective-permute-start.3 = (f32[4,64,256]{2,1,0:T(8,128)S(1)}, f32[4,64,256]{2,1,0:T(8,128)S(1)}, u32[]{:S(2)}, u32[]{:S(2)}) collective-permute-start(f32[4,64,256]{2,1,0:T(8,128)S(1)} %pad_maximum_fusion.1), channel_id=1, source_target_pairs={{0,0},{1,4},{2,2},{3,6},{4,1},{5,5},{6,3},{7,7},{8,8},{9,12},{10,1... | collective-permute-start | bytes 786440 | tf_op jit(solution)/shard_map/ppermute | solution.py:27
  45.5 8.7 %collective-permute-done.15 = f32[4,64,128]{2,1,0:T(8,128)S(1)} collective-permute-done((f32[4,64,128]{2,1,0:T(8,128)S(1)}, f32[4,64,128]{2,1,0:T(8,128)S(1)}, u32[]{:S(2)}, u32[]{:S(2)}) %collective-permute-start.15) | collective-permute-done | bytes 131104 | tf_op jit(solution)/shard_map/ppermute | solution.py:27
  54.1 0.6 convolution_bitcast_fusion.3
  54.8 0.1 collective-permute-start.16
  54.8 0.4 fusion.24
  55.2 0.7 %collective-permute-start.10 = (f32[4,64,128]{2,1,0:T(8,128)S(1)}, f32[4,64,128]{2,1,0:T(8,128)S(1)}, u32[]{:S(2)}, u32[]{:S(2)}) collective-permute-start(f32[4,64,128]{2,1,0:T(8,128)S(1)} %fusion.24), channel_id=1, source_target_pairs={{0,0},{1,4},{2,2},{3,6},{4,1},{5,5},{6,3},{7,7},{8,8},{9,12},{10,1... | collective-permute-start | bytes 393224 | tf_op jit(solution)/shard_map/ppermute | solution.py:27
  55.9 4.8 %collective-permute-done.16 = f32[4,64,128]{2,1,0:T(8,128)S(1)} collective-permute-done((f32[4,64,128]{2,1,0:T(8,128)S(1)}, f32[4,64,128]{2,1,0:T(8,128)S(1)}, u32[]{:S(2)}, u32[]{:S(2)}) %collective-permute-start.16) | collective-permute-done | bytes 131104 | tf_op jit(solution)/shard_map/ppermute | solution.py:27
  60.7 0.6 convolution_bitcast_fusion.2
  61.3 0.1 collective-permute-start.17
  61.4 0.0 collective-permute-done.3
  61.4 1.8 %fusion.68 = f32[4,256,128]{2,1,0:T(8,128)} fusion(f32[4,64,256]{2,1,0:T(8,128)S(1)} %collective-permute-done.3, f32[4,64,128]{2,1,0:T(8,128)S(1)} %collective-permute-done.10), kind=kOutput, calls=%fused_computation.123 | convolution fusion | flops 100663296 | bytes 917504 | tf_op jit(solution)/shard_map/krs,krv->ksv/dot_general | solution.py:131
  63.3 0.4 fusion.70
  63.7 0.4 fusion.22
  64.1 0.6 convolution_bitcast_fusion
  64.7 1.0 %copy.21 = f32[4,256,128]{2,1,0:T(8,128)} copy(f32[4,256,128]{1,2,0:T(8,128)S(1)} %convolution_bitcast_fusion) | data formatting | bytes 1048576 | tf_op jit(solution)/shard_map/ksr,krv->ksv/dot_general | solution.py:142
  (42 shorter events, 0.6 us)
Async XLA Ops:
  0.6 6.7 %copy-start = (f32[1024,128]{1,0:T(8,128)S(1)}, f32[1024,128]{1,0:T(8,128)}, u32[]{:S(2)}) copy-start(f32[1024,128]{1,0:T(8,128)} %param.5) | copy-start | bytes 1572868
  0.7 1.3 %copy-start.3 = (f32[4,256,64]{1,2,0:T(8,128)S(1)}, f32[4,256,64]{1,2,0:T(8,128)}, u32[]{:S(2)}) copy-start(f32[4,256,64]{1,2,0:T(8,128)} %param.9) | copy-start | bytes 786436
  2.1 5.3 %copy-start.2 = (f32[4,256,64]{1,2,0:T(8,128)S(1)}, f32[4,256,64]{1,2,0:T(8,128)}, u32[]{:S(2)}) copy-start(f32[4,256,64]{1,2,0:T(8,128)} %param.7) | copy-start | bytes 786436
  2.1 4.6 %copy-start.4 = (f32[1024]{0:T(1024)S(1)}, f32[1024]{0:T(1024)}, u32[]{:S(2)}) copy-start(f32[1024]{0:T(1024)} %param.6) | copy-start | bytes 12292
  2.1 11.3 %collective-permute-start = (f32[256,128]{1,0:T(8,128)S(1)}, f32[256,128]{1,0:T(8,128)S(1)}, u32[]{:S(2)}, u32[]{:S(2)}) collective-permute-start(f32[256,128]{1,0:T(8,128)S(1)} %get-tuple-element.12), channel_id=1, source_target_pairs={{0,8},{1,9},{2,10},{3,11},{4,12},{5,13},{6,14},{7,15},{8,0},{9,1},... | collective-permute-start | bytes 393224 | tf_op jit(solution)/shard_map/ppermute | solution.py:27
  5.2 8.3 %collective-permute-start.1 = (f32[256,128]{1,0:T(8,128)S(1)}, f32[256,128]{1,0:T(8,128)S(1)}, u32[]{:S(2)}, u32[]{:S(2)}) collective-permute-start(f32[256,128]{1,0:T(8,128)S(1)} %get-tuple-element.11), channel_id=1, source_target_pairs={{0,16},{1,17},{2,18},{3,19},{4,20},{5,21},{6,22},{7,23},{8,24},{9,... | collective-permute-start | bytes 393224 | tf_op jit(solution)/shard_map/ppermute | solution.py:27
  6.7 6.8 %collective-permute-start.2 = (f32[256,128]{1,0:T(8,128)S(1)}, f32[256,128]{1,0:T(8,128)S(1)}, u32[]{:S(2)}, u32[]{:S(2)}) collective-permute-start(f32[256,128]{1,0:T(8,128)S(1)} %get-tuple-element.10), channel_id=1, source_target_pairs={{0,24},{1,25},{2,26},{3,27},{4,28},{5,29},{6,30},{7,31},{8,16},{9,... | collective-permute-start | bytes 393224 | tf_op jit(solution)/shard_map/ppermute | solution.py:27
  6.7 6.7 %collective-permute-start.11 = (f32[1024]{0:T(1024)S(1)}, f32[1024]{0:T(1024)S(1)}, u32[]{:S(2)}, u32[]{:S(2)}) collective-permute-start(f32[1024]{0:T(1024)S(1)} %copy-done.4), channel_id=1, source_target_pairs={{0,0},{1,4},{2,2},{3,6},{4,1},{5,5},{6,3},{7,7},{8,8},{9,12},{10,1... | collective-permute-start | bytes 12296 | tf_op jit(solution)/shard_map/ppermute | solution.py:27
  8.4 5.6 %collective-permute-start.4 = (f32[4,64,128]{2,1,0:T(8,128)S(1)}, f32[4,64,128]{2,1,0:T(8,128)S(1)}, u32[]{:S(2)}, u32[]{:S(2)}) collective-permute-start(f32[4,64,128]{2,1,0:T(8,128)S(1)} %bitcast.205), channel_id=1, source_target_pairs={{0,1},{1,0},{2,3},{3,2},{4,5},{5,4},{6,7},{7,6},{8,9},{9,8},{10,11... | collective-permute-start | bytes 393224 | tf_op jit(solution)/shard_map/ppermute | solution.py:27
  13.6 1.2 %copy-start.1 = (f32[7,4,64,128]{3,2,1,0:T(8,128)S(1)}, f32[7,4,64,128]{3,2,1,0:T(8,128)}, u32[]{:S(2)}) copy-start(f32[7,4,64,128]{3,2,1,0:T(8,128)} %param.8) | copy-start | bytes 2752516
  15.1 5.5 %collective-permute-start.5 = (f32[4,64,128]{2,1,0:T(8,128)S(1)}, f32[4,64,128]{2,1,0:T(8,128)S(1)}, u32[]{:S(2)}, u32[]{:S(2)}) collective-permute-start(f32[4,64,128]{2,1,0:T(8,128)S(1)} %convolution_bitcast_fusion.6), channel_id=1, source_target_pairs={{0,2},{1,3},{2,0},{3,1},{4,6},{5,7},{6,4},{7,5},{8,10},{9,11},{10,... | collective-permute-start | bytes 393224 | tf_op jit(solution)/shard_map/ppermute | solution.py:27
  21.0 8.3 %collective-permute-start.6 = (f32[4,64,128]{2,1,0:T(8,128)S(1)}, f32[4,64,128]{2,1,0:T(8,128)S(1)}, u32[]{:S(2)}, u32[]{:S(2)}) collective-permute-start(f32[4,64,128]{2,1,0:T(8,128)S(1)} %convolution_bitcast_fusion.5), channel_id=1, source_target_pairs={{0,4},{1,5},{2,6},{3,7},{4,0},{5,1},{6,2},{7,3},{8,12},{9,13},{10,... | collective-permute-start | bytes 393224 | tf_op jit(solution)/shard_map/ppermute | solution.py:27
  29.7 4.2 %collective-permute-start.7 = (f32[64,128]{1,0:T(8,128)S(1)}, f32[64,128]{1,0:T(8,128)S(1)}, u32[]{:S(2)}, u32[]{:S(2)}) collective-permute-start(f32[64,128]{1,0:T(8,128)S(1)} %get-tuple-element.30), channel_id=1, source_target_pairs={{0,8},{1,9},{2,10},{3,11},{4,12},{5,13},{6,14},{7,15},{8,0},{9,1},... | collective-permute-start | bytes 98312 | tf_op jit(solution)/shard_map/ppermute | solution.py:27
  31.3 4.2 %collective-permute-start.8 = (f32[64,128]{1,0:T(8,128)S(1)}, f32[64,128]{1,0:T(8,128)S(1)}, u32[]{:S(2)}, u32[]{:S(2)}) collective-permute-start(f32[64,128]{1,0:T(8,128)S(1)} %get-tuple-element.29), channel_id=1, source_target_pairs={{0,16},{1,17},{2,18},{3,19},{4,20},{5,21},{6,22},{7,23},{8,24},{9,... | collective-permute-start | bytes 98312 | tf_op jit(solution)/shard_map/ppermute | solution.py:27
  32.8 4.8 %collective-permute-start.9 = (f32[64,128]{1,0:T(8,128)S(1)}, f32[64,128]{1,0:T(8,128)S(1)}, u32[]{:S(2)}, u32[]{:S(2)}) collective-permute-start(f32[64,128]{1,0:T(8,128)S(1)} %get-tuple-element.28), channel_id=1, source_target_pairs={{0,24},{1,25},{2,26},{3,27},{4,28},{5,29},{6,30},{7,31},{8,16},{9,... | collective-permute-start | bytes 98312 | tf_op jit(solution)/shard_map/ppermute | solution.py:27
  38.0 4.0 %collective-permute-start.12 = (f32[64,128]{1,0:T(8,128)S(1)}, f32[64,128]{1,0:T(8,128)S(1)}, u32[]{:S(2)}, u32[]{:S(2)}) collective-permute-start(f32[64,128]{1,0:T(8,128)S(1)} %get-tuple-element.26), channel_id=1, source_target_pairs={{0,8},{1,9},{2,10},{3,11},{4,12},{5,13},{6,14},{7,15},{8,0},{9,1},... | collective-permute-start | bytes 98312 | tf_op jit(solution)/shard_map/ppermute | solution.py:27
  38.6 4.0 %collective-permute-start.13 = (f32[64,128]{1,0:T(8,128)S(1)}, f32[64,128]{1,0:T(8,128)S(1)}, u32[]{:S(2)}, u32[]{:S(2)}) collective-permute-start(f32[64,128]{1,0:T(8,128)S(1)} %get-tuple-element.25), channel_id=1, source_target_pairs={{0,16},{1,17},{2,18},{3,19},{4,20},{5,21},{6,22},{7,23},{8,24},{9,... | collective-permute-start | bytes 98312 | tf_op jit(solution)/shard_map/ppermute | solution.py:27
  39.2 4.8 %collective-permute-start.14 = (f32[64,128]{1,0:T(8,128)S(1)}, f32[64,128]{1,0:T(8,128)S(1)}, u32[]{:S(2)}, u32[]{:S(2)}) collective-permute-start(f32[64,128]{1,0:T(8,128)S(1)} %get-tuple-element.24), channel_id=1, source_target_pairs={{0,24},{1,25},{2,26},{3,27},{4,28},{5,29},{6,30},{7,31},{8,16},{9,... | collective-permute-start | bytes 98312 | tf_op jit(solution)/shard_map/ppermute | solution.py:27
  44.7 9.5 %collective-permute-start.15 = (f32[4,64,128]{2,1,0:T(8,128)S(1)}, f32[4,64,128]{2,1,0:T(8,128)S(1)}, u32[]{:S(2)}, u32[]{:S(2)}) collective-permute-start(f32[4,64,128]{2,1,0:T(8,128)S(1)} %slice_select_fusion.2), channel_id=1, source_target_pairs={{0,4},{1,5},{2,6},{3,7},{4,0},{5,1},{6,2},{7,3},{8,12},{9,13},{10,... | collective-permute-start | bytes 393224 | tf_op jit(solution)/shard_map/ppermute | solution.py:27
  44.8 16.6 %collective-permute-start.3 = (f32[4,64,256]{2,1,0:T(8,128)S(1)}, f32[4,64,256]{2,1,0:T(8,128)S(1)}, u32[]{:S(2)}, u32[]{:S(2)}) collective-permute-start(f32[4,64,256]{2,1,0:T(8,128)S(1)} %pad_maximum_fusion.1), channel_id=1, source_target_pairs={{0,0},{1,4},{2,2},{3,6},{4,1},{5,5},{6,3},{7,7},{8,8},{9,12},{10,1... | collective-permute-start | bytes 786440 | tf_op jit(solution)/shard_map/ppermute | solution.py:27
  54.8 5.9 %collective-permute-start.16 = (f32[4,64,128]{2,1,0:T(8,128)S(1)}, f32[4,64,128]{2,1,0:T(8,128)S(1)}, u32[]{:S(2)}, u32[]{:S(2)}) collective-permute-start(f32[4,64,128]{2,1,0:T(8,128)S(1)} %slice_select_fusion.1), channel_id=1, source_target_pairs={{0,2},{1,3},{2,0},{3,1},{4,6},{5,7},{6,4},{7,5},{8,10},{9,11},{10,... | collective-permute-start | bytes 393224 | tf_op jit(solution)/shard_map/ppermute | solution.py:27
  55.2 6.2 %collective-permute-start.10 = (f32[4,64,128]{2,1,0:T(8,128)S(1)}, f32[4,64,128]{2,1,0:T(8,128)S(1)}, u32[]{:S(2)}, u32[]{:S(2)}) collective-permute-start(f32[4,64,128]{2,1,0:T(8,128)S(1)} %fusion.24), channel_id=1, source_target_pairs={{0,0},{1,4},{2,2},{3,6},{4,1},{5,5},{6,3},{7,7},{8,8},{9,12},{10,1... | collective-permute-start | bytes 393224 | tf_op jit(solution)/shard_map/ppermute | solution.py:27
  61.3 1.9 %collective-permute-start.17 = (f32[4,64,128]{2,1,0:T(8,128)S(1)}, f32[4,64,128]{2,1,0:T(8,128)S(1)}, u32[]{:S(2)}, u32[]{:S(2)}) collective-permute-start(f32[4,64,128]{2,1,0:T(8,128)S(1)} %slice_select_fusion), channel_id=1, source_target_pairs={{0,1},{1,0},{2,3},{3,2},{4,5},{5,4},{6,7},{7,6},{8,9},{9,8},{10,11... | collective-permute-start | bytes 393224 | tf_op jit(solution)/shard_map/ppermute | solution.py:27

commit v5 on v2

v5 whole, which is shorter than its diff:
```python
import functools

import jax
import jax.numpy as jnp
from jax import lax
from jax.experimental import pallas as pl
from jax.experimental.pallas import tpu as pltpu
from jax.sharding import PartitionSpec as P


SLOT_BITS = 2
SLOTS = 2**SLOT_BITS
BOTH = ("row", "col")
NN, TN, NT = ((1,), (0,)), ((0,), (0,)), ((1,), (1,))
VMEM = pl.BlockSpec(memory_space=pltpu.VMEM)
SMEM = pl.BlockSpec(memory_space=pltpu.SMEM)
ANY = pl.BlockSpec(memory_space=pl.ANY)
HBM = pl.BlockSpec(memory_space=pltpu.HBM)


def reverse_bits(value, bits):
    out = 0
    for i in range(bits):
        out = out | ((value >> i) & 1) << (bits - 1 - i)
    return out


class Places:
    def __init__(self, slot_bits):
        self.devices = lax.axis_size("row") * lax.axis_size("col")
        self.slot_bits = slot_bits
        self.low_bits = self.devices.bit_length() - 1 - slot_bits
        self.place = lax.axis_index("row") * lax.axis_size("col") + lax.axis_index("col")
        self.top = self.place >> self.low_bits

    def permute(self, block, route):
        return lax.ppermute(block, BOTH, [(d, route(d)) for d in range(self.devices)])

    def partner(self, block, bit):
        return self.permute(block, lambda d: d ^ (1 << bit))

    def reverse_low(self, block):
        low = self.low_bits
        return self.permute(
            block, lambda d: (d >> low) << low | reverse_bits(d & (2**low - 1), low)
        )

    def across(self, blocks):
        return [
            b if k == 0 else self.permute(b, lambda d: d ^ (k << self.low_bits))
            for k, b in enumerate(blocks)
        ]

    def scalars(self):
        order = [reverse_bits(self.top ^ k, self.slot_bits) for k in range(SLOTS)]
        bits = [(self.place >> bit) & 1 for bit in range(self.low_bits)]
        return jnp.stack(order + bits).astype(jnp.int32)


def split(x):
    high = x.astype(jnp.bfloat16)
    return high, (x - high.astype(jnp.float32)).astype(jnp.bfloat16)


def product(a, b, dims):
    (ah, al), (bh, bl) = split(a), split(b)

    def dot(x, y):
        return lax.dot_general(x, y, (dims, ((), ())), preferred_element_type=jnp.float32)

    return dot(ah, bh) + (dot(ah, bl) + dot(al, bh))


def call(kernel, outs, operands, specs=None, out_specs=None, scratch=(), flops=1 << 24):
    shapes = [jax.ShapeDtypeStruct(s, jnp.float32) for s in outs]
    return pl.pallas_call(
        kernel,
        out_shape=shapes,
        in_specs=specs or [VMEM] * len(operands),
        out_specs=out_specs or [VMEM] * len(outs),
        scratch_shapes=list(scratch),
        compiler_params=pltpu.CompilerParams(vmem_limit_bytes=8 << 20),
        cost_estimate=pl.CostEstimate(flops=flops, bytes_accessed=1 << 19, transcendentals=0),
    )(*operands)


def pairs(bit):
    return [(s, s | 1 << bit) for s in range(SLOTS) if not s >> bit & 1]


def head_kernel(vectors_in, basis_in, transfer_in, target_in, out, basis, transfer, target, vectors, sems):
    leaf = basis.shape[2]
    copies = []

    def fetch(source, to):
        copies.append(pltpu.make_async_copy(source, to, sems.at[len(copies)]))
        copies[-1].start()
        return copies[-1]

    slots = []
    for s in range(SLOTS):
        rows = pl.ds(s * leaf, leaf)
        slots.append(
            (fetch(basis_in.at[s], basis.at[s]), fetch(vectors_in.at[rows], vectors.at[rows]))
        )
    first = fetch(transfer_in.at[pl.ds(0, SLOT_BITS)], transfer.at[pl.ds(0, SLOT_BITS)])
    rest = pl.ds(SLOT_BITS, transfer.shape[0] - SLOT_BITS)
    later = [fetch(transfer_in.at[rest], transfer.at[rest]), fetch(target_in, target)]
    c = []
    for s in range(SLOTS):
        for copy in slots[s]:
            copy.wait()
        c.append(product(basis[s], vectors[s * leaf : (s + 1) * leaf], NN))
    first.wait()
    for level in range(SLOT_BITS):
        for low, high in pairs(level):
            both = jnp.concatenate([c[low], c[high]], axis=0)
            c[low] = product(transfer[level, low], both, NN)
            c[high] = product(transfer[level, high], both, NN)
    for s in range(SLOTS):
        out[s] = c[s]
    for copy in later:
        copy.wait()


def join(level, bit, s, meta, own, partner, transfer):
    upper = meta[SLOTS + bit] == 1
    lower_half = jnp.where(upper, partner[s], own[s])
    upper_half = jnp.where(upper, own[s], partner[s])
    return product(transfer[level, s], jnp.concatenate([lower_half, upper_half], axis=0), NN)


def pair_kernel(level, bit, meta, own, partner, transfer, out):
    for s in range(SLOTS):
        out[s] = join(level, bit, s, meta, own, partner, transfer)


def last_pair_kernel(level, bit, meta, own, partner, transfer, *outs):
    for k in range(SLOTS):
        outs[k][...] = join(level, bit, meta[k], meta, own, partner, transfer)


def pick_kernel(tops, meta, transfer, basis, *outs):
    rank, leaf = basis.shape[1:]
    width = transfer.shape[3]
    for k in range(SLOTS):
        s = meta[k]
        parts = [transfer[level, s] for level in tops]
        parts += [basis[s, :, j : j + width] for j in range(0, leaf, width)]
        for j, part in enumerate(parts):
            outs[k][j * rank : (j + 1) * rank] = part


def arrange_kernel(meta, *refs):
    moved, tops, basis = refs[:SLOTS], refs[SLOTS], refs[SLOTS + 1]
    rank, width = tops.shape[2:]
    for k in range(SLOTS):
        s = meta[k]
        for j in range(SLOT_BITS):
            tops[j, s] = moved[k][j * rank : (j + 1) * rank]
        for j in range(basis.shape[2] // width):
            row = (SLOT_BITS + j) * rank
            basis[s, :, j * width : (j + 1) * width] = moved[k][row : row + rank]


def fold_kernel(meta, tops, basis, weights, wide, middle, columns):
    rank = basis.shape[1]
    blocks = [tops[0, s] for s in range(SLOTS)]
    high = 1 << (SLOT_BITS - 1)
    sources = [[s & ~high, s | high] for s in range(SLOTS)]
    for j in range(1, SLOT_BITS):
        bit = 1 << (SLOT_BITS - 1 - j)
        old, old_sources = blocks, sources
        blocks, sources = [], []
        for s in range(SLOTS):
            halves = [
                product(tops[j, s][:, e * rank : (e + 1) * rank], old[q], NN)
                for e, q in enumerate((s & ~bit, s | bit))
            ]
            blocks.append(jnp.concatenate(halves, axis=1))
            sources.append(old_sources[s & ~bit] + old_sources[s | bit])
    for s in range(SLOTS):
        for at, source in enumerate(sources[s]):
            columns[source, s * rank : (s + 1) * rank] = blocks[s][:, at * rank : (at + 1) * rank]
    ordered = jnp.concatenate([columns[meta[k]] for k in range(SLOTS)], axis=1)
    wide[...] = ordered
    inner = []
    for s in range(SLOTS):
        gram = product(basis[s] * weights[s : s + 1, :], basis[s], NT)
        inner.append(product(gram, ordered[s * rank : (s + 1) * rank], NN))
    middle[...] = product(ordered, jnp.concatenate(inner, axis=0), TN)


def middle_kernel(middle, *refs):
    blocks, outs = refs[:SLOTS], refs[SLOTS:]
    rank = blocks[0].shape[0]
    out = product(middle[...], jnp.concatenate([b[...] for b in blocks], axis=0), NN)
    for k in range(SLOTS):
        outs[k][...] = out[k * rank : (k + 1) * rank]


def top_kernel(wide, *refs):
    blocks, out = refs[:SLOTS], refs[SLOTS]
    rank = blocks[0].shape[0]
    rows = product(wide[...], jnp.concatenate([b[...] for b in blocks], axis=0), NN)
    for s in range(SLOTS):
        out[s] = rows[s * rank : (s + 1) * rank]


def part(level, bit, s, meta, block, transfer, sent, kept):
    upper = meta[SLOTS + bit] == 1
    out = product(transfer[level, s], block, TN)
    rank = sent.shape[1]
    sent[s] = jnp.where(upper, out[:rank], out[rank:])
    kept[s] = jnp.where(upper, out[rank:], out[:rank])


def first_part_kernel(level, bit, meta, transfer, *refs):
    for k in range(SLOTS):
        part(level, bit, meta[k], meta, refs[k][...], transfer, *refs[SLOTS:])


def part_kernel(level, bit, meta, transfer, kept_in, arrived, sent, kept):
    for s in range(SLOTS):
        part(level, bit, s, meta, kept_in[s] + arrived[s], transfer, sent, kept)


def write_rows(rows, out, buffer, sems):
    copies = []
    for s in range(SLOTS):
        leaf = buffer.shape[1]
        buffer[s] = rows(s)
        copies.append(
            pltpu.make_async_copy(buffer.at[s], out.at[pl.ds(s * leaf, leaf)], sems.at[s])
        )
        copies[-1].start()
    for copy in copies:
        copy.wait()


def tail_kernel(kept, arrived, transfer, basis, out, buffer, sems):
    b = [kept[s] + arrived[s] for s in range(SLOTS)]
    rank = b[0].shape[0]
    for level in reversed(range(SLOT_BITS)):
        for low, high in pairs(level):
            blocks = jnp.concatenate([transfer[level, low], transfer[level, high]], axis=0)
            both = product(blocks, jnp.concatenate([b[low], b[high]], axis=0), TN)
            b[low], b[high] = both[:rank], both[rank:]
    write_rows(lambda s: product(basis[s], b[s], TN), out, buffer, sems)


def image_kernel(basis, coeffs, out, buffer, sems):
    write_rows(lambda s: product(basis[s], coeffs[s], TN), out, buffer, sems)


def body(vectors, diagonal, source_basis, transfer, target_basis):
    slots, leaf, rank = source_basis.shape
    vecs = vectors.shape[-1]
    places = Places(SLOT_BITS)
    pair_bits = list(range(places.low_bits))
    nodes, node = (slots, rank, vecs), (rank, vecs)
    basis_shape = (slots, rank, leaf)
    rows_scratch = [pltpu.VMEM((slots, leaf, vecs), jnp.float32), pltpu.SemaphoreType.DMA((slots,))]
    source_t = jnp.swapaxes(source_basis, 1, 2)
    target_t = jnp.swapaxes(target_basis, 1, 2)
    coeffs, source_t, transfer, target_t = call(
        head_kernel,
        [nodes, basis_shape, transfer.shape, basis_shape],
        [
            pltpu.with_memory_space_constraint(x, pltpu.HBM)
            for x in (vectors, source_t, transfer, target_t)
        ],
        [HBM] * 4,
        scratch=[
            pltpu.VMEM(vectors.shape, jnp.float32),
            pltpu.SemaphoreType.DMA((2 * slots + 3,)),
        ],
    )
    meta = places.scalars()
    tops = [SLOT_BITS + places.low_bits + j for j in range(SLOT_BITS)]

    message = (SLOT_BITS * rank + leaf * rank // transfer.shape[3], transfer.shape[3])
    moving = call(
        functools.partial(pick_kernel, tops),
        [message] * slots,
        [meta, transfer, target_t],
        [SMEM, VMEM, VMEM],
    )
    moved = places.across(moving)
    weights = places.reverse_low(diagonal).reshape(slots, leaf)
    top_blocks, basis_t = call(
        arrange_kernel,
        [(SLOT_BITS,) + transfer.shape[1:], basis_shape],
        [meta] + moved,
        [SMEM] + [VMEM] * slots,
    )
    image_basis = places.reverse_low(basis_t)
    square = (slots * rank, slots * rank)
    wide, middle = call(
        fold_kernel,
        [square, square],
        [meta, top_blocks, basis_t, weights],
        [SMEM, VMEM, VMEM, VMEM],
        scratch=[pltpu.VMEM((slots, slots * rank, rank), jnp.float32)],
    )

    for bit in pair_bits:
        partner = places.partner(coeffs, bit)
        last = bit == pair_bits[-1]
        kernel = last_pair_kernel if last else pair_kernel
        blocks = call(
            functools.partial(kernel, SLOT_BITS + bit, bit),
            [node] * slots if last else [nodes],
            [meta, coeffs, partner, transfer],
            [SMEM, VMEM, VMEM, VMEM],
        )
        coeffs = blocks[0]

    blocks = places.across(blocks)
    back = places.across(call(middle_kernel, [node] * slots, [middle] + blocks))
    (coeffs,) = call(top_kernel, [nodes], [wide] + blocks)
    image_coeffs = places.reverse_low(coeffs)
    (forward_image,) = call(
        image_kernel,
        [vectors.shape],
        [image_basis, image_coeffs],
        out_specs=[ANY],
        scratch=rows_scratch,
    )

    for bit in reversed(pair_bits):
        if bit == pair_bits[-1]:
            kernel, operands = first_part_kernel, back
        else:
            kernel, operands = part_kernel, [kept, arrived]
        sent, kept = call(
            functools.partial(kernel, SLOT_BITS + bit, bit),
            [nodes, nodes],
            [meta, transfer] + operands,
            [SMEM] + [VMEM] * (1 + len(operands)),
        )
        arrived = places.partner(sent, bit)
    (adjoint,) = call(
        tail_kernel,
        [vectors.shape],
        [kept, arrived, transfer, source_t],
        out_specs=[ANY],
        scratch=rows_scratch,
    )
    return forward_image, adjoint


def solution(mesh):
    placed = (
        P(BOTH, None),
        P(BOTH),
        P(BOTH, None, None),
        P(None, BOTH, None, None),
        P(BOTH, None, None),
    )

    return jax.shard_map(
        body, mesh=mesh, in_specs=placed, out_specs=(P(BOTH, None), P(BOTH, None)), check_vma=False
    )
```

time: 69.8 us -> 63.5 us (0.910)
  the two profiles are of different devices: /device:TPU:0 before, /device:TPU:1 now
where the time goes in v5:
time: 63.5 us; the launch traced here: 63.4 us
  starting transfers between devices  28.7 us (45%)
  waiting for transfers between devices  20.6 us (32%)
  Pallas kernels  13.1 us (21%)
  between operations  0.83 us (1%)
    ppermute x18, starting transfers between devices, permute(): lax.ppermute(block, BOTH, [(d, route(d)) for d in range(self.devices)])  28.7 us
    ppermute x18, waiting for transfers between devices, permute(): lax.ppermute(block, BOTH, [(d, route(d)) for d in range(self.devices)])  20.6 us
    pallas_call x14, Pallas kernels, call(): pl.pallas_call(kernel, out_shape=shapes, in_specs=specs or [VMEM] * len(o...  13.1 us
  transfers between devices with their start and end apart: 18, of which 9 were waited for; matrix products, arithmetic and copies ran while one was open for 0% of the time, Pallas kernels for 9%

profile of v5, /device:TPU:1, one launch (start us, length us, event | category | flops | bytes accessed | tf_op | source)
XLA Modules:
  0.0 63.4 jit_solution(12770700362911508162)
XLA Ops:
  0.6 2.2 %shard_map.68 = (f32[4,64,128]{2,1,0:T(8,128)S(1)}, f32[4,64,256]{2,1,0:T(8,128)S(1)}, f32[7,4,64,128]{3,2,1,0:T(8,128)S(1)}, f32[4,64,256]{2,1,0:T(8,128)S(1)}) custom-call(f32[1024,128]{1,0:T(8,128)} %vectors_in.1, f32[4,64,256]{2,1,0:T(8,128)} %bitcast.9, f32[7,4,64,128]{3,2,1,0:T(8,128)} %transfer_in.1, f32[4,64,256]{2,1,0:T(8,128)} %bitcast.10), custom_call_target="tpu_custom_call" | custom-call | flops 16777216 | bytes 524288 | tf_op jit(solution)/shard_map/pallas_call | solution.py:76
  2.9 0.1 collective-permute-start.5
  3.0 0.1 stack.31.meta
  3.0 1.2 %collective-permute-done.5.partner = f32[4,64,128]{2,1,0:T(8,128)S(1)} collective-permute-done((f32[4,64,128]{2,1,0:T(8,128)S(1)}, f32[4,64,128]{2,1,0:T(8,128)S(1)}, u32[]{:S(2)}, u32[]{:S(2)}) %collective-permute-start.5) | collective-permute-done | bytes 131104 | tf_op jit(solution)/shard_map/ppermute | solution.py:37
  4.3 0.8 %shard_map.72.own = f32[4,64,128]{2,1,0:T(8,128)S(1)} custom-call(s32[7]{0:T(128)S(1)} %stack.31.meta, f32[4,64,128]{2,1,0:T(8,128)S(1)} %get-tuple-element.37.own, f32[4,64,128]{2,1,0:T(8,128)S(1)} %collective-permute-done.5.partner, f32[7,4,64,128]{3,2,1,0:T(8,128)S(1)} %get-tuple-element.28.transfer), custom_call_target="tpu_custom_call" | custom-call | flops 16777216 | bytes 524288 | tf_op jit(solution)/shard_map/pallas_call | solution.py:76
  5.0 2.5 %collective-permute-start.6 = (f32[4,64,128]{2,1,0:T(8,128)S(1)}, f32[4,64,128]{2,1,0:T(8,128)S(1)}, u32[]{:S(2)}, u32[]{:S(2)}) collective-permute-start(f32[4,64,128]{2,1,0:T(8,128)S(1)} %shard_map.72.own), channel_id=1, source_target_pairs={{0,2},{1,3},{2,0},{3,1},{4,6},{5,7},{6,4},{7,5},{8,10},{9,11},{10,... | collective-permute-start | bytes 393224 | tf_op jit(solution)/shard_map/ppermute | solution.py:37
  7.5 3.5 %collective-permute-done.6.partner = f32[4,64,128]{2,1,0:T(8,128)S(1)} collective-permute-done((f32[4,64,128]{2,1,0:T(8,128)S(1)}, f32[4,64,128]{2,1,0:T(8,128)S(1)}, u32[]{:S(2)}, u32[]{:S(2)}) %collective-permute-start.6) | collective-permute-done | bytes 131104 | tf_op jit(solution)/shard_map/ppermute | solution.py:37
  11.0 0.8 %shard_map.73.own = f32[4,64,128]{2,1,0:T(8,128)S(1)} custom-call(s32[7]{0:T(128)S(1)} %stack.31.meta, f32[4,64,128]{2,1,0:T(8,128)S(1)} %shard_map.72.own, f32[4,64,128]{2,1,0:T(8,128)S(1)} %collective-permute-done.6.partner, f32[7,4,64,128]{3,2,1,0:T(8,128)S(1)} %get-tuple-element.28.transfer), custom_call_target="tpu_custom_call" | custom-call | flops 16777216 | bytes 524288 | tf_op jit(solution)/shard_map/pallas_call | solution.py:76
  11.8 2.2 %collective-permute-start.7 = (f32[4,64,128]{2,1,0:T(8,128)S(1)}, f32[4,64,128]{2,1,0:T(8,128)S(1)}, u32[]{:S(2)}, u32[]{:S(2)}) collective-permute-start(f32[4,64,128]{2,1,0:T(8,128)S(1)} %shard_map.73.own), channel_id=1, source_target_pairs={{0,4},{1,5},{2,6},{3,7},{4,0},{5,1},{6,2},{7,3},{8,12},{9,13},{10,... | collective-permute-start | bytes 393224 | tf_op jit(solution)/shard_map/ppermute | solution.py:37
  14.0 0.6 shard_map.69
  14.6 0.0 copy-start
  14.6 1.3 %collective-permute-start = (f32[256,128]{1,0:T(8,128)S(1)}, f32[256,128]{1,0:T(8,128)S(1)}, u32[]{:S(2)}, u32[]{:S(2)}) collective-permute-start(f32[256,128]{1,0:T(8,128)S(1)} %get-tuple-element.31), channel_id=1, source_target_pairs={{0,8},{1,9},{2,10},{3,11},{4,12},{5,13},{6,14},{7,15},{8,0},{9,1},... | collective-permute-start | bytes 393224 | tf_op jit(solution)/shard_map/ppermute | solution.py:37
  15.9 1.2 %collective-permute-start.1 = (f32[256,128]{1,0:T(8,128)S(1)}, f32[256,128]{1,0:T(8,128)S(1)}, u32[]{:S(2)}, u32[]{:S(2)}) collective-permute-start(f32[256,128]{1,0:T(8,128)S(1)} %get-tuple-element.32), channel_id=1, source_target_pairs={{0,16},{1,17},{2,18},{3,19},{4,20},{5,21},{6,22},{7,23},{8,24},{9,... | collective-permute-start | bytes 393224 | tf_op jit(solution)/shard_map/ppermute | solution.py:37
  17.1 0.2 collective-permute-start.2
  17.3 0.0 copy-done
  17.3 4.0 %collective-permute-start.4 = (f32[1024]{0:T(1024)S(1)}, f32[1024]{0:T(1024)S(1)}, u32[]{:S(2)}, u32[]{:S(2)}) collective-permute-start(f32[1024]{0:T(1024)S(1)} %copy-done), channel_id=1, source_target_pairs={{0,0},{1,4},{2,2},{3,6},{4,1},{5,5},{6,3},{7,7},{8,8},{9,12},{10,1... | collective-permute-start | bytes 12296 | tf_op jit(solution)/shard_map/ppermute | solution.py:37
  21.3 0.0 collective-permute-done.7.partner
  21.4 0.8 %shard_map.74 = (f32[64,128]{1,0:T(8,128)S(1)}, f32[64,128]{1,0:T(8,128)S(1)}, f32[64,128]{1,0:T(8,128)S(1)}, f32[64,128]{1,0:T(8,128)S(1)}) custom-call(s32[7]{0:T(128)S(1)} %stack.31.meta, f32[4,64,128]{2,1,0:T(8,128)S(1)} %shard_map.73.own, f32[4,64,128]{2,1,0:T(8,128)S(1)} %collective-permute-done.7.partner, f32[7,4,64,128]{3,2,1,0:T(8,128)S(1)} %get-tuple-element.28.transfer), custom_call_target="tpu_custom_call" | custom-call | flops 16777216 | bytes 524288 | tf_op jit(solution)/shard_map/pallas_call | solution.py:76
  22.1 1.4 %collective-permute-start.8 = (f32[64,128]{1,0:T(8,128)S(1)}, f32[64,128]{1,0:T(8,128)S(1)}, u32[]{:S(2)}, u32[]{:S(2)}) collective-permute-start(f32[64,128]{1,0:T(8,128)S(1)} %get-tuple-element.39), channel_id=1, source_target_pairs={{0,8},{1,9},{2,10},{3,11},{4,12},{5,13},{6,14},{7,15},{8,0},{9,1},... | collective-permute-start | bytes 98312 | tf_op jit(solution)/shard_map/ppermute | solution.py:37
  23.6 0.0 collective-permute-done.4
  23.6 1.2 %collective-permute-start.9 = (f32[64,128]{1,0:T(8,128)S(1)}, f32[64,128]{1,0:T(8,128)S(1)}, u32[]{:S(2)}, u32[]{:S(2)}) collective-permute-start(f32[64,128]{1,0:T(8,128)S(1)} %get-tuple-element.40), channel_id=1, source_target_pairs={{0,16},{1,17},{2,18},{3,19},{4,20},{5,21},{6,22},{7,23},{8,24},{9,... | collective-permute-start | bytes 98312 | tf_op jit(solution)/shard_map/ppermute | solution.py:37
  24.8 0.0 collective-permute-done.refs_1_
  24.8 1.0 %collective-permute-start.10 = (f32[64,128]{1,0:T(8,128)S(1)}, f32[64,128]{1,0:T(8,128)S(1)}, u32[]{:S(2)}, u32[]{:S(2)}) collective-permute-start(f32[64,128]{1,0:T(8,128)S(1)} %get-tuple-element.41), channel_id=1, source_target_pairs={{0,24},{1,25},{2,26},{3,27},{4,28},{5,29},{6,30},{7,31},{8,16},{9,... | collective-permute-start | bytes 98312 | tf_op jit(solution)/shard_map/ppermute | solution.py:37
  25.8 0.0 collective-permute-done.1.refs_2_
  25.8 0.0 collective-permute-done.2.refs_3_
  25.8 0.6 shard_map.70
  26.4 1.7 %shard_map.71 = (f32[256,256]{1,0:T(8,128)S(1)}, f32[256,256]{1,0:T(8,128)S(1)}) custom-call(s32[7]{0:T(128)S(1)} %stack.31.meta, f32[2,4,64,128]{3,2,1,0:T(8,128)S(1)} %get-tuple-element.35.tops, f32[4,64,256]{2,1,0:T(8,128)S(1)} %get-tuple-element.34.basis, f32[4,256]{1,0:T(4,128)S(1)} %reshape.7.weights), custom_call_target="tpu_custom_call" | custom-call | flops 16777216 | bytes 524288 | tf_op jit(solution)/shard_map/pallas_call | solution.py:76
  28.2 0.0 collective-permute-done.8.refs_1_
  28.2 0.0 collective-permute-done.9.refs_2_
  28.2 0.3 collective-permute-done.10.refs_3_
  28.5 0.2 shard_map.77
  28.7 1.2 %collective-permute-start.12 = (f32[64,128]{1,0:T(8,128)S(1)}, f32[64,128]{1,0:T(8,128)S(1)}, u32[]{:S(2)}, u32[]{:S(2)}) collective-permute-start(f32[64,128]{1,0:T(8,128)S(1)} %get-tuple-element.44), channel_id=1, source_target_pairs={{0,8},{1,9},{2,10},{3,11},{4,12},{5,13},{6,14},{7,15},{8,0},{9,1},... | collective-permute-start | bytes 98312 | tf_op jit(solution)/shard_map/ppermute | solution.py:37
  30.0 0.7 %collective-permute-start.13 = (f32[64,128]{1,0:T(8,128)S(1)}, f32[64,128]{1,0:T(8,128)S(1)}, u32[]{:S(2)}, u32[]{:S(2)}) collective-permute-start(f32[64,128]{1,0:T(8,128)S(1)} %get-tuple-element.45), channel_id=1, source_target_pairs={{0,16},{1,17},{2,18},{3,19},{4,20},{5,21},{6,22},{7,23},{8,24},{9,... | collective-permute-start | bytes 98312 | tf_op jit(solution)/shard_map/ppermute | solution.py:37
  30.6 0.8 %collective-permute-start.14 = (f32[64,128]{1,0:T(8,128)S(1)}, f32[64,128]{1,0:T(8,128)S(1)}, u32[]{:S(2)}, u32[]{:S(2)}) collective-permute-start(f32[64,128]{1,0:T(8,128)S(1)} %get-tuple-element.46), channel_id=1, source_target_pairs={{0,24},{1,25},{2,26},{3,27},{4,28},{5,29},{6,30},{7,31},{8,16},{9,... | collective-permute-start | bytes 98312 | tf_op jit(solution)/shard_map/ppermute | solution.py:37
  31.4 0.1 collective-permute-done.12.refs_1_
  31.6 1.2 %collective-permute-done.13.refs_2_ = f32[64,128]{1,0:T(8,128)S(1)} collective-permute-done((f32[64,128]{1,0:T(8,128)S(1)}, f32[64,128]{1,0:T(8,128)S(1)}, u32[]{:S(2)}, u32[]{:S(2)}) %collective-permute-start.13) | collective-permute-done | bytes 32800 | tf_op jit(solution)/shard_map/ppermute | solution.py:37
  32.7 1.7 %collective-permute-done.14.refs_3_ = f32[64,128]{1,0:T(8,128)S(1)} collective-permute-done((f32[64,128]{1,0:T(8,128)S(1)}, f32[64,128]{1,0:T(8,128)S(1)}, u32[]{:S(2)}, u32[]{:S(2)}) %collective-permute-start.14) | collective-permute-done | bytes 32800 | tf_op jit(solution)/shard_map/ppermute | solution.py:37
  34.4 0.8 %shard_map.78 = (f32[4,64,128]{2,1,0:T(8,128)S(1)}, f32[4,64,128]{2,1,0:T(8,128)S(1)}) custom-call(s32[7]{0:T(128)S(1)} %stack.31.meta, f32[7,4,64,128]{3,2,1,0:T(8,128)S(1)} %get-tuple-element.28.transfer, f32[64,128]{1,0:T(8,128)S(1)} %get-tuple-element.43.refs_0_, f32[64,128]{1,0:T(8,128)S(1)} %collective-permute-done.12.refs_1_, ...), custom_call_target="tpu_custom_call" | custom-call | flops 16777216 | bytes 524288 | tf_op jit(solution)/shard_map/pallas_call | solution.py:76
  35.3 0.1 collective-permute-start.15
  35.3 6.6 %collective-permute-done.15.arrived = f32[4,64,128]{2,1,0:T(8,128)S(1)} collective-permute-done((f32[4,64,128]{2,1,0:T(8,128)S(1)}, f32[4,64,128]{2,1,0:T(8,128)S(1)}, u32[]{:S(2)}, u32[]{:S(2)}) %collective-permute-start.15) | collective-permute-done | bytes 131104 | tf_op jit(solution)/shard_map/ppermute | solution.py:37
  42.0 0.8 %shard_map.79 = (f32[4,64,128]{2,1,0:T(8,128)S(1)}, f32[4,64,128]{2,1,0:T(8,128)S(1)}) custom-call(s32[7]{0:T(128)S(1)} %stack.31.meta, f32[7,4,64,128]{3,2,1,0:T(8,128)S(1)} %get-tuple-element.28.transfer, f32[4,64,128]{2,1,0:T(8,128)S(1)} %get-tuple-element.47.kept_in, f32[4,64,128]{2,1,0:T(8,128)S(1)} %collective-permute-done.15.arrived), custom_call_target="tpu_custom_call" | custom-call | flops 16777216 | bytes 524288 | tf_op jit(solution)/shard_map/pallas_call | solution.py:76
  42.8 0.1 collective-permute-start.16
  42.9 8.7 %collective-permute-start.3 = (f32[4,64,256]{2,1,0:T(8,128)S(1)}, f32[4,64,256]{2,1,0:T(8,128)S(1)}, u32[]{:S(2)}, u32[]{:S(2)}) collective-permute-start(f32[4,64,256]{2,1,0:T(8,128)S(1)} %get-tuple-element.34.basis), channel_id=1, source_target_pairs={{0,0},{1,4},{2,2},{3,6},{4,1},{5,5},{6,3},{7,7},{8,8},{9,12},{10,1... | collective-permute-start | bytes 786440 | tf_op jit(solution)/shard_map/ppermute | solution.py:37
  51.6 0.2 shard_map.75
  51.8 1.9 %collective-permute-start.11 = (f32[4,64,128]{2,1,0:T(8,128)S(1)}, f32[4,64,128]{2,1,0:T(8,128)S(1)}, u32[]{:S(2)}, u32[]{:S(2)}) collective-permute-start(f32[4,64,128]{2,1,0:T(8,128)S(1)} %shard_map.75), channel_id=1, source_target_pairs={{0,0},{1,4},{2,2},{3,6},{4,1},{5,5},{6,3},{7,7},{8,8},{9,12},{10,1... | collective-permute-start | bytes 393224 | tf_op jit(solution)/shard_map/ppermute | solution.py:37
  53.8 0.0 collective-permute-done.16.arrived
  53.8 0.8 %shard_map.80 = (f32[4,64,128]{2,1,0:T(8,128)S(1)}, f32[4,64,128]{2,1,0:T(8,128)S(1)}) custom-call(s32[7]{0:T(128)S(1)} %stack.31.meta, f32[7,4,64,128]{3,2,1,0:T(8,128)S(1)} %get-tuple-element.28.transfer, f32[4,64,128]{2,1,0:T(8,128)S(1)} %get-tuple-element.49.kept_in, f32[4,64,128]{2,1,0:T(8,128)S(1)} %collective-permute-done.16.arrived), custom_call_target="tpu_custom_call" | custom-call | flops 16777216 | bytes 524288 | tf_op jit(solution)/shard_map/pallas_call | solution.py:76
  54.6 0.1 collective-permute-start.17
  54.7 4.6 %collective-permute-done.3.basis = f32[4,64,256]{2,1,0:T(8,128)S(1)} collective-permute-done((f32[4,64,256]{2,1,0:T(8,128)S(1)}, f32[4,64,256]{2,1,0:T(8,128)S(1)}, u32[]{:S(2)}, u32[]{:S(2)}) %collective-permute-start.3) | collective-permute-done | bytes 262176 | tf_op jit(solution)/shard_map/ppermute | solution.py:37
  59.3 1.4 %collective-permute-done.11.coeffs = f32[4,64,128]{2,1,0:T(8,128)S(1)} collective-permute-done((f32[4,64,128]{2,1,0:T(8,128)S(1)}, f32[4,64,128]{2,1,0:T(8,128)S(1)}, u32[]{:S(2)}, u32[]{:S(2)}) %collective-permute-start.11) | collective-permute-done | bytes 131104 | tf_op jit(solution)/shard_map/ppermute | solution.py:37
  60.7 1.1 %shard_map.76 = f32[1024,128]{1,0:T(8,128)} custom-call(f32[4,64,256]{2,1,0:T(8,128)S(1)} %collective-permute-done.3.basis, f32[4,64,128]{2,1,0:T(8,128)S(1)} %collective-permute-done.11.coeffs), custom_call_target="tpu_custom_call" | custom-call | flops 16777216 | bytes 524288 | tf_op jit(solution)/shard_map/pallas_call | solution.py:76
  61.9 0.0 collective-permute-done.17.arrived
  61.9 1.5 %shard_map.81 = f32[1024,128]{1,0:T(8,128)} custom-call(f32[4,64,128]{2,1,0:T(8,128)S(1)} %get-tuple-element.51.kept, f32[4,64,128]{2,1,0:T(8,128)S(1)} %collective-permute-done.17.arrived, f32[7,4,64,128]{3,2,1,0:T(8,128)S(1)} %get-tuple-element.28.transfer, f32[4,64,256]{2,1,0:T(8,128)S(1)} %get-tuple-element.53.basis), custom_call_target="tpu_custom_call" | custom-call | flops 16777216 | bytes 524288 | tf_op jit(solution)/shard_map/pallas_call | solution.py:76
  (1 shorter events, 0.0 us)
Async XLA Ops:
  2.9 1.4 %collective-permute-start.5 = (f32[4,64,128]{2,1,0:T(8,128)S(1)}, f32[4,64,128]{2,1,0:T(8,128)S(1)}, u32[]{:S(2)}, u32[]{:S(2)}) collective-permute-start(f32[4,64,128]{2,1,0:T(8,128)S(1)} %get-tuple-element.37.own), channel_id=1, source_target_pairs={{0,1},{1,0},{2,3},{3,2},{4,5},{5,4},{6,7},{7,6},{8,9},{9,8},{10,11... | collective-permute-start | bytes 393224 | tf_op jit(solution)/shard_map/ppermute | solution.py:37
  5.0 6.0 %collective-permute-start.6 = (f32[4,64,128]{2,1,0:T(8,128)S(1)}, f32[4,64,128]{2,1,0:T(8,128)S(1)}, u32[]{:S(2)}, u32[]{:S(2)}) collective-permute-start(f32[4,64,128]{2,1,0:T(8,128)S(1)} %shard_map.72.own), channel_id=1, source_target_pairs={{0,2},{1,3},{2,0},{3,1},{4,6},{5,7},{6,4},{7,5},{8,10},{9,11},{10,... | collective-permute-start | bytes 393224 | tf_op jit(solution)/shard_map/ppermute | solution.py:37
  11.8 9.6 %collective-permute-start.7 = (f32[4,64,128]{2,1,0:T(8,128)S(1)}, f32[4,64,128]{2,1,0:T(8,128)S(1)}, u32[]{:S(2)}, u32[]{:S(2)}) collective-permute-start(f32[4,64,128]{2,1,0:T(8,128)S(1)} %shard_map.73.own), channel_id=1, source_target_pairs={{0,4},{1,5},{2,6},{3,7},{4,0},{5,1},{6,2},{7,3},{8,12},{9,13},{10,... | collective-permute-start | bytes 393224 | tf_op jit(solution)/shard_map/ppermute | solution.py:37
  14.6 2.7 %copy-start = (f32[1024]{0:T(1024)S(1)}, f32[1024]{0:T(1024)}, u32[]{:S(2)}) copy-start(f32[1024]{0:T(1024)} %param.6) | copy-start | bytes 12292
  14.6 10.2 %collective-permute-start = (f32[256,128]{1,0:T(8,128)S(1)}, f32[256,128]{1,0:T(8,128)S(1)}, u32[]{:S(2)}, u32[]{:S(2)}) collective-permute-start(f32[256,128]{1,0:T(8,128)S(1)} %get-tuple-element.31), channel_id=1, source_target_pairs={{0,8},{1,9},{2,10},{3,11},{4,12},{5,13},{6,14},{7,15},{8,0},{9,1},... | collective-permute-start | bytes 393224 | tf_op jit(solution)/shard_map/ppermute | solution.py:37
  15.9 10.0 %collective-permute-start.1 = (f32[256,128]{1,0:T(8,128)S(1)}, f32[256,128]{1,0:T(8,128)S(1)}, u32[]{:S(2)}, u32[]{:S(2)}) collective-permute-start(f32[256,128]{1,0:T(8,128)S(1)} %get-tuple-element.32), channel_id=1, source_target_pairs={{0,16},{1,17},{2,18},{3,19},{4,20},{5,21},{6,22},{7,23},{8,24},{9,... | collective-permute-start | bytes 393224 | tf_op jit(solution)/shard_map/ppermute | solution.py:37
  17.1 8.7 %collective-permute-start.2 = (f32[256,128]{1,0:T(8,128)S(1)}, f32[256,128]{1,0:T(8,128)S(1)}, u32[]{:S(2)}, u32[]{:S(2)}) collective-permute-start(f32[256,128]{1,0:T(8,128)S(1)} %get-tuple-element.33), channel_id=1, source_target_pairs={{0,24},{1,25},{2,26},{3,27},{4,28},{5,29},{6,30},{7,31},{8,16},{9,... | collective-permute-start | bytes 393224 | tf_op jit(solution)/shard_map/ppermute | solution.py:37
  17.3 6.2 %collective-permute-start.4 = (f32[1024]{0:T(1024)S(1)}, f32[1024]{0:T(1024)S(1)}, u32[]{:S(2)}, u32[]{:S(2)}) collective-permute-start(f32[1024]{0:T(1024)S(1)} %copy-done), channel_id=1, source_target_pairs={{0,0},{1,4},{2,2},{3,6},{4,1},{5,5},{6,3},{7,7},{8,8},{9,12},{10,1... | collective-permute-start | bytes 12296 | tf_op jit(solution)/shard_map/ppermute | solution.py:37
  22.1 6.0 %collective-permute-start.8 = (f32[64,128]{1,0:T(8,128)S(1)}, f32[64,128]{1,0:T(8,128)S(1)}, u32[]{:S(2)}, u32[]{:S(2)}) collective-permute-start(f32[64,128]{1,0:T(8,128)S(1)} %get-tuple-element.39), channel_id=1, source_target_pairs={{0,8},{1,9},{2,10},{3,11},{4,12},{5,13},{6,14},{7,15},{8,0},{9,1},... | collective-permute-start | bytes 98312 | tf_op jit(solution)/shard_map/ppermute | solution.py:37
  23.6 4.6 %collective-permute-start.9 = (f32[64,128]{1,0:T(8,128)S(1)}, f32[64,128]{1,0:T(8,128)S(1)}, u32[]{:S(2)}, u32[]{:S(2)}) collective-permute-start(f32[64,128]{1,0:T(8,128)S(1)} %get-tuple-element.40), channel_id=1, source_target_pairs={{0,16},{1,17},{2,18},{3,19},{4,20},{5,21},{6,22},{7,23},{8,24},{9,... | collective-permute-start | bytes 98312 | tf_op jit(solution)/shard_map/ppermute | solution.py:37
  24.8 3.7 %collective-permute-start.10 = (f32[64,128]{1,0:T(8,128)S(1)}, f32[64,128]{1,0:T(8,128)S(1)}, u32[]{:S(2)}, u32[]{:S(2)}) collective-permute-start(f32[64,128]{1,0:T(8,128)S(1)} %get-tuple-element.41), channel_id=1, source_target_pairs={{0,24},{1,25},{2,26},{3,27},{4,28},{5,29},{6,30},{7,31},{8,16},{9,... | collective-permute-start | bytes 98312 | tf_op jit(solution)/shard_map/ppermute | solution.py:37
  28.7 2.8 %collective-permute-start.12 = (f32[64,128]{1,0:T(8,128)S(1)}, f32[64,128]{1,0:T(8,128)S(1)}, u32[]{:S(2)}, u32[]{:S(2)}) collective-permute-start(f32[64,128]{1,0:T(8,128)S(1)} %get-tuple-element.44), channel_id=1, source_target_pairs={{0,8},{1,9},{2,10},{3,11},{4,12},{5,13},{6,14},{7,15},{8,0},{9,1},... | collective-permute-start | bytes 98312 | tf_op jit(solution)/shard_map/ppermute | solution.py:37
  30.0 2.8 %collective-permute-start.13 = (f32[64,128]{1,0:T(8,128)S(1)}, f32[64,128]{1,0:T(8,128)S(1)}, u32[]{:S(2)}, u32[]{:S(2)}) collective-permute-start(f32[64,128]{1,0:T(8,128)S(1)} %get-tuple-element.45), channel_id=1, source_target_pairs={{0,16},{1,17},{2,18},{3,19},{4,20},{5,21},{6,22},{7,23},{8,24},{9,... | collective-permute-start | bytes 98312 | tf_op jit(solution)/shard_map/ppermute | solution.py:37
  30.6 3.8 %collective-permute-start.14 = (f32[64,128]{1,0:T(8,128)S(1)}, f32[64,128]{1,0:T(8,128)S(1)}, u32[]{:S(2)}, u32[]{:S(2)}) collective-permute-start(f32[64,128]{1,0:T(8,128)S(1)} %get-tuple-element.46), channel_id=1, source_target_pairs={{0,24},{1,25},{2,26},{3,27},{4,28},{5,29},{6,30},{7,31},{8,16},{9,... | collective-permute-start | bytes 98312 | tf_op jit(solution)/shard_map/ppermute | solution.py:37
  35.3 6.7 %collective-permute-start.15 = (f32[4,64,128]{2,1,0:T(8,128)S(1)}, f32[4,64,128]{2,1,0:T(8,128)S(1)}, u32[]{:S(2)}, u32[]{:S(2)}) collective-permute-start(f32[4,64,128]{2,1,0:T(8,128)S(1)} %get-tuple-element.48), channel_id=1, source_target_pairs={{0,4},{1,5},{2,6},{3,7},{4,0},{5,1},{6,2},{7,3},{8,12},{9,13},{10,... | collective-permute-start | bytes 393224 | tf_op jit(solution)/shard_map/ppermute | solution.py:37
  42.8 11.0 %collective-permute-start.16 = (f32[4,64,128]{2,1,0:T(8,128)S(1)}, f32[4,64,128]{2,1,0:T(8,128)S(1)}, u32[]{:S(2)}, u32[]{:S(2)}) collective-permute-start(f32[4,64,128]{2,1,0:T(8,128)S(1)} %get-tuple-element.50), channel_id=1, source_target_pairs={{0,2},{1,3},{2,0},{3,1},{4,6},{5,7},{6,4},{7,5},{8,10},{9,11},{10,... | collective-permute-start | bytes 393224 | tf_op jit(solution)/shard_map/ppermute | solution.py:37
  42.9 16.4 %collective-permute-start.3 = (f32[4,64,256]{2,1,0:T(8,128)S(1)}, f32[4,64,256]{2,1,0:T(8,128)S(1)}, u32[]{:S(2)}, u32[]{:S(2)}) collective-permute-start(f32[4,64,256]{2,1,0:T(8,128)S(1)} %get-tuple-element.34.basis), channel_id=1, source_target_pairs={{0,0},{1,4},{2,2},{3,6},{4,1},{5,5},{6,3},{7,7},{8,8},{9,12},{10,1... | collective-permute-start | bytes 786440 | tf_op jit(solution)/shard_map/ppermute | solution.py:37
  51.8 8.9 %collective-permute-start.11 = (f32[4,64,128]{2,1,0:T(8,128)S(1)}, f32[4,64,128]{2,1,0:T(8,128)S(1)}, u32[]{:S(2)}, u32[]{:S(2)}) collective-permute-start(f32[4,64,128]{2,1,0:T(8,128)S(1)} %shard_map.75), channel_id=1, source_target_pairs={{0,0},{1,4},{2,2},{3,6},{4,1},{5,5},{6,3},{7,7},{8,8},{9,12},{10,1... | collective-permute-start | bytes 393224 | tf_op jit(solution)/shard_map/ppermute | solution.py:37
  54.6 7.2 %collective-permute-start.17 = (f32[4,64,128]{2,1,0:T(8,128)S(1)}, f32[4,64,128]{2,1,0:T(8,128)S(1)}, u32[]{:S(2)}, u32[]{:S(2)}) collective-permute-start(f32[4,64,128]{2,1,0:T(8,128)S(1)} %get-tuple-element.52), channel_id=1, source_target_pairs={{0,1},{1,0},{2,3},{3,2},{4,5},{5,4},{6,7},{7,6},{8,9},{9,8},{10,11... | collective-permute-start | bytes 393224 | tf_op jit(solution)/shard_map/ppermute | solution.py:37

commit v6 on v5

--- a/solution.py
+++ b/solution.py
@@ -13,7 +13,6 @@
 BOTH = ("row", "col")
 NN, TN, NT = ((1,), (0,)), ((0,), (0,)), ((1,), (1,))
 VMEM = pl.BlockSpec(memory_space=pltpu.VMEM)
-SMEM = pl.BlockSpec(memory_space=pltpu.SMEM)
 ANY = pl.BlockSpec(memory_space=pl.ANY)
 HBM = pl.BlockSpec(memory_space=pltpu.HBM)
 
@@ -28,10 +27,7 @@
 class Places:
     def __init__(self, slot_bits):
         self.devices = lax.axis_size("row") * lax.axis_size("col")
-        self.slot_bits = slot_bits
         self.low_bits = self.devices.bit_length() - 1 - slot_bits
-        self.place = lax.axis_index("row") * lax.axis_size("col") + lax.axis_index("col")
-        self.top = self.place >> self.low_bits
 
     def permute(self, block, route):
         return lax.ppermute(block, BOTH, [(d, route(d)) for d in range(self.devices)])
@@ -51,10 +47,21 @@
             for k, b in enumerate(blocks)
         ]
 
-    def scalars(self):
-        order = [reverse_bits(self.top ^ k, self.slot_bits) for k in range(SLOTS)]
-        bits = [(self.place >> bit) & 1 for bit in range(self.low_bits)]
-        return jnp.stack(order + bits).astype(jnp.int32)
+
+def place():
+    return lax.axis_index("row") * lax.axis_size("col") + lax.axis_index("col")
+
+
+def low_bits():
+    return (lax.axis_size("row") * lax.axis_size("col")).bit_length() - 1 - SLOT_BITS
+
+
+def met(k):
+    return reverse_bits((place() >> low_bits()) ^ k, SLOT_BITS)
+
+
+def is_upper(bit):
+    return (place() >> bit) & 1 == 1
 
 
 def split(x):
@@ -123,39 +130,39 @@
         copy.wait()
 
 
-def join(level, bit, s, meta, own, partner, transfer):
-    upper = meta[SLOTS + bit] == 1
+def join(level, bit, s, own, partner, transfer):
+    upper = is_upper(bit)
     lower_half = jnp.where(upper, partner[s], own[s])
     upper_half = jnp.where(upper, own[s], partner[s])
     return product(transfer[level, s], jnp.concatenate([lower_half, upper_half], axis=0), NN)
 
 
-def pair_kernel(level, bit, meta, own, partner, transfer, out):
-    for s in range(SLOTS):
-        out[s] = join(level, bit, s, meta, own, partner, transfer)
-
-
-def last_pair_kernel(level, bit, meta, own, partner, transfer, *outs):
-    for k in range(SLOTS):
-        outs[k][...] = join(level, bit, meta[k], meta, own, partner, transfer)
-
-
-def pick_kernel(tops, meta, transfer, basis, *outs):
+def pair_kernel(level, bit, own, partner, transfer, out):
+    for s in range(SLOTS):
+        out[s] = join(level, bit, s, own, partner, transfer)
+
+
+def last_pair_kernel(level, bit, own, partner, transfer, *outs):
+    for k in range(SLOTS):
+        outs[k][...] = join(level, bit, met(k), own, partner, transfer)
+
+
+def pick_kernel(tops, transfer, basis, *outs):
     rank, leaf = basis.shape[1:]
     width = transfer.shape[3]
     for k in range(SLOTS):
-        s = meta[k]
+        s = met(k)
         parts = [transfer[level, s] for level in tops]
         parts += [basis[s, :, j : j + width] for j in range(0, leaf, width)]
         for j, part in enumerate(parts):
             outs[k][j * rank : (j + 1) * rank] = part
 
 
-def arrange_kernel(meta, *refs):
+def arrange_kernel(*refs):
     moved, tops, basis = refs[:SLOTS], refs[SLOTS], refs[SLOTS + 1]
     rank, width = tops.shape[2:]
     for k in range(SLOTS):
-        s = meta[k]
+        s = met(k)
         for j in range(SLOT_BITS):
             tops[j, s] = moved[k][j * rank : (j + 1) * rank]
         for j in range(basis.shape[2] // width):
@@ -163,7 +170,7 @@
             basis[s, :, j * width : (j + 1) * width] = moved[k][row : row + rank]
 
 
-def fold_kernel(meta, tops, basis, weights, wide, middle, columns):
+def fold_kernel(tops, basis, weights, wide, middle, columns):
     rank = basis.shape[1]
     blocks = [tops[0, s] for s in range(SLOTS)]
     high = 1 << (SLOT_BITS - 1)
@@ -182,7 +189,7 @@
     for s in range(SLOTS):
         for at, source in enumerate(sources[s]):
             columns[source, s * rank : (s + 1) * rank] = blocks[s][:, at * rank : (at + 1) * rank]
-    ordered = jnp.concatenate([columns[meta[k]] for k in range(SLOTS)], axis=1)
+    ordered = jnp.concatenate([columns[met(k)] for k in range(SLOTS)], axis=1)
     wide[...] = ordered
     inner = []
     for s in range(SLOTS):
@@ -207,22 +214,22 @@
         out[s] = rows[s * rank : (s + 1) * rank]
 
 
-def part(level, bit, s, meta, block, transfer, sent, kept):
-    upper = meta[SLOTS + bit] == 1
+def part(level, bit, s, block, transfer, sent, kept):
+    upper = is_upper(bit)
     out = product(transfer[level, s], block, TN)
     rank = sent.shape[1]
     sent[s] = jnp.where(upper, out[:rank], out[rank:])
     kept[s] = jnp.where(upper, out[rank:], out[:rank])
 
 
-def first_part_kernel(level, bit, meta, transfer, *refs):
-    for k in range(SLOTS):
-        part(level, bit, meta[k], meta, refs[k][...], transfer, *refs[SLOTS:])
-
-
-def part_kernel(level, bit, meta, transfer, kept_in, arrived, sent, kept):
-    for s in range(SLOTS):
-        part(level, bit, s, meta, kept_in[s] + arrived[s], transfer, sent, kept)
+def first_part_kernel(level, bit, transfer, *refs):
+    for k in range(SLOTS):
+        part(level, bit, met(k), refs[k][...], transfer, *refs[SLOTS:])
+
+
+def part_kernel(level, bit, transfer, kept_in, arrived, sent, kept):
+    for s in range(SLOTS):
+        part(level, bit, s, kept_in[s] + arrived[s], transfer, sent, kept)
 
 
 def write_rows(rows, out, buffer, sems):
@@ -276,31 +283,21 @@
             pltpu.SemaphoreType.DMA((2 * slots + 3,)),
         ],
     )
-    meta = places.scalars()
     tops = [SLOT_BITS + places.low_bits + j for j in range(SLOT_BITS)]
 
     message = (SLOT_BITS * rank + leaf * rank // transfer.shape[3], transfer.shape[3])
-    moving = call(
-        functools.partial(pick_kernel, tops),
-        [message] * slots,
-        [meta, transfer, target_t],
-        [SMEM, VMEM, VMEM],
-    )
+    moving = call(functools.partial(pick_kernel, tops), [message] * slots, [transfer, target_t])
     moved = places.across(moving)
     weights = places.reverse_low(diagonal).reshape(slots, leaf)
     top_blocks, basis_t = call(
-        arrange_kernel,
-        [(SLOT_BITS,) + transfer.shape[1:], basis_shape],
-        [meta] + moved,
-        [SMEM] + [VMEM] * slots,
+        arrange_kernel, [(SLOT_BITS,) + transfer.shape[1:], basis_shape], moved
     )
     image_basis = places.reverse_low(basis_t)
     square = (slots * rank, slots * rank)
     wide, middle = call(
         fold_kernel,
         [square, square],
-        [meta, top_blocks, basis_t, weights],
-        [SMEM, VMEM, VMEM, VMEM],
+        [top_blocks, basis_t, weights],
         scratch=[pltpu.VMEM((slots, slots * rank, rank), jnp.float32)],
     )
 
@@ -311,8 +308,7 @@
         blocks = call(
             functools.partial(kernel, SLOT_BITS + bit, bit),
             [node] * slots if last else [nodes],
-            [meta, coeffs, partner, transfer],
-            [SMEM, VMEM, VMEM, VMEM],
+            [coeffs, partner, transfer],
         )
         coeffs = blocks[0]
 
@@ -334,10 +330,7 @@
         else:
             kernel, operands = part_kernel, [kept, arrived]
         sent, kept = call(
-            functools.partial(kernel, SLOT_BITS + bit, bit),
-            [nodes, nodes],
-            [meta, transfer] + operands,
-            [SMEM] + [VMEM] * (1 + len(operands)),
+            functools.partial(kernel, SLOT_BITS + bit, bit), [nodes, nodes], [transfer] + operands
         )
         arrived = places.partner(sent, bit)
     (adjoint,) = call(

time: 63.5 us -> 60.9 us (0.959)
  Pallas kernels: 13.1 us -> 8.27 us
  waiting for transfers between devices: 20.6 us -> 22.7 us
    pallas_call x14, Pallas kernels: 13.1 us -> 8.27 us  [call(): pl.pallas_call(kernel, out_shape=shapes, in_specs=specs or [VMEM] * len(o...]
    ppermute x18, waiting for transfers between devices: 20.6 us -> 22.7 us  [permute(): lax.ppermute(block, BOTH, [(d, route(d)) for d in range(self.devices)])]
  transfers between devices with their start and end apart: 18 -> 18, of which waited for: 9 -> 10; matrix products, arithmetic and copies ran while one was open for 0% -> 0% of each run, Pallas kernels for 9% -> 5%
where the time goes in v6:
time: 60.9 us; the launch traced here: 60.7 us
  starting transfers between devices  28.9 us (47%)
  waiting for transfers between devices  22.7 us (37%)
  Pallas kernels  8.27 us (14%)
  between operations  0.81 us (1%)
    ppermute x18, starting transfers between devices, permute(): lax.ppermute(block, BOTH, [(d, route(d)) for d in range(self.devices)])  28.9 us
    ppermute x18, waiting for transfers between devices, permute(): lax.ppermute(block, BOTH, [(d, route(d)) for d in range(self.devices)])  22.7 us
    pallas_call x14, Pallas kernels, call(): pl.pallas_call(kernel, out_shape=shapes, in_specs=specs or [VMEM] * len(o...  8.27 us
  transfers between devices with their start and end apart: 18, of which 10 were waited for; matrix products, arithmetic and copies ran while one was open for 0% of the time, Pallas kernels for 5%

profile of v6, /device:TPU:1, one launch (start us, length us, event | category | flops | bytes accessed | tf_op | source)
XLA Modules:
  0.0 60.7 jit_solution(3229722505188196732)
XLA Ops:
  0.6 2.2 %shard_map.68 = (f32[4,64,128]{2,1,0:T(8,128)S(1)}, f32[4,64,256]{2,1,0:T(8,128)S(1)}, f32[7,4,64,128]{3,2,1,0:T(8,128)S(1)}, f32[4,64,256]{2,1,0:T(8,128)S(1)}) custom-call(f32[1024,128]{1,0:T(8,128)} %vectors_in.1, f32[4,64,256]{2,1,0:T(8,128)} %bitcast.2, f32[7,4,64,128]{3,2,1,0:T(8,128)} %transfer_in.1, f32[4,64,256]{2,1,0:T(8,128)} %bitcast.3), custom_call_target="tpu_custom_call" | custom-call | flops 16777216 | bytes 524288 | tf_op jit(solution)/shard_map/pallas_call | solution.py:83
  2.9 0.1 collective-permute-start.5
  2.9 1.3 %collective-permute-done.5.partner = f32[4,64,128]{2,1,0:T(8,128)S(1)} collective-permute-done((f32[4,64,128]{2,1,0:T(8,128)S(1)}, f32[4,64,128]{2,1,0:T(8,128)S(1)}, u32[]{:S(2)}, u32[]{:S(2)}) %collective-permute-start.5) | collective-permute-done | bytes 131104 | tf_op jit(solution)/shard_map/ppermute | solution.py:33
  4.3 0.2 shard_map.72.own
  4.5 2.5 %collective-permute-start.6 = (f32[4,64,128]{2,1,0:T(8,128)S(1)}, f32[4,64,128]{2,1,0:T(8,128)S(1)}, u32[]{:S(2)}, u32[]{:S(2)}) collective-permute-start(f32[4,64,128]{2,1,0:T(8,128)S(1)} %shard_map.72.own), channel_id=1, source_target_pairs={{0,2},{1,3},{2,0},{3,1},{4,6},{5,7},{6,4},{7,5},{8,10},{9,11},{10,... | collective-permute-start | bytes 393224 | tf_op jit(solution)/shard_map/ppermute | solution.py:33
  7.0 3.5 %collective-permute-done.6.partner = f32[4,64,128]{2,1,0:T(8,128)S(1)} collective-permute-done((f32[4,64,128]{2,1,0:T(8,128)S(1)}, f32[4,64,128]{2,1,0:T(8,128)S(1)}, u32[]{:S(2)}, u32[]{:S(2)}) %collective-permute-start.6) | collective-permute-done | bytes 131104 | tf_op jit(solution)/shard_map/ppermute | solution.py:33
  10.5 0.2 shard_map.73.own
  10.7 2.2 %collective-permute-start.7 = (f32[4,64,128]{2,1,0:T(8,128)S(1)}, f32[4,64,128]{2,1,0:T(8,128)S(1)}, u32[]{:S(2)}, u32[]{:S(2)}) collective-permute-start(f32[4,64,128]{2,1,0:T(8,128)S(1)} %shard_map.73.own), channel_id=1, source_target_pairs={{0,4},{1,5},{2,6},{3,7},{4,0},{5,1},{6,2},{7,3},{8,12},{9,13},{10,... | collective-permute-start | bytes 393224 | tf_op jit(solution)/shard_map/ppermute | solution.py:33
  13.0 0.0 copy-start
  13.0 1.3 %collective-permute-start = (f32[256,128]{1,0:T(8,128)S(1)}, f32[256,128]{1,0:T(8,128)S(1)}, u32[]{:S(2)}, u32[]{:S(2)}) collective-permute-start(f32[256,128]{1,0:T(8,128)S(1)} %get-tuple-element.31), channel_id=1, source_target_pairs={{0,8},{1,9},{2,10},{3,11},{4,12},{5,13},{6,14},{7,15},{8,0},{9,1},... | collective-permute-start | bytes 393224 | tf_op jit(solution)/shard_map/ppermute | solution.py:33
  14.3 1.2 %collective-permute-start.1 = (f32[256,128]{1,0:T(8,128)S(1)}, f32[256,128]{1,0:T(8,128)S(1)}, u32[]{:S(2)}, u32[]{:S(2)}) collective-permute-start(f32[256,128]{1,0:T(8,128)S(1)} %get-tuple-element.32), channel_id=1, source_target_pairs={{0,16},{1,17},{2,18},{3,19},{4,20},{5,21},{6,22},{7,23},{8,24},{9,... | collective-permute-start | bytes 393224 | tf_op jit(solution)/shard_map/ppermute | solution.py:33
  15.5 0.2 collective-permute-start.2
  15.7 0.0 copy-done
  15.7 4.0 %collective-permute-start.4 = (f32[1024]{0:T(1024)S(1)}, f32[1024]{0:T(1024)S(1)}, u32[]{:S(2)}, u32[]{:S(2)}) collective-permute-start(f32[1024]{0:T(1024)S(1)} %copy-done), channel_id=1, source_target_pairs={{0,0},{1,4},{2,2},{3,6},{4,1},{5,5},{6,3},{7,7},{8,8},{9,12},{10,1... | collective-permute-start | bytes 12296 | tf_op jit(solution)/shard_map/ppermute | solution.py:33
  19.7 0.0 collective-permute-done.7.partner
  19.7 0.2 shard_map.74
  20.0 1.4 %collective-permute-start.8 = (f32[64,128]{1,0:T(8,128)S(1)}, f32[64,128]{1,0:T(8,128)S(1)}, u32[]{:S(2)}, u32[]{:S(2)}) collective-permute-start(f32[64,128]{1,0:T(8,128)S(1)} %get-tuple-element.39), channel_id=1, source_target_pairs={{0,8},{1,9},{2,10},{3,11},{4,12},{5,13},{6,14},{7,15},{8,0},{9,1},... | collective-permute-start | bytes 98312 | tf_op jit(solution)/shard_map/ppermute | solution.py:33
  21.4 0.4 collective-permute-done.4
  21.8 1.2 %collective-permute-start.9 = (f32[64,128]{1,0:T(8,128)S(1)}, f32[64,128]{1,0:T(8,128)S(1)}, u32[]{:S(2)}, u32[]{:S(2)}) collective-permute-start(f32[64,128]{1,0:T(8,128)S(1)} %get-tuple-element.40), channel_id=1, source_target_pairs={{0,16},{1,17},{2,18},{3,19},{4,20},{5,21},{6,22},{7,23},{8,24},{9,... | collective-permute-start | bytes 98312 | tf_op jit(solution)/shard_map/ppermute | solution.py:33
  23.1 0.0 collective-permute-done.refs_1_
  23.1 1.2 %collective-permute-start.10 = (f32[64,128]{1,0:T(8,128)S(1)}, f32[64,128]{1,0:T(8,128)S(1)}, u32[]{:S(2)}, u32[]{:S(2)}) collective-permute-start(f32[64,128]{1,0:T(8,128)S(1)} %get-tuple-element.41), channel_id=1, source_target_pairs={{0,24},{1,25},{2,26},{3,27},{4,28},{5,29},{6,30},{7,31},{8,16},{9,... | collective-permute-start | bytes 98312 | tf_op jit(solution)/shard_map/ppermute | solution.py:33
  24.2 0.0 collective-permute-done.1.refs_2_
  24.2 0.0 collective-permute-done.2.refs_3_
  24.3 1.2 %shard_map.71 = (f32[256,256]{1,0:T(8,128)S(1)}, f32[256,256]{1,0:T(8,128)S(1)}) custom-call(f32[2,4,64,128]{3,2,1,0:T(8,128)S(1)} %get-tuple-element.35.tops, f32[4,64,256]{2,1,0:T(8,128)S(1)} %get-tuple-element.34.basis, f32[4,256]{1,0:T(4,128)S(1)} %reshape.7.weights), custom_call_target="tpu_custom_call" | custom-call | flops 16777216 | bytes 524288 | tf_op jit(solution)/shard_map/pallas_call | solution.py:83
  25.5 0.0 collective-permute-done.8.refs_1_
  25.5 0.0 collective-permute-done.9.refs_2_
  25.5 1.2 %collective-permute-done.10.refs_3_ = f32[64,128]{1,0:T(8,128)S(1)} collective-permute-done((f32[64,128]{1,0:T(8,128)S(1)}, f32[64,128]{1,0:T(8,128)S(1)}, u32[]{:S(2)}, u32[]{:S(2)}) %collective-permute-start.10) | collective-permute-done | bytes 32800 | tf_op jit(solution)/shard_map/ppermute | solution.py:33
  26.7 0.2 shard_map.77
  27.0 1.3 %collective-permute-start.12 = (f32[64,128]{1,0:T(8,128)S(1)}, f32[64,128]{1,0:T(8,128)S(1)}, u32[]{:S(2)}, u32[]{:S(2)}) collective-permute-start(f32[64,128]{1,0:T(8,128)S(1)} %get-tuple-element.44), channel_id=1, source_target_pairs={{0,8},{1,9},{2,10},{3,11},{4,12},{5,13},{6,14},{7,15},{8,0},{9,1},... | collective-permute-start | bytes 98312 | tf_op jit(solution)/shard_map/ppermute | solution.py:33
  28.3 0.7 %collective-permute-start.13 = (f32[64,128]{1,0:T(8,128)S(1)}, f32[64,128]{1,0:T(8,128)S(1)}, u32[]{:S(2)}, u32[]{:S(2)}) collective-permute-start(f32[64,128]{1,0:T(8,128)S(1)} %get-tuple-element.45), channel_id=1, source_target_pairs={{0,16},{1,17},{2,18},{3,19},{4,20},{5,21},{6,22},{7,23},{8,24},{9,... | collective-permute-start | bytes 98312 | tf_op jit(solution)/shard_map/ppermute | solution.py:33
  29.0 0.7 %collective-permute-start.14 = (f32[64,128]{1,0:T(8,128)S(1)}, f32[64,128]{1,0:T(8,128)S(1)}, u32[]{:S(2)}, u32[]{:S(2)}) collective-permute-start(f32[64,128]{1,0:T(8,128)S(1)} %get-tuple-element.46), channel_id=1, source_target_pairs={{0,24},{1,25},{2,26},{3,27},{4,28},{5,29},{6,30},{7,31},{8,16},{9,... | collective-permute-start | bytes 98312 | tf_op jit(solution)/shard_map/ppermute | solution.py:33
  29.7 0.1 collective-permute-done.12.refs_1_
  29.8 1.3 %collective-permute-done.13.refs_2_ = f32[64,128]{1,0:T(8,128)S(1)} collective-permute-done((f32[64,128]{1,0:T(8,128)S(1)}, f32[64,128]{1,0:T(8,128)S(1)}, u32[]{:S(2)}, u32[]{:S(2)}) %collective-permute-start.13) | collective-permute-done | bytes 32800 | tf_op jit(solution)/shard_map/ppermute | solution.py:33
  31.1 1.7 %collective-permute-done.14.refs_3_ = f32[64,128]{1,0:T(8,128)S(1)} collective-permute-done((f32[64,128]{1,0:T(8,128)S(1)}, f32[64,128]{1,0:T(8,128)S(1)}, u32[]{:S(2)}, u32[]{:S(2)}) %collective-permute-start.14) | collective-permute-done | bytes 32800 | tf_op jit(solution)/shard_map/ppermute | solution.py:33
  32.8 0.3 shard_map.78
  33.1 0.1 collective-permute-start.15
  33.2 6.6 %collective-permute-done.15.arrived = f32[4,64,128]{2,1,0:T(8,128)S(1)} collective-permute-done((f32[4,64,128]{2,1,0:T(8,128)S(1)}, f32[4,64,128]{2,1,0:T(8,128)S(1)}, u32[]{:S(2)}, u32[]{:S(2)}) %collective-permute-start.15) | collective-permute-done | bytes 131104 | tf_op jit(solution)/shard_map/ppermute | solution.py:33
  39.8 0.3 shard_map.79
  40.1 0.1 collective-permute-start.16
  40.2 8.7 %collective-permute-start.3 = (f32[4,64,256]{2,1,0:T(8,128)S(1)}, f32[4,64,256]{2,1,0:T(8,128)S(1)}, u32[]{:S(2)}, u32[]{:S(2)}) collective-permute-start(f32[4,64,256]{2,1,0:T(8,128)S(1)} %get-tuple-element.34.basis), channel_id=1, source_target_pairs={{0,0},{1,4},{2,2},{3,6},{4,1},{5,5},{6,3},{7,7},{8,8},{9,12},{10,1... | collective-permute-start | bytes 786440 | tf_op jit(solution)/shard_map/ppermute | solution.py:33
  48.9 0.2 shard_map.75
  49.2 1.9 %collective-permute-start.11 = (f32[4,64,128]{2,1,0:T(8,128)S(1)}, f32[4,64,128]{2,1,0:T(8,128)S(1)}, u32[]{:S(2)}, u32[]{:S(2)}) collective-permute-start(f32[4,64,128]{2,1,0:T(8,128)S(1)} %shard_map.75), channel_id=1, source_target_pairs={{0,0},{1,4},{2,2},{3,6},{4,1},{5,5},{6,3},{7,7},{8,8},{9,12},{10,1... | collective-permute-start | bytes 393224 | tf_op jit(solution)/shard_map/ppermute | solution.py:33
  51.1 0.0 collective-permute-done.16.arrived
  51.1 0.3 shard_map.80
  51.4 0.1 collective-permute-start.17
  51.5 5.1 %collective-permute-done.3.basis = f32[4,64,256]{2,1,0:T(8,128)S(1)} collective-permute-done((f32[4,64,256]{2,1,0:T(8,128)S(1)}, f32[4,64,256]{2,1,0:T(8,128)S(1)}, u32[]{:S(2)}, u32[]{:S(2)}) %collective-permute-start.3) | collective-permute-done | bytes 262176 | tf_op jit(solution)/shard_map/ppermute | solution.py:33
  56.6 1.4 %collective-permute-done.11.coeffs = f32[4,64,128]{2,1,0:T(8,128)S(1)} collective-permute-done((f32[4,64,128]{2,1,0:T(8,128)S(1)}, f32[4,64,128]{2,1,0:T(8,128)S(1)}, u32[]{:S(2)}, u32[]{:S(2)}) %collective-permute-start.11) | collective-permute-done | bytes 131104 | tf_op jit(solution)/shard_map/ppermute | solution.py:33
  58.0 1.1 %shard_map.76 = f32[1024,128]{1,0:T(8,128)} custom-call(f32[4,64,256]{2,1,0:T(8,128)S(1)} %collective-permute-done.3.basis, f32[4,64,128]{2,1,0:T(8,128)S(1)} %collective-permute-done.11.coeffs), custom_call_target="tpu_custom_call" | custom-call | flops 16777216 | bytes 524288 | tf_op jit(solution)/shard_map/pallas_call | solution.py:83
  59.2 0.0 collective-permute-done.17.arrived
  59.2 1.5 %shard_map.81 = f32[1024,128]{1,0:T(8,128)} custom-call(f32[4,64,128]{2,1,0:T(8,128)S(1)} %get-tuple-element.51.kept, f32[4,64,128]{2,1,0:T(8,128)S(1)} %collective-permute-done.17.arrived, f32[7,4,64,128]{3,2,1,0:T(8,128)S(1)} %get-tuple-element.28.transfer, f32[4,64,256]{2,1,0:T(8,128)S(1)} %get-tuple-element.53.basis), custom_call_target="tpu_custom_call" | custom-call | flops 16777216 | bytes 524288 | tf_op jit(solution)/shard_map/pallas_call | solution.py:83
  (3 shorter events, 0.1 us)
Async XLA Ops:
  2.9 1.4 %collective-permute-start.5 = (f32[4,64,128]{2,1,0:T(8,128)S(1)}, f32[4,64,128]{2,1,0:T(8,128)S(1)}, u32[]{:S(2)}, u32[]{:S(2)}) collective-permute-start(f32[4,64,128]{2,1,0:T(8,128)S(1)} %get-tuple-element.37.own), channel_id=1, source_target_pairs={{0,1},{1,0},{2,3},{3,2},{4,5},{5,4},{6,7},{7,6},{8,9},{9,8},{10,11... | collective-permute-start | bytes 393224 | tf_op jit(solution)/shard_map/ppermute | solution.py:33
  4.5 6.0 %collective-permute-start.6 = (f32[4,64,128]{2,1,0:T(8,128)S(1)}, f32[4,64,128]{2,1,0:T(8,128)S(1)}, u32[]{:S(2)}, u32[]{:S(2)}) collective-permute-start(f32[4,64,128]{2,1,0:T(8,128)S(1)} %shard_map.72.own), channel_id=1, source_target_pairs={{0,2},{1,3},{2,0},{3,1},{4,6},{5,7},{6,4},{7,5},{8,10},{9,11},{10,... | collective-permute-start | bytes 393224 | tf_op jit(solution)/shard_map/ppermute | solution.py:33
  10.7 9.0 %collective-permute-start.7 = (f32[4,64,128]{2,1,0:T(8,128)S(1)}, f32[4,64,128]{2,1,0:T(8,128)S(1)}, u32[]{:S(2)}, u32[]{:S(2)}) collective-permute-start(f32[4,64,128]{2,1,0:T(8,128)S(1)} %shard_map.73.own), channel_id=1, source_target_pairs={{0,4},{1,5},{2,6},{3,7},{4,0},{5,1},{6,2},{7,3},{8,12},{9,13},{10,... | collective-permute-start | bytes 393224 | tf_op jit(solution)/shard_map/ppermute | solution.py:33
  13.0 2.7 %copy-start = (f32[1024]{0:T(1024)S(1)}, f32[1024]{0:T(1024)}, u32[]{:S(2)}) copy-start(f32[1024]{0:T(1024)} %param.6) | copy-start | bytes 12292
  13.0 10.1 %collective-permute-start = (f32[256,128]{1,0:T(8,128)S(1)}, f32[256,128]{1,0:T(8,128)S(1)}, u32[]{:S(2)}, u32[]{:S(2)}) collective-permute-start(f32[256,128]{1,0:T(8,128)S(1)} %get-tuple-element.31), channel_id=1, source_target_pairs={{0,8},{1,9},{2,10},{3,11},{4,12},{5,13},{6,14},{7,15},{8,0},{9,1},... | collective-permute-start | bytes 393224 | tf_op jit(solution)/shard_map/ppermute | solution.py:33
  14.3 10.0 %collective-permute-start.1 = (f32[256,128]{1,0:T(8,128)S(1)}, f32[256,128]{1,0:T(8,128)S(1)}, u32[]{:S(2)}, u32[]{:S(2)}) collective-permute-start(f32[256,128]{1,0:T(8,128)S(1)} %get-tuple-element.32), channel_id=1, source_target_pairs={{0,16},{1,17},{2,18},{3,19},{4,20},{5,21},{6,22},{7,23},{8,24},{9,... | collective-permute-start | bytes 393224 | tf_op jit(solution)/shard_map/ppermute | solution.py:33
  15.5 8.7 %collective-permute-start.2 = (f32[256,128]{1,0:T(8,128)S(1)}, f32[256,128]{1,0:T(8,128)S(1)}, u32[]{:S(2)}, u32[]{:S(2)}) collective-permute-start(f32[256,128]{1,0:T(8,128)S(1)} %get-tuple-element.33), channel_id=1, source_target_pairs={{0,24},{1,25},{2,26},{3,27},{4,28},{5,29},{6,30},{7,31},{8,16},{9,... | collective-permute-start | bytes 393224 | tf_op jit(solution)/shard_map/ppermute | solution.py:33
  15.7 6.1 %collective-permute-start.4 = (f32[1024]{0:T(1024)S(1)}, f32[1024]{0:T(1024)S(1)}, u32[]{:S(2)}, u32[]{:S(2)}) collective-permute-start(f32[1024]{0:T(1024)S(1)} %copy-done), channel_id=1, source_target_pairs={{0,0},{1,4},{2,2},{3,6},{4,1},{5,5},{6,3},{7,7},{8,8},{9,12},{10,1... | collective-permute-start | bytes 12296 | tf_op jit(solution)/shard_map/ppermute | solution.py:33
  20.0 5.5 %collective-permute-start.8 = (f32[64,128]{1,0:T(8,128)S(1)}, f32[64,128]{1,0:T(8,128)S(1)}, u32[]{:S(2)}, u32[]{:S(2)}) collective-permute-start(f32[64,128]{1,0:T(8,128)S(1)} %get-tuple-element.39), channel_id=1, source_target_pairs={{0,8},{1,9},{2,10},{3,11},{4,12},{5,13},{6,14},{7,15},{8,0},{9,1},... | collective-permute-start | bytes 98312 | tf_op jit(solution)/shard_map/ppermute | solution.py:33
  21.8 3.7 %collective-permute-start.9 = (f32[64,128]{1,0:T(8,128)S(1)}, f32[64,128]{1,0:T(8,128)S(1)}, u32[]{:S(2)}, u32[]{:S(2)}) collective-permute-start(f32[64,128]{1,0:T(8,128)S(1)} %get-tuple-element.40), channel_id=1, source_target_pairs={{0,16},{1,17},{2,18},{3,19},{4,20},{5,21},{6,22},{7,23},{8,24},{9,... | collective-permute-start | bytes 98312 | tf_op jit(solution)/shard_map/ppermute | solution.py:33
  23.1 3.7 %collective-permute-start.10 = (f32[64,128]{1,0:T(8,128)S(1)}, f32[64,128]{1,0:T(8,128)S(1)}, u32[]{:S(2)}, u32[]{:S(2)}) collective-permute-start(f32[64,128]{1,0:T(8,128)S(1)} %get-tuple-element.41), channel_id=1, source_target_pairs={{0,24},{1,25},{2,26},{3,27},{4,28},{5,29},{6,30},{7,31},{8,16},{9,... | collective-permute-start | bytes 98312 | tf_op jit(solution)/shard_map/ppermute | solution.py:33
  27.0 2.8 %collective-permute-start.12 = (f32[64,128]{1,0:T(8,128)S(1)}, f32[64,128]{1,0:T(8,128)S(1)}, u32[]{:S(2)}, u32[]{:S(2)}) collective-permute-start(f32[64,128]{1,0:T(8,128)S(1)} %get-tuple-element.44), channel_id=1, source_target_pairs={{0,8},{1,9},{2,10},{3,11},{4,12},{5,13},{6,14},{7,15},{8,0},{9,1},... | collective-permute-start | bytes 98312 | tf_op jit(solution)/shard_map/ppermute | solution.py:33
  28.3 2.8 %collective-permute-start.13 = (f32[64,128]{1,0:T(8,128)S(1)}, f32[64,128]{1,0:T(8,128)S(1)}, u32[]{:S(2)}, u32[]{:S(2)}) collective-permute-start(f32[64,128]{1,0:T(8,128)S(1)} %get-tuple-element.45), channel_id=1, source_target_pairs={{0,16},{1,17},{2,18},{3,19},{4,20},{5,21},{6,22},{7,23},{8,24},{9,... | collective-permute-start | bytes 98312 | tf_op jit(solution)/shard_map/ppermute | solution.py:33
  29.0 3.8 %collective-permute-start.14 = (f32[64,128]{1,0:T(8,128)S(1)}, f32[64,128]{1,0:T(8,128)S(1)}, u32[]{:S(2)}, u32[]{:S(2)}) collective-permute-start(f32[64,128]{1,0:T(8,128)S(1)} %get-tuple-element.46), channel_id=1, source_target_pairs={{0,24},{1,25},{2,26},{3,27},{4,28},{5,29},{6,30},{7,31},{8,16},{9,... | collective-permute-start | bytes 98312 | tf_op jit(solution)/shard_map/ppermute | solution.py:33
  33.1 6.7 %collective-permute-start.15 = (f32[4,64,128]{2,1,0:T(8,128)S(1)}, f32[4,64,128]{2,1,0:T(8,128)S(1)}, u32[]{:S(2)}, u32[]{:S(2)}) collective-permute-start(f32[4,64,128]{2,1,0:T(8,128)S(1)} %get-tuple-element.48), channel_id=1, source_target_pairs={{0,4},{1,5},{2,6},{3,7},{4,0},{5,1},{6,2},{7,3},{8,12},{9,13},{10,... | collective-permute-start | bytes 393224 | tf_op jit(solution)/shard_map/ppermute | solution.py:33
  40.1 11.0 %collective-permute-start.16 = (f32[4,64,128]{2,1,0:T(8,128)S(1)}, f32[4,64,128]{2,1,0:T(8,128)S(1)}, u32[]{:S(2)}, u32[]{:S(2)}) collective-permute-start(f32[4,64,128]{2,1,0:T(8,128)S(1)} %get-tuple-element.50), channel_id=1, source_target_pairs={{0,2},{1,3},{2,0},{3,1},{4,6},{5,7},{6,4},{7,5},{8,10},{9,11},{10,... | collective-permute-start | bytes 393224 | tf_op jit(solution)/shard_map/ppermute | solution.py:33
  40.2 16.5 %collective-permute-start.3 = (f32[4,64,256]{2,1,0:T(8,128)S(1)}, f32[4,64,256]{2,1,0:T(8,128)S(1)}, u32[]{:S(2)}, u32[]{:S(2)}) collective-permute-start(f32[4,64,256]{2,1,0:T(8,128)S(1)} %get-tuple-element.34.basis), channel_id=1, source_target_pairs={{0,0},{1,4},{2,2},{3,6},{4,1},{5,5},{6,3},{7,7},{8,8},{9,12},{10,1... | collective-permute-start | bytes 786440 | tf_op jit(solution)/shard_map/ppermute | solution.py:33
  49.2 8.9 %collective-permute-start.11 = (f32[4,64,128]{2,1,0:T(8,128)S(1)}, f32[4,64,128]{2,1,0:T(8,128)S(1)}, u32[]{:S(2)}, u32[]{:S(2)}) collective-permute-start(f32[4,64,128]{2,1,0:T(8,128)S(1)} %shard_map.75), channel_id=1, source_target_pairs={{0,0},{1,4},{2,2},{3,6},{4,1},{5,5},{6,3},{7,7},{8,8},{9,12},{10,1... | collective-permute-start | bytes 393224 | tf_op jit(solution)/shard_map/ppermute | solution.py:33
  51.4 7.8 %collective-permute-start.17 = (f32[4,64,128]{2,1,0:T(8,128)S(1)}, f32[4,64,128]{2,1,0:T(8,128)S(1)}, u32[]{:S(2)}, u32[]{:S(2)}) collective-permute-start(f32[4,64,128]{2,1,0:T(8,128)S(1)} %get-tuple-element.52), channel_id=1, source_target_pairs={{0,1},{1,0},{2,3},{3,2},{4,5},{5,4},{6,7},{7,6},{8,9},{9,8},{10,11... | collective-permute-start | bytes 393224 | tf_op jit(solution)/shard_map/ppermute | solution.py:33

commit v7 on v6

--- a/solution.py
+++ b/solution.py
@@ -232,20 +232,19 @@
         part(level, bit, s, kept_in[s] + arrived[s], transfer, sent, kept)
 
 
-def write_rows(rows, out, buffer, sems):
+def tail_kernel(
+    kept, arrived, transfer, basis, image_basis, image_coeffs, image, adjoint, buffers, sems
+):
+    leaf = buffers.shape[2]
     copies = []
-    for s in range(SLOTS):
-        leaf = buffer.shape[1]
-        buffer[s] = rows(s)
+
+    def write(out, j, s, rows):
+        buffers[j, s] = rows
         copies.append(
-            pltpu.make_async_copy(buffer.at[s], out.at[pl.ds(s * leaf, leaf)], sems.at[s])
+            pltpu.make_async_copy(buffers.at[j, s], out.at[pl.ds(s * leaf, leaf)], sems.at[j, s])
         )
         copies[-1].start()
-    for copy in copies:
-        copy.wait()
-
-
-def tail_kernel(kept, arrived, transfer, basis, out, buffer, sems):
+
     b = [kept[s] + arrived[s] for s in range(SLOTS)]
     rank = b[0].shape[0]
     for level in reversed(range(SLOT_BITS)):
@@ -253,11 +252,12 @@
             blocks = jnp.concatenate([transfer[level, low], transfer[level, high]], axis=0)
             both = product(blocks, jnp.concatenate([b[low], b[high]], axis=0), TN)
             b[low], b[high] = both[:rank], both[rank:]
-    write_rows(lambda s: product(basis[s], b[s], TN), out, buffer, sems)
-
-
-def image_kernel(basis, coeffs, out, buffer, sems):
-    write_rows(lambda s: product(basis[s], coeffs[s], TN), out, buffer, sems)
+    for s in range(SLOTS):
+        write(adjoint, 0, s, product(basis[s], b[s], TN))
+    for s in range(SLOTS):
+        write(image, 1, s, product(image_basis[s], image_coeffs[s], TN))
+    for copy in copies:
+        copy.wait()
 
 
 def body(vectors, diagonal, source_basis, transfer, target_basis):
@@ -267,7 +267,6 @@
     pair_bits = list(range(places.low_bits))
     nodes, node = (slots, rank, vecs), (rank, vecs)
     basis_shape = (slots, rank, leaf)
-    rows_scratch = [pltpu.VMEM((slots, leaf, vecs), jnp.float32), pltpu.SemaphoreType.DMA((slots,))]
     source_t = jnp.swapaxes(source_basis, 1, 2)
     target_t = jnp.swapaxes(target_basis, 1, 2)
     coeffs, source_t, transfer, target_t = call(
@@ -316,14 +315,6 @@
     back = places.across(call(middle_kernel, [node] * slots, [middle] + blocks))
     (coeffs,) = call(top_kernel, [nodes], [wide] + blocks)
     image_coeffs = places.reverse_low(coeffs)
-    (forward_image,) = call(
-        image_kernel,
-        [vectors.shape],
-        [image_basis, image_coeffs],
-        out_specs=[ANY],
-        scratch=rows_scratch,
-    )
-
     for bit in reversed(pair_bits):
         if bit == pair_bits[-1]:
             kernel, operands = first_part_kernel, back
@@ -333,12 +324,15 @@
             functools.partial(kernel, SLOT_BITS + bit, bit), [nodes, nodes], [transfer] + operands
         )
         arrived = places.partner(sent, bit)
-    (adjoint,) = call(
+    forward_image, adjoint = call(
         tail_kernel,
-        [vectors.shape],
-        [kept, arrived, transfer, source_t],
-        out_specs=[ANY],
-        scratch=rows_scratch,
+        [vectors.shape] * 2,
+        [kept, arrived, transfer, source_t, image_basis, image_coeffs],
+        out_specs=[ANY] * 2,
+        scratch=[
+            pltpu.VMEM((2, slots, leaf, vecs), jnp.float32),
+            pltpu.SemaphoreType.DMA((2, slots)),
+        ],
     )
     return forward_image, adjoint
 

time: 60.9 us -> 60 us (0.985)
  Pallas kernels: 8.27 us -> 7.37 us
    pallas_call x14 -> x13, Pallas kernels: 8.27 us -> 7.37 us  [call(): pl.pallas_call(kernel, out_shape=shapes, in_specs=specs or [VMEM] * len(o...]
  transfers between devices with their start and end apart: 18 -> 18, of which waited for: 10 -> 10; matrix products, arithmetic and copies ran while one was open for 0% -> 0% of each run, Pallas kernels for 5% -> 3%
where the time goes in v7:
time: 60 us; the launch traced here: 59.8 us
  starting transfers between devices  28.9 us (48%)
  waiting for transfers between devices  22.7 us (38%)
  Pallas kernels  7.37 us (12%)
  between operations  0.8 us (1%)
    ppermute x18, starting transfers between devices, permute(): lax.ppermute(block, BOTH, [(d, route(d)) for d in range(self.devices)])  28.9 us
    ppermute x18, waiting for transfers between devices, permute(): lax.ppermute(block, BOTH, [(d, route(d)) for d in range(self.devices)])  22.7 us
    pallas_call x13, Pallas kernels, call(): pl.pallas_call(kernel, out_shape=shapes, in_specs=specs or [VMEM] * len(o...  7.37 us
  transfers between devices with their start and end apart: 18, of which 10 were waited for; matrix products, arithmetic and copies ran while one was open for 0% of the time, Pallas kernels for 3%

profile of v7, /device:TPU:1, one launch (start us, length us, event | category | flops | bytes accessed | tf_op | source)
XLA Modules:
  0.0 59.8 jit_solution(15640835107107854202)
XLA Ops:
  0.6 2.2 %shard_map.68 = (f32[4,64,128]{2,1,0:T(8,128)S(1)}, f32[4,64,256]{2,1,0:T(8,128)S(1)}, f32[7,4,64,128]{3,2,1,0:T(8,128)S(1)}, f32[4,64,256]{2,1,0:T(8,128)S(1)}) custom-call(f32[1024,128]{1,0:T(8,128)} %vectors_in.1, f32[4,64,256]{2,1,0:T(8,128)} %bitcast.2, f32[7,4,64,128]{3,2,1,0:T(8,128)} %transfer_in.1, f32[4,64,256]{2,1,0:T(8,128)} %bitcast.3), custom_call_target="tpu_custom_call" | custom-call | flops 16777216 | bytes 524288 | tf_op jit(solution)/shard_map/pallas_call | solution.py:83
  2.9 0.1 collective-permute-start.4
  2.9 1.3 %collective-permute-done.4.partner = f32[4,64,128]{2,1,0:T(8,128)S(1)} collective-permute-done((f32[4,64,128]{2,1,0:T(8,128)S(1)}, f32[4,64,128]{2,1,0:T(8,128)S(1)}, u32[]{:S(2)}, u32[]{:S(2)}) %collective-permute-start.4) | collective-permute-done | bytes 131104 | tf_op jit(solution)/shard_map/ppermute | solution.py:33
  4.3 0.2 shard_map.72.own
  4.5 2.5 %collective-permute-start.5 = (f32[4,64,128]{2,1,0:T(8,128)S(1)}, f32[4,64,128]{2,1,0:T(8,128)S(1)}, u32[]{:S(2)}, u32[]{:S(2)}) collective-permute-start(f32[4,64,128]{2,1,0:T(8,128)S(1)} %shard_map.72.own), channel_id=1, source_target_pairs={{0,2},{1,3},{2,0},{3,1},{4,6},{5,7},{6,4},{7,5},{8,10},{9,11},{10,... | collective-permute-start | bytes 393224 | tf_op jit(solution)/shard_map/ppermute | solution.py:33
  7.0 3.5 %collective-permute-done.5.partner = f32[4,64,128]{2,1,0:T(8,128)S(1)} collective-permute-done((f32[4,64,128]{2,1,0:T(8,128)S(1)}, f32[4,64,128]{2,1,0:T(8,128)S(1)}, u32[]{:S(2)}, u32[]{:S(2)}) %collective-permute-start.5) | collective-permute-done | bytes 131104 | tf_op jit(solution)/shard_map/ppermute | solution.py:33
  10.5 0.2 shard_map.73.own
  10.7 2.2 %collective-permute-start.6 = (f32[4,64,128]{2,1,0:T(8,128)S(1)}, f32[4,64,128]{2,1,0:T(8,128)S(1)}, u32[]{:S(2)}, u32[]{:S(2)}) collective-permute-start(f32[4,64,128]{2,1,0:T(8,128)S(1)} %shard_map.73.own), channel_id=1, source_target_pairs={{0,4},{1,5},{2,6},{3,7},{4,0},{5,1},{6,2},{7,3},{8,12},{9,13},{10,... | collective-permute-start | bytes 393224 | tf_op jit(solution)/shard_map/ppermute | solution.py:33
  13.0 0.0 copy-start
  13.0 1.3 %collective-permute-start = (f32[256,128]{1,0:T(8,128)S(1)}, f32[256,128]{1,0:T(8,128)S(1)}, u32[]{:S(2)}, u32[]{:S(2)}) collective-permute-start(f32[256,128]{1,0:T(8,128)S(1)} %get-tuple-element.31), channel_id=1, source_target_pairs={{0,8},{1,9},{2,10},{3,11},{4,12},{5,13},{6,14},{7,15},{8,0},{9,1},... | collective-permute-start | bytes 393224 | tf_op jit(solution)/shard_map/ppermute | solution.py:33
  14.3 1.2 %collective-permute-start.1 = (f32[256,128]{1,0:T(8,128)S(1)}, f32[256,128]{1,0:T(8,128)S(1)}, u32[]{:S(2)}, u32[]{:S(2)}) collective-permute-start(f32[256,128]{1,0:T(8,128)S(1)} %get-tuple-element.32), channel_id=1, source_target_pairs={{0,16},{1,17},{2,18},{3,19},{4,20},{5,21},{6,22},{7,23},{8,24},{9,... | collective-permute-start | bytes 393224 | tf_op jit(solution)/shard_map/ppermute | solution.py:33
  15.5 0.2 collective-permute-start.2
  15.7 0.0 copy-done
  15.7 4.0 %collective-permute-start.3 = (f32[1024]{0:T(1024)S(1)}, f32[1024]{0:T(1024)S(1)}, u32[]{:S(2)}, u32[]{:S(2)}) collective-permute-start(f32[1024]{0:T(1024)S(1)} %copy-done), channel_id=1, source_target_pairs={{0,0},{1,4},{2,2},{3,6},{4,1},{5,5},{6,3},{7,7},{8,8},{9,12},{10,1... | collective-permute-start | bytes 12296 | tf_op jit(solution)/shard_map/ppermute | solution.py:33
  19.7 0.0 collective-permute-done.6.partner
  19.7 0.2 shard_map.74
  20.0 1.4 %collective-permute-start.7 = (f32[64,128]{1,0:T(8,128)S(1)}, f32[64,128]{1,0:T(8,128)S(1)}, u32[]{:S(2)}, u32[]{:S(2)}) collective-permute-start(f32[64,128]{1,0:T(8,128)S(1)} %get-tuple-element.39), channel_id=1, source_target_pairs={{0,8},{1,9},{2,10},{3,11},{4,12},{5,13},{6,14},{7,15},{8,0},{9,1},... | collective-permute-start | bytes 98312 | tf_op jit(solution)/shard_map/ppermute | solution.py:33
  21.4 0.4 collective-permute-done.3
  21.8 1.2 %collective-permute-start.8 = (f32[64,128]{1,0:T(8,128)S(1)}, f32[64,128]{1,0:T(8,128)S(1)}, u32[]{:S(2)}, u32[]{:S(2)}) collective-permute-start(f32[64,128]{1,0:T(8,128)S(1)} %get-tuple-element.40), channel_id=1, source_target_pairs={{0,16},{1,17},{2,18},{3,19},{4,20},{5,21},{6,22},{7,23},{8,24},{9,... | collective-permute-start | bytes 98312 | tf_op jit(solution)/shard_map/ppermute | solution.py:33
  23.1 0.0 collective-permute-done.refs_1_
  23.1 1.2 %collective-permute-start.9 = (f32[64,128]{1,0:T(8,128)S(1)}, f32[64,128]{1,0:T(8,128)S(1)}, u32[]{:S(2)}, u32[]{:S(2)}) collective-permute-start(f32[64,128]{1,0:T(8,128)S(1)} %get-tuple-element.41), channel_id=1, source_target_pairs={{0,24},{1,25},{2,26},{3,27},{4,28},{5,29},{6,30},{7,31},{8,16},{9,... | collective-permute-start | bytes 98312 | tf_op jit(solution)/shard_map/ppermute | solution.py:33
  24.2 0.0 collective-permute-done.1.refs_2_
  24.2 0.0 collective-permute-done.2.refs_3_
  24.3 1.2 %shard_map.71 = (f32[256,256]{1,0:T(8,128)S(1)}, f32[256,256]{1,0:T(8,128)S(1)}) custom-call(f32[2,4,64,128]{3,2,1,0:T(8,128)S(1)} %get-tuple-element.34.tops, f32[4,64,256]{2,1,0:T(8,128)S(1)} %get-tuple-element.35.basis, f32[4,256]{1,0:T(4,128)S(1)} %reshape.7.weights), custom_call_target="tpu_custom_call" | custom-call | flops 16777216 | bytes 524288 | tf_op jit(solution)/shard_map/pallas_call | solution.py:83
  25.5 0.0 collective-permute-done.7.refs_1_
  25.5 0.0 collective-permute-done.8.refs_2_
  25.5 1.2 %collective-permute-done.9.refs_3_ = f32[64,128]{1,0:T(8,128)S(1)} collective-permute-done((f32[64,128]{1,0:T(8,128)S(1)}, f32[64,128]{1,0:T(8,128)S(1)}, u32[]{:S(2)}, u32[]{:S(2)}) %collective-permute-start.9) | collective-permute-done | bytes 32800 | tf_op jit(solution)/shard_map/ppermute | solution.py:33
  26.7 0.2 shard_map.75
  27.0 1.3 %collective-permute-start.10 = (f32[64,128]{1,0:T(8,128)S(1)}, f32[64,128]{1,0:T(8,128)S(1)}, u32[]{:S(2)}, u32[]{:S(2)}) collective-permute-start(f32[64,128]{1,0:T(8,128)S(1)} %get-tuple-element.43), channel_id=1, source_target_pairs={{0,8},{1,9},{2,10},{3,11},{4,12},{5,13},{6,14},{7,15},{8,0},{9,1},... | collective-permute-start | bytes 98312 | tf_op jit(solution)/shard_map/ppermute | solution.py:33
  28.3 0.7 %collective-permute-start.11 = (f32[64,128]{1,0:T(8,128)S(1)}, f32[64,128]{1,0:T(8,128)S(1)}, u32[]{:S(2)}, u32[]{:S(2)}) collective-permute-start(f32[64,128]{1,0:T(8,128)S(1)} %get-tuple-element.44), channel_id=1, source_target_pairs={{0,16},{1,17},{2,18},{3,19},{4,20},{5,21},{6,22},{7,23},{8,24},{9,... | collective-permute-start | bytes 98312 | tf_op jit(solution)/shard_map/ppermute | solution.py:33
  29.0 0.7 %collective-permute-start.12 = (f32[64,128]{1,0:T(8,128)S(1)}, f32[64,128]{1,0:T(8,128)S(1)}, u32[]{:S(2)}, u32[]{:S(2)}) collective-permute-start(f32[64,128]{1,0:T(8,128)S(1)} %get-tuple-element.45), channel_id=1, source_target_pairs={{0,24},{1,25},{2,26},{3,27},{4,28},{5,29},{6,30},{7,31},{8,16},{9,... | collective-permute-start | bytes 98312 | tf_op jit(solution)/shard_map/ppermute | solution.py:33
  29.7 0.1 collective-permute-done.10.refs_1_
  29.8 1.3 %collective-permute-done.11.refs_2_ = f32[64,128]{1,0:T(8,128)S(1)} collective-permute-done((f32[64,128]{1,0:T(8,128)S(1)}, f32[64,128]{1,0:T(8,128)S(1)}, u32[]{:S(2)}, u32[]{:S(2)}) %collective-permute-start.11) | collective-permute-done | bytes 32800 | tf_op jit(solution)/shard_map/ppermute | solution.py:33
  31.1 1.7 %collective-permute-done.12.refs_3_ = f32[64,128]{1,0:T(8,128)S(1)} collective-permute-done((f32[64,128]{1,0:T(8,128)S(1)}, f32[64,128]{1,0:T(8,128)S(1)}, u32[]{:S(2)}, u32[]{:S(2)}) %collective-permute-start.12) | collective-permute-done | bytes 32800 | tf_op jit(solution)/shard_map/ppermute | solution.py:33
  32.8 0.3 shard_map.76
  33.1 0.1 collective-permute-start.13
  33.2 6.6 %collective-permute-done.13.arrived = f32[4,64,128]{2,1,0:T(8,128)S(1)} collective-permute-done((f32[4,64,128]{2,1,0:T(8,128)S(1)}, f32[4,64,128]{2,1,0:T(8,128)S(1)}, u32[]{:S(2)}, u32[]{:S(2)}) %collective-permute-start.13) | collective-permute-done | bytes 131104 | tf_op jit(solution)/shard_map/ppermute | solution.py:33
  39.8 0.3 shard_map.77
  40.1 0.1 collective-permute-start.14
  40.2 8.7 %collective-permute-start.16 = (f32[4,64,256]{2,1,0:T(8,128)S(1)}, f32[4,64,256]{2,1,0:T(8,128)S(1)}, u32[]{:S(2)}, u32[]{:S(2)}) collective-permute-start(f32[4,64,256]{2,1,0:T(8,128)S(1)} %get-tuple-element.35.basis), channel_id=1, source_target_pairs={{0,0},{1,4},{2,2},{3,6},{4,1},{5,5},{6,3},{7,7},{8,8},{9,12},{10,1... | collective-permute-start | bytes 786440 | tf_op jit(solution)/shard_map/ppermute | solution.py:33
  48.9 0.2 shard_map.79
  49.2 1.9 %collective-permute-start.17 = (f32[4,64,128]{2,1,0:T(8,128)S(1)}, f32[4,64,128]{2,1,0:T(8,128)S(1)}, u32[]{:S(2)}, u32[]{:S(2)}) collective-permute-start(f32[4,64,128]{2,1,0:T(8,128)S(1)} %shard_map.79), channel_id=1, source_target_pairs={{0,0},{1,4},{2,2},{3,6},{4,1},{5,5},{6,3},{7,7},{8,8},{9,12},{10,1... | collective-permute-start | bytes 393224 | tf_op jit(solution)/shard_map/ppermute | solution.py:33
  51.1 0.0 collective-permute-done.14.arrived
  51.1 0.3 shard_map.78
  51.4 0.1 collective-permute-start.15
  51.5 5.1 %collective-permute-done.16.image_basis = f32[4,64,256]{2,1,0:T(8,128)S(1)} collective-permute-done((f32[4,64,256]{2,1,0:T(8,128)S(1)}, f32[4,64,256]{2,1,0:T(8,128)S(1)}, u32[]{:S(2)}, u32[]{:S(2)}) %collective-permute-start.16) | collective-permute-done | bytes 262176 | tf_op jit(solution)/shard_map/ppermute | solution.py:33
  56.6 1.4 %collective-permute-done.17.image_coeffs = f32[4,64,128]{2,1,0:T(8,128)S(1)} collective-permute-done((f32[4,64,128]{2,1,0:T(8,128)S(1)}, f32[4,64,128]{2,1,0:T(8,128)S(1)}, u32[]{:S(2)}, u32[]{:S(2)}) %collective-permute-start.17) | collective-permute-done | bytes 131104 | tf_op jit(solution)/shard_map/ppermute | solution.py:33
  58.0 0.0 collective-permute-done.15.arrived
  58.0 1.7 %shard_map.80 = (f32[1024,128]{1,0:T(8,128)}, f32[1024,128]{1,0:T(8,128)}) custom-call(f32[4,64,128]{2,1,0:T(8,128)S(1)} %get-tuple-element.50.kept, f32[4,64,128]{2,1,0:T(8,128)S(1)} %collective-permute-done.15.arrived, f32[7,4,64,128]{3,2,1,0:T(8,128)S(1)} %get-tuple-element.28.transfer, f32[4,64,256]{2,1,0:T(8,128)S(1)} %get-tuple-element.52.basis, ...), custom_call_target="tpu_custom_call" | custom-call | flops 16777216 | bytes 524288 | tf_op jit(solution)/shard_map/pallas_call | solution.py:83
  (3 shorter events, 0.1 us)
Async XLA Ops:
  2.9 1.4 %collective-permute-start.4 = (f32[4,64,128]{2,1,0:T(8,128)S(1)}, f32[4,64,128]{2,1,0:T(8,128)S(1)}, u32[]{:S(2)}, u32[]{:S(2)}) collective-permute-start(f32[4,64,128]{2,1,0:T(8,128)S(1)} %get-tuple-element.37.own), channel_id=1, source_target_pairs={{0,1},{1,0},{2,3},{3,2},{4,5},{5,4},{6,7},{7,6},{8,9},{9,8},{10,11... | collective-permute-start | bytes 393224 | tf_op jit(solution)/shard_map/ppermute | solution.py:33
  4.5 6.0 %collective-permute-start.5 = (f32[4,64,128]{2,1,0:T(8,128)S(1)}, f32[4,64,128]{2,1,0:T(8,128)S(1)}, u32[]{:S(2)}, u32[]{:S(2)}) collective-permute-start(f32[4,64,128]{2,1,0:T(8,128)S(1)} %shard_map.72.own), channel_id=1, source_target_pairs={{0,2},{1,3},{2,0},{3,1},{4,6},{5,7},{6,4},{7,5},{8,10},{9,11},{10,... | collective-permute-start | bytes 393224 | tf_op jit(solution)/shard_map/ppermute | solution.py:33
  10.7 9.0 %collective-permute-start.6 = (f32[4,64,128]{2,1,0:T(8,128)S(1)}, f32[4,64,128]{2,1,0:T(8,128)S(1)}, u32[]{:S(2)}, u32[]{:S(2)}) collective-permute-start(f32[4,64,128]{2,1,0:T(8,128)S(1)} %shard_map.73.own), channel_id=1, source_target_pairs={{0,4},{1,5},{2,6},{3,7},{4,0},{5,1},{6,2},{7,3},{8,12},{9,13},{10,... | collective-permute-start | bytes 393224 | tf_op jit(solution)/shard_map/ppermute | solution.py:33
  13.0 2.7 %copy-start = (f32[1024]{0:T(1024)S(1)}, f32[1024]{0:T(1024)}, u32[]{:S(2)}) copy-start(f32[1024]{0:T(1024)} %param.6) | copy-start | bytes 12292
  13.0 10.1 %collective-permute-start = (f32[256,128]{1,0:T(8,128)S(1)}, f32[256,128]{1,0:T(8,128)S(1)}, u32[]{:S(2)}, u32[]{:S(2)}) collective-permute-start(f32[256,128]{1,0:T(8,128)S(1)} %get-tuple-element.31), channel_id=1, source_target_pairs={{0,8},{1,9},{2,10},{3,11},{4,12},{5,13},{6,14},{7,15},{8,0},{9,1},... | collective-permute-start | bytes 393224 | tf_op jit(solution)/shard_map/ppermute | solution.py:33
  14.3 10.0 %collective-permute-start.1 = (f32[256,128]{1,0:T(8,128)S(1)}, f32[256,128]{1,0:T(8,128)S(1)}, u32[]{:S(2)}, u32[]{:S(2)}) collective-permute-start(f32[256,128]{1,0:T(8,128)S(1)} %get-tuple-element.32), channel_id=1, source_target_pairs={{0,16},{1,17},{2,18},{3,19},{4,20},{5,21},{6,22},{7,23},{8,24},{9,... | collective-permute-start | bytes 393224 | tf_op jit(solution)/shard_map/ppermute | solution.py:33
  15.5 8.7 %collective-permute-start.2 = (f32[256,128]{1,0:T(8,128)S(1)}, f32[256,128]{1,0:T(8,128)S(1)}, u32[]{:S(2)}, u32[]{:S(2)}) collective-permute-start(f32[256,128]{1,0:T(8,128)S(1)} %get-tuple-element.33), channel_id=1, source_target_pairs={{0,24},{1,25},{2,26},{3,27},{4,28},{5,29},{6,30},{7,31},{8,16},{9,... | collective-permute-start | bytes 393224 | tf_op jit(solution)/shard_map/ppermute | solution.py:33
  15.7 6.1 %collective-permute-start.3 = (f32[1024]{0:T(1024)S(1)}, f32[1024]{0:T(1024)S(1)}, u32[]{:S(2)}, u32[]{:S(2)}) collective-permute-start(f32[1024]{0:T(1024)S(1)} %copy-done), channel_id=1, source_target_pairs={{0,0},{1,4},{2,2},{3,6},{4,1},{5,5},{6,3},{7,7},{8,8},{9,12},{10,1... | collective-permute-start | bytes 12296 | tf_op jit(solution)/shard_map/ppermute | solution.py:33
  20.0 5.5 %collective-permute-start.7 = (f32[64,128]{1,0:T(8,128)S(1)}, f32[64,128]{1,0:T(8,128)S(1)}, u32[]{:S(2)}, u32[]{:S(2)}) collective-permute-start(f32[64,128]{1,0:T(8,128)S(1)} %get-tuple-element.39), channel_id=1, source_target_pairs={{0,8},{1,9},{2,10},{3,11},{4,12},{5,13},{6,14},{7,15},{8,0},{9,1},... | collective-permute-start | bytes 98312 | tf_op jit(solution)/shard_map/ppermute | solution.py:33
  21.8 3.7 %collective-permute-start.8 = (f32[64,128]{1,0:T(8,128)S(1)}, f32[64,128]{1,0:T(8,128)S(1)}, u32[]{:S(2)}, u32[]{:S(2)}) collective-permute-start(f32[64,128]{1,0:T(8,128)S(1)} %get-tuple-element.40), channel_id=1, source_target_pairs={{0,16},{1,17},{2,18},{3,19},{4,20},{5,21},{6,22},{7,23},{8,24},{9,... | collective-permute-start | bytes 98312 | tf_op jit(solution)/shard_map/ppermute | solution.py:33
  23.1 3.7 %collective-permute-start.9 = (f32[64,128]{1,0:T(8,128)S(1)}, f32[64,128]{1,0:T(8,128)S(1)}, u32[]{:S(2)}, u32[]{:S(2)}) collective-permute-start(f32[64,128]{1,0:T(8,128)S(1)} %get-tuple-element.41), channel_id=1, source_target_pairs={{0,24},{1,25},{2,26},{3,27},{4,28},{5,29},{6,30},{7,31},{8,16},{9,... | collective-permute-start | bytes 98312 | tf_op jit(solution)/shard_map/ppermute | solution.py:33
  27.0 2.8 %collective-permute-start.10 = (f32[64,128]{1,0:T(8,128)S(1)}, f32[64,128]{1,0:T(8,128)S(1)}, u32[]{:S(2)}, u32[]{:S(2)}) collective-permute-start(f32[64,128]{1,0:T(8,128)S(1)} %get-tuple-element.43), channel_id=1, source_target_pairs={{0,8},{1,9},{2,10},{3,11},{4,12},{5,13},{6,14},{7,15},{8,0},{9,1},... | collective-permute-start | bytes 98312 | tf_op jit(solution)/shard_map/ppermute | solution.py:33
  28.3 2.8 %collective-permute-start.11 = (f32[64,128]{1,0:T(8,128)S(1)}, f32[64,128]{1,0:T(8,128)S(1)}, u32[]{:S(2)}, u32[]{:S(2)}) collective-permute-start(f32[64,128]{1,0:T(8,128)S(1)} %get-tuple-element.44), channel_id=1, source_target_pairs={{0,16},{1,17},{2,18},{3,19},{4,20},{5,21},{6,22},{7,23},{8,24},{9,... | collective-permute-start | bytes 98312 | tf_op jit(solution)/shard_map/ppermute | solution.py:33
  29.0 3.8 %collective-permute-start.12 = (f32[64,128]{1,0:T(8,128)S(1)}, f32[64,128]{1,0:T(8,128)S(1)}, u32[]{:S(2)}, u32[]{:S(2)}) collective-permute-start(f32[64,128]{1,0:T(8,128)S(1)} %get-tuple-element.45), channel_id=1, source_target_pairs={{0,24},{1,25},{2,26},{3,27},{4,28},{5,29},{6,30},{7,31},{8,16},{9,... | collective-permute-start | bytes 98312 | tf_op jit(solution)/shard_map/ppermute | solution.py:33
  33.1 6.7 %collective-permute-start.13 = (f32[4,64,128]{2,1,0:T(8,128)S(1)}, f32[4,64,128]{2,1,0:T(8,128)S(1)}, u32[]{:S(2)}, u32[]{:S(2)}) collective-permute-start(f32[4,64,128]{2,1,0:T(8,128)S(1)} %get-tuple-element.47), channel_id=1, source_target_pairs={{0,4},{1,5},{2,6},{3,7},{4,0},{5,1},{6,2},{7,3},{8,12},{9,13},{10,... | collective-permute-start | bytes 393224 | tf_op jit(solution)/shard_map/ppermute | solution.py:33
  40.1 11.0 %collective-permute-start.14 = (f32[4,64,128]{2,1,0:T(8,128)S(1)}, f32[4,64,128]{2,1,0:T(8,128)S(1)}, u32[]{:S(2)}, u32[]{:S(2)}) collective-permute-start(f32[4,64,128]{2,1,0:T(8,128)S(1)} %get-tuple-element.49), channel_id=1, source_target_pairs={{0,2},{1,3},{2,0},{3,1},{4,6},{5,7},{6,4},{7,5},{8,10},{9,11},{10,... | collective-permute-start | bytes 393224 | tf_op jit(solution)/shard_map/ppermute | solution.py:33
  40.2 16.5 %collective-permute-start.16 = (f32[4,64,256]{2,1,0:T(8,128)S(1)}, f32[4,64,256]{2,1,0:T(8,128)S(1)}, u32[]{:S(2)}, u32[]{:S(2)}) collective-permute-start(f32[4,64,256]{2,1,0:T(8,128)S(1)} %get-tuple-element.35.basis), channel_id=1, source_target_pairs={{0,0},{1,4},{2,2},{3,6},{4,1},{5,5},{6,3},{7,7},{8,8},{9,12},{10,1... | collective-permute-start | bytes 786440 | tf_op jit(solution)/shard_map/ppermute | solution.py:33
  49.2 8.9 %collective-permute-start.17 = (f32[4,64,128]{2,1,0:T(8,128)S(1)}, f32[4,64,128]{2,1,0:T(8,128)S(1)}, u32[]{:S(2)}, u32[]{:S(2)}) collective-permute-start(f32[4,64,128]{2,1,0:T(8,128)S(1)} %shard_map.79), channel_id=1, source_target_pairs={{0,0},{1,4},{2,2},{3,6},{4,1},{5,5},{6,3},{7,7},{8,8},{9,12},{10,1... | collective-permute-start | bytes 393224 | tf_op jit(solution)/shard_map/ppermute | solution.py:33
  51.4 6.6 %collective-permute-start.15 = (f32[4,64,128]{2,1,0:T(8,128)S(1)}, f32[4,64,128]{2,1,0:T(8,128)S(1)}, u32[]{:S(2)}, u32[]{:S(2)}) collective-permute-start(f32[4,64,128]{2,1,0:T(8,128)S(1)} %get-tuple-element.51), channel_id=1, source_target_pairs={{0,1},{1,0},{2,3},{3,2},{4,5},{5,4},{6,7},{7,6},{8,9},{9,8},{10,11... | collective-permute-start | bytes 393224 | tf_op jit(solution)/shard_map/ppermute | solution.py:33

commit v8 on v6

--- a/solution.py
+++ b/solution.py
@@ -41,6 +41,9 @@
             block, lambda d: (d >> low) << low | reverse_bits(d & (2**low - 1), low)
         )
 
+    def flip_top(self, block, bit):
+        return self.permute(block, lambda d: d ^ (1 << (self.low_bits + bit)))
+
     def across(self, blocks):
         return [
             b if k == 0 else self.permute(b, lambda d: d ^ (k << self.low_bits))
@@ -60,8 +63,16 @@
     return reverse_bits((place() >> low_bits()) ^ k, SLOT_BITS)
 
 
+def bit_of_place(bit):
+    return (place() >> bit) & 1
+
+
 def is_upper(bit):
-    return (place() >> bit) & 1 == 1
+    return bit_of_place(bit) == 1
+
+
+def top_pair():
+    return bit_of_place(low_bits()), bit_of_place(low_bits() + 1)
 
 
 def split(x):
@@ -95,7 +106,27 @@
     return [(s, s | 1 << bit) for s in range(SLOTS) if not s >> bit & 1]
 
 
-def head_kernel(vectors_in, basis_in, transfer_in, target_in, out, basis, transfer, target, vectors, sems):
+def store(out, nodes, weights):
+    rank = nodes[0].shape[0]
+    for s in range(SLOTS):
+        out[s * rank : (s + 1) * rank] = nodes[s]
+    out[SLOTS * rank :] = weights
+
+
+def head_kernel(
+    vectors_in,
+    basis_in,
+    transfer_in,
+    target_in,
+    diagonal_in,
+    out,
+    basis,
+    transfer,
+    target,
+    diagonal,
+    vectors,
+    sems,
+):
     leaf = basis.shape[2]
     copies = []
 
@@ -112,7 +143,8 @@
         )
     first = fetch(transfer_in.at[pl.ds(0, SLOT_BITS)], transfer.at[pl.ds(0, SLOT_BITS)])
     rest = pl.ds(SLOT_BITS, transfer.shape[0] - SLOT_BITS)
-    later = [fetch(transfer_in.at[rest], transfer.at[rest]), fetch(target_in, target)]
+    weights = fetch(diagonal_in, diagonal)
+    later = [fetch(target_in, target), fetch(transfer_in.at[rest], transfer.at[rest])]
     c = []
     for s in range(SLOTS):
         for copy in slots[s]:
@@ -124,54 +156,89 @@
             both = jnp.concatenate([c[low], c[high]], axis=0)
             c[low] = product(transfer[level, low], both, NN)
             c[high] = product(transfer[level, high], both, NN)
-    for s in range(SLOTS):
-        out[s] = c[s]
+    weights.wait()
+    store(out, c, diagonal[...])
     for copy in later:
         copy.wait()
 
 
 def join(level, bit, s, own, partner, transfer):
+    rank = transfer.shape[2]
+    rows = pl.ds(pl.multiple_of(s * rank, rank), rank)
     upper = is_upper(bit)
-    lower_half = jnp.where(upper, partner[s], own[s])
-    upper_half = jnp.where(upper, own[s], partner[s])
+    lower_half = jnp.where(upper, partner[rows], own[rows])
+    upper_half = jnp.where(upper, own[rows], partner[rows])
     return product(transfer[level, s], jnp.concatenate([lower_half, upper_half], axis=0), NN)
 
 
 def pair_kernel(level, bit, own, partner, transfer, out):
-    for s in range(SLOTS):
-        out[s] = join(level, bit, s, own, partner, transfer)
-
-
-def last_pair_kernel(level, bit, own, partner, transfer, *outs):
+    nodes = [join(level, bit, s, own, partner, transfer) for s in range(SLOTS)]
+    source = partner if bit == 0 else own
+    store(out, nodes, source[SLOTS * transfer.shape[2] :])
+
+
+def last_pair_kernel(level, bit, own, partner, transfer, diagonal, *outs):
     for k in range(SLOTS):
         outs[k][...] = join(level, bit, met(k), own, partner, transfer)
-
-
-def pick_kernel(tops, transfer, basis, *outs):
-    rank, leaf = basis.shape[1:]
-    width = transfer.shape[3]
-    for k in range(SLOTS):
-        s = met(k)
-        parts = [transfer[level, s] for level in tops]
-        parts += [basis[s, :, j : j + width] for j in range(0, leaf, width)]
-        for j, part in enumerate(parts):
-            outs[k][j * rank : (j + 1) * rank] = part
-
-
-def arrange_kernel(*refs):
-    moved, tops, basis = refs[:SLOTS], refs[SLOTS], refs[SLOTS + 1]
-    rank, width = tops.shape[2:]
-    for k in range(SLOTS):
-        s = met(k)
+    same = bit_of_place(0) == bit_of_place(bit)
+    outs[SLOTS][...] = jnp.where(same, diagonal[...], partner[SLOTS * transfer.shape[2] :])
+
+
+def tops_of(transfer, levels, s):
+    return jnp.concatenate([transfer[level, s] for level in levels], axis=0)
+
+
+def first_step(read, out):
+    x, _ = top_pair()
+    for v in range(2):
+        out[v] = read((x ^ 1) << 1 | v)
+
+
+def second_step(read, first, out):
+    x, y = top_pair()
+    out[x] = read(x << 1 | (y ^ 1))
+    out[x ^ 1] = first[y ^ 1]
+
+
+def settle(read, first, second, write):
+    x, y = top_pair()
+    write(x << 1 | y, read(x << 1 | y))
+    write((x ^ 1) << 1 | y, first[y])
+    for w in range(2):
+        write(w << 1 | (y ^ 1), second[w])
+
+
+def basis_first_kernel(basis, out):
+    first_step(lambda s: basis[s], out)
+
+
+def basis_second_kernel(basis, first, out):
+    second_step(lambda s: basis[s], first, out)
+
+
+def basis_settle_kernel(basis, first, second, out):
+    def write(s, block):
+        out[s] = block
+
+    settle(lambda s: basis[s], first, second, write)
+
+
+def tops_first_kernel(levels, transfer, out):
+    first_step(lambda s: tops_of(transfer, levels, s), out)
+
+
+def tops_second_kernel(levels, transfer, first, out):
+    second_step(lambda s: tops_of(transfer, levels, s), first, out)
+
+
+def fold_kernel(levels, transfer, first, second, basis, weights, wide, middle, tops, columns):
+    rank = basis.shape[1]
+
+    def write(s, block):
         for j in range(SLOT_BITS):
-            tops[j, s] = moved[k][j * rank : (j + 1) * rank]
-        for j in range(basis.shape[2] // width):
-            row = (SLOT_BITS + j) * rank
-            basis[s, :, j * width : (j + 1) * width] = moved[k][row : row + rank]
-
-
-def fold_kernel(tops, basis, weights, wide, middle, columns):
-    rank = basis.shape[1]
+            tops[j, s] = block[j * rank : (j + 1) * rank]
+
+    settle(lambda s: tops_of(transfer, levels, s), first, second, write)
     blocks = [tops[0, s] for s in range(SLOTS)]
     high = 1 << (SLOT_BITS - 1)
     sources = [[s & ~high, s | high] for s in range(SLOTS)]
@@ -193,7 +260,9 @@
     wide[...] = ordered
     inner = []
     for s in range(SLOTS):
-        gram = product(basis[s] * weights[s : s + 1, :], basis[s], NT)
+        rows = weights.shape[0] // SLOTS
+        weight = jnp.concatenate([weights[j : j + 1] for j in range(s * rows, (s + 1) * rows)], axis=1)
+        gram = product(basis[s] * weight, basis[s], NT)
         inner.append(product(gram, ordered[s * rank : (s + 1) * rank], NN))
     middle[...] = product(ordered, jnp.concatenate(inner, axis=0), TN)
 
@@ -270,36 +339,36 @@
     rows_scratch = [pltpu.VMEM((slots, leaf, vecs), jnp.float32), pltpu.SemaphoreType.DMA((slots,))]
     source_t = jnp.swapaxes(source_basis, 1, 2)
     target_t = jnp.swapaxes(target_basis, 1, 2)
-    coeffs, source_t, transfer, target_t = call(
+    lanes = transfer.shape[3]
+    diagonal_rows = diagonal.reshape(-1, lanes)
+    packed = (slots * rank + diagonal_rows.shape[0], vecs)
+    coeffs, source_t, transfer, target_t, diagonal_rows = call(
         head_kernel,
-        [nodes, basis_shape, transfer.shape, basis_shape],
+        [packed, basis_shape, transfer.shape, basis_shape, diagonal_rows.shape],
         [
             pltpu.with_memory_space_constraint(x, pltpu.HBM)
-            for x in (vectors, source_t, transfer, target_t)
+            for x in (vectors, source_t, transfer, target_t, diagonal_rows)
         ],
-        [HBM] * 4,
+        [HBM] * 5,
         scratch=[
             pltpu.VMEM(vectors.shape, jnp.float32),
-            pltpu.SemaphoreType.DMA((2 * slots + 3,)),
+            pltpu.SemaphoreType.DMA((2 * slots + 4,)),
         ],
     )
     tops = [SLOT_BITS + places.low_bits + j for j in range(SLOT_BITS)]
 
-    message = (SLOT_BITS * rank + leaf * rank // transfer.shape[3], transfer.shape[3])
-    moving = call(functools.partial(pick_kernel, tops), [message] * slots, [transfer, target_t])
-    moved = places.across(moving)
-    weights = places.reverse_low(diagonal).reshape(slots, leaf)
-    top_blocks, basis_t = call(
-        arrange_kernel, [(SLOT_BITS,) + transfer.shape[1:], basis_shape], moved
-    )
+    half = (slots // 2, rank, leaf)
+    (sent,) = call(basis_first_kernel, [half], [target_t])
+    first = places.flip_top(sent, 0)
+    (sent,) = call(basis_second_kernel, [half], [target_t, first])
+    second = places.flip_top(sent, 1)
+    (basis_t,) = call(basis_settle_kernel, [basis_shape], [target_t, first, second])
     image_basis = places.reverse_low(basis_t)
-    square = (slots * rank, slots * rank)
-    wide, middle = call(
-        fold_kernel,
-        [square, square],
-        [top_blocks, basis_t, weights],
-        scratch=[pltpu.VMEM((slots, slots * rank, rank), jnp.float32)],
-    )
+    half = (slots // 2, SLOT_BITS * rank, lanes)
+    (sent,) = call(functools.partial(tops_first_kernel, tops), [half], [transfer])
+    first = places.flip_top(sent, 0)
+    (sent,) = call(functools.partial(tops_second_kernel, tops), [half], [transfer, first])
+    second = places.flip_top(sent, 1)
 
     for bit in pair_bits:
         partner = places.partner(coeffs, bit)
@@ -307,10 +376,24 @@
         kernel = last_pair_kernel if last else pair_kernel
         blocks = call(
             functools.partial(kernel, SLOT_BITS + bit, bit),
-            [node] * slots if last else [nodes],
-            [coeffs, partner, transfer],
+            [node] * slots + [diagonal_rows.shape] if last else [packed],
+            [coeffs, partner, transfer] + ([diagonal_rows] if last else []),
         )
         coeffs = blocks[0]
+    *blocks, weights = blocks
+    if places.low_bits // 2 != 1:
+        weights = places.reverse_low(diagonal).reshape(diagonal_rows.shape)
+
+    square = (slots * rank, slots * rank)
+    wide, middle = call(
+        functools.partial(fold_kernel, tops),
+        [square, square],
+        [transfer, first, second, basis_t, weights],
+        scratch=[
+            pltpu.VMEM((SLOT_BITS, slots, rank, lanes), jnp.float32),
+            pltpu.VMEM((slots, slots * rank, rank), jnp.float32),
+        ],
+    )
 
     blocks = places.across(blocks)
     back = places.across(call(middle_kernel, [node] * slots, [middle] + blocks))

time: 60.9 us -> 59.1 us (0.970)
  starting transfers between devices: 28.9 us -> 27.9 us
  waiting for transfers between devices: 22.7 us -> 22 us
    ppermute x18, starting transfers between devices: 28.9 us -> 27.9 us  [permute(): lax.ppermute(block, BOTH, [(d, route(d)) for d in range(self.devices)])]
    ppermute x18, waiting for transfers between devices: 22.7 us -> 22 us  [permute(): lax.ppermute(block, BOTH, [(d, route(d)) for d in range(self.devices)])]
    pallas_call x14 -> x17, Pallas kernels: 8.27 us -> 8.3 us  [call(): pl.pallas_call(kernel, out_shape=shapes, in_specs=specs or [VMEM] * len(o...]
  transfers between devices with their start and end apart: 18 -> 18, of which waited for: 10 -> 10; matrix products, arithmetic and copies ran while one was open for 0% -> 0% of each run, Pallas kernels for 5% -> 6%
where the time goes in v8:
time: 59.1 us; the launch traced here: 58.9 us
  starting transfers between devices  27.9 us (47%)
  waiting for transfers between devices  22 us (37%)
  Pallas kernels  8.3 us (14%)
  between operations  0.8 us (1%)
    ppermute x18, starting transfers between devices, permute(): lax.ppermute(block, BOTH, [(d, route(d)) for d in range(self.devices)])  27.9 us
    ppermute x18, waiting for transfers between devices, permute(): lax.ppermute(block, BOTH, [(d, route(d)) for d in range(self.devices)])  22 us
    pallas_call x17, Pallas kernels, call(): pl.pallas_call(kernel, out_shape=shapes, in_specs=specs or [VMEM] * len(o...  8.3 us
  transfers between devices with their start and end apart: 18, of which 10 were waited for; matrix products, arithmetic and copies ran while one was open for 0% of the time, Pallas kernels for 6%

profile of v8, /device:TPU:1, one launch (start us, length us, event | category | flops | bytes accessed | tf_op | source)
XLA Modules:
  0.0 58.9 jit_solution(16598078650871798557)
XLA Ops:
  0.6 2.2 %shard_map.68 = (f32[264,128]{1,0:T(8,128)S(1)}, f32[4,64,256]{2,1,0:T(8,128)S(1)}, f32[7,4,64,128]{3,2,1,0:T(8,128)S(1)}, f32[4,64,256]{2,1,0:T(8,128)S(1)}, f32[8,128]{1,0:T(8,128)S(1)}) custom-call(f32[1024,128]{1,0:T(8,128)} %vectors_in.1, f32[4,64,256]{2,1,0:T(8,128)} %bitcast.3, f32[7,4,64,128]{3,2,1,0:T(8,128)} %transfer_in.1, f32[4,64,256]{2,1,0:T(8,128)} %bitcast.4, ...), custom_call_target="tpu_custom_call" | custom-call | flops 16777216 | bytes 524288 | tf_op jit(solution)/shard_map/pallas_call | solution.py:94
  2.9 0.1 collective-permute-start.5
  3.0 1.3 %collective-permute-done.5.partner = f32[264,128]{1,0:T(8,128)S(1)} collective-permute-done((f32[264,128]{1,0:T(8,128)S(1)}, f32[264,128]{1,0:T(8,128)S(1)}, u32[]{:S(2)}, u32[]{:S(2)}) %collective-permute-start.5) | collective-permute-done | bytes 135200 | tf_op jit(solution)/shard_map/ppermute | solution.py:33
  4.3 0.3 shard_map.74.own
  4.6 2.5 %collective-permute-start.6 = (f32[264,128]{1,0:T(8,128)S(1)}, f32[264,128]{1,0:T(8,128)S(1)}, u32[]{:S(2)}, u32[]{:S(2)}) collective-permute-start(f32[264,128]{1,0:T(8,128)S(1)} %shard_map.74.own), channel_id=1, source_target_pairs={{0,2},{1,3},{2,0},{3,1},{4,6},{5,7},{6,4},{7,5},{8,10},{9,11},{10,... | collective-permute-start | bytes 405512 | tf_op jit(solution)/shard_map/ppermute | solution.py:33
  7.0 1.3 %collective-permute-start = (f32[2,64,256]{2,1,0:T(8,128)S(1)}, f32[2,64,256]{2,1,0:T(8,128)S(1)}, u32[]{:S(2)}, u32[]{:S(2)}) collective-permute-start(f32[2,64,256]{2,1,0:T(8,128)S(1)} %shard_map.69), channel_id=1, source_target_pairs={{0,8},{1,9},{2,10},{3,11},{4,12},{5,13},{6,14},{7,15},{8,0},{9,1},... | collective-permute-start | bytes 393224 | tf_op jit(solution)/shard_map/ppermute | solution.py:33
  8.3 0.3 collective-permute-start.3
  8.6 2.0 %collective-permute-done.6.partner = f32[264,128]{1,0:T(8,128)S(1)} collective-permute-done((f32[264,128]{1,0:T(8,128)S(1)}, f32[264,128]{1,0:T(8,128)S(1)}, u32[]{:S(2)}, u32[]{:S(2)}) %collective-permute-start.6) | collective-permute-done | bytes 135200 | tf_op jit(solution)/shard_map/ppermute | solution.py:33
  10.6 0.2 shard_map.75.own
  10.9 2.2 %collective-permute-start.7 = (f32[264,128]{1,0:T(8,128)S(1)}, f32[264,128]{1,0:T(8,128)S(1)}, u32[]{:S(2)}, u32[]{:S(2)}) collective-permute-start(f32[264,128]{1,0:T(8,128)S(1)} %shard_map.75.own), channel_id=1, source_target_pairs={{0,4},{1,5},{2,6},{3,7},{4,0},{5,1},{6,2},{7,3},{8,12},{9,13},{10,... | collective-permute-start | bytes 405512 | tf_op jit(solution)/shard_map/ppermute | solution.py:33
  13.1 0.0 collective-permute-done.first
  13.1 1.3 %collective-permute-start.1 = (f32[2,64,256]{2,1,0:T(8,128)S(1)}, f32[2,64,256]{2,1,0:T(8,128)S(1)}, u32[]{:S(2)}, u32[]{:S(2)}) collective-permute-start(f32[2,64,256]{2,1,0:T(8,128)S(1)} %shard_map.70), channel_id=1, source_target_pairs={{0,16},{1,17},{2,18},{3,19},{4,20},{5,21},{6,22},{7,23},{8,24},{9,... | collective-permute-start | bytes 393224 | tf_op jit(solution)/shard_map/ppermute | solution.py:33
  14.4 0.0 collective-permute-done.3.first
  14.4 1.2 %collective-permute-start.4 = (f32[2,128,128]{2,1,0:T(8,128)S(1)}, f32[2,128,128]{2,1,0:T(8,128)S(1)}, u32[]{:S(2)}, u32[]{:S(2)}) collective-permute-start(f32[2,128,128]{2,1,0:T(8,128)S(1)} %shard_map.73), channel_id=1, source_target_pairs={{0,16},{1,17},{2,18},{3,19},{4,20},{5,21},{6,22},{7,23},{8,24},{9,... | collective-permute-start | bytes 393224 | tf_op jit(solution)/shard_map/ppermute | solution.py:33
  15.6 3.7 %collective-permute-done.7.partner = f32[264,128]{1,0:T(8,128)S(1)} collective-permute-done((f32[264,128]{1,0:T(8,128)S(1)}, f32[264,128]{1,0:T(8,128)S(1)}, u32[]{:S(2)}, u32[]{:S(2)}) %collective-permute-start.7) | collective-permute-done | bytes 135200 | tf_op jit(solution)/shard_map/ppermute | solution.py:33
  19.3 0.2 shard_map.76
  19.5 1.0 %collective-permute-start.8 = (f32[64,128]{1,0:T(8,128)S(1)}, f32[64,128]{1,0:T(8,128)S(1)}, u32[]{:S(2)}, u32[]{:S(2)}) collective-permute-start(f32[64,128]{1,0:T(8,128)S(1)} %get-tuple-element.31), channel_id=1, source_target_pairs={{0,8},{1,9},{2,10},{3,11},{4,12},{5,13},{6,14},{7,15},{8,0},{9,1},... | collective-permute-start | bytes 98312 | tf_op jit(solution)/shard_map/ppermute | solution.py:33
  20.6 1.2 %collective-permute-start.9 = (f32[64,128]{1,0:T(8,128)S(1)}, f32[64,128]{1,0:T(8,128)S(1)}, u32[]{:S(2)}, u32[]{:S(2)}) collective-permute-start(f32[64,128]{1,0:T(8,128)S(1)} %get-tuple-element.32), channel_id=1, source_target_pairs={{0,16},{1,17},{2,18},{3,19},{4,20},{5,21},{6,22},{7,23},{8,24},{9,... | collective-permute-start | bytes 98312 | tf_op jit(solution)/shard_map/ppermute | solution.py:33
  21.8 0.4 collective-permute-start.10
  22.2 0.0 collective-permute-done.1.second
  22.3 0.0 collective-permute-done.4.second
  22.3 1.2 %shard_map.77 = (f32[256,256]{1,0:T(8,128)S(1)}, f32[256,256]{1,0:T(8,128)S(1)}) custom-call(f32[7,4,64,128]{3,2,1,0:T(8,128)S(1)} %get-tuple-element.25.transfer, f32[2,128,128]{2,1,0:T(8,128)S(1)} %collective-permute-done.3.first, f32[2,128,128]{2,1,0:T(8,128)S(1)} %collective-permute-done.4.second, f32[4,64,256]{2,1,0:T(8,128)S(1)} %shard_map.71.basis, ...), custom_call_target="tpu_custom_call" | custom-call | flops 16777216 | bytes 524288 | tf_op jit(solution)/shard_map/pallas_call | solution.py:94
  23.5 0.0 collective-permute-done.8.refs_1_
  23.5 0.0 collective-permute-done.9.refs_2_
  23.5 2.0 %collective-permute-done.10.refs_3_ = f32[64,128]{1,0:T(8,128)S(1)} collective-permute-done((f32[64,128]{1,0:T(8,128)S(1)}, f32[64,128]{1,0:T(8,128)S(1)}, u32[]{:S(2)}, u32[]{:S(2)}) %collective-permute-start.10) | collective-permute-done | bytes 32800 | tf_op jit(solution)/shard_map/ppermute | solution.py:33
  25.5 0.2 shard_map.80
  25.7 0.3 collective-permute-start.12
  26.1 0.5 collective-permute-start.13
  26.6 1.9 %collective-permute-start.14 = (f32[64,128]{1,0:T(8,128)S(1)}, f32[64,128]{1,0:T(8,128)S(1)}, u32[]{:S(2)}, u32[]{:S(2)}) collective-permute-start(f32[64,128]{1,0:T(8,128)S(1)} %get-tuple-element.38), channel_id=1, source_target_pairs={{0,24},{1,25},{2,26},{3,27},{4,28},{5,29},{6,30},{7,31},{8,16},{9,... | collective-permute-start | bytes 98312 | tf_op jit(solution)/shard_map/ppermute | solution.py:33
  28.5 0.1 collective-permute-done.12.refs_1_
  28.6 0.3 collective-permute-done.13.refs_2_
  28.8 1.4 %collective-permute-done.14.refs_3_ = f32[64,128]{1,0:T(8,128)S(1)} collective-permute-done((f32[64,128]{1,0:T(8,128)S(1)}, f32[64,128]{1,0:T(8,128)S(1)}, u32[]{:S(2)}, u32[]{:S(2)}) %collective-permute-start.14) | collective-permute-done | bytes 32800 | tf_op jit(solution)/shard_map/ppermute | solution.py:33
  30.2 0.3 shard_map.81
  30.5 0.1 collective-permute-start.15
  30.6 4.7 %collective-permute-done.15.arrived = f32[4,64,128]{2,1,0:T(8,128)S(1)} collective-permute-done((f32[4,64,128]{2,1,0:T(8,128)S(1)}, f32[4,64,128]{2,1,0:T(8,128)S(1)}, u32[]{:S(2)}, u32[]{:S(2)}) %collective-permute-start.15) | collective-permute-done | bytes 131104 | tf_op jit(solution)/shard_map/ppermute | solution.py:33
  35.3 0.3 shard_map.82
  35.6 1.8 %collective-permute-start.16 = (f32[4,64,128]{2,1,0:T(8,128)S(1)}, f32[4,64,128]{2,1,0:T(8,128)S(1)}, u32[]{:S(2)}, u32[]{:S(2)}) collective-permute-start(f32[4,64,128]{2,1,0:T(8,128)S(1)} %get-tuple-element.42), channel_id=1, source_target_pairs={{0,2},{1,3},{2,0},{3,1},{4,6},{5,7},{6,4},{7,5},{8,10},{9,11},{10,... | collective-permute-start | bytes 393224 | tf_op jit(solution)/shard_map/ppermute | solution.py:33
  37.4 9.7 %collective-permute-start.2 = (f32[4,64,256]{2,1,0:T(8,128)S(1)}, f32[4,64,256]{2,1,0:T(8,128)S(1)}, u32[]{:S(2)}, u32[]{:S(2)}) collective-permute-start(f32[4,64,256]{2,1,0:T(8,128)S(1)} %shard_map.71.basis), channel_id=1, source_target_pairs={{0,0},{1,4},{2,2},{3,6},{4,1},{5,5},{6,3},{7,7},{8,8},{9,12},{10,1... | collective-permute-start | bytes 786440 | tf_op jit(solution)/shard_map/ppermute | solution.py:33
  47.2 0.2 shard_map.78
  47.4 1.9 %collective-permute-start.11 = (f32[4,64,128]{2,1,0:T(8,128)S(1)}, f32[4,64,128]{2,1,0:T(8,128)S(1)}, u32[]{:S(2)}, u32[]{:S(2)}) collective-permute-start(f32[4,64,128]{2,1,0:T(8,128)S(1)} %shard_map.78), channel_id=1, source_target_pairs={{0,0},{1,4},{2,2},{3,6},{4,1},{5,5},{6,3},{7,7},{8,8},{9,12},{10,1... | collective-permute-start | bytes 393224 | tf_op jit(solution)/shard_map/ppermute | solution.py:33
  49.3 0.0 collective-permute-done.16.arrived
  49.4 0.3 shard_map.83
  49.7 0.1 collective-permute-start.17
  49.7 5.1 %collective-permute-done.2.basis = f32[4,64,256]{2,1,0:T(8,128)S(1)} collective-permute-done((f32[4,64,256]{2,1,0:T(8,128)S(1)}, f32[4,64,256]{2,1,0:T(8,128)S(1)}, u32[]{:S(2)}, u32[]{:S(2)}) %collective-permute-start.2) | collective-permute-done | bytes 262176 | tf_op jit(solution)/shard_map/ppermute | solution.py:33
  54.9 1.4 %collective-permute-done.11.coeffs = f32[4,64,128]{2,1,0:T(8,128)S(1)} collective-permute-done((f32[4,64,128]{2,1,0:T(8,128)S(1)}, f32[4,64,128]{2,1,0:T(8,128)S(1)}, u32[]{:S(2)}, u32[]{:S(2)}) %collective-permute-start.11) | collective-permute-done | bytes 131104 | tf_op jit(solution)/shard_map/ppermute | solution.py:33
  56.3 1.1 %shard_map.79 = f32[1024,128]{1,0:T(8,128)} custom-call(f32[4,64,256]{2,1,0:T(8,128)S(1)} %collective-permute-done.2.basis, f32[4,64,128]{2,1,0:T(8,128)S(1)} %collective-permute-done.11.coeffs), custom_call_target="tpu_custom_call" | custom-call | flops 16777216 | bytes 524288 | tf_op jit(solution)/shard_map/pallas_call | solution.py:94
  57.4 0.0 collective-permute-done.17.arrived
  57.4 1.5 %shard_map.84 = f32[1024,128]{1,0:T(8,128)} custom-call(f32[4,64,128]{2,1,0:T(8,128)S(1)} %get-tuple-element.43.kept, f32[4,64,128]{2,1,0:T(8,128)S(1)} %collective-permute-done.17.arrived, f32[7,4,64,128]{3,2,1,0:T(8,128)S(1)} %get-tuple-element.25.transfer, f32[4,64,256]{2,1,0:T(8,128)S(1)} %get-tuple-element.45.basis), custom_call_target="tpu_custom_call" | custom-call | flops 16777216 | bytes 524288 | tf_op jit(solution)/shard_map/pallas_call | solution.py:94
  (5 shorter events, 0.1 us)
Async XLA Ops:
  2.9 1.4 %collective-permute-start.5 = (f32[264,128]{1,0:T(8,128)S(1)}, f32[264,128]{1,0:T(8,128)S(1)}, u32[]{:S(2)}, u32[]{:S(2)}) collective-permute-start(f32[264,128]{1,0:T(8,128)S(1)} %get-tuple-element.26.own), channel_id=1, source_target_pairs={{0,1},{1,0},{2,3},{3,2},{4,5},{5,4},{6,7},{7,6},{8,9},{9,8},{10,11... | collective-permute-start | bytes 405512 | tf_op jit(solution)/shard_map/ppermute | solution.py:33
  4.6 6.1 %collective-permute-start.6 = (f32[264,128]{1,0:T(8,128)S(1)}, f32[264,128]{1,0:T(8,128)S(1)}, u32[]{:S(2)}, u32[]{:S(2)}) collective-permute-start(f32[264,128]{1,0:T(8,128)S(1)} %shard_map.74.own), channel_id=1, source_target_pairs={{0,2},{1,3},{2,0},{3,1},{4,6},{5,7},{6,4},{7,5},{8,10},{9,11},{10,... | collective-permute-start | bytes 405512 | tf_op jit(solution)/shard_map/ppermute | solution.py:33
  7.0 6.1 %collective-permute-start = (f32[2,64,256]{2,1,0:T(8,128)S(1)}, f32[2,64,256]{2,1,0:T(8,128)S(1)}, u32[]{:S(2)}, u32[]{:S(2)}) collective-permute-start(f32[2,64,256]{2,1,0:T(8,128)S(1)} %shard_map.69), channel_id=1, source_target_pairs={{0,8},{1,9},{2,10},{3,11},{4,12},{5,13},{6,14},{7,15},{8,0},{9,1},... | collective-permute-start | bytes 393224 | tf_op jit(solution)/shard_map/ppermute | solution.py:33
  8.3 6.1 %collective-permute-start.3 = (f32[2,128,128]{2,1,0:T(8,128)S(1)}, f32[2,128,128]{2,1,0:T(8,128)S(1)}, u32[]{:S(2)}, u32[]{:S(2)}) collective-permute-start(f32[2,128,128]{2,1,0:T(8,128)S(1)} %shard_map.72), channel_id=1, source_target_pairs={{0,8},{1,9},{2,10},{3,11},{4,12},{5,13},{6,14},{7,15},{8,0},{9,1},... | collective-permute-start | bytes 393224 | tf_op jit(solution)/shard_map/ppermute | solution.py:33
  10.9 8.4 %collective-permute-start.7 = (f32[264,128]{1,0:T(8,128)S(1)}, f32[264,128]{1,0:T(8,128)S(1)}, u32[]{:S(2)}, u32[]{:S(2)}) collective-permute-start(f32[264,128]{1,0:T(8,128)S(1)} %shard_map.75.own), channel_id=1, source_target_pairs={{0,4},{1,5},{2,6},{3,7},{4,0},{5,1},{6,2},{7,3},{8,12},{9,13},{10,... | collective-permute-start | bytes 405512 | tf_op jit(solution)/shard_map/ppermute | solution.py:33
  13.1 9.1 %collective-permute-start.1 = (f32[2,64,256]{2,1,0:T(8,128)S(1)}, f32[2,64,256]{2,1,0:T(8,128)S(1)}, u32[]{:S(2)}, u32[]{:S(2)}) collective-permute-start(f32[2,64,256]{2,1,0:T(8,128)S(1)} %shard_map.70), channel_id=1, source_target_pairs={{0,16},{1,17},{2,18},{3,19},{4,20},{5,21},{6,22},{7,23},{8,24},{9,... | collective-permute-start | bytes 393224 | tf_op jit(solution)/shard_map/ppermute | solution.py:33
  14.4 7.9 %collective-permute-start.4 = (f32[2,128,128]{2,1,0:T(8,128)S(1)}, f32[2,128,128]{2,1,0:T(8,128)S(1)}, u32[]{:S(2)}, u32[]{:S(2)}) collective-permute-start(f32[2,128,128]{2,1,0:T(8,128)S(1)} %shard_map.73), channel_id=1, source_target_pairs={{0,16},{1,17},{2,18},{3,19},{4,20},{5,21},{6,22},{7,23},{8,24},{9,... | collective-permute-start | bytes 393224 | tf_op jit(solution)/shard_map/ppermute | solution.py:33
  19.5 4.0 %collective-permute-start.8 = (f32[64,128]{1,0:T(8,128)S(1)}, f32[64,128]{1,0:T(8,128)S(1)}, u32[]{:S(2)}, u32[]{:S(2)}) collective-permute-start(f32[64,128]{1,0:T(8,128)S(1)} %get-tuple-element.31), channel_id=1, source_target_pairs={{0,8},{1,9},{2,10},{3,11},{4,12},{5,13},{6,14},{7,15},{8,0},{9,1},... | collective-permute-start | bytes 98312 | tf_op jit(solution)/shard_map/ppermute | solution.py:33
  20.6 2.9 %collective-permute-start.9 = (f32[64,128]{1,0:T(8,128)S(1)}, f32[64,128]{1,0:T(8,128)S(1)}, u32[]{:S(2)}, u32[]{:S(2)}) collective-permute-start(f32[64,128]{1,0:T(8,128)S(1)} %get-tuple-element.32), channel_id=1, source_target_pairs={{0,16},{1,17},{2,18},{3,19},{4,20},{5,21},{6,22},{7,23},{8,24},{9,... | collective-permute-start | bytes 98312 | tf_op jit(solution)/shard_map/ppermute | solution.py:33
  21.8 3.7 %collective-permute-start.10 = (f32[64,128]{1,0:T(8,128)S(1)}, f32[64,128]{1,0:T(8,128)S(1)}, u32[]{:S(2)}, u32[]{:S(2)}) collective-permute-start(f32[64,128]{1,0:T(8,128)S(1)} %get-tuple-element.33), channel_id=1, source_target_pairs={{0,24},{1,25},{2,26},{3,27},{4,28},{5,29},{6,30},{7,31},{8,16},{9,... | collective-permute-start | bytes 98312 | tf_op jit(solution)/shard_map/ppermute | solution.py:33
  25.7 2.8 %collective-permute-start.12 = (f32[64,128]{1,0:T(8,128)S(1)}, f32[64,128]{1,0:T(8,128)S(1)}, u32[]{:S(2)}, u32[]{:S(2)}) collective-permute-start(f32[64,128]{1,0:T(8,128)S(1)} %get-tuple-element.36), channel_id=1, source_target_pairs={{0,8},{1,9},{2,10},{3,11},{4,12},{5,13},{6,14},{7,15},{8,0},{9,1},... | collective-permute-start | bytes 98312 | tf_op jit(solution)/shard_map/ppermute | solution.py:33
  26.1 2.8 %collective-permute-start.13 = (f32[64,128]{1,0:T(8,128)S(1)}, f32[64,128]{1,0:T(8,128)S(1)}, u32[]{:S(2)}, u32[]{:S(2)}) collective-permute-start(f32[64,128]{1,0:T(8,128)S(1)} %get-tuple-element.37), channel_id=1, source_target_pairs={{0,16},{1,17},{2,18},{3,19},{4,20},{5,21},{6,22},{7,23},{8,24},{9,... | collective-permute-start | bytes 98312 | tf_op jit(solution)/shard_map/ppermute | solution.py:33
  26.6 3.7 %collective-permute-start.14 = (f32[64,128]{1,0:T(8,128)S(1)}, f32[64,128]{1,0:T(8,128)S(1)}, u32[]{:S(2)}, u32[]{:S(2)}) collective-permute-start(f32[64,128]{1,0:T(8,128)S(1)} %get-tuple-element.38), channel_id=1, source_target_pairs={{0,24},{1,25},{2,26},{3,27},{4,28},{5,29},{6,30},{7,31},{8,16},{9,... | collective-permute-start | bytes 98312 | tf_op jit(solution)/shard_map/ppermute | solution.py:33
  30.5 4.8 %collective-permute-start.15 = (f32[4,64,128]{2,1,0:T(8,128)S(1)}, f32[4,64,128]{2,1,0:T(8,128)S(1)}, u32[]{:S(2)}, u32[]{:S(2)}) collective-permute-start(f32[4,64,128]{2,1,0:T(8,128)S(1)} %get-tuple-element.40), channel_id=1, source_target_pairs={{0,4},{1,5},{2,6},{3,7},{4,0},{5,1},{6,2},{7,3},{8,12},{9,13},{10,... | collective-permute-start | bytes 393224 | tf_op jit(solution)/shard_map/ppermute | solution.py:33
  35.6 13.7 %collective-permute-start.16 = (f32[4,64,128]{2,1,0:T(8,128)S(1)}, f32[4,64,128]{2,1,0:T(8,128)S(1)}, u32[]{:S(2)}, u32[]{:S(2)}) collective-permute-start(f32[4,64,128]{2,1,0:T(8,128)S(1)} %get-tuple-element.42), channel_id=1, source_target_pairs={{0,2},{1,3},{2,0},{3,1},{4,6},{5,7},{6,4},{7,5},{8,10},{9,11},{10,... | collective-permute-start | bytes 393224 | tf_op jit(solution)/shard_map/ppermute | solution.py:33
  37.4 17.4 %collective-permute-start.2 = (f32[4,64,256]{2,1,0:T(8,128)S(1)}, f32[4,64,256]{2,1,0:T(8,128)S(1)}, u32[]{:S(2)}, u32[]{:S(2)}) collective-permute-start(f32[4,64,256]{2,1,0:T(8,128)S(1)} %shard_map.71.basis), channel_id=1, source_target_pairs={{0,0},{1,4},{2,2},{3,6},{4,1},{5,5},{6,3},{7,7},{8,8},{9,12},{10,1... | collective-permute-start | bytes 786440 | tf_op jit(solution)/shard_map/ppermute | solution.py:33
  47.4 8.9 %collective-permute-start.11 = (f32[4,64,128]{2,1,0:T(8,128)S(1)}, f32[4,64,128]{2,1,0:T(8,128)S(1)}, u32[]{:S(2)}, u32[]{:S(2)}) collective-permute-start(f32[4,64,128]{2,1,0:T(8,128)S(1)} %shard_map.78), channel_id=1, source_target_pairs={{0,0},{1,4},{2,2},{3,6},{4,1},{5,5},{6,3},{7,7},{8,8},{9,12},{10,1... | collective-permute-start | bytes 393224 | tf_op jit(solution)/shard_map/ppermute | solution.py:33
  49.7 7.8 %collective-permute-start.17 = (f32[4,64,128]{2,1,0:T(8,128)S(1)}, f32[4,64,128]{2,1,0:T(8,128)S(1)}, u32[]{:S(2)}, u32[]{:S(2)}) collective-permute-start(f32[4,64,128]{2,1,0:T(8,128)S(1)} %get-tuple-element.44), channel_id=1, source_target_pairs={{0,1},{1,0},{2,3},{3,2},{4,5},{5,4},{6,7},{7,6},{8,9},{9,8},{10,11... | collective-permute-start | bytes 393224 | tf_op jit(solution)/shard_map/ppermute | solution.py:33

commit v9 on v8

--- a/solution.py
+++ b/solution.py
@@ -11,6 +11,9 @@
 SLOT_BITS = 2
 SLOTS = 2**SLOT_BITS
 BOTH = ("row", "col")
+CROSSING = sorted(range(1, SLOTS), key=lambda k: -k.bit_count())
+FORWARD_PIECES = [CROSSING[: SLOTS // 2], CROSSING[SLOTS // 2 :] + [0]]
+BACK_PIECES = [[0], CROSSING]
 NN, TN, NT = ((1,), (0,)), ((0,), (0,)), ((1,), (1,))
 VMEM = pl.BlockSpec(memory_space=pltpu.VMEM)
 ANY = pl.BlockSpec(memory_space=pl.ANY)
@@ -108,9 +111,10 @@
 
 def store(out, nodes, weights):
     rank = nodes[0].shape[0]
-    for s in range(SLOTS):
-        out[s * rank : (s + 1) * rank] = nodes[s]
-    out[SLOTS * rank :] = weights
+    for at, node in enumerate(nodes):
+        out[at * rank : (at + 1) * rank] = node
+    if weights is not None:
+        out[len(nodes) * rank :] = weights
 
 
 def head_kernel(
@@ -162,26 +166,39 @@
         copy.wait()
 
 
-def join(level, bit, s, own, partner, transfer):
+def join(level, bit, s, at, own, partner, transfer):
     rank = transfer.shape[2]
-    rows = pl.ds(pl.multiple_of(s * rank, rank), rank)
+    rows = pl.ds(pl.multiple_of(at * rank, rank), rank)
     upper = is_upper(bit)
     lower_half = jnp.where(upper, partner[rows], own[rows])
     upper_half = jnp.where(upper, own[rows], partner[rows])
     return product(transfer[level, s], jnp.concatenate([lower_half, upper_half], axis=0), NN)
 
 
+def weights_of(bit, own, partner, rank):
+    return (partner if bit == 0 else own)[SLOTS * rank :]
+
+
 def pair_kernel(level, bit, own, partner, transfer, out):
-    nodes = [join(level, bit, s, own, partner, transfer) for s in range(SLOTS)]
-    source = partner if bit == 0 else own
-    store(out, nodes, source[SLOTS * transfer.shape[2] :])
-
-
-def last_pair_kernel(level, bit, own, partner, transfer, diagonal, *outs):
-    for k in range(SLOTS):
-        outs[k][...] = join(level, bit, met(k), own, partner, transfer)
+    nodes = [join(level, bit, s, s, own, partner, transfer) for s in range(SLOTS)]
+    store(out, nodes, weights_of(bit, own, partner, transfer.shape[2]))
+
+
+def cutting_pair_kernel(level, bit, own, partner, transfer, *outs):
+    for j, piece in enumerate(FORWARD_PIECES):
+        nodes = [join(level, bit, met(k), met(k), own, partner, transfer) for k in piece]
+        weights = weights_of(bit, own, partner, transfer.shape[2]) if j == 0 else None
+        store(outs[j], nodes, weights)
+
+
+def last_pair_kernel(level, bit, piece, own, partner, transfer, *outs):
+    for at, k in enumerate(piece):
+        outs[at][...] = join(level, bit, met(k), at, own, partner, transfer)
+
+
+def weights_kernel(bit, rows, diagonal, partner, out):
     same = bit_of_place(0) == bit_of_place(bit)
-    outs[SLOTS][...] = jnp.where(same, diagonal[...], partner[SLOTS * transfer.shape[2] :])
+    out[...] = jnp.where(same, diagonal[...], partner[rows:])
 
 
 def tops_of(transfer, levels, s):
@@ -283,22 +300,32 @@
         out[s] = rows[s * rank : (s + 1) * rank]
 
 
-def part(level, bit, s, block, transfer, sent, kept):
+def part(level, bit, s, at, block, transfer, sent, kept):
     upper = is_upper(bit)
     out = product(transfer[level, s], block, TN)
     rank = sent.shape[1]
-    sent[s] = jnp.where(upper, out[:rank], out[rank:])
-    kept[s] = jnp.where(upper, out[rank:], out[:rank])
-
-
-def first_part_kernel(level, bit, transfer, *refs):
-    for k in range(SLOTS):
-        part(level, bit, met(k), refs[k][...], transfer, *refs[SLOTS:])
+    sent[at] = jnp.where(upper, out[:rank], out[rank:])
+    kept[at] = jnp.where(upper, out[rank:], out[:rank])
+
+
+def first_part_kernel(level, bit, piece, transfer, *refs):
+    sent, kept = refs[len(piece) :]
+    for at, k in enumerate(piece):
+        part(level, bit, met(k), at, refs[at][...], transfer, sent, kept)
+
+
+def joining_part_kernel(level, bit, transfer, *refs):
+    sent, kept = refs[-2:]
+    for j, piece in enumerate(BACK_PIECES):
+        kept_in, arrived = refs[2 * j : 2 * j + 2]
+        for at, k in enumerate(piece):
+            s = met(k)
+            part(level, bit, s, s, kept_in[at] + arrived[at], transfer, sent, kept)
 
 
 def part_kernel(level, bit, transfer, kept_in, arrived, sent, kept):
     for s in range(SLOTS):
-        part(level, bit, s, kept_in[s] + arrived[s], transfer, sent, kept)
+        part(level, bit, s, s, kept_in[s] + arrived[s], transfer, sent, kept)
 
 
 def write_rows(rows, out, buffer, sems):
@@ -370,18 +397,36 @@
     (sent,) = call(functools.partial(tops_second_kernel, tops), [half], [transfer, first])
     second = places.flip_top(sent, 1)
 
-    for bit in pair_bits:
+    *early_bits, last_bit = pair_bits
+    weight_rows = diagonal_rows.shape[0]
+    for bit in early_bits:
         partner = places.partner(coeffs, bit)
-        last = bit == pair_bits[-1]
-        kernel = last_pair_kernel if last else pair_kernel
-        blocks = call(
-            functools.partial(kernel, SLOT_BITS + bit, bit),
-            [node] * slots + [diagonal_rows.shape] if last else [packed],
-            [coeffs, partner, transfer] + ([diagonal_rows] if last else []),
-        )
-        coeffs = blocks[0]
-    *blocks, weights = blocks
-    if places.low_bits // 2 != 1:
+        cut = bit == early_bits[-1]
+        rows = [len(piece) * rank for piece in FORWARD_PIECES]
+        rows[0] += weight_rows
+        coeffs, *others = call(
+            functools.partial(cutting_pair_kernel if cut else pair_kernel, SLOT_BITS + bit, bit),
+            [(n, vecs) for n in rows] if cut else [packed],
+            [coeffs, partner, transfer],
+        )
+    messages = [coeffs] + others
+    partners = [places.partner(message, last_bit) for message in messages]
+    blocks = {}
+    for j, piece in enumerate(FORWARD_PIECES):
+        outs = call(
+            functools.partial(last_pair_kernel, SLOT_BITS + last_bit, last_bit, piece),
+            [node] * len(piece),
+            [messages[j], partners[j], transfer],
+        )
+        blocks.update(zip(piece, outs))
+    blocks = [blocks[k] for k in range(SLOTS)]
+    if places.low_bits // 2 == 1:
+        (weights,) = call(
+            functools.partial(weights_kernel, last_bit, len(FORWARD_PIECES[0]) * rank),
+            [diagonal_rows.shape],
+            [diagonal_rows, partners[0]],
+        )
+    else:
         weights = places.reverse_low(diagonal).reshape(diagonal_rows.shape)
 
     square = (slots * rank, slots * rank)
@@ -407,15 +452,25 @@
         scratch=rows_scratch,
     )
 
-    for bit in reversed(pair_bits):
-        if bit == pair_bits[-1]:
-            kernel, operands = first_part_kernel, back
-        else:
-            kernel, operands = part_kernel, [kept, arrived]
+    pieces = []
+    for piece in BACK_PIECES:
+        shape = (len(piece), rank, vecs)
         sent, kept = call(
-            functools.partial(kernel, SLOT_BITS + bit, bit), [nodes, nodes], [transfer] + operands
-        )
-        arrived = places.partner(sent, bit)
+            functools.partial(first_part_kernel, SLOT_BITS + last_bit, last_bit, piece),
+            [shape, shape],
+            [transfer] + [back[k] for k in piece],
+        )
+        pieces += [kept, places.partner(sent, last_bit)]
+    for bit in reversed(early_bits):
+        sent, kept = call(
+            functools.partial(
+                joining_part_kernel if bit == early_bits[-1] else part_kernel, SLOT_BITS + bit, bit
+            ),
+            [nodes, nodes],
+            [transfer] + pieces,
+        )
+        pieces = [kept, places.partner(sent, bit)]
+    kept, arrived = pieces
     (adjoint,) = call(
         tail_kernel,
         [vectors.shape],

time: 59.1 us -> 62.9 us (1.064)
  starting transfers between devices: 27.9 us -> 29.7 us
  waiting for transfers between devices: 22 us -> 23.5 us
    ppermute x18 -> x20, starting transfers between devices: 27.9 us -> 29.7 us  [permute(): lax.ppermute(block, BOTH, [(d, route(d)) for d in range(self.devices)])]
    ppermute x18 -> x20, waiting for transfers between devices: 22 us -> 23.5 us  [permute(): lax.ppermute(block, BOTH, [(d, route(d)) for d in range(self.devices)])]
    pallas_call x17 -> x20, Pallas kernels: 8.3 us -> 8.63 us  [call(): pl.pallas_call(kernel, out_shape=shapes, in_specs=specs or [VMEM] * len(o...]
  transfers between devices with their start and end apart: 18 -> 20, of which waited for: 10 -> 9; matrix products, arithmetic and copies ran while one was open for 0% -> 0% of each run, Pallas kernels for 6% -> 6%
where the time goes in v9:
time: 62.9 us; the launch traced here: 62.7 us
  starting transfers between devices  29.7 us (47%)
  waiting for transfers between devices  23.5 us (37%)
  Pallas kernels  8.63 us (14%)
  between operations  0.83 us (1%)
    ppermute x20, starting transfers between devices, permute(): lax.ppermute(block, BOTH, [(d, route(d)) for d in range(self.devices)])  29.7 us
    ppermute x20, waiting for transfers between devices, permute(): lax.ppermute(block, BOTH, [(d, route(d)) for d in range(self.devices)])  23.5 us
    pallas_call x20, Pallas kernels, call(): pl.pallas_call(kernel, out_shape=shapes, in_specs=specs or [VMEM] * len(o...  8.63 us
  transfers between devices with their start and end apart: 20, of which 9 were waited for; matrix products, arithmetic and copies ran while one was open for 0% of the time, Pallas kernels for 6%

profile of v9, /device:TPU:1, one launch (start us, length us, event | category | flops | bytes accessed | tf_op | source)
XLA Modules:
  0.0 62.7 jit_solution(1091219981852464545)
XLA Ops:
  0.6 2.2 %shard_map.68 = (f32[264,128]{1,0:T(8,128)S(1)}, f32[4,64,256]{2,1,0:T(8,128)S(1)}, f32[7,4,64,128]{3,2,1,0:T(8,128)S(1)}, f32[4,64,256]{2,1,0:T(8,128)S(1)}, f32[8,128]{1,0:T(8,128)S(1)}) custom-call(f32[1024,128]{1,0:T(8,128)} %vectors_in.1, f32[4,64,256]{2,1,0:T(8,128)} %bitcast.3, f32[7,4,64,128]{3,2,1,0:T(8,128)} %transfer_in.1, f32[4,64,256]{2,1,0:T(8,128)} %bitcast.4, ...), custom_call_target="tpu_custom_call" | custom-call | flops 16777216 | bytes 524288 | tf_op jit(solution)/shard_map/pallas_call | solution.py:97
  2.9 0.1 collective-permute-start.5
  3.0 2.7 %collective-permute-start = (f32[2,64,256]{2,1,0:T(8,128)S(1)}, f32[2,64,256]{2,1,0:T(8,128)S(1)}, u32[]{:S(2)}, u32[]{:S(2)}) collective-permute-start(f32[2,64,256]{2,1,0:T(8,128)S(1)} %shard_map.69), channel_id=1, source_target_pairs={{0,8},{1,9},{2,10},{3,11},{4,12},{5,13},{6,14},{7,15},{8,0},{9,1},... | collective-permute-start | bytes 393224 | tf_op jit(solution)/shard_map/ppermute | solution.py:36
  5.7 0.1 collective-permute-start.3
  5.8 0.0 collective-permute-done.5.partner
  5.8 0.2 shard_map.74.own
  6.1 1.6 %collective-permute-start.6 = (f32[264,128]{1,0:T(8,128)S(1)}, f32[264,128]{1,0:T(8,128)S(1)}, u32[]{:S(2)}, u32[]{:S(2)}) collective-permute-start(f32[264,128]{1,0:T(8,128)S(1)} %shard_map.74.own), channel_id=1, source_target_pairs={{0,2},{1,3},{2,0},{3,1},{4,6},{5,7},{6,4},{7,5},{8,10},{9,11},{10,... | collective-permute-start | bytes 405512 | tf_op jit(solution)/shard_map/ppermute | solution.py:36
  7.6 1.9 %collective-permute-done.first = f32[2,64,256]{2,1,0:T(8,128)S(1)} collective-permute-done((f32[2,64,256]{2,1,0:T(8,128)S(1)}, f32[2,64,256]{2,1,0:T(8,128)S(1)}, u32[]{:S(2)}, u32[]{:S(2)}) %collective-permute-start) | collective-permute-done | bytes 131104 | tf_op jit(solution)/shard_map/ppermute | solution.py:36
  9.6 1.3 %collective-permute-start.1 = (f32[2,64,256]{2,1,0:T(8,128)S(1)}, f32[2,64,256]{2,1,0:T(8,128)S(1)}, u32[]{:S(2)}, u32[]{:S(2)}) collective-permute-start(f32[2,64,256]{2,1,0:T(8,128)S(1)} %shard_map.70), channel_id=1, source_target_pairs={{0,16},{1,17},{2,18},{3,19},{4,20},{5,21},{6,22},{7,23},{8,24},{9,... | collective-permute-start | bytes 393224 | tf_op jit(solution)/shard_map/ppermute | solution.py:36
  10.9 1.5 %collective-permute-done.3.first = f32[2,128,128]{2,1,0:T(8,128)S(1)} collective-permute-done((f32[2,128,128]{2,1,0:T(8,128)S(1)}, f32[2,128,128]{2,1,0:T(8,128)S(1)}, u32[]{:S(2)}, u32[]{:S(2)}) %collective-permute-start.3) | collective-permute-done | bytes 131104 | tf_op jit(solution)/shard_map/ppermute | solution.py:36
  12.4 1.3 %collective-permute-start.4 = (f32[2,128,128]{2,1,0:T(8,128)S(1)}, f32[2,128,128]{2,1,0:T(8,128)S(1)}, u32[]{:S(2)}, u32[]{:S(2)}) collective-permute-start(f32[2,128,128]{2,1,0:T(8,128)S(1)} %shard_map.73), channel_id=1, source_target_pairs={{0,16},{1,17},{2,18},{3,19},{4,20},{5,21},{6,22},{7,23},{8,24},{9,... | collective-permute-start | bytes 393224 | tf_op jit(solution)/shard_map/ppermute | solution.py:36
  13.7 0.0 collective-permute-done.6.partner
  13.7 0.2 shard_map.75
  13.9 2.4 %collective-permute-start.7 = (f32[136,128]{1,0:T(8,128)S(1)}, f32[136,128]{1,0:T(8,128)S(1)}, u32[]{:S(2)}, u32[]{:S(2)}) collective-permute-start(f32[136,128]{1,0:T(8,128)S(1)} %get-tuple-element.31.own), channel_id=1, source_target_pairs={{0,4},{1,5},{2,6},{3,7},{4,0},{5,1},{6,2},{7,3},{8,12},{9,13},{10,... | collective-permute-start | bytes 208904 | tf_op jit(solution)/shard_map/ppermute | solution.py:36
  16.3 0.1 collective-permute-start.8
  16.4 6.3 %collective-permute-done.8.partner = f32[128,128]{1,0:T(8,128)S(1)} collective-permute-done((f32[128,128]{1,0:T(8,128)S(1)}, f32[128,128]{1,0:T(8,128)S(1)}, u32[]{:S(2)}, u32[]{:S(2)}) %collective-permute-start.8) | collective-permute-done | bytes 65568 | tf_op jit(solution)/shard_map/ppermute | solution.py:36
  22.7 0.2 shard_map.78
  22.8 0.2 collective-permute-start.10
  23.1 0.0 collective-permute-done.7.partner
  23.1 0.2 shard_map.79
  23.3 1.2 %collective-permute-start.9 = (f32[64,128]{1,0:T(8,128)S(1)}, f32[64,128]{1,0:T(8,128)S(1)}, u32[]{:S(2)}, u32[]{:S(2)}) collective-permute-start(f32[64,128]{1,0:T(8,128)S(1)} %get-tuple-element.35), channel_id=1, source_target_pairs={{0,8},{1,9},{2,10},{3,11},{4,12},{5,13},{6,14},{7,15},{8,0},{9,1},... | collective-permute-start | bytes 98312 | tf_op jit(solution)/shard_map/ppermute | solution.py:36
  24.5 1.2 %collective-permute-start.11 = (f32[64,128]{1,0:T(8,128)S(1)}, f32[64,128]{1,0:T(8,128)S(1)}, u32[]{:S(2)}, u32[]{:S(2)}) collective-permute-start(f32[64,128]{1,0:T(8,128)S(1)} %get-tuple-element.37), channel_id=1, source_target_pairs={{0,24},{1,25},{2,26},{3,27},{4,28},{5,29},{6,30},{7,31},{8,16},{9,... | collective-permute-start | bytes 98312 | tf_op jit(solution)/shard_map/ppermute | solution.py:36
  25.7 0.0 collective-permute-done.1.second
  25.8 0.0 collective-permute-done.4.second
  25.8 1.2 %shard_map.77 = (f32[256,256]{1,0:T(8,128)S(1)}, f32[256,256]{1,0:T(8,128)S(1)}) custom-call(f32[7,4,64,128]{3,2,1,0:T(8,128)S(1)} %get-tuple-element.28.transfer, f32[2,128,128]{2,1,0:T(8,128)S(1)} %collective-permute-done.3.first, f32[2,128,128]{2,1,0:T(8,128)S(1)} %collective-permute-done.4.second, f32[4,64,256]{2,1,0:T(8,128)S(1)} %shard_map.71.basis, ...), custom_call_target="tpu_custom_call" | custom-call | flops 16777216 | bytes 524288 | tf_op jit(solution)/shard_map/pallas_call | solution.py:97
  27.0 0.0 collective-permute-done.10.refs_2_
  27.0 0.0 collective-permute-done.9.refs_1_
  27.0 1.2 %collective-permute-done.11.refs_3_ = f32[64,128]{1,0:T(8,128)S(1)} collective-permute-done((f32[64,128]{1,0:T(8,128)S(1)}, f32[64,128]{1,0:T(8,128)S(1)}, u32[]{:S(2)}, u32[]{:S(2)}) %collective-permute-start.11) | collective-permute-done | bytes 32800 | tf_op jit(solution)/shard_map/ppermute | solution.py:36
  28.2 0.2 shard_map.82
  28.4 1.3 %collective-permute-start.14 = (f32[64,128]{1,0:T(8,128)S(1)}, f32[64,128]{1,0:T(8,128)S(1)}, u32[]{:S(2)}, u32[]{:S(2)}) collective-permute-start(f32[64,128]{1,0:T(8,128)S(1)} %get-tuple-element.42), channel_id=1, source_target_pairs={{0,24},{1,25},{2,26},{3,27},{4,28},{5,29},{6,30},{7,31},{8,16},{9,... | collective-permute-start | bytes 98312 | tf_op jit(solution)/shard_map/ppermute | solution.py:36
  29.7 1.5 %collective-permute-start.15 = (f32[64,128]{1,0:T(8,128)S(1)}, f32[64,128]{1,0:T(8,128)S(1)}, u32[]{:S(2)}, u32[]{:S(2)}) collective-permute-start(f32[64,128]{1,0:T(8,128)S(1)} %get-tuple-element.43), channel_id=1, source_target_pairs={{0,8},{1,9},{2,10},{3,11},{4,12},{5,13},{6,14},{7,15},{8,0},{9,1},... | collective-permute-start | bytes 98312 | tf_op jit(solution)/shard_map/ppermute | solution.py:36
  31.2 0.0 collective-permute-start.16
  31.2 0.9 %collective-permute-done.14.refs_0_ = f32[64,128]{1,0:T(8,128)S(1)} collective-permute-done((f32[64,128]{1,0:T(8,128)S(1)}, f32[64,128]{1,0:T(8,128)S(1)}, u32[]{:S(2)}, u32[]{:S(2)}) %collective-permute-start.14) | collective-permute-done | bytes 32800 | tf_op jit(solution)/shard_map/ppermute | solution.py:36
  32.1 0.7 %collective-permute-done.15.refs_1_ = f32[64,128]{1,0:T(8,128)S(1)} collective-permute-done((f32[64,128]{1,0:T(8,128)S(1)}, f32[64,128]{1,0:T(8,128)S(1)}, u32[]{:S(2)}, u32[]{:S(2)}) %collective-permute-start.15) | collective-permute-done | bytes 32800 | tf_op jit(solution)/shard_map/ppermute | solution.py:36
  32.8 1.1 %collective-permute-done.16.refs_2_ = f32[64,128]{1,0:T(8,128)S(1)} collective-permute-done((f32[64,128]{1,0:T(8,128)S(1)}, f32[64,128]{1,0:T(8,128)S(1)}, u32[]{:S(2)}, u32[]{:S(2)}) %collective-permute-start.16) | collective-permute-done | bytes 32800 | tf_op jit(solution)/shard_map/ppermute | solution.py:36
  34.0 0.3 shard_map.84
  34.3 0.1 collective-permute-start.17
  34.3 0.2 shard_map.83
  34.6 2.4 %collective-permute-start.13 = (f32[1,64,128]{2,1,0:T(8,128)S(1)}, f32[1,64,128]{2,1,0:T(8,128)S(1)}, u32[]{:S(2)}, u32[]{:S(2)}) collective-permute-start(f32[1,64,128]{2,1,0:T(8,128)S(1)} %get-tuple-element.41), channel_id=1, source_target_pairs={{0,4},{1,5},{2,6},{3,7},{4,0},{5,1},{6,2},{7,3},{8,12},{9,13},{10,... | collective-permute-start | bytes 98312 | tf_op jit(solution)/shard_map/ppermute | solution.py:36
  37.0 3.1 %collective-permute-done.13.refs_1_ = f32[1,64,128]{2,1,0:T(8,128)S(1)} collective-permute-done((f32[1,64,128]{2,1,0:T(8,128)S(1)}, f32[1,64,128]{2,1,0:T(8,128)S(1)}, u32[]{:S(2)}, u32[]{:S(2)}) %collective-permute-start.13) | collective-permute-done | bytes 32800 | tf_op jit(solution)/shard_map/ppermute | solution.py:36
  40.1 0.0 collective-permute-done.17.refs_3_
  40.1 0.3 shard_map.85
  40.4 2.0 %collective-permute-start.18 = (f32[4,64,128]{2,1,0:T(8,128)S(1)}, f32[4,64,128]{2,1,0:T(8,128)S(1)}, u32[]{:S(2)}, u32[]{:S(2)}) collective-permute-start(f32[4,64,128]{2,1,0:T(8,128)S(1)} %get-tuple-element.48), channel_id=1, source_target_pairs={{0,2},{1,3},{2,0},{3,1},{4,6},{5,7},{6,4},{7,5},{8,10},{9,11},{10,... | collective-permute-start | bytes 393224 | tf_op jit(solution)/shard_map/ppermute | solution.py:36
  42.4 8.3 %collective-permute-start.2 = (f32[4,64,256]{2,1,0:T(8,128)S(1)}, f32[4,64,256]{2,1,0:T(8,128)S(1)}, u32[]{:S(2)}, u32[]{:S(2)}) collective-permute-start(f32[4,64,256]{2,1,0:T(8,128)S(1)} %shard_map.71.basis), channel_id=1, source_target_pairs={{0,0},{1,4},{2,2},{3,6},{4,1},{5,5},{6,3},{7,7},{8,8},{9,12},{10,1... | collective-permute-start | bytes 786440 | tf_op jit(solution)/shard_map/ppermute | solution.py:36
  50.7 0.2 shard_map.80
  51.0 1.9 %collective-permute-start.12 = (f32[4,64,128]{2,1,0:T(8,128)S(1)}, f32[4,64,128]{2,1,0:T(8,128)S(1)}, u32[]{:S(2)}, u32[]{:S(2)}) collective-permute-start(f32[4,64,128]{2,1,0:T(8,128)S(1)} %shard_map.80), channel_id=1, source_target_pairs={{0,0},{1,4},{2,2},{3,6},{4,1},{5,5},{6,3},{7,7},{8,8},{9,12},{10,1... | collective-permute-start | bytes 393224 | tf_op jit(solution)/shard_map/ppermute | solution.py:36
  52.9 0.0 collective-permute-done.18.arrived
  52.9 0.3 shard_map.86
  53.2 0.1 collective-permute-start.19
  53.3 6.7 %collective-permute-done.12.coeffs = f32[4,64,128]{2,1,0:T(8,128)S(1)} collective-permute-done((f32[4,64,128]{2,1,0:T(8,128)S(1)}, f32[4,64,128]{2,1,0:T(8,128)S(1)}, u32[]{:S(2)}, u32[]{:S(2)}) %collective-permute-start.12) | collective-permute-done | bytes 131104 | tf_op jit(solution)/shard_map/ppermute | solution.py:36
  60.0 0.0 collective-permute-done.2.basis
  60.0 1.1 %shard_map.81 = f32[1024,128]{1,0:T(8,128)} custom-call(f32[4,64,256]{2,1,0:T(8,128)S(1)} %collective-permute-done.2.basis, f32[4,64,128]{2,1,0:T(8,128)S(1)} %collective-permute-done.12.coeffs), custom_call_target="tpu_custom_call" | custom-call | flops 16777216 | bytes 524288 | tf_op jit(solution)/shard_map/pallas_call | solution.py:97
  61.2 0.0 collective-permute-done.19.arrived
  61.2 1.5 %shard_map.87 = f32[1024,128]{1,0:T(8,128)} custom-call(f32[4,64,128]{2,1,0:T(8,128)S(1)} %get-tuple-element.49.kept, f32[4,64,128]{2,1,0:T(8,128)S(1)} %collective-permute-done.19.arrived, f32[7,4,64,128]{3,2,1,0:T(8,128)S(1)} %get-tuple-element.28.transfer, f32[4,64,256]{2,1,0:T(8,128)S(1)} %get-tuple-element.51.basis), custom_call_target="tpu_custom_call" | custom-call | flops 16777216 | bytes 524288 | tf_op jit(solution)/shard_map/pallas_call | solution.py:97
  (6 shorter events, 0.1 us)
Async XLA Ops:
  2.9 3.0 %collective-permute-start.5 = (f32[264,128]{1,0:T(8,128)S(1)}, f32[264,128]{1,0:T(8,128)S(1)}, u32[]{:S(2)}, u32[]{:S(2)}) collective-permute-start(f32[264,128]{1,0:T(8,128)S(1)} %get-tuple-element.30.own), channel_id=1, source_target_pairs={{0,1},{1,0},{2,3},{3,2},{4,5},{5,4},{6,7},{7,6},{8,9},{9,8},{10,11... | collective-permute-start | bytes 405512 | tf_op jit(solution)/shard_map/ppermute | solution.py:36
  3.0 6.6 %collective-permute-start = (f32[2,64,256]{2,1,0:T(8,128)S(1)}, f32[2,64,256]{2,1,0:T(8,128)S(1)}, u32[]{:S(2)}, u32[]{:S(2)}) collective-permute-start(f32[2,64,256]{2,1,0:T(8,128)S(1)} %shard_map.69), channel_id=1, source_target_pairs={{0,8},{1,9},{2,10},{3,11},{4,12},{5,13},{6,14},{7,15},{8,0},{9,1},... | collective-permute-start | bytes 393224 | tf_op jit(solution)/shard_map/ppermute | solution.py:36
  5.7 6.6 %collective-permute-start.3 = (f32[2,128,128]{2,1,0:T(8,128)S(1)}, f32[2,128,128]{2,1,0:T(8,128)S(1)}, u32[]{:S(2)}, u32[]{:S(2)}) collective-permute-start(f32[2,128,128]{2,1,0:T(8,128)S(1)} %shard_map.72), channel_id=1, source_target_pairs={{0,8},{1,9},{2,10},{3,11},{4,12},{5,13},{6,14},{7,15},{8,0},{9,1},... | collective-permute-start | bytes 393224 | tf_op jit(solution)/shard_map/ppermute | solution.py:36
  6.1 7.6 %collective-permute-start.6 = (f32[264,128]{1,0:T(8,128)S(1)}, f32[264,128]{1,0:T(8,128)S(1)}, u32[]{:S(2)}, u32[]{:S(2)}) collective-permute-start(f32[264,128]{1,0:T(8,128)S(1)} %shard_map.74.own), channel_id=1, source_target_pairs={{0,2},{1,3},{2,0},{3,1},{4,6},{5,7},{6,4},{7,5},{8,10},{9,11},{10,... | collective-permute-start | bytes 405512 | tf_op jit(solution)/shard_map/ppermute | solution.py:36
  9.6 16.1 %collective-permute-start.1 = (f32[2,64,256]{2,1,0:T(8,128)S(1)}, f32[2,64,256]{2,1,0:T(8,128)S(1)}, u32[]{:S(2)}, u32[]{:S(2)}) collective-permute-start(f32[2,64,256]{2,1,0:T(8,128)S(1)} %shard_map.70), channel_id=1, source_target_pairs={{0,16},{1,17},{2,18},{3,19},{4,20},{5,21},{6,22},{7,23},{8,24},{9,... | collective-permute-start | bytes 393224 | tf_op jit(solution)/shard_map/ppermute | solution.py:36
  12.4 13.4 %collective-permute-start.4 = (f32[2,128,128]{2,1,0:T(8,128)S(1)}, f32[2,128,128]{2,1,0:T(8,128)S(1)}, u32[]{:S(2)}, u32[]{:S(2)}) collective-permute-start(f32[2,128,128]{2,1,0:T(8,128)S(1)} %shard_map.73), channel_id=1, source_target_pairs={{0,16},{1,17},{2,18},{3,19},{4,20},{5,21},{6,22},{7,23},{8,24},{9,... | collective-permute-start | bytes 393224 | tf_op jit(solution)/shard_map/ppermute | solution.py:36
  13.9 9.2 %collective-permute-start.7 = (f32[136,128]{1,0:T(8,128)S(1)}, f32[136,128]{1,0:T(8,128)S(1)}, u32[]{:S(2)}, u32[]{:S(2)}) collective-permute-start(f32[136,128]{1,0:T(8,128)S(1)} %get-tuple-element.31.own), channel_id=1, source_target_pairs={{0,4},{1,5},{2,6},{3,7},{4,0},{5,1},{6,2},{7,3},{8,12},{9,13},{10,... | collective-permute-start | bytes 208904 | tf_op jit(solution)/shard_map/ppermute | solution.py:36
  16.3 6.4 %collective-permute-start.8 = (f32[128,128]{1,0:T(8,128)S(1)}, f32[128,128]{1,0:T(8,128)S(1)}, u32[]{:S(2)}, u32[]{:S(2)}) collective-permute-start(f32[128,128]{1,0:T(8,128)S(1)} %get-tuple-element.33.own), channel_id=1, source_target_pairs={{0,4},{1,5},{2,6},{3,7},{4,0},{5,1},{6,2},{7,3},{8,12},{9,13},{10,... | collective-permute-start | bytes 196616 | tf_op jit(solution)/shard_map/ppermute | solution.py:36
  22.8 4.1 %collective-permute-start.10 = (f32[64,128]{1,0:T(8,128)S(1)}, f32[64,128]{1,0:T(8,128)S(1)}, u32[]{:S(2)}, u32[]{:S(2)}) collective-permute-start(f32[64,128]{1,0:T(8,128)S(1)} %get-tuple-element.36), channel_id=1, source_target_pairs={{0,16},{1,17},{2,18},{3,19},{4,20},{5,21},{6,22},{7,23},{8,24},{9,... | collective-permute-start | bytes 98312 | tf_op jit(solution)/shard_map/ppermute | solution.py:36
  23.3 3.7 %collective-permute-start.9 = (f32[64,128]{1,0:T(8,128)S(1)}, f32[64,128]{1,0:T(8,128)S(1)}, u32[]{:S(2)}, u32[]{:S(2)}) collective-permute-start(f32[64,128]{1,0:T(8,128)S(1)} %get-tuple-element.35), channel_id=1, source_target_pairs={{0,8},{1,9},{2,10},{3,11},{4,12},{5,13},{6,14},{7,15},{8,0},{9,1},... | collective-permute-start | bytes 98312 | tf_op jit(solution)/shard_map/ppermute | solution.py:36
  24.5 3.7 %collective-permute-start.11 = (f32[64,128]{1,0:T(8,128)S(1)}, f32[64,128]{1,0:T(8,128)S(1)}, u32[]{:S(2)}, u32[]{:S(2)}) collective-permute-start(f32[64,128]{1,0:T(8,128)S(1)} %get-tuple-element.37), channel_id=1, source_target_pairs={{0,24},{1,25},{2,26},{3,27},{4,28},{5,29},{6,30},{7,31},{8,16},{9,... | collective-permute-start | bytes 98312 | tf_op jit(solution)/shard_map/ppermute | solution.py:36
  28.4 3.7 %collective-permute-start.14 = (f32[64,128]{1,0:T(8,128)S(1)}, f32[64,128]{1,0:T(8,128)S(1)}, u32[]{:S(2)}, u32[]{:S(2)}) collective-permute-start(f32[64,128]{1,0:T(8,128)S(1)} %get-tuple-element.42), channel_id=1, source_target_pairs={{0,24},{1,25},{2,26},{3,27},{4,28},{5,29},{6,30},{7,31},{8,16},{9,... | collective-permute-start | bytes 98312 | tf_op jit(solution)/shard_map/ppermute | solution.py:36
  29.7 3.2 %collective-permute-start.15 = (f32[64,128]{1,0:T(8,128)S(1)}, f32[64,128]{1,0:T(8,128)S(1)}, u32[]{:S(2)}, u32[]{:S(2)}) collective-permute-start(f32[64,128]{1,0:T(8,128)S(1)} %get-tuple-element.43), channel_id=1, source_target_pairs={{0,8},{1,9},{2,10},{3,11},{4,12},{5,13},{6,14},{7,15},{8,0},{9,1},... | collective-permute-start | bytes 98312 | tf_op jit(solution)/shard_map/ppermute | solution.py:36
  31.2 2.8 %collective-permute-start.16 = (f32[64,128]{1,0:T(8,128)S(1)}, f32[64,128]{1,0:T(8,128)S(1)}, u32[]{:S(2)}, u32[]{:S(2)}) collective-permute-start(f32[64,128]{1,0:T(8,128)S(1)} %get-tuple-element.44), channel_id=1, source_target_pairs={{0,16},{1,17},{2,18},{3,19},{4,20},{5,21},{6,22},{7,23},{8,24},{9,... | collective-permute-start | bytes 98312 | tf_op jit(solution)/shard_map/ppermute | solution.py:36
  34.3 5.8 %collective-permute-start.17 = (f32[3,64,128]{2,1,0:T(8,128)S(1)}, f32[3,64,128]{2,1,0:T(8,128)S(1)}, u32[]{:S(2)}, u32[]{:S(2)}) collective-permute-start(f32[3,64,128]{2,1,0:T(8,128)S(1)} %get-tuple-element.46), channel_id=1, source_target_pairs={{0,4},{1,5},{2,6},{3,7},{4,0},{5,1},{6,2},{7,3},{8,12},{9,13},{10,... | collective-permute-start | bytes 294920 | tf_op jit(solution)/shard_map/ppermute | solution.py:36
  34.6 5.5 %collective-permute-start.13 = (f32[1,64,128]{2,1,0:T(8,128)S(1)}, f32[1,64,128]{2,1,0:T(8,128)S(1)}, u32[]{:S(2)}, u32[]{:S(2)}) collective-permute-start(f32[1,64,128]{2,1,0:T(8,128)S(1)} %get-tuple-element.41), channel_id=1, source_target_pairs={{0,4},{1,5},{2,6},{3,7},{4,0},{5,1},{6,2},{7,3},{8,12},{9,13},{10,... | collective-permute-start | bytes 98312 | tf_op jit(solution)/shard_map/ppermute | solution.py:36
  40.4 12.5 %collective-permute-start.18 = (f32[4,64,128]{2,1,0:T(8,128)S(1)}, f32[4,64,128]{2,1,0:T(8,128)S(1)}, u32[]{:S(2)}, u32[]{:S(2)}) collective-permute-start(f32[4,64,128]{2,1,0:T(8,128)S(1)} %get-tuple-element.48), channel_id=1, source_target_pairs={{0,2},{1,3},{2,0},{3,1},{4,6},{5,7},{6,4},{7,5},{8,10},{9,11},{10,... | collective-permute-start | bytes 393224 | tf_op jit(solution)/shard_map/ppermute | solution.py:36
  42.4 17.6 %collective-permute-start.2 = (f32[4,64,256]{2,1,0:T(8,128)S(1)}, f32[4,64,256]{2,1,0:T(8,128)S(1)}, u32[]{:S(2)}, u32[]{:S(2)}) collective-permute-start(f32[4,64,256]{2,1,0:T(8,128)S(1)} %shard_map.71.basis), channel_id=1, source_target_pairs={{0,0},{1,4},{2,2},{3,6},{4,1},{5,5},{6,3},{7,7},{8,8},{9,12},{10,1... | collective-permute-start | bytes 786440 | tf_op jit(solution)/shard_map/ppermute | solution.py:36
  51.0 9.1 %collective-permute-start.12 = (f32[4,64,128]{2,1,0:T(8,128)S(1)}, f32[4,64,128]{2,1,0:T(8,128)S(1)}, u32[]{:S(2)}, u32[]{:S(2)}) collective-permute-start(f32[4,64,128]{2,1,0:T(8,128)S(1)} %shard_map.80), channel_id=1, source_target_pairs={{0,0},{1,4},{2,2},{3,6},{4,1},{5,5},{6,3},{7,7},{8,8},{9,12},{10,1... | collective-permute-start | bytes 393224 | tf_op jit(solution)/shard_map/ppermute | solution.py:36
  53.2 8.0 %collective-permute-start.19 = (f32[4,64,128]{2,1,0:T(8,128)S(1)}, f32[4,64,128]{2,1,0:T(8,128)S(1)}, u32[]{:S(2)}, u32[]{:S(2)}) collective-permute-start(f32[4,64,128]{2,1,0:T(8,128)S(1)} %get-tuple-element.50), channel_id=1, source_target_pairs={{0,1},{1,0},{2,3},{3,2},{4,5},{5,4},{6,7},{7,6},{8,9},{9,8},{10,11... | collective-permute-start | bytes 393224 | tf_op jit(solution)/shard_map/ppermute | solution.py:36

commit v10 on v9

--- a/solution.py
+++ b/solution.py
@@ -125,9 +125,9 @@
     diagonal_in,
     out,
     basis,
-    transfer,
     target,
     diagonal,
+    transfer,
     vectors,
     sems,
 ):
@@ -145,10 +145,9 @@
         slots.append(
             (fetch(basis_in.at[s], basis.at[s]), fetch(vectors_in.at[rows], vectors.at[rows]))
         )
-    first = fetch(transfer_in.at[pl.ds(0, SLOT_BITS)], transfer.at[pl.ds(0, SLOT_BITS)])
-    rest = pl.ds(SLOT_BITS, transfer.shape[0] - SLOT_BITS)
+    first = fetch(transfer_in.at[pl.ds(0, SLOT_BITS)], transfer)
     weights = fetch(diagonal_in, diagonal)
-    later = [fetch(target_in, target), fetch(transfer_in.at[rest], transfer.at[rest])]
+    later = fetch(target_in, target)
     c = []
     for s in range(SLOTS):
         for copy in slots[s]:
@@ -162,8 +161,7 @@
             c[high] = product(transfer[level, high], both, NN)
     weights.wait()
     store(out, c, diagonal[...])
-    for copy in later:
-        copy.wait()
+    later.wait()
 
 
 def join(level, bit, s, at, own, partner, transfer):
@@ -369,17 +367,18 @@
     lanes = transfer.shape[3]
     diagonal_rows = diagonal.reshape(-1, lanes)
     packed = (slots * rank + diagonal_rows.shape[0], vecs)
-    coeffs, source_t, transfer, target_t, diagonal_rows = call(
+    coeffs, source_t, target_t, diagonal_rows = call(
         head_kernel,
-        [packed, basis_shape, transfer.shape, basis_shape, diagonal_rows.shape],
+        [packed, basis_shape, basis_shape, diagonal_rows.shape],
         [
             pltpu.with_memory_space_constraint(x, pltpu.HBM)
             for x in (vectors, source_t, transfer, target_t, diagonal_rows)
         ],
         [HBM] * 5,
         scratch=[
+            pltpu.VMEM((SLOT_BITS,) + transfer.shape[1:], jnp.float32),
             pltpu.VMEM(vectors.shape, jnp.float32),
-            pltpu.SemaphoreType.DMA((2 * slots + 4,)),
+            pltpu.SemaphoreType.DMA((2 * slots + 3,)),
         ],
     )
     tops = [SLOT_BITS + places.low_bits + j for j in range(SLOT_BITS)]

time: 62.9 us -> 62.9 us (level)
  no operation moved by 1% of the time
where the time goes in v10:
time: 62.9 us; the launch traced here: 62.8 us
  starting transfers between devices  29.7 us (47%)
  waiting for transfers between devices  23.6 us (38%)
  Pallas kernels  8.68 us (14%)
  between operations  0.84 us (1%)
    ppermute x20, starting transfers between devices, permute(): lax.ppermute(block, BOTH, [(d, route(d)) for d in range(self.devices)])  29.7 us
    ppermute x20, waiting for transfers between devices, permute(): lax.ppermute(block, BOTH, [(d, route(d)) for d in range(self.devices)])  23.6 us
    pallas_call x20, Pallas kernels, call(): pl.pallas_call(kernel, out_shape=shapes, in_specs=specs or [VMEM] * len(o...  8.68 us
  transfers between devices with their start and end apart: 20, of which 9 were waited for; matrix products, arithmetic and copies ran while one was open for 0% of the time, Pallas kernels for 6%

profile of v10, /device:TPU:1, one launch (start us, length us, event | category | flops | bytes accessed | tf_op | source)
XLA Modules:
  0.0 62.8 jit_solution(8156886422295222576)
XLA Ops:
  0.6 0.0 copy-start
  0.6 2.3 %shard_map.68 = (f32[264,128]{1,0:T(8,128)S(1)}, f32[4,64,256]{2,1,0:T(8,128)S(1)}, f32[4,64,256]{2,1,0:T(8,128)S(1)}, f32[8,128]{1,0:T(8,128)S(1)}) custom-call(f32[1024,128]{1,0:T(8,128)} %vectors_in.1, f32[4,64,256]{2,1,0:T(8,128)} %bitcast.3, f32[7,4,64,128]{3,2,1,0:T(8,128)} %transfer.23, f32[4,64,256]{2,1,0:T(8,128)} %bitcast.4, f32[8,128]{1,0:T(8,128)} %bitcast.5), custom_call_target="tpu_custom_call" | custom-call | flops 16777216 | bytes 524288 | tf_op jit(solution)/shard_map/pallas_call | solution.py:97
  2.9 0.1 collective-permute-start.5
  3.1 2.7 %collective-permute-start = (f32[2,64,256]{2,1,0:T(8,128)S(1)}, f32[2,64,256]{2,1,0:T(8,128)S(1)}, u32[]{:S(2)}, u32[]{:S(2)}) collective-permute-start(f32[2,64,256]{2,1,0:T(8,128)S(1)} %shard_map.69), channel_id=1, source_target_pairs={{0,8},{1,9},{2,10},{3,11},{4,12},{5,13},{6,14},{7,15},{8,0},{9,1},... | collective-permute-start | bytes 393224 | tf_op jit(solution)/shard_map/ppermute | solution.py:36
  5.8 0.0 copy-done
  5.8 0.1 collective-permute-start.3
  5.9 0.0 collective-permute-done.5.partner
  5.9 0.2 shard_map.74.own
  6.2 1.5 %collective-permute-start.6 = (f32[264,128]{1,0:T(8,128)S(1)}, f32[264,128]{1,0:T(8,128)S(1)}, u32[]{:S(2)}, u32[]{:S(2)}) collective-permute-start(f32[264,128]{1,0:T(8,128)S(1)} %shard_map.74.own), channel_id=1, source_target_pairs={{0,2},{1,3},{2,0},{3,1},{4,6},{5,7},{6,4},{7,5},{8,10},{9,11},{10,... | collective-permute-start | bytes 405512 | tf_op jit(solution)/shard_map/ppermute | solution.py:36
  7.7 1.9 %collective-permute-done.first = f32[2,64,256]{2,1,0:T(8,128)S(1)} collective-permute-done((f32[2,64,256]{2,1,0:T(8,128)S(1)}, f32[2,64,256]{2,1,0:T(8,128)S(1)}, u32[]{:S(2)}, u32[]{:S(2)}) %collective-permute-start) | collective-permute-done | bytes 131104 | tf_op jit(solution)/shard_map/ppermute | solution.py:36
  9.7 1.3 %collective-permute-start.1 = (f32[2,64,256]{2,1,0:T(8,128)S(1)}, f32[2,64,256]{2,1,0:T(8,128)S(1)}, u32[]{:S(2)}, u32[]{:S(2)}) collective-permute-start(f32[2,64,256]{2,1,0:T(8,128)S(1)} %shard_map.70), channel_id=1, source_target_pairs={{0,16},{1,17},{2,18},{3,19},{4,20},{5,21},{6,22},{7,23},{8,24},{9,... | collective-permute-start | bytes 393224 | tf_op jit(solution)/shard_map/ppermute | solution.py:36
  10.9 1.5 %collective-permute-done.3.first = f32[2,128,128]{2,1,0:T(8,128)S(1)} collective-permute-done((f32[2,128,128]{2,1,0:T(8,128)S(1)}, f32[2,128,128]{2,1,0:T(8,128)S(1)}, u32[]{:S(2)}, u32[]{:S(2)}) %collective-permute-start.3) | collective-permute-done | bytes 131104 | tf_op jit(solution)/shard_map/ppermute | solution.py:36
  12.5 1.3 %collective-permute-start.4 = (f32[2,128,128]{2,1,0:T(8,128)S(1)}, f32[2,128,128]{2,1,0:T(8,128)S(1)}, u32[]{:S(2)}, u32[]{:S(2)}) collective-permute-start(f32[2,128,128]{2,1,0:T(8,128)S(1)} %shard_map.73), channel_id=1, source_target_pairs={{0,16},{1,17},{2,18},{3,19},{4,20},{5,21},{6,22},{7,23},{8,24},{9,... | collective-permute-start | bytes 393224 | tf_op jit(solution)/shard_map/ppermute | solution.py:36
  13.7 0.0 collective-permute-done.6.partner
  13.7 0.2 shard_map.75
  14.0 2.4 %collective-permute-start.7 = (f32[136,128]{1,0:T(8,128)S(1)}, f32[136,128]{1,0:T(8,128)S(1)}, u32[]{:S(2)}, u32[]{:S(2)}) collective-permute-start(f32[136,128]{1,0:T(8,128)S(1)} %get-tuple-element.29.own), channel_id=1, source_target_pairs={{0,4},{1,5},{2,6},{3,7},{4,0},{5,1},{6,2},{7,3},{8,12},{9,13},{10,... | collective-permute-start | bytes 208904 | tf_op jit(solution)/shard_map/ppermute | solution.py:36
  16.4 0.1 collective-permute-start.8
  16.4 6.3 %collective-permute-done.8.partner = f32[128,128]{1,0:T(8,128)S(1)} collective-permute-done((f32[128,128]{1,0:T(8,128)S(1)}, f32[128,128]{1,0:T(8,128)S(1)}, u32[]{:S(2)}, u32[]{:S(2)}) %collective-permute-start.8) | collective-permute-done | bytes 65568 | tf_op jit(solution)/shard_map/ppermute | solution.py:36
  22.8 0.2 shard_map.78
  22.9 0.2 collective-permute-start.10
  23.2 0.0 collective-permute-done.7.partner
  23.2 0.2 shard_map.79
  23.3 1.2 %collective-permute-start.9 = (f32[64,128]{1,0:T(8,128)S(1)}, f32[64,128]{1,0:T(8,128)S(1)}, u32[]{:S(2)}, u32[]{:S(2)}) collective-permute-start(f32[64,128]{1,0:T(8,128)S(1)} %get-tuple-element.33), channel_id=1, source_target_pairs={{0,8},{1,9},{2,10},{3,11},{4,12},{5,13},{6,14},{7,15},{8,0},{9,1},... | collective-permute-start | bytes 98312 | tf_op jit(solution)/shard_map/ppermute | solution.py:36
  24.6 1.2 %collective-permute-start.11 = (f32[64,128]{1,0:T(8,128)S(1)}, f32[64,128]{1,0:T(8,128)S(1)}, u32[]{:S(2)}, u32[]{:S(2)}) collective-permute-start(f32[64,128]{1,0:T(8,128)S(1)} %get-tuple-element.35), channel_id=1, source_target_pairs={{0,24},{1,25},{2,26},{3,27},{4,28},{5,29},{6,30},{7,31},{8,16},{9,... | collective-permute-start | bytes 98312 | tf_op jit(solution)/shard_map/ppermute | solution.py:36
  25.8 0.0 collective-permute-done.1.second
  25.9 0.0 collective-permute-done.4.second
  25.9 1.2 %shard_map.77 = (f32[256,256]{1,0:T(8,128)S(1)}, f32[256,256]{1,0:T(8,128)S(1)}) custom-call(f32[7,4,64,128]{3,2,1,0:T(8,128)S(1)} %copy-done, f32[2,128,128]{2,1,0:T(8,128)S(1)} %collective-permute-done.3.first, f32[2,128,128]{2,1,0:T(8,128)S(1)} %collective-permute-done.4.second, f32[4,64,256]{2,1,0:T(8,128)S(1)} %shard_map.71.basis, ...), custom_call_target="tpu_custom_call" | custom-call | flops 16777216 | bytes 524288 | tf_op jit(solution)/shard_map/pallas_call | solution.py:97
  27.1 0.0 collective-permute-done.10.refs_2_
  27.1 0.0 collective-permute-done.9.refs_1_
  27.1 1.1 %collective-permute-done.11.refs_3_ = f32[64,128]{1,0:T(8,128)S(1)} collective-permute-done((f32[64,128]{1,0:T(8,128)S(1)}, f32[64,128]{1,0:T(8,128)S(1)}, u32[]{:S(2)}, u32[]{:S(2)}) %collective-permute-start.11) | collective-permute-done | bytes 32800 | tf_op jit(solution)/shard_map/ppermute | solution.py:36
  28.2 0.2 shard_map.82
  28.5 1.3 %collective-permute-start.14 = (f32[64,128]{1,0:T(8,128)S(1)}, f32[64,128]{1,0:T(8,128)S(1)}, u32[]{:S(2)}, u32[]{:S(2)}) collective-permute-start(f32[64,128]{1,0:T(8,128)S(1)} %get-tuple-element.40), channel_id=1, source_target_pairs={{0,24},{1,25},{2,26},{3,27},{4,28},{5,29},{6,30},{7,31},{8,16},{9,... | collective-permute-start | bytes 98312 | tf_op jit(solution)/shard_map/ppermute | solution.py:36
  29.8 1.5 %collective-permute-start.15 = (f32[64,128]{1,0:T(8,128)S(1)}, f32[64,128]{1,0:T(8,128)S(1)}, u32[]{:S(2)}, u32[]{:S(2)}) collective-permute-start(f32[64,128]{1,0:T(8,128)S(1)} %get-tuple-element.41), channel_id=1, source_target_pairs={{0,8},{1,9},{2,10},{3,11},{4,12},{5,13},{6,14},{7,15},{8,0},{9,1},... | collective-permute-start | bytes 98312 | tf_op jit(solution)/shard_map/ppermute | solution.py:36
  31.3 0.0 collective-permute-start.16
  31.3 0.9 %collective-permute-done.14.refs_0_ = f32[64,128]{1,0:T(8,128)S(1)} collective-permute-done((f32[64,128]{1,0:T(8,128)S(1)}, f32[64,128]{1,0:T(8,128)S(1)}, u32[]{:S(2)}, u32[]{:S(2)}) %collective-permute-start.14) | collective-permute-done | bytes 32800 | tf_op jit(solution)/shard_map/ppermute | solution.py:36
  32.2 0.7 %collective-permute-done.15.refs_1_ = f32[64,128]{1,0:T(8,128)S(1)} collective-permute-done((f32[64,128]{1,0:T(8,128)S(1)}, f32[64,128]{1,0:T(8,128)S(1)}, u32[]{:S(2)}, u32[]{:S(2)}) %collective-permute-start.15) | collective-permute-done | bytes 32800 | tf_op jit(solution)/shard_map/ppermute | solution.py:36
  32.9 1.1 %collective-permute-done.16.refs_2_ = f32[64,128]{1,0:T(8,128)S(1)} collective-permute-done((f32[64,128]{1,0:T(8,128)S(1)}, f32[64,128]{1,0:T(8,128)S(1)}, u32[]{:S(2)}, u32[]{:S(2)}) %collective-permute-start.16) | collective-permute-done | bytes 32800 | tf_op jit(solution)/shard_map/ppermute | solution.py:36
  34.0 0.3 shard_map.84
  34.3 0.1 collective-permute-start.17
  34.4 0.2 shard_map.83
  34.6 2.4 %collective-permute-start.13 = (f32[1,64,128]{2,1,0:T(8,128)S(1)}, f32[1,64,128]{2,1,0:T(8,128)S(1)}, u32[]{:S(2)}, u32[]{:S(2)}) collective-permute-start(f32[1,64,128]{2,1,0:T(8,128)S(1)} %get-tuple-element.39), channel_id=1, source_target_pairs={{0,4},{1,5},{2,6},{3,7},{4,0},{5,1},{6,2},{7,3},{8,12},{9,13},{10,... | collective-permute-start | bytes 98312 | tf_op jit(solution)/shard_map/ppermute | solution.py:36
  37.0 3.1 %collective-permute-done.13.refs_1_ = f32[1,64,128]{2,1,0:T(8,128)S(1)} collective-permute-done((f32[1,64,128]{2,1,0:T(8,128)S(1)}, f32[1,64,128]{2,1,0:T(8,128)S(1)}, u32[]{:S(2)}, u32[]{:S(2)}) %collective-permute-start.13) | collective-permute-done | bytes 32800 | tf_op jit(solution)/shard_map/ppermute | solution.py:36
  40.2 0.0 collective-permute-done.17.refs_3_
  40.2 0.3 shard_map.85
  40.5 2.0 %collective-permute-start.18 = (f32[4,64,128]{2,1,0:T(8,128)S(1)}, f32[4,64,128]{2,1,0:T(8,128)S(1)}, u32[]{:S(2)}, u32[]{:S(2)}) collective-permute-start(f32[4,64,128]{2,1,0:T(8,128)S(1)} %get-tuple-element.46), channel_id=1, source_target_pairs={{0,2},{1,3},{2,0},{3,1},{4,6},{5,7},{6,4},{7,5},{8,10},{9,11},{10,... | collective-permute-start | bytes 393224 | tf_op jit(solution)/shard_map/ppermute | solution.py:36
  42.5 8.3 %collective-permute-start.2 = (f32[4,64,256]{2,1,0:T(8,128)S(1)}, f32[4,64,256]{2,1,0:T(8,128)S(1)}, u32[]{:S(2)}, u32[]{:S(2)}) collective-permute-start(f32[4,64,256]{2,1,0:T(8,128)S(1)} %shard_map.71.basis), channel_id=1, source_target_pairs={{0,0},{1,4},{2,2},{3,6},{4,1},{5,5},{6,3},{7,7},{8,8},{9,12},{10,1... | collective-permute-start | bytes 786440 | tf_op jit(solution)/shard_map/ppermute | solution.py:36
  50.8 0.2 shard_map.80
  51.0 1.9 %collective-permute-start.12 = (f32[4,64,128]{2,1,0:T(8,128)S(1)}, f32[4,64,128]{2,1,0:T(8,128)S(1)}, u32[]{:S(2)}, u32[]{:S(2)}) collective-permute-start(f32[4,64,128]{2,1,0:T(8,128)S(1)} %shard_map.80), channel_id=1, source_target_pairs={{0,0},{1,4},{2,2},{3,6},{4,1},{5,5},{6,3},{7,7},{8,8},{9,12},{10,1... | collective-permute-start | bytes 393224 | tf_op jit(solution)/shard_map/ppermute | solution.py:36
  53.0 0.0 collective-permute-done.18.arrived
  53.0 0.3 shard_map.86
  53.3 0.1 collective-permute-start.19
  53.4 6.7 %collective-permute-done.12.coeffs = f32[4,64,128]{2,1,0:T(8,128)S(1)} collective-permute-done((f32[4,64,128]{2,1,0:T(8,128)S(1)}, f32[4,64,128]{2,1,0:T(8,128)S(1)}, u32[]{:S(2)}, u32[]{:S(2)}) %collective-permute-start.12) | collective-permute-done | bytes 131104 | tf_op jit(solution)/shard_map/ppermute | solution.py:36
  60.1 0.0 collective-permute-done.2.basis
  60.1 1.1 %shard_map.81 = f32[1024,128]{1,0:T(8,128)} custom-call(f32[4,64,256]{2,1,0:T(8,128)S(1)} %collective-permute-done.2.basis, f32[4,64,128]{2,1,0:T(8,128)S(1)} %collective-permute-done.12.coeffs), custom_call_target="tpu_custom_call" | custom-call | flops 16777216 | bytes 524288 | tf_op jit(solution)/shard_map/pallas_call | solution.py:97
  61.3 0.0 collective-permute-done.19.arrived
  61.3 1.5 %shard_map.87 = f32[1024,128]{1,0:T(8,128)} custom-call(f32[4,64,128]{2,1,0:T(8,128)S(1)} %get-tuple-element.47.kept, f32[4,64,128]{2,1,0:T(8,128)S(1)} %collective-permute-done.19.arrived, f32[7,4,64,128]{3,2,1,0:T(8,128)S(1)} %copy-done, f32[4,64,256]{2,1,0:T(8,128)S(1)} %get-tuple-element.49.basis), custom_call_target="tpu_custom_call" | custom-call | flops 16777216 | bytes 524288 | tf_op jit(solution)/shard_map/pallas_call | solution.py:97
  (6 shorter events, 0.1 us)
Async XLA Ops:
  0.6 5.2 %copy-start = (f32[7,4,64,128]{3,2,1,0:T(8,128)S(1)}, f32[7,4,64,128]{3,2,1,0:T(8,128)}, u32[]{:S(2)}) copy-start(f32[7,4,64,128]{3,2,1,0:T(8,128)} %transfer.23) | copy-start | bytes 2752516
  2.9 3.0 %collective-permute-start.5 = (f32[264,128]{1,0:T(8,128)S(1)}, f32[264,128]{1,0:T(8,128)S(1)}, u32[]{:S(2)}, u32[]{:S(2)}) collective-permute-start(f32[264,128]{1,0:T(8,128)S(1)} %get-tuple-element.28.own), channel_id=1, source_target_pairs={{0,1},{1,0},{2,3},{3,2},{4,5},{5,4},{6,7},{7,6},{8,9},{9,8},{10,11... | collective-permute-start | bytes 405512 | tf_op jit(solution)/shard_map/ppermute | solution.py:36
  3.1 6.6 %collective-permute-start = (f32[2,64,256]{2,1,0:T(8,128)S(1)}, f32[2,64,256]{2,1,0:T(8,128)S(1)}, u32[]{:S(2)}, u32[]{:S(2)}) collective-permute-start(f32[2,64,256]{2,1,0:T(8,128)S(1)} %shard_map.69), channel_id=1, source_target_pairs={{0,8},{1,9},{2,10},{3,11},{4,12},{5,13},{6,14},{7,15},{8,0},{9,1},... | collective-permute-start | bytes 393224 | tf_op jit(solution)/shard_map/ppermute | solution.py:36
  5.8 6.6 %collective-permute-start.3 = (f32[2,128,128]{2,1,0:T(8,128)S(1)}, f32[2,128,128]{2,1,0:T(8,128)S(1)}, u32[]{:S(2)}, u32[]{:S(2)}) collective-permute-start(f32[2,128,128]{2,1,0:T(8,128)S(1)} %shard_map.72), channel_id=1, source_target_pairs={{0,8},{1,9},{2,10},{3,11},{4,12},{5,13},{6,14},{7,15},{8,0},{9,1},... | collective-permute-start | bytes 393224 | tf_op jit(solution)/shard_map/ppermute | solution.py:36
  6.2 7.6 %collective-permute-start.6 = (f32[264,128]{1,0:T(8,128)S(1)}, f32[264,128]{1,0:T(8,128)S(1)}, u32[]{:S(2)}, u32[]{:S(2)}) collective-permute-start(f32[264,128]{1,0:T(8,128)S(1)} %shard_map.74.own), channel_id=1, source_target_pairs={{0,2},{1,3},{2,0},{3,1},{4,6},{5,7},{6,4},{7,5},{8,10},{9,11},{10,... | collective-permute-start | bytes 405512 | tf_op jit(solution)/shard_map/ppermute | solution.py:36
  9.7 16.1 %collective-permute-start.1 = (f32[2,64,256]{2,1,0:T(8,128)S(1)}, f32[2,64,256]{2,1,0:T(8,128)S(1)}, u32[]{:S(2)}, u32[]{:S(2)}) collective-permute-start(f32[2,64,256]{2,1,0:T(8,128)S(1)} %shard_map.70), channel_id=1, source_target_pairs={{0,16},{1,17},{2,18},{3,19},{4,20},{5,21},{6,22},{7,23},{8,24},{9,... | collective-permute-start | bytes 393224 | tf_op jit(solution)/shard_map/ppermute | solution.py:36
  12.5 13.4 %collective-permute-start.4 = (f32[2,128,128]{2,1,0:T(8,128)S(1)}, f32[2,128,128]{2,1,0:T(8,128)S(1)}, u32[]{:S(2)}, u32[]{:S(2)}) collective-permute-start(f32[2,128,128]{2,1,0:T(8,128)S(1)} %shard_map.73), channel_id=1, source_target_pairs={{0,16},{1,17},{2,18},{3,19},{4,20},{5,21},{6,22},{7,23},{8,24},{9,... | collective-permute-start | bytes 393224 | tf_op jit(solution)/shard_map/ppermute | solution.py:36
  14.0 9.2 %collective-permute-start.7 = (f32[136,128]{1,0:T(8,128)S(1)}, f32[136,128]{1,0:T(8,128)S(1)}, u32[]{:S(2)}, u32[]{:S(2)}) collective-permute-start(f32[136,128]{1,0:T(8,128)S(1)} %get-tuple-element.29.own), channel_id=1, source_target_pairs={{0,4},{1,5},{2,6},{3,7},{4,0},{5,1},{6,2},{7,3},{8,12},{9,13},{10,... | collective-permute-start | bytes 208904 | tf_op jit(solution)/shard_map/ppermute | solution.py:36
  16.4 6.4 %collective-permute-start.8 = (f32[128,128]{1,0:T(8,128)S(1)}, f32[128,128]{1,0:T(8,128)S(1)}, u32[]{:S(2)}, u32[]{:S(2)}) collective-permute-start(f32[128,128]{1,0:T(8,128)S(1)} %get-tuple-element.31.own), channel_id=1, source_target_pairs={{0,4},{1,5},{2,6},{3,7},{4,0},{5,1},{6,2},{7,3},{8,12},{9,13},{10,... | collective-permute-start | bytes 196616 | tf_op jit(solution)/shard_map/ppermute | solution.py:36
  22.9 4.1 %collective-permute-start.10 = (f32[64,128]{1,0:T(8,128)S(1)}, f32[64,128]{1,0:T(8,128)S(1)}, u32[]{:S(2)}, u32[]{:S(2)}) collective-permute-start(f32[64,128]{1,0:T(8,128)S(1)} %get-tuple-element.34), channel_id=1, source_target_pairs={{0,16},{1,17},{2,18},{3,19},{4,20},{5,21},{6,22},{7,23},{8,24},{9,... | collective-permute-start | bytes 98312 | tf_op jit(solution)/shard_map/ppermute | solution.py:36
  23.3 3.7 %collective-permute-start.9 = (f32[64,128]{1,0:T(8,128)S(1)}, f32[64,128]{1,0:T(8,128)S(1)}, u32[]{:S(2)}, u32[]{:S(2)}) collective-permute-start(f32[64,128]{1,0:T(8,128)S(1)} %get-tuple-element.33), channel_id=1, source_target_pairs={{0,8},{1,9},{2,10},{3,11},{4,12},{5,13},{6,14},{7,15},{8,0},{9,1},... | collective-permute-start | bytes 98312 | tf_op jit(solution)/shard_map/ppermute | solution.py:36
  24.6 3.7 %collective-permute-start.11 = (f32[64,128]{1,0:T(8,128)S(1)}, f32[64,128]{1,0:T(8,128)S(1)}, u32[]{:S(2)}, u32[]{:S(2)}) collective-permute-start(f32[64,128]{1,0:T(8,128)S(1)} %get-tuple-element.35), channel_id=1, source_target_pairs={{0,24},{1,25},{2,26},{3,27},{4,28},{5,29},{6,30},{7,31},{8,16},{9,... | collective-permute-start | bytes 98312 | tf_op jit(solution)/shard_map/ppermute | solution.py:36
  28.5 3.7 %collective-permute-start.14 = (f32[64,128]{1,0:T(8,128)S(1)}, f32[64,128]{1,0:T(8,128)S(1)}, u32[]{:S(2)}, u32[]{:S(2)}) collective-permute-start(f32[64,128]{1,0:T(8,128)S(1)} %get-tuple-element.40), channel_id=1, source_target_pairs={{0,24},{1,25},{2,26},{3,27},{4,28},{5,29},{6,30},{7,31},{8,16},{9,... | collective-permute-start | bytes 98312 | tf_op jit(solution)/shard_map/ppermute | solution.py:36
  29.8 3.1 %collective-permute-start.15 = (f32[64,128]{1,0:T(8,128)S(1)}, f32[64,128]{1,0:T(8,128)S(1)}, u32[]{:S(2)}, u32[]{:S(2)}) collective-permute-start(f32[64,128]{1,0:T(8,128)S(1)} %get-tuple-element.41), channel_id=1, source_target_pairs={{0,8},{1,9},{2,10},{3,11},{4,12},{5,13},{6,14},{7,15},{8,0},{9,1},... | collective-permute-start | bytes 98312 | tf_op jit(solution)/shard_map/ppermute | solution.py:36
  31.3 2.8 %collective-permute-start.16 = (f32[64,128]{1,0:T(8,128)S(1)}, f32[64,128]{1,0:T(8,128)S(1)}, u32[]{:S(2)}, u32[]{:S(2)}) collective-permute-start(f32[64,128]{1,0:T(8,128)S(1)} %get-tuple-element.42), channel_id=1, source_target_pairs={{0,16},{1,17},{2,18},{3,19},{4,20},{5,21},{6,22},{7,23},{8,24},{9,... | collective-permute-start | bytes 98312 | tf_op jit(solution)/shard_map/ppermute | solution.py:36
  34.3 5.8 %collective-permute-start.17 = (f32[3,64,128]{2,1,0:T(8,128)S(1)}, f32[3,64,128]{2,1,0:T(8,128)S(1)}, u32[]{:S(2)}, u32[]{:S(2)}) collective-permute-start(f32[3,64,128]{2,1,0:T(8,128)S(1)} %get-tuple-element.44), channel_id=1, source_target_pairs={{0,4},{1,5},{2,6},{3,7},{4,0},{5,1},{6,2},{7,3},{8,12},{9,13},{10,... | collective-permute-start | bytes 294920 | tf_op jit(solution)/shard_map/ppermute | solution.py:36
  34.6 5.5 %collective-permute-start.13 = (f32[1,64,128]{2,1,0:T(8,128)S(1)}, f32[1,64,128]{2,1,0:T(8,128)S(1)}, u32[]{:S(2)}, u32[]{:S(2)}) collective-permute-start(f32[1,64,128]{2,1,0:T(8,128)S(1)} %get-tuple-element.39), channel_id=1, source_target_pairs={{0,4},{1,5},{2,6},{3,7},{4,0},{5,1},{6,2},{7,3},{8,12},{9,13},{10,... | collective-permute-start | bytes 98312 | tf_op jit(solution)/shard_map/ppermute | solution.py:36
  40.5 12.5 %collective-permute-start.18 = (f32[4,64,128]{2,1,0:T(8,128)S(1)}, f32[4,64,128]{2,1,0:T(8,128)S(1)}, u32[]{:S(2)}, u32[]{:S(2)}) collective-permute-start(f32[4,64,128]{2,1,0:T(8,128)S(1)} %get-tuple-element.46), channel_id=1, source_target_pairs={{0,2},{1,3},{2,0},{3,1},{4,6},{5,7},{6,4},{7,5},{8,10},{9,11},{10,... | collective-permute-start | bytes 393224 | tf_op jit(solution)/shard_map/ppermute | solution.py:36
  42.5 17.7 %collective-permute-start.2 = (f32[4,64,256]{2,1,0:T(8,128)S(1)}, f32[4,64,256]{2,1,0:T(8,128)S(1)}, u32[]{:S(2)}, u32[]{:S(2)}) collective-permute-start(f32[4,64,256]{2,1,0:T(8,128)S(1)} %shard_map.71.basis), channel_id=1, source_target_pairs={{0,0},{1,4},{2,2},{3,6},{4,1},{5,5},{6,3},{7,7},{8,8},{9,12},{10,1... | collective-permute-start | bytes 786440 | tf_op jit(solution)/shard_map/ppermute | solution.py:36
  51.0 9.1 %collective-permute-start.12 = (f32[4,64,128]{2,1,0:T(8,128)S(1)}, f32[4,64,128]{2,1,0:T(8,128)S(1)}, u32[]{:S(2)}, u32[]{:S(2)}) collective-permute-start(f32[4,64,128]{2,1,0:T(8,128)S(1)} %shard_map.80), channel_id=1, source_target_pairs={{0,0},{1,4},{2,2},{3,6},{4,1},{5,5},{6,3},{7,7},{8,8},{9,12},{10,1... | collective-permute-start | bytes 393224 | tf_op jit(solution)/shard_map/ppermute | solution.py:36
  53.3 8.0 %collective-permute-start.19 = (f32[4,64,128]{2,1,0:T(8,128)S(1)}, f32[4,64,128]{2,1,0:T(8,128)S(1)}, u32[]{:S(2)}, u32[]{:S(2)}) collective-permute-start(f32[4,64,128]{2,1,0:T(8,128)S(1)} %get-tuple-element.48), channel_id=1, source_target_pairs={{0,1},{1,0},{2,3},{3,2},{4,5},{5,4},{6,7},{7,6},{8,9},{9,8},{10,11... | collective-permute-start | bytes 393224 | tf_op jit(solution)/shard_map/ppermute | solution.py:36

commit v11 on v10

--- a/solution.py
+++ b/solution.py
@@ -92,8 +92,10 @@
     return dot(ah, bh) + (dot(ah, bl) + dot(al, bh))
 
 
-def call(kernel, outs, operands, specs=None, out_specs=None, scratch=(), flops=1 << 24):
-    shapes = [jax.ShapeDtypeStruct(s, jnp.float32) for s in outs]
+def call(
+    kernel, outs, operands, specs=None, out_specs=None, scratch=(), flops=1 << 24, kind=jnp.float32
+):
+    shapes = [jax.ShapeDtypeStruct(s, kind) for s in outs]
     return pl.pallas_call(
         kernel,
         out_shape=shapes,
@@ -103,10 +105,6 @@
         compiler_params=pltpu.CompilerParams(vmem_limit_bytes=8 << 20),
         cost_estimate=pl.CostEstimate(flops=flops, bytes_accessed=1 << 19, transcendentals=0),
     )(*operands)
-
-
-def pairs(bit):
-    return [(s, s | 1 << bit) for s in range(SLOTS) if not s >> bit & 1]
 
 
 def store(out, nodes, weights):
@@ -139,26 +137,26 @@
         copies[-1].start()
         return copies[-1]
 
+    first = fetch(transfer_in.at[pl.ds(0, SLOT_BITS)], transfer)
     slots = []
     for s in range(SLOTS):
         rows = pl.ds(s * leaf, leaf)
         slots.append(
             (fetch(basis_in.at[s], basis.at[s]), fetch(vectors_in.at[rows], vectors.at[rows]))
         )
-    first = fetch(transfer_in.at[pl.ds(0, SLOT_BITS)], transfer)
     weights = fetch(diagonal_in, diagonal)
     later = fetch(target_in, target)
+    first.wait()
+    rank = basis.shape[1]
+    blocks, sources = compose(transfer, list(range(SLOT_BITS)), rank)
+    levels = jnp.concatenate(blocks, axis=0)
     c = []
     for s in range(SLOTS):
         for copy in slots[s]:
             copy.wait()
         c.append(product(basis[s], vectors[s * leaf : (s + 1) * leaf], NN))
-    first.wait()
-    for level in range(SLOT_BITS):
-        for low, high in pairs(level):
-            both = jnp.concatenate([c[low], c[high]], axis=0)
-            c[low] = product(transfer[level, low], both, NN)
-            c[high] = product(transfer[level, high], both, NN)
+    out_rows = product(levels, jnp.concatenate([c[s] for s in sources[0]], axis=0), NN)
+    c = [out_rows[s * rank : (s + 1) * rank] for s in range(SLOTS)]
     weights.wait()
     store(out, c, diagonal[...])
     later.wait()
@@ -246,28 +244,32 @@
     second_step(lambda s: tops_of(transfer, levels, s), first, out)
 
 
-def fold_kernel(levels, transfer, first, second, basis, weights, wide, middle, tops, columns):
-    rank = basis.shape[1]
-
-    def write(s, block):
-        for j in range(SLOT_BITS):
-            tops[j, s] = block[j * rank : (j + 1) * rank]
-
-    settle(lambda s: tops_of(transfer, levels, s), first, second, write)
-    blocks = [tops[0, s] for s in range(SLOTS)]
-    high = 1 << (SLOT_BITS - 1)
-    sources = [[s & ~high, s | high] for s in range(SLOTS)]
+def compose(levels, bits, rank):
+    blocks = [levels[0, s] for s in range(SLOTS)]
+    sources = [[s & ~(1 << bits[0]), s | 1 << bits[0]] for s in range(SLOTS)]
     for j in range(1, SLOT_BITS):
-        bit = 1 << (SLOT_BITS - 1 - j)
+        bit = 1 << bits[j]
         old, old_sources = blocks, sources
         blocks, sources = [], []
         for s in range(SLOTS):
             halves = [
-                product(tops[j, s][:, e * rank : (e + 1) * rank], old[q], NN)
+                product(levels[j, s][:, e * rank : (e + 1) * rank], old[q], NN)
                 for e, q in enumerate((s & ~bit, s | bit))
             ]
             blocks.append(jnp.concatenate(halves, axis=1))
             sources.append(old_sources[s & ~bit] + old_sources[s | bit])
+    return blocks, sources
+
+
+def fold_kernel(levels, transfer, first, second, basis, weights, wide, middle, tops, columns):
+    rank = basis.shape[1]
+
+    def write(s, block):
+        for j in range(SLOT_BITS):
+            tops[j, s] = block[j * rank : (j + 1) * rank]
+
+    settle(lambda s: tops_of(transfer, levels, s), first, second, write)
+    blocks, sources = compose(tops, list(reversed(range(SLOT_BITS))), rank)
     for s in range(SLOTS):
         for at, source in enumerate(sources[s]):
             columns[source, s * rank : (s + 1) * rank] = blocks[s][:, at * rank : (at + 1) * rank]
@@ -339,15 +341,25 @@
         copy.wait()
 
 
-def tail_kernel(kept, arrived, transfer, basis, out, buffer, sems):
-    b = [kept[s] + arrived[s] for s in range(SLOTS)]
-    rank = b[0].shape[0]
-    for level in reversed(range(SLOT_BITS)):
-        for low, high in pairs(level):
-            blocks = jnp.concatenate([transfer[level, low], transfer[level, high]], axis=0)
-            both = product(blocks, jnp.concatenate([b[low], b[high]], axis=0), TN)
-            b[low], b[high] = both[:rank], both[rank:]
-    write_rows(lambda s: product(basis[s], b[s], TN), out, buffer, sems)
+def source_fold_kernel(transfer, basis, high, low):
+    rank = basis.shape[1]
+    blocks, sources = compose(transfer, list(range(SLOT_BITS)), rank)
+    rows = jnp.concatenate(blocks, axis=0)
+    for at, source in enumerate(sources[0]):
+        through = product(rows[:, at * rank : (at + 1) * rank], basis[source], NN)
+        high[source], low[source] = split(through.T)
+
+
+def tail_kernel(kept, arrived, high, low, out, buffer, sems):
+    b = jnp.concatenate([kept[s] + arrived[s] for s in range(SLOTS)], axis=0)
+    bh, bl = split(b)
+
+    def dot(x, y):
+        return lax.dot_general(x, y, (NN, ((), ())), preferred_element_type=jnp.float32)
+
+    write_rows(
+        lambda s: dot(high[s], bh) + (dot(high[s], bl) + dot(low[s], bh)), out, buffer, sems
+    )
 
 
 def image_kernel(basis, coeffs, out, buffer, sems):
@@ -451,6 +463,12 @@
         scratch=rows_scratch,
     )
 
+    source_fold = call(
+        source_fold_kernel,
+        [(slots, leaf, slots * rank)] * 2,
+        [transfer, source_t],
+        kind=jnp.bfloat16,
+    )
     pieces = []
     for piece in BACK_PIECES:
         shape = (len(piece), rank, vecs)
@@ -473,7 +491,7 @@
     (adjoint,) = call(
         tail_kernel,
         [vectors.shape],
-        [kept, arrived, transfer, source_t],
+        [kept, arrived, *source_fold],
         out_specs=[ANY],
         scratch=rows_scratch,
     )

time: 62.9 us -> 62.7 us (level)
  waiting for transfers between devices: 23.6 us -> 22.7 us
  Pallas kernels: 8.68 us -> 9.36 us
    ppermute x20, waiting for transfers between devices: 23.6 us -> 22.7 us  [permute(): lax.ppermute(block, BOTH, [(d, route(d)) for d in range(self.devices)])]
    pallas_call x20 -> x21, Pallas kernels: 8.68 us -> 9.36 us  [call(): pl.pallas_call(kernel, out_shape=shapes, in_specs=specs or [VMEM] * len(o...]
  transfers between devices with their start and end apart: 20 -> 20, of which waited for: 9 -> 9; matrix products, arithmetic and copies ran while one was open for 0% -> 0% of each run, Pallas kernels for 6% -> 8%
where the time goes in v11:
time: 62.7 us; the launch traced here: 62.6 us
  starting transfers between devices  29.7 us (47%)
  waiting for transfers between devices  22.7 us (36%)
  Pallas kernels  9.36 us (15%)
  between operations  0.84 us (1%)
    ppermute x20, starting transfers between devices, permute(): lax.ppermute(block, BOTH, [(d, route(d)) for d in range(self.devices)])  29.7 us
    ppermute x20, waiting for transfers between devices, permute(): lax.ppermute(block, BOTH, [(d, route(d)) for d in range(self.devices)])  22.7 us
    pallas_call x21, Pallas kernels, call(): pl.pallas_call(kernel, out_shape=shapes, in_specs=specs or [VMEM] * len(o...  9.36 us
  transfers between devices with their start and end apart: 20, of which 9 were waited for; matrix products, arithmetic and copies ran while one was open for 0% of the time, Pallas kernels for 8%

profile of v11, /device:TPU:1, one launch (start us, length us, event | category | flops | bytes accessed | tf_op | source)
XLA Modules:
  0.0 62.6 jit_solution(10035900925049178153)
XLA Ops:
  0.6 0.0 copy-start
  0.6 2.4 %shard_map.68 = (f32[264,128]{1,0:T(8,128)S(1)}, f32[4,64,256]{2,1,0:T(8,128)S(1)}, f32[4,64,256]{2,1,0:T(8,128)S(1)}, f32[8,128]{1,0:T(8,128)S(1)}) custom-call(f32[1024,128]{1,0:T(8,128)} %vectors_in.1, f32[4,64,256]{2,1,0:T(8,128)} %bitcast.3, f32[7,4,64,128]{3,2,1,0:T(8,128)} %transfer.23, f32[4,64,256]{2,1,0:T(8,128)} %bitcast.4, f32[8,128]{1,0:T(8,128)} %bitcast.5), custom_call_target="tpu_custom_call" | custom-call | flops 16777216 | bytes 524288 | tf_op jit(solution)/shard_map/pallas_call | solution.py:99
  3.0 0.1 collective-permute-start.5
  3.1 2.7 %collective-permute-start = (f32[2,64,256]{2,1,0:T(8,128)S(1)}, f32[2,64,256]{2,1,0:T(8,128)S(1)}, u32[]{:S(2)}, u32[]{:S(2)}) collective-permute-start(f32[2,64,256]{2,1,0:T(8,128)S(1)} %shard_map.69), channel_id=1, source_target_pairs={{0,8},{1,9},{2,10},{3,11},{4,12},{5,13},{6,14},{7,15},{8,0},{9,1},... | collective-permute-start | bytes 393224 | tf_op jit(solution)/shard_map/ppermute | solution.py:36
  5.9 0.0 copy-done
  5.9 0.1 collective-permute-start.3
  6.0 0.0 collective-permute-done.5.partner
  6.0 0.2 shard_map.74.own
  6.3 1.5 %collective-permute-start.6 = (f32[264,128]{1,0:T(8,128)S(1)}, f32[264,128]{1,0:T(8,128)S(1)}, u32[]{:S(2)}, u32[]{:S(2)}) collective-permute-start(f32[264,128]{1,0:T(8,128)S(1)} %shard_map.74.own), channel_id=1, source_target_pairs={{0,2},{1,3},{2,0},{3,1},{4,6},{5,7},{6,4},{7,5},{8,10},{9,11},{10,... | collective-permute-start | bytes 405512 | tf_op jit(solution)/shard_map/ppermute | solution.py:36
  7.8 1.9 %collective-permute-done.first = f32[2,64,256]{2,1,0:T(8,128)S(1)} collective-permute-done((f32[2,64,256]{2,1,0:T(8,128)S(1)}, f32[2,64,256]{2,1,0:T(8,128)S(1)}, u32[]{:S(2)}, u32[]{:S(2)}) %collective-permute-start) | collective-permute-done | bytes 131104 | tf_op jit(solution)/shard_map/ppermute | solution.py:36
  9.7 1.3 %collective-permute-start.1 = (f32[2,64,256]{2,1,0:T(8,128)S(1)}, f32[2,64,256]{2,1,0:T(8,128)S(1)}, u32[]{:S(2)}, u32[]{:S(2)}) collective-permute-start(f32[2,64,256]{2,1,0:T(8,128)S(1)} %shard_map.70), channel_id=1, source_target_pairs={{0,16},{1,17},{2,18},{3,19},{4,20},{5,21},{6,22},{7,23},{8,24},{9,... | collective-permute-start | bytes 393224 | tf_op jit(solution)/shard_map/ppermute | solution.py:36
  11.0 1.5 %collective-permute-done.3.first = f32[2,128,128]{2,1,0:T(8,128)S(1)} collective-permute-done((f32[2,128,128]{2,1,0:T(8,128)S(1)}, f32[2,128,128]{2,1,0:T(8,128)S(1)}, u32[]{:S(2)}, u32[]{:S(2)}) %collective-permute-start.3) | collective-permute-done | bytes 131104 | tf_op jit(solution)/shard_map/ppermute | solution.py:36
  12.5 1.3 %collective-permute-start.4 = (f32[2,128,128]{2,1,0:T(8,128)S(1)}, f32[2,128,128]{2,1,0:T(8,128)S(1)}, u32[]{:S(2)}, u32[]{:S(2)}) collective-permute-start(f32[2,128,128]{2,1,0:T(8,128)S(1)} %shard_map.73), channel_id=1, source_target_pairs={{0,16},{1,17},{2,18},{3,19},{4,20},{5,21},{6,22},{7,23},{8,24},{9,... | collective-permute-start | bytes 393224 | tf_op jit(solution)/shard_map/ppermute | solution.py:36
  13.8 0.0 collective-permute-done.6.partner
  13.8 0.2 shard_map.75
  14.1 2.4 %collective-permute-start.7 = (f32[136,128]{1,0:T(8,128)S(1)}, f32[136,128]{1,0:T(8,128)S(1)}, u32[]{:S(2)}, u32[]{:S(2)}) collective-permute-start(f32[136,128]{1,0:T(8,128)S(1)} %get-tuple-element.31.own), channel_id=1, source_target_pairs={{0,4},{1,5},{2,6},{3,7},{4,0},{5,1},{6,2},{7,3},{8,12},{9,13},{10,... | collective-permute-start | bytes 208904 | tf_op jit(solution)/shard_map/ppermute | solution.py:36
  16.4 0.1 collective-permute-start.8
  16.5 6.3 %collective-permute-done.8.partner = f32[128,128]{1,0:T(8,128)S(1)} collective-permute-done((f32[128,128]{1,0:T(8,128)S(1)}, f32[128,128]{1,0:T(8,128)S(1)}, u32[]{:S(2)}, u32[]{:S(2)}) %collective-permute-start.8) | collective-permute-done | bytes 65568 | tf_op jit(solution)/shard_map/ppermute | solution.py:36
  22.8 0.2 shard_map.78
  23.0 0.2 collective-permute-start.10
  23.2 0.0 collective-permute-done.7.partner
  23.2 0.2 shard_map.79
  23.4 1.2 %collective-permute-start.9 = (f32[64,128]{1,0:T(8,128)S(1)}, f32[64,128]{1,0:T(8,128)S(1)}, u32[]{:S(2)}, u32[]{:S(2)}) collective-permute-start(f32[64,128]{1,0:T(8,128)S(1)} %get-tuple-element.35), channel_id=1, source_target_pairs={{0,8},{1,9},{2,10},{3,11},{4,12},{5,13},{6,14},{7,15},{8,0},{9,1},... | collective-permute-start | bytes 98312 | tf_op jit(solution)/shard_map/ppermute | solution.py:36
  24.7 1.2 %collective-permute-start.11 = (f32[64,128]{1,0:T(8,128)S(1)}, f32[64,128]{1,0:T(8,128)S(1)}, u32[]{:S(2)}, u32[]{:S(2)}) collective-permute-start(f32[64,128]{1,0:T(8,128)S(1)} %get-tuple-element.37), channel_id=1, source_target_pairs={{0,24},{1,25},{2,26},{3,27},{4,28},{5,29},{6,30},{7,31},{8,16},{9,... | collective-permute-start | bytes 98312 | tf_op jit(solution)/shard_map/ppermute | solution.py:36
  25.9 0.0 collective-permute-done.1.second
  25.9 0.0 collective-permute-done.4.second
  25.9 1.2 %shard_map.77 = (f32[256,256]{1,0:T(8,128)S(1)}, f32[256,256]{1,0:T(8,128)S(1)}) custom-call(f32[7,4,64,128]{3,2,1,0:T(8,128)S(1)} %copy-done, f32[2,128,128]{2,1,0:T(8,128)S(1)} %collective-permute-done.3.first, f32[2,128,128]{2,1,0:T(8,128)S(1)} %collective-permute-done.4.second, f32[4,64,256]{2,1,0:T(8,128)S(1)} %shard_map.71.basis, ...), custom_call_target="tpu_custom_call" | custom-call | flops 16777216 | bytes 524288 | tf_op jit(solution)/shard_map/pallas_call | solution.py:99
  27.2 0.0 collective-permute-done.10.refs_2_
  27.2 0.0 collective-permute-done.9.refs_1_
  27.2 1.1 %collective-permute-done.11.refs_3_ = f32[64,128]{1,0:T(8,128)S(1)} collective-permute-done((f32[64,128]{1,0:T(8,128)S(1)}, f32[64,128]{1,0:T(8,128)S(1)}, u32[]{:S(2)}, u32[]{:S(2)}) %collective-permute-start.11) | collective-permute-done | bytes 32800 | tf_op jit(solution)/shard_map/ppermute | solution.py:36
  28.3 0.2 shard_map.82
  28.6 1.3 %collective-permute-start.14 = (f32[64,128]{1,0:T(8,128)S(1)}, f32[64,128]{1,0:T(8,128)S(1)}, u32[]{:S(2)}, u32[]{:S(2)}) collective-permute-start(f32[64,128]{1,0:T(8,128)S(1)} %get-tuple-element.42), channel_id=1, source_target_pairs={{0,24},{1,25},{2,26},{3,27},{4,28},{5,29},{6,30},{7,31},{8,16},{9,... | collective-permute-start | bytes 98312 | tf_op jit(solution)/shard_map/ppermute | solution.py:36
  29.9 1.5 %collective-permute-start.15 = (f32[64,128]{1,0:T(8,128)S(1)}, f32[64,128]{1,0:T(8,128)S(1)}, u32[]{:S(2)}, u32[]{:S(2)}) collective-permute-start(f32[64,128]{1,0:T(8,128)S(1)} %get-tuple-element.43), channel_id=1, source_target_pairs={{0,8},{1,9},{2,10},{3,11},{4,12},{5,13},{6,14},{7,15},{8,0},{9,1},... | collective-permute-start | bytes 98312 | tf_op jit(solution)/shard_map/ppermute | solution.py:36
  31.3 0.0 collective-permute-start.16
  31.3 1.0 %collective-permute-done.14.refs_0_ = f32[64,128]{1,0:T(8,128)S(1)} collective-permute-done((f32[64,128]{1,0:T(8,128)S(1)}, f32[64,128]{1,0:T(8,128)S(1)}, u32[]{:S(2)}, u32[]{:S(2)}) %collective-permute-start.14) | collective-permute-done | bytes 32800 | tf_op jit(solution)/shard_map/ppermute | solution.py:36
  32.3 0.7 %collective-permute-done.15.refs_1_ = f32[64,128]{1,0:T(8,128)S(1)} collective-permute-done((f32[64,128]{1,0:T(8,128)S(1)}, f32[64,128]{1,0:T(8,128)S(1)}, u32[]{:S(2)}, u32[]{:S(2)}) %collective-permute-start.15) | collective-permute-done | bytes 32800 | tf_op jit(solution)/shard_map/ppermute | solution.py:36
  33.0 1.1 %collective-permute-done.16.refs_2_ = f32[64,128]{1,0:T(8,128)S(1)} collective-permute-done((f32[64,128]{1,0:T(8,128)S(1)}, f32[64,128]{1,0:T(8,128)S(1)}, u32[]{:S(2)}, u32[]{:S(2)}) %collective-permute-start.16) | collective-permute-done | bytes 32800 | tf_op jit(solution)/shard_map/ppermute | solution.py:36
  34.1 0.3 shard_map.84
  34.4 0.1 collective-permute-start.17
  34.5 0.2 shard_map.83
  34.7 2.4 %collective-permute-start.13 = (f32[1,64,128]{2,1,0:T(8,128)S(1)}, f32[1,64,128]{2,1,0:T(8,128)S(1)}, u32[]{:S(2)}, u32[]{:S(2)}) collective-permute-start(f32[1,64,128]{2,1,0:T(8,128)S(1)} %get-tuple-element.41), channel_id=1, source_target_pairs={{0,4},{1,5},{2,6},{3,7},{4,0},{5,1},{6,2},{7,3},{8,12},{9,13},{10,... | collective-permute-start | bytes 98312 | tf_op jit(solution)/shard_map/ppermute | solution.py:36
  37.1 3.1 %collective-permute-done.13.refs_1_ = f32[1,64,128]{2,1,0:T(8,128)S(1)} collective-permute-done((f32[1,64,128]{2,1,0:T(8,128)S(1)}, f32[1,64,128]{2,1,0:T(8,128)S(1)}, u32[]{:S(2)}, u32[]{:S(2)}) %collective-permute-start.13) | collective-permute-done | bytes 32800 | tf_op jit(solution)/shard_map/ppermute | solution.py:36
  40.2 0.0 collective-permute-done.17.refs_3_
  40.2 0.3 shard_map.85
  40.6 2.0 %collective-permute-start.18 = (f32[4,64,128]{2,1,0:T(8,128)S(1)}, f32[4,64,128]{2,1,0:T(8,128)S(1)}, u32[]{:S(2)}, u32[]{:S(2)}) collective-permute-start(f32[4,64,128]{2,1,0:T(8,128)S(1)} %get-tuple-element.48), channel_id=1, source_target_pairs={{0,2},{1,3},{2,0},{3,1},{4,6},{5,7},{6,4},{7,5},{8,10},{9,11},{10,... | collective-permute-start | bytes 393224 | tf_op jit(solution)/shard_map/ppermute | solution.py:36
  42.5 8.3 %collective-permute-start.2 = (f32[4,64,256]{2,1,0:T(8,128)S(1)}, f32[4,64,256]{2,1,0:T(8,128)S(1)}, u32[]{:S(2)}, u32[]{:S(2)}) collective-permute-start(f32[4,64,256]{2,1,0:T(8,128)S(1)} %shard_map.71.basis), channel_id=1, source_target_pairs={{0,0},{1,4},{2,2},{3,6},{4,1},{5,5},{6,3},{7,7},{8,8},{9,12},{10,1... | collective-permute-start | bytes 786440 | tf_op jit(solution)/shard_map/ppermute | solution.py:36
  50.9 0.2 shard_map.80
  51.1 1.9 %collective-permute-start.12 = (f32[4,64,128]{2,1,0:T(8,128)S(1)}, f32[4,64,128]{2,1,0:T(8,128)S(1)}, u32[]{:S(2)}, u32[]{:S(2)}) collective-permute-start(f32[4,64,128]{2,1,0:T(8,128)S(1)} %shard_map.80), channel_id=1, source_target_pairs={{0,0},{1,4},{2,2},{3,6},{4,1},{5,5},{6,3},{7,7},{8,8},{9,12},{10,1... | collective-permute-start | bytes 393224 | tf_op jit(solution)/shard_map/ppermute | solution.py:36
  53.0 0.0 collective-permute-done.18.arrived
  53.1 0.3 shard_map.86
  53.4 0.1 collective-permute-start.19
  53.4 0.8 %shard_map.87 = (bf16[4,256,256]{2,1,0:T(8,128)(2,1)S(1)}, bf16[4,256,256]{2,1,0:T(8,128)(2,1)S(1)}) custom-call(f32[7,4,64,128]{3,2,1,0:T(8,128)S(1)} %copy-done, f32[4,64,256]{2,1,0:T(8,128)S(1)} %get-tuple-element.51.basis), custom_call_target="tpu_custom_call" | custom-call | flops 16777216 | bytes 524288 | tf_op jit(solution)/shard_map/pallas_call | solution.py:99
  54.3 5.9 %collective-permute-done.12.coeffs = f32[4,64,128]{2,1,0:T(8,128)S(1)} collective-permute-done((f32[4,64,128]{2,1,0:T(8,128)S(1)}, f32[4,64,128]{2,1,0:T(8,128)S(1)}, u32[]{:S(2)}, u32[]{:S(2)}) %collective-permute-start.12) | collective-permute-done | bytes 131104 | tf_op jit(solution)/shard_map/ppermute | solution.py:36
  60.2 0.0 collective-permute-done.2.basis
  60.2 1.1 %shard_map.81 = f32[1024,128]{1,0:T(8,128)} custom-call(f32[4,64,256]{2,1,0:T(8,128)S(1)} %collective-permute-done.2.basis, f32[4,64,128]{2,1,0:T(8,128)S(1)} %collective-permute-done.12.coeffs), custom_call_target="tpu_custom_call" | custom-call | flops 16777216 | bytes 524288 | tf_op jit(solution)/shard_map/pallas_call | solution.py:99
  61.3 0.0 collective-permute-done.19.arrived
  61.3 1.3 %shard_map.88 = f32[1024,128]{1,0:T(8,128)} custom-call(f32[4,64,128]{2,1,0:T(8,128)S(1)} %get-tuple-element.49.kept, f32[4,64,128]{2,1,0:T(8,128)S(1)} %collective-permute-done.19.arrived, bf16[4,256,256]{2,1,0:T(8,128)(2,1)S(1)} %get-tuple-element.52.high, bf16[4,256,256]{2,1,0:T(8,128)(2,1)S(1)} %get-tuple-element.53.low), custom_call_target="tpu_custom_call" | custom-call | flops 16777216 | bytes 524288 | tf_op jit(solution)/shard_map/pallas_call | solution.py:99
  (6 shorter events, 0.1 us)
Async XLA Ops:
  0.6 5.2 %copy-start = (f32[7,4,64,128]{3,2,1,0:T(8,128)S(1)}, f32[7,4,64,128]{3,2,1,0:T(8,128)}, u32[]{:S(2)}) copy-start(f32[7,4,64,128]{3,2,1,0:T(8,128)} %transfer.23) | copy-start | bytes 2752516
  3.0 3.0 %collective-permute-start.5 = (f32[264,128]{1,0:T(8,128)S(1)}, f32[264,128]{1,0:T(8,128)S(1)}, u32[]{:S(2)}, u32[]{:S(2)}) collective-permute-start(f32[264,128]{1,0:T(8,128)S(1)} %get-tuple-element.30.own), channel_id=1, source_target_pairs={{0,1},{1,0},{2,3},{3,2},{4,5},{5,4},{6,7},{7,6},{8,9},{9,8},{10,11... | collective-permute-start | bytes 405512 | tf_op jit(solution)/shard_map/ppermute | solution.py:36
  3.1 6.6 %collective-permute-start = (f32[2,64,256]{2,1,0:T(8,128)S(1)}, f32[2,64,256]{2,1,0:T(8,128)S(1)}, u32[]{:S(2)}, u32[]{:S(2)}) collective-permute-start(f32[2,64,256]{2,1,0:T(8,128)S(1)} %shard_map.69), channel_id=1, source_target_pairs={{0,8},{1,9},{2,10},{3,11},{4,12},{5,13},{6,14},{7,15},{8,0},{9,1},... | collective-permute-start | bytes 393224 | tf_op jit(solution)/shard_map/ppermute | solution.py:36
  5.9 6.6 %collective-permute-start.3 = (f32[2,128,128]{2,1,0:T(8,128)S(1)}, f32[2,128,128]{2,1,0:T(8,128)S(1)}, u32[]{:S(2)}, u32[]{:S(2)}) collective-permute-start(f32[2,128,128]{2,1,0:T(8,128)S(1)} %shard_map.72), channel_id=1, source_target_pairs={{0,8},{1,9},{2,10},{3,11},{4,12},{5,13},{6,14},{7,15},{8,0},{9,1},... | collective-permute-start | bytes 393224 | tf_op jit(solution)/shard_map/ppermute | solution.py:36
  6.3 7.6 %collective-permute-start.6 = (f32[264,128]{1,0:T(8,128)S(1)}, f32[264,128]{1,0:T(8,128)S(1)}, u32[]{:S(2)}, u32[]{:S(2)}) collective-permute-start(f32[264,128]{1,0:T(8,128)S(1)} %shard_map.74.own), channel_id=1, source_target_pairs={{0,2},{1,3},{2,0},{3,1},{4,6},{5,7},{6,4},{7,5},{8,10},{9,11},{10,... | collective-permute-start | bytes 405512 | tf_op jit(solution)/shard_map/ppermute | solution.py:36
  9.7 16.1 %collective-permute-start.1 = (f32[2,64,256]{2,1,0:T(8,128)S(1)}, f32[2,64,256]{2,1,0:T(8,128)S(1)}, u32[]{:S(2)}, u32[]{:S(2)}) collective-permute-start(f32[2,64,256]{2,1,0:T(8,128)S(1)} %shard_map.70), channel_id=1, source_target_pairs={{0,16},{1,17},{2,18},{3,19},{4,20},{5,21},{6,22},{7,23},{8,24},{9,... | collective-permute-start | bytes 393224 | tf_op jit(solution)/shard_map/ppermute | solution.py:36
  12.5 13.4 %collective-permute-start.4 = (f32[2,128,128]{2,1,0:T(8,128)S(1)}, f32[2,128,128]{2,1,0:T(8,128)S(1)}, u32[]{:S(2)}, u32[]{:S(2)}) collective-permute-start(f32[2,128,128]{2,1,0:T(8,128)S(1)} %shard_map.73), channel_id=1, source_target_pairs={{0,16},{1,17},{2,18},{3,19},{4,20},{5,21},{6,22},{7,23},{8,24},{9,... | collective-permute-start | bytes 393224 | tf_op jit(solution)/shard_map/ppermute | solution.py:36
  14.1 9.2 %collective-permute-start.7 = (f32[136,128]{1,0:T(8,128)S(1)}, f32[136,128]{1,0:T(8,128)S(1)}, u32[]{:S(2)}, u32[]{:S(2)}) collective-permute-start(f32[136,128]{1,0:T(8,128)S(1)} %get-tuple-element.31.own), channel_id=1, source_target_pairs={{0,4},{1,5},{2,6},{3,7},{4,0},{5,1},{6,2},{7,3},{8,12},{9,13},{10,... | collective-permute-start | bytes 208904 | tf_op jit(solution)/shard_map/ppermute | solution.py:36
  16.4 6.4 %collective-permute-start.8 = (f32[128,128]{1,0:T(8,128)S(1)}, f32[128,128]{1,0:T(8,128)S(1)}, u32[]{:S(2)}, u32[]{:S(2)}) collective-permute-start(f32[128,128]{1,0:T(8,128)S(1)} %get-tuple-element.33.own), channel_id=1, source_target_pairs={{0,4},{1,5},{2,6},{3,7},{4,0},{5,1},{6,2},{7,3},{8,12},{9,13},{10,... | collective-permute-start | bytes 196616 | tf_op jit(solution)/shard_map/ppermute | solution.py:36
  23.0 4.1 %collective-permute-start.10 = (f32[64,128]{1,0:T(8,128)S(1)}, f32[64,128]{1,0:T(8,128)S(1)}, u32[]{:S(2)}, u32[]{:S(2)}) collective-permute-start(f32[64,128]{1,0:T(8,128)S(1)} %get-tuple-element.36), channel_id=1, source_target_pairs={{0,16},{1,17},{2,18},{3,19},{4,20},{5,21},{6,22},{7,23},{8,24},{9,... | collective-permute-start | bytes 98312 | tf_op jit(solution)/shard_map/ppermute | solution.py:36
  23.4 3.8 %collective-permute-start.9 = (f32[64,128]{1,0:T(8,128)S(1)}, f32[64,128]{1,0:T(8,128)S(1)}, u32[]{:S(2)}, u32[]{:S(2)}) collective-permute-start(f32[64,128]{1,0:T(8,128)S(1)} %get-tuple-element.35), channel_id=1, source_target_pairs={{0,8},{1,9},{2,10},{3,11},{4,12},{5,13},{6,14},{7,15},{8,0},{9,1},... | collective-permute-start | bytes 98312 | tf_op jit(solution)/shard_map/ppermute | solution.py:36
  24.7 3.7 %collective-permute-start.11 = (f32[64,128]{1,0:T(8,128)S(1)}, f32[64,128]{1,0:T(8,128)S(1)}, u32[]{:S(2)}, u32[]{:S(2)}) collective-permute-start(f32[64,128]{1,0:T(8,128)S(1)} %get-tuple-element.37), channel_id=1, source_target_pairs={{0,24},{1,25},{2,26},{3,27},{4,28},{5,29},{6,30},{7,31},{8,16},{9,... | collective-permute-start | bytes 98312 | tf_op jit(solution)/shard_map/ppermute | solution.py:36
  28.6 3.7 %collective-permute-start.14 = (f32[64,128]{1,0:T(8,128)S(1)}, f32[64,128]{1,0:T(8,128)S(1)}, u32[]{:S(2)}, u32[]{:S(2)}) collective-permute-start(f32[64,128]{1,0:T(8,128)S(1)} %get-tuple-element.42), channel_id=1, source_target_pairs={{0,24},{1,25},{2,26},{3,27},{4,28},{5,29},{6,30},{7,31},{8,16},{9,... | collective-permute-start | bytes 98312 | tf_op jit(solution)/shard_map/ppermute | solution.py:36
  29.9 3.1 %collective-permute-start.15 = (f32[64,128]{1,0:T(8,128)S(1)}, f32[64,128]{1,0:T(8,128)S(1)}, u32[]{:S(2)}, u32[]{:S(2)}) collective-permute-start(f32[64,128]{1,0:T(8,128)S(1)} %get-tuple-element.43), channel_id=1, source_target_pairs={{0,8},{1,9},{2,10},{3,11},{4,12},{5,13},{6,14},{7,15},{8,0},{9,1},... | collective-permute-start | bytes 98312 | tf_op jit(solution)/shard_map/ppermute | solution.py:36
  31.3 2.8 %collective-permute-start.16 = (f32[64,128]{1,0:T(8,128)S(1)}, f32[64,128]{1,0:T(8,128)S(1)}, u32[]{:S(2)}, u32[]{:S(2)}) collective-permute-start(f32[64,128]{1,0:T(8,128)S(1)} %get-tuple-element.44), channel_id=1, source_target_pairs={{0,16},{1,17},{2,18},{3,19},{4,20},{5,21},{6,22},{7,23},{8,24},{9,... | collective-permute-start | bytes 98312 | tf_op jit(solution)/shard_map/ppermute | solution.py:36
  34.4 5.8 %collective-permute-start.17 = (f32[3,64,128]{2,1,0:T(8,128)S(1)}, f32[3,64,128]{2,1,0:T(8,128)S(1)}, u32[]{:S(2)}, u32[]{:S(2)}) collective-permute-start(f32[3,64,128]{2,1,0:T(8,128)S(1)} %get-tuple-element.46), channel_id=1, source_target_pairs={{0,4},{1,5},{2,6},{3,7},{4,0},{5,1},{6,2},{7,3},{8,12},{9,13},{10,... | collective-permute-start | bytes 294920 | tf_op jit(solution)/shard_map/ppermute | solution.py:36
  34.7 5.5 %collective-permute-start.13 = (f32[1,64,128]{2,1,0:T(8,128)S(1)}, f32[1,64,128]{2,1,0:T(8,128)S(1)}, u32[]{:S(2)}, u32[]{:S(2)}) collective-permute-start(f32[1,64,128]{2,1,0:T(8,128)S(1)} %get-tuple-element.41), channel_id=1, source_target_pairs={{0,4},{1,5},{2,6},{3,7},{4,0},{5,1},{6,2},{7,3},{8,12},{9,13},{10,... | collective-permute-start | bytes 98312 | tf_op jit(solution)/shard_map/ppermute | solution.py:36
  40.6 12.5 %collective-permute-start.18 = (f32[4,64,128]{2,1,0:T(8,128)S(1)}, f32[4,64,128]{2,1,0:T(8,128)S(1)}, u32[]{:S(2)}, u32[]{:S(2)}) collective-permute-start(f32[4,64,128]{2,1,0:T(8,128)S(1)} %get-tuple-element.48), channel_id=1, source_target_pairs={{0,2},{1,3},{2,0},{3,1},{4,6},{5,7},{6,4},{7,5},{8,10},{9,11},{10,... | collective-permute-start | bytes 393224 | tf_op jit(solution)/shard_map/ppermute | solution.py:36
  42.5 17.6 %collective-permute-start.2 = (f32[4,64,256]{2,1,0:T(8,128)S(1)}, f32[4,64,256]{2,1,0:T(8,128)S(1)}, u32[]{:S(2)}, u32[]{:S(2)}) collective-permute-start(f32[4,64,256]{2,1,0:T(8,128)S(1)} %shard_map.71.basis), channel_id=1, source_target_pairs={{0,0},{1,4},{2,2},{3,6},{4,1},{5,5},{6,3},{7,7},{8,8},{9,12},{10,1... | collective-permute-start | bytes 786440 | tf_op jit(solution)/shard_map/ppermute | solution.py:36
  51.1 9.0 %collective-permute-start.12 = (f32[4,64,128]{2,1,0:T(8,128)S(1)}, f32[4,64,128]{2,1,0:T(8,128)S(1)}, u32[]{:S(2)}, u32[]{:S(2)}) collective-permute-start(f32[4,64,128]{2,1,0:T(8,128)S(1)} %shard_map.80), channel_id=1, source_target_pairs={{0,0},{1,4},{2,2},{3,6},{4,1},{5,5},{6,3},{7,7},{8,8},{9,12},{10,1... | collective-permute-start | bytes 393224 | tf_op jit(solution)/shard_map/ppermute | solution.py:36
  53.4 8.0 %collective-permute-start.19 = (f32[4,64,128]{2,1,0:T(8,128)S(1)}, f32[4,64,128]{2,1,0:T(8,128)S(1)}, u32[]{:S(2)}, u32[]{:S(2)}) collective-permute-start(f32[4,64,128]{2,1,0:T(8,128)S(1)} %get-tuple-element.50), channel_id=1, source_target_pairs={{0,1},{1,0},{2,3},{3,2},{4,5},{5,4},{6,7},{7,6},{8,9},{9,8},{10,11... | collective-permute-start | bytes 393224 | tf_op jit(solution)/shard_map/ppermute | solution.py:36

commit v12 on v11

--- a/solution.py
+++ b/solution.py
@@ -107,6 +107,10 @@
     )(*operands)
 
 
+def pairs(bit):
+    return [(s, s | 1 << bit) for s in range(SLOTS) if not s >> bit & 1]
+
+
 def store(out, nodes, weights):
     rank = nodes[0].shape[0]
     for at, node in enumerate(nodes):
@@ -119,11 +123,9 @@
     vectors_in,
     basis_in,
     transfer_in,
-    target_in,
     diagonal_in,
     out,
     basis,
-    target,
     diagonal,
     transfer,
     vectors,
@@ -137,29 +139,27 @@
         copies[-1].start()
         return copies[-1]
 
-    first = fetch(transfer_in.at[pl.ds(0, SLOT_BITS)], transfer)
     slots = []
     for s in range(SLOTS):
         rows = pl.ds(s * leaf, leaf)
         slots.append(
             (fetch(basis_in.at[s], basis.at[s]), fetch(vectors_in.at[rows], vectors.at[rows]))
         )
+    first = fetch(transfer_in.at[pl.ds(0, SLOT_BITS)], transfer)
     weights = fetch(diagonal_in, diagonal)
-    later = fetch(target_in, target)
-    first.wait()
-    rank = basis.shape[1]
-    blocks, sources = compose(transfer, list(range(SLOT_BITS)), rank)
-    levels = jnp.concatenate(blocks, axis=0)
     c = []
     for s in range(SLOTS):
         for copy in slots[s]:
             copy.wait()
         c.append(product(basis[s], vectors[s * leaf : (s + 1) * leaf], NN))
-    out_rows = product(levels, jnp.concatenate([c[s] for s in sources[0]], axis=0), NN)
-    c = [out_rows[s * rank : (s + 1) * rank] for s in range(SLOTS)]
+    first.wait()
+    for level in range(SLOT_BITS):
+        for low, high in pairs(level):
+            both = jnp.concatenate([c[low], c[high]], axis=0)
+            c[low] = product(transfer[level, low], both, NN)
+            c[high] = product(transfer[level, high], both, NN)
     weights.wait()
     store(out, c, diagonal[...])
-    later.wait()
 
 
 def join(level, bit, s, at, own, partner, transfer):
@@ -379,18 +379,18 @@
     lanes = transfer.shape[3]
     diagonal_rows = diagonal.reshape(-1, lanes)
     packed = (slots * rank + diagonal_rows.shape[0], vecs)
-    coeffs, source_t, target_t, diagonal_rows = call(
+    coeffs, source_t, diagonal_rows = call(
         head_kernel,
-        [packed, basis_shape, basis_shape, diagonal_rows.shape],
+        [packed, basis_shape, diagonal_rows.shape],
         [
             pltpu.with_memory_space_constraint(x, pltpu.HBM)
-            for x in (vectors, source_t, transfer, target_t, diagonal_rows)
+            for x in (vectors, source_t, transfer, diagonal_rows)
         ],
-        [HBM] * 5,
+        [HBM] * 4,
         scratch=[
             pltpu.VMEM((SLOT_BITS,) + transfer.shape[1:], jnp.float32),
             pltpu.VMEM(vectors.shape, jnp.float32),
-            pltpu.SemaphoreType.DMA((2 * slots + 3,)),
+            pltpu.SemaphoreType.DMA((2 * slots + 2,)),
         ],
     )
     tops = [SLOT_BITS + places.low_bits + j for j in range(SLOT_BITS)]

time: 62.7 us -> 62.7 us (level)
  no operation moved by 1% of the time
where the time goes in v12:
time: 62.7 us; the launch traced here: 62.5 us
  starting transfers between devices  29.7 us (47%)
  waiting for transfers between devices  22.7 us (36%)
  Pallas kernels  9.28 us (15%)
  between operations  0.86 us (1%)
    ppermute x20, starting transfers between devices, permute(): lax.ppermute(block, BOTH, [(d, route(d)) for d in range(self.devices)])  29.7 us
    ppermute x20, waiting for transfers between devices, permute(): lax.ppermute(block, BOTH, [(d, route(d)) for d in range(self.devices)])  22.7 us
    pallas_call x21, Pallas kernels, call(): pl.pallas_call(kernel, out_shape=shapes, in_specs=specs or [VMEM] * len(o...  9.28 us
  transfers between devices with their start and end apart: 20, of which 9 were waited for; matrix products, arithmetic and copies ran while one was open for 0% of the time, Pallas kernels for 8%

profile of v12, /device:TPU:1, one launch (start us, length us, event | category | flops | bytes accessed | tf_op | source)
XLA Modules:
  0.0 62.5 jit_solution(14200905004888423115)
XLA Ops:
  0.6 0.0 copy-start.1
  0.6 0.0 copy-start
  0.7 2.3 %shard_map.73 = (f32[264,128]{1,0:T(8,128)S(1)}, f32[4,64,256]{2,1,0:T(8,128)S(1)}, f32[8,128]{1,0:T(8,128)S(1)}) custom-call(f32[1024,128]{1,0:T(8,128)} %vectors_in.1, f32[4,64,256]{2,1,0:T(8,128)} %bitcast.6, f32[7,4,64,128]{3,2,1,0:T(8,128)} %transfer.23, f32[8,128]{1,0:T(8,128)} %bitcast.7), custom_call_target="tpu_custom_call" | custom-call | flops 16777216 | bytes 524288 | tf_op jit(solution)/shard_map/pallas_call | solution.py:99
  3.0 0.1 collective-permute-start.5
  3.0 0.0 copy-done.1
  3.1 2.7 %collective-permute-start = (f32[2,64,256]{2,1,0:T(8,128)S(1)}, f32[2,64,256]{2,1,0:T(8,128)S(1)}, u32[]{:S(2)}, u32[]{:S(2)}) collective-permute-start(f32[2,64,256]{2,1,0:T(8,128)S(1)} %shard_map.68), channel_id=1, source_target_pairs={{0,8},{1,9},{2,10},{3,11},{4,12},{5,13},{6,14},{7,15},{8,0},{9,1},... | collective-permute-start | bytes 393224 | tf_op jit(solution)/shard_map/ppermute | solution.py:36
  5.8 0.0 copy-done
  5.8 0.1 collective-permute-start.3
  5.9 0.0 collective-permute-done.5.partner
  5.9 0.2 shard_map.74.own
  6.2 1.5 %collective-permute-start.6 = (f32[264,128]{1,0:T(8,128)S(1)}, f32[264,128]{1,0:T(8,128)S(1)}, u32[]{:S(2)}, u32[]{:S(2)}) collective-permute-start(f32[264,128]{1,0:T(8,128)S(1)} %shard_map.74.own), channel_id=1, source_target_pairs={{0,2},{1,3},{2,0},{3,1},{4,6},{5,7},{6,4},{7,5},{8,10},{9,11},{10,... | collective-permute-start | bytes 405512 | tf_op jit(solution)/shard_map/ppermute | solution.py:36
  7.7 1.9 %collective-permute-done.first = f32[2,64,256]{2,1,0:T(8,128)S(1)} collective-permute-done((f32[2,64,256]{2,1,0:T(8,128)S(1)}, f32[2,64,256]{2,1,0:T(8,128)S(1)}, u32[]{:S(2)}, u32[]{:S(2)}) %collective-permute-start) | collective-permute-done | bytes 131104 | tf_op jit(solution)/shard_map/ppermute | solution.py:36
  9.7 1.3 %collective-permute-start.1 = (f32[2,64,256]{2,1,0:T(8,128)S(1)}, f32[2,64,256]{2,1,0:T(8,128)S(1)}, u32[]{:S(2)}, u32[]{:S(2)}) collective-permute-start(f32[2,64,256]{2,1,0:T(8,128)S(1)} %shard_map.69), channel_id=1, source_target_pairs={{0,16},{1,17},{2,18},{3,19},{4,20},{5,21},{6,22},{7,23},{8,24},{9,... | collective-permute-start | bytes 393224 | tf_op jit(solution)/shard_map/ppermute | solution.py:36
  10.9 1.5 %collective-permute-done.3.first = f32[2,128,128]{2,1,0:T(8,128)S(1)} collective-permute-done((f32[2,128,128]{2,1,0:T(8,128)S(1)}, f32[2,128,128]{2,1,0:T(8,128)S(1)}, u32[]{:S(2)}, u32[]{:S(2)}) %collective-permute-start.3) | collective-permute-done | bytes 131104 | tf_op jit(solution)/shard_map/ppermute | solution.py:36
  12.5 1.3 %collective-permute-start.4 = (f32[2,128,128]{2,1,0:T(8,128)S(1)}, f32[2,128,128]{2,1,0:T(8,128)S(1)}, u32[]{:S(2)}, u32[]{:S(2)}) collective-permute-start(f32[2,128,128]{2,1,0:T(8,128)S(1)} %shard_map.72), channel_id=1, source_target_pairs={{0,16},{1,17},{2,18},{3,19},{4,20},{5,21},{6,22},{7,23},{8,24},{9,... | collective-permute-start | bytes 393224 | tf_op jit(solution)/shard_map/ppermute | solution.py:36
  13.7 0.0 collective-permute-done.6.partner
  13.8 0.2 shard_map.75
  14.0 2.4 %collective-permute-start.7 = (f32[136,128]{1,0:T(8,128)S(1)}, f32[136,128]{1,0:T(8,128)S(1)}, u32[]{:S(2)}, u32[]{:S(2)}) collective-permute-start(f32[136,128]{1,0:T(8,128)S(1)} %get-tuple-element.29.own), channel_id=1, source_target_pairs={{0,4},{1,5},{2,6},{3,7},{4,0},{5,1},{6,2},{7,3},{8,12},{9,13},{10,... | collective-permute-start | bytes 208904 | tf_op jit(solution)/shard_map/ppermute | solution.py:36
  16.4 0.1 collective-permute-start.8
  16.4 6.3 %collective-permute-done.8.partner = f32[128,128]{1,0:T(8,128)S(1)} collective-permute-done((f32[128,128]{1,0:T(8,128)S(1)}, f32[128,128]{1,0:T(8,128)S(1)}, u32[]{:S(2)}, u32[]{:S(2)}) %collective-permute-start.8) | collective-permute-done | bytes 65568 | tf_op jit(solution)/shard_map/ppermute | solution.py:36
  22.7 0.2 shard_map.78
  22.9 0.2 collective-permute-start.10
  23.2 0.0 collective-permute-done.7.partner
  23.2 0.2 shard_map.79
  23.3 1.2 %collective-permute-start.9 = (f32[64,128]{1,0:T(8,128)S(1)}, f32[64,128]{1,0:T(8,128)S(1)}, u32[]{:S(2)}, u32[]{:S(2)}) collective-permute-start(f32[64,128]{1,0:T(8,128)S(1)} %get-tuple-element.33), channel_id=1, source_target_pairs={{0,8},{1,9},{2,10},{3,11},{4,12},{5,13},{6,14},{7,15},{8,0},{9,1},... | collective-permute-start | bytes 98312 | tf_op jit(solution)/shard_map/ppermute | solution.py:36
  24.6 1.2 %collective-permute-start.11 = (f32[64,128]{1,0:T(8,128)S(1)}, f32[64,128]{1,0:T(8,128)S(1)}, u32[]{:S(2)}, u32[]{:S(2)}) collective-permute-start(f32[64,128]{1,0:T(8,128)S(1)} %get-tuple-element.35), channel_id=1, source_target_pairs={{0,24},{1,25},{2,26},{3,27},{4,28},{5,29},{6,30},{7,31},{8,16},{9,... | collective-permute-start | bytes 98312 | tf_op jit(solution)/shard_map/ppermute | solution.py:36
  25.8 0.0 collective-permute-done.1.second
  25.8 0.0 collective-permute-done.4.second
  25.9 1.2 %shard_map.77 = (f32[256,256]{1,0:T(8,128)S(1)}, f32[256,256]{1,0:T(8,128)S(1)}) custom-call(f32[7,4,64,128]{3,2,1,0:T(8,128)S(1)} %copy-done, f32[2,128,128]{2,1,0:T(8,128)S(1)} %collective-permute-done.3.first, f32[2,128,128]{2,1,0:T(8,128)S(1)} %collective-permute-done.4.second, f32[4,64,256]{2,1,0:T(8,128)S(1)} %shard_map.70.basis, ...), custom_call_target="tpu_custom_call" | custom-call | flops 16777216 | bytes 524288 | tf_op jit(solution)/shard_map/pallas_call | solution.py:99
  27.1 0.0 collective-permute-done.10.refs_2_
  27.1 0.0 collective-permute-done.9.refs_1_
  27.1 1.1 %collective-permute-done.11.refs_3_ = f32[64,128]{1,0:T(8,128)S(1)} collective-permute-done((f32[64,128]{1,0:T(8,128)S(1)}, f32[64,128]{1,0:T(8,128)S(1)}, u32[]{:S(2)}, u32[]{:S(2)}) %collective-permute-start.11) | collective-permute-done | bytes 32800 | tf_op jit(solution)/shard_map/ppermute | solution.py:36
  28.2 0.2 shard_map.82
  28.5 1.3 %collective-permute-start.14 = (f32[64,128]{1,0:T(8,128)S(1)}, f32[64,128]{1,0:T(8,128)S(1)}, u32[]{:S(2)}, u32[]{:S(2)}) collective-permute-start(f32[64,128]{1,0:T(8,128)S(1)} %get-tuple-element.40), channel_id=1, source_target_pairs={{0,24},{1,25},{2,26},{3,27},{4,28},{5,29},{6,30},{7,31},{8,16},{9,... | collective-permute-start | bytes 98312 | tf_op jit(solution)/shard_map/ppermute | solution.py:36
  29.8 1.5 %collective-permute-start.15 = (f32[64,128]{1,0:T(8,128)S(1)}, f32[64,128]{1,0:T(8,128)S(1)}, u32[]{:S(2)}, u32[]{:S(2)}) collective-permute-start(f32[64,128]{1,0:T(8,128)S(1)} %get-tuple-element.41), channel_id=1, source_target_pairs={{0,8},{1,9},{2,10},{3,11},{4,12},{5,13},{6,14},{7,15},{8,0},{9,1},... | collective-permute-start | bytes 98312 | tf_op jit(solution)/shard_map/ppermute | solution.py:36
  31.3 0.0 collective-permute-start.16
  31.3 0.9 %collective-permute-done.14.refs_0_ = f32[64,128]{1,0:T(8,128)S(1)} collective-permute-done((f32[64,128]{1,0:T(8,128)S(1)}, f32[64,128]{1,0:T(8,128)S(1)}, u32[]{:S(2)}, u32[]{:S(2)}) %collective-permute-start.14) | collective-permute-done | bytes 32800 | tf_op jit(solution)/shard_map/ppermute | solution.py:36
  32.2 0.7 %collective-permute-done.15.refs_1_ = f32[64,128]{1,0:T(8,128)S(1)} collective-permute-done((f32[64,128]{1,0:T(8,128)S(1)}, f32[64,128]{1,0:T(8,128)S(1)}, u32[]{:S(2)}, u32[]{:S(2)}) %collective-permute-start.15) | collective-permute-done | bytes 32800 | tf_op jit(solution)/shard_map/ppermute | solution.py:36
  32.9 1.1 %collective-permute-done.16.refs_2_ = f32[64,128]{1,0:T(8,128)S(1)} collective-permute-done((f32[64,128]{1,0:T(8,128)S(1)}, f32[64,128]{1,0:T(8,128)S(1)}, u32[]{:S(2)}, u32[]{:S(2)}) %collective-permute-start.16) | collective-permute-done | bytes 32800 | tf_op jit(solution)/shard_map/ppermute | solution.py:36
  34.0 0.3 shard_map.84
  34.3 0.1 collective-permute-start.17
  34.4 0.2 shard_map.83
  34.6 2.4 %collective-permute-start.13 = (f32[1,64,128]{2,1,0:T(8,128)S(1)}, f32[1,64,128]{2,1,0:T(8,128)S(1)}, u32[]{:S(2)}, u32[]{:S(2)}) collective-permute-start(f32[1,64,128]{2,1,0:T(8,128)S(1)} %get-tuple-element.39), channel_id=1, source_target_pairs={{0,4},{1,5},{2,6},{3,7},{4,0},{5,1},{6,2},{7,3},{8,12},{9,13},{10,... | collective-permute-start | bytes 98312 | tf_op jit(solution)/shard_map/ppermute | solution.py:36
  37.1 3.1 %collective-permute-done.13.refs_1_ = f32[1,64,128]{2,1,0:T(8,128)S(1)} collective-permute-done((f32[1,64,128]{2,1,0:T(8,128)S(1)}, f32[1,64,128]{2,1,0:T(8,128)S(1)}, u32[]{:S(2)}, u32[]{:S(2)}) %collective-permute-start.13) | collective-permute-done | bytes 32800 | tf_op jit(solution)/shard_map/ppermute | solution.py:36
  40.2 0.0 collective-permute-done.17.refs_3_
  40.2 0.3 shard_map.85
  40.5 2.0 %collective-permute-start.18 = (f32[4,64,128]{2,1,0:T(8,128)S(1)}, f32[4,64,128]{2,1,0:T(8,128)S(1)}, u32[]{:S(2)}, u32[]{:S(2)}) collective-permute-start(f32[4,64,128]{2,1,0:T(8,128)S(1)} %get-tuple-element.46), channel_id=1, source_target_pairs={{0,2},{1,3},{2,0},{3,1},{4,6},{5,7},{6,4},{7,5},{8,10},{9,11},{10,... | collective-permute-start | bytes 393224 | tf_op jit(solution)/shard_map/ppermute | solution.py:36
  42.5 8.3 %collective-permute-start.2 = (f32[4,64,256]{2,1,0:T(8,128)S(1)}, f32[4,64,256]{2,1,0:T(8,128)S(1)}, u32[]{:S(2)}, u32[]{:S(2)}) collective-permute-start(f32[4,64,256]{2,1,0:T(8,128)S(1)} %shard_map.70.basis), channel_id=1, source_target_pairs={{0,0},{1,4},{2,2},{3,6},{4,1},{5,5},{6,3},{7,7},{8,8},{9,12},{10,1... | collective-permute-start | bytes 786440 | tf_op jit(solution)/shard_map/ppermute | solution.py:36
  50.8 0.2 shard_map.80
  51.1 1.9 %collective-permute-start.12 = (f32[4,64,128]{2,1,0:T(8,128)S(1)}, f32[4,64,128]{2,1,0:T(8,128)S(1)}, u32[]{:S(2)}, u32[]{:S(2)}) collective-permute-start(f32[4,64,128]{2,1,0:T(8,128)S(1)} %shard_map.80), channel_id=1, source_target_pairs={{0,0},{1,4},{2,2},{3,6},{4,1},{5,5},{6,3},{7,7},{8,8},{9,12},{10,1... | collective-permute-start | bytes 393224 | tf_op jit(solution)/shard_map/ppermute | solution.py:36
  53.0 0.0 collective-permute-done.18.arrived
  53.0 0.3 shard_map.86
  53.3 0.1 collective-permute-start.19
  53.4 0.8 %shard_map.87 = (bf16[4,256,256]{2,1,0:T(8,128)(2,1)S(1)}, bf16[4,256,256]{2,1,0:T(8,128)(2,1)S(1)}) custom-call(f32[7,4,64,128]{3,2,1,0:T(8,128)S(1)} %copy-done, f32[4,64,256]{2,1,0:T(8,128)S(1)} %get-tuple-element.49.basis), custom_call_target="tpu_custom_call" | custom-call | flops 16777216 | bytes 524288 | tf_op jit(solution)/shard_map/pallas_call | solution.py:99
  54.2 5.9 %collective-permute-done.12.coeffs = f32[4,64,128]{2,1,0:T(8,128)S(1)} collective-permute-done((f32[4,64,128]{2,1,0:T(8,128)S(1)}, f32[4,64,128]{2,1,0:T(8,128)S(1)}, u32[]{:S(2)}, u32[]{:S(2)}) %collective-permute-start.12) | collective-permute-done | bytes 131104 | tf_op jit(solution)/shard_map/ppermute | solution.py:36
  60.1 0.0 collective-permute-done.2.basis
  60.1 1.1 %shard_map.81 = f32[1024,128]{1,0:T(8,128)} custom-call(f32[4,64,256]{2,1,0:T(8,128)S(1)} %collective-permute-done.2.basis, f32[4,64,128]{2,1,0:T(8,128)S(1)} %collective-permute-done.12.coeffs), custom_call_target="tpu_custom_call" | custom-call | flops 16777216 | bytes 524288 | tf_op jit(solution)/shard_map/pallas_call | solution.py:99
  61.3 0.0 collective-permute-done.19.arrived
  61.3 1.3 %shard_map.88 = f32[1024,128]{1,0:T(8,128)} custom-call(f32[4,64,128]{2,1,0:T(8,128)S(1)} %get-tuple-element.47.kept, f32[4,64,128]{2,1,0:T(8,128)S(1)} %collective-permute-done.19.arrived, bf16[4,256,256]{2,1,0:T(8,128)(2,1)S(1)} %get-tuple-element.50.high, bf16[4,256,256]{2,1,0:T(8,128)(2,1)S(1)} %get-tuple-element.51.low), custom_call_target="tpu_custom_call" | custom-call | flops 16777216 | bytes 524288 | tf_op jit(solution)/shard_map/pallas_call | solution.py:99
  (6 shorter events, 0.1 us)
Async XLA Ops:
  0.6 2.4 %copy-start.1 = (f32[4,256,64]{1,2,0:T(8,128)S(1)}, f32[4,256,64]{1,2,0:T(8,128)}, u32[]{:S(2)}) copy-start(f32[4,256,64]{1,2,0:T(8,128)} %param.9) | copy-start | bytes 786436
  0.6 5.2 %copy-start = (f32[7,4,64,128]{3,2,1,0:T(8,128)S(1)}, f32[7,4,64,128]{3,2,1,0:T(8,128)}, u32[]{:S(2)}) copy-start(f32[7,4,64,128]{3,2,1,0:T(8,128)} %transfer.23) | copy-start | bytes 2752516
  3.0 3.0 %collective-permute-start.5 = (f32[264,128]{1,0:T(8,128)S(1)}, f32[264,128]{1,0:T(8,128)S(1)}, u32[]{:S(2)}, u32[]{:S(2)}) collective-permute-start(f32[264,128]{1,0:T(8,128)S(1)} %get-tuple-element.28.own), channel_id=1, source_target_pairs={{0,1},{1,0},{2,3},{3,2},{4,5},{5,4},{6,7},{7,6},{8,9},{9,8},{10,11... | collective-permute-start | bytes 405512 | tf_op jit(solution)/shard_map/ppermute | solution.py:36
  3.1 6.6 %collective-permute-start = (f32[2,64,256]{2,1,0:T(8,128)S(1)}, f32[2,64,256]{2,1,0:T(8,128)S(1)}, u32[]{:S(2)}, u32[]{:S(2)}) collective-permute-start(f32[2,64,256]{2,1,0:T(8,128)S(1)} %shard_map.68), channel_id=1, source_target_pairs={{0,8},{1,9},{2,10},{3,11},{4,12},{5,13},{6,14},{7,15},{8,0},{9,1},... | collective-permute-start | bytes 393224 | tf_op jit(solution)/shard_map/ppermute | solution.py:36
  5.8 6.6 %collective-permute-start.3 = (f32[2,128,128]{2,1,0:T(8,128)S(1)}, f32[2,128,128]{2,1,0:T(8,128)S(1)}, u32[]{:S(2)}, u32[]{:S(2)}) collective-permute-start(f32[2,128,128]{2,1,0:T(8,128)S(1)} %shard_map.71), channel_id=1, source_target_pairs={{0,8},{1,9},{2,10},{3,11},{4,12},{5,13},{6,14},{7,15},{8,0},{9,1},... | collective-permute-start | bytes 393224 | tf_op jit(solution)/shard_map/ppermute | solution.py:36
  6.2 7.6 %collective-permute-start.6 = (f32[264,128]{1,0:T(8,128)S(1)}, f32[264,128]{1,0:T(8,128)S(1)}, u32[]{:S(2)}, u32[]{:S(2)}) collective-permute-start(f32[264,128]{1,0:T(8,128)S(1)} %shard_map.74.own), channel_id=1, source_target_pairs={{0,2},{1,3},{2,0},{3,1},{4,6},{5,7},{6,4},{7,5},{8,10},{9,11},{10,... | collective-permute-start | bytes 405512 | tf_op jit(solution)/shard_map/ppermute | solution.py:36
  9.7 16.1 %collective-permute-start.1 = (f32[2,64,256]{2,1,0:T(8,128)S(1)}, f32[2,64,256]{2,1,0:T(8,128)S(1)}, u32[]{:S(2)}, u32[]{:S(2)}) collective-permute-start(f32[2,64,256]{2,1,0:T(8,128)S(1)} %shard_map.69), channel_id=1, source_target_pairs={{0,16},{1,17},{2,18},{3,19},{4,20},{5,21},{6,22},{7,23},{8,24},{9,... | collective-permute-start | bytes 393224 | tf_op jit(solution)/shard_map/ppermute | solution.py:36
  12.5 13.4 %collective-permute-start.4 = (f32[2,128,128]{2,1,0:T(8,128)S(1)}, f32[2,128,128]{2,1,0:T(8,128)S(1)}, u32[]{:S(2)}, u32[]{:S(2)}) collective-permute-start(f32[2,128,128]{2,1,0:T(8,128)S(1)} %shard_map.72), channel_id=1, source_target_pairs={{0,16},{1,17},{2,18},{3,19},{4,20},{5,21},{6,22},{7,23},{8,24},{9,... | collective-permute-start | bytes 393224 | tf_op jit(solution)/shard_map/ppermute | solution.py:36
  14.0 9.2 %collective-permute-start.7 = (f32[136,128]{1,0:T(8,128)S(1)}, f32[136,128]{1,0:T(8,128)S(1)}, u32[]{:S(2)}, u32[]{:S(2)}) collective-permute-start(f32[136,128]{1,0:T(8,128)S(1)} %get-tuple-element.29.own), channel_id=1, source_target_pairs={{0,4},{1,5},{2,6},{3,7},{4,0},{5,1},{6,2},{7,3},{8,12},{9,13},{10,... | collective-permute-start | bytes 208904 | tf_op jit(solution)/shard_map/ppermute | solution.py:36
  16.4 6.4 %collective-permute-start.8 = (f32[128,128]{1,0:T(8,128)S(1)}, f32[128,128]{1,0:T(8,128)S(1)}, u32[]{:S(2)}, u32[]{:S(2)}) collective-permute-start(f32[128,128]{1,0:T(8,128)S(1)} %get-tuple-element.31.own), channel_id=1, source_target_pairs={{0,4},{1,5},{2,6},{3,7},{4,0},{5,1},{6,2},{7,3},{8,12},{9,13},{10,... | collective-permute-start | bytes 196616 | tf_op jit(solution)/shard_map/ppermute | solution.py:36
  22.9 4.1 %collective-permute-start.10 = (f32[64,128]{1,0:T(8,128)S(1)}, f32[64,128]{1,0:T(8,128)S(1)}, u32[]{:S(2)}, u32[]{:S(2)}) collective-permute-start(f32[64,128]{1,0:T(8,128)S(1)} %get-tuple-element.34), channel_id=1, source_target_pairs={{0,16},{1,17},{2,18},{3,19},{4,20},{5,21},{6,22},{7,23},{8,24},{9,... | collective-permute-start | bytes 98312 | tf_op jit(solution)/shard_map/ppermute | solution.py:36
  23.3 3.7 %collective-permute-start.9 = (f32[64,128]{1,0:T(8,128)S(1)}, f32[64,128]{1,0:T(8,128)S(1)}, u32[]{:S(2)}, u32[]{:S(2)}) collective-permute-start(f32[64,128]{1,0:T(8,128)S(1)} %get-tuple-element.33), channel_id=1, source_target_pairs={{0,8},{1,9},{2,10},{3,11},{4,12},{5,13},{6,14},{7,15},{8,0},{9,1},... | collective-permute-start | bytes 98312 | tf_op jit(solution)/shard_map/ppermute | solution.py:36
  24.6 3.7 %collective-permute-start.11 = (f32[64,128]{1,0:T(8,128)S(1)}, f32[64,128]{1,0:T(8,128)S(1)}, u32[]{:S(2)}, u32[]{:S(2)}) collective-permute-start(f32[64,128]{1,0:T(8,128)S(1)} %get-tuple-element.35), channel_id=1, source_target_pairs={{0,24},{1,25},{2,26},{3,27},{4,28},{5,29},{6,30},{7,31},{8,16},{9,... | collective-permute-start | bytes 98312 | tf_op jit(solution)/shard_map/ppermute | solution.py:36
  28.5 3.7 %collective-permute-start.14 = (f32[64,128]{1,0:T(8,128)S(1)}, f32[64,128]{1,0:T(8,128)S(1)}, u32[]{:S(2)}, u32[]{:S(2)}) collective-permute-start(f32[64,128]{1,0:T(8,128)S(1)} %get-tuple-element.40), channel_id=1, source_target_pairs={{0,24},{1,25},{2,26},{3,27},{4,28},{5,29},{6,30},{7,31},{8,16},{9,... | collective-permute-start | bytes 98312 | tf_op jit(solution)/shard_map/ppermute | solution.py:36
  29.8 3.2 %collective-permute-start.15 = (f32[64,128]{1,0:T(8,128)S(1)}, f32[64,128]{1,0:T(8,128)S(1)}, u32[]{:S(2)}, u32[]{:S(2)}) collective-permute-start(f32[64,128]{1,0:T(8,128)S(1)} %get-tuple-element.41), channel_id=1, source_target_pairs={{0,8},{1,9},{2,10},{3,11},{4,12},{5,13},{6,14},{7,15},{8,0},{9,1},... | collective-permute-start | bytes 98312 | tf_op jit(solution)/shard_map/ppermute | solution.py:36
  31.3 2.8 %collective-permute-start.16 = (f32[64,128]{1,0:T(8,128)S(1)}, f32[64,128]{1,0:T(8,128)S(1)}, u32[]{:S(2)}, u32[]{:S(2)}) collective-permute-start(f32[64,128]{1,0:T(8,128)S(1)} %get-tuple-element.42), channel_id=1, source_target_pairs={{0,16},{1,17},{2,18},{3,19},{4,20},{5,21},{6,22},{7,23},{8,24},{9,... | collective-permute-start | bytes 98312 | tf_op jit(solution)/shard_map/ppermute | solution.py:36
  34.3 5.8 %collective-permute-start.17 = (f32[3,64,128]{2,1,0:T(8,128)S(1)}, f32[3,64,128]{2,1,0:T(8,128)S(1)}, u32[]{:S(2)}, u32[]{:S(2)}) collective-permute-start(f32[3,64,128]{2,1,0:T(8,128)S(1)} %get-tuple-element.44), channel_id=1, source_target_pairs={{0,4},{1,5},{2,6},{3,7},{4,0},{5,1},{6,2},{7,3},{8,12},{9,13},{10,... | collective-permute-start | bytes 294920 | tf_op jit(solution)/shard_map/ppermute | solution.py:36
  34.6 5.5 %collective-permute-start.13 = (f32[1,64,128]{2,1,0:T(8,128)S(1)}, f32[1,64,128]{2,1,0:T(8,128)S(1)}, u32[]{:S(2)}, u32[]{:S(2)}) collective-permute-start(f32[1,64,128]{2,1,0:T(8,128)S(1)} %get-tuple-element.39), channel_id=1, source_target_pairs={{0,4},{1,5},{2,6},{3,7},{4,0},{5,1},{6,2},{7,3},{8,12},{9,13},{10,... | collective-permute-start | bytes 98312 | tf_op jit(solution)/shard_map/ppermute | solution.py:36
  40.5 12.5 %collective-permute-start.18 = (f32[4,64,128]{2,1,0:T(8,128)S(1)}, f32[4,64,128]{2,1,0:T(8,128)S(1)}, u32[]{:S(2)}, u32[]{:S(2)}) collective-permute-start(f32[4,64,128]{2,1,0:T(8,128)S(1)} %get-tuple-element.46), channel_id=1, source_target_pairs={{0,2},{1,3},{2,0},{3,1},{4,6},{5,7},{6,4},{7,5},{8,10},{9,11},{10,... | collective-permute-start | bytes 393224 | tf_op jit(solution)/shard_map/ppermute | solution.py:36
  42.5 17.6 %collective-permute-start.2 = (f32[4,64,256]{2,1,0:T(8,128)S(1)}, f32[4,64,256]{2,1,0:T(8,128)S(1)}, u32[]{:S(2)}, u32[]{:S(2)}) collective-permute-start(f32[4,64,256]{2,1,0:T(8,128)S(1)} %shard_map.70.basis), channel_id=1, source_target_pairs={{0,0},{1,4},{2,2},{3,6},{4,1},{5,5},{6,3},{7,7},{8,8},{9,12},{10,1... | collective-permute-start | bytes 786440 | tf_op jit(solution)/shard_map/ppermute | solution.py:36
  51.1 9.0 %collective-permute-start.12 = (f32[4,64,128]{2,1,0:T(8,128)S(1)}, f32[4,64,128]{2,1,0:T(8,128)S(1)}, u32[]{:S(2)}, u32[]{:S(2)}) collective-permute-start(f32[4,64,128]{2,1,0:T(8,128)S(1)} %shard_map.80), channel_id=1, source_target_pairs={{0,0},{1,4},{2,2},{3,6},{4,1},{5,5},{6,3},{7,7},{8,8},{9,12},{10,1... | collective-permute-start | bytes 393224 | tf_op jit(solution)/shard_map/ppermute | solution.py:36
  53.3 8.0 %collective-permute-start.19 = (f32[4,64,128]{2,1,0:T(8,128)S(1)}, f32[4,64,128]{2,1,0:T(8,128)S(1)}, u32[]{:S(2)}, u32[]{:S(2)}) collective-permute-start(f32[4,64,128]{2,1,0:T(8,128)S(1)} %get-tuple-element.48), channel_id=1, source_target_pairs={{0,1},{1,0},{2,3},{3,2},{4,5},{5,4},{6,7},{7,6},{8,9},{9,8},{10,11... | collective-permute-start | bytes 393224 | tf_op jit(solution)/shard_map/ppermute | solution.py:36

commit v13 on v12

--- a/solution.py
+++ b/solution.py
@@ -13,7 +13,7 @@
 BOTH = ("row", "col")
 CROSSING = sorted(range(1, SLOTS), key=lambda k: -k.bit_count())
 FORWARD_PIECES = [CROSSING[: SLOTS // 2], CROSSING[SLOTS // 2 :] + [0]]
-BACK_PIECES = [[0], CROSSING]
+BACK_PIECES = [[0] + CROSSING[:1], CROSSING[1:]]
 NN, TN, NT = ((1,), (0,)), ((0,), (0,)), ((1,), (1,))
 VMEM = pl.BlockSpec(memory_space=pltpu.VMEM)
 ANY = pl.BlockSpec(memory_space=pl.ANY)
@@ -123,9 +123,11 @@
     vectors_in,
     basis_in,
     transfer_in,
+    target_in,
     diagonal_in,
     out,
     basis,
+    target,
     diagonal,
     transfer,
     vectors,
@@ -147,6 +149,7 @@
         )
     first = fetch(transfer_in.at[pl.ds(0, SLOT_BITS)], transfer)
     weights = fetch(diagonal_in, diagonal)
+    later = fetch(target_in, target)
     c = []
     for s in range(SLOTS):
         for copy in slots[s]:
@@ -160,6 +163,7 @@
             c[high] = product(transfer[level, high], both, NN)
     weights.wait()
     store(out, c, diagonal[...])
+    later.wait()
 
 
 def join(level, bit, s, at, own, partner, transfer):
@@ -379,18 +383,18 @@
     lanes = transfer.shape[3]
     diagonal_rows = diagonal.reshape(-1, lanes)
     packed = (slots * rank + diagonal_rows.shape[0], vecs)
-    coeffs, source_t, diagonal_rows = call(
+    coeffs, source_t, target_t, diagonal_rows = call(
         head_kernel,
-        [packed, basis_shape, diagonal_rows.shape],
+        [packed, basis_shape, basis_shape, diagonal_rows.shape],
         [
             pltpu.with_memory_space_constraint(x, pltpu.HBM)
-            for x in (vectors, source_t, transfer, diagonal_rows)
+            for x in (vectors, source_t, transfer, target_t, diagonal_rows)
         ],
-        [HBM] * 4,
+        [HBM] * 5,
         scratch=[
             pltpu.VMEM((SLOT_BITS,) + transfer.shape[1:], jnp.float32),
             pltpu.VMEM(vectors.shape, jnp.float32),
-            pltpu.SemaphoreType.DMA((2 * slots + 2,)),
+            pltpu.SemaphoreType.DMA((2 * slots + 3,)),
         ],
     )
     tops = [SLOT_BITS + places.low_bits + j for j in range(SLOT_BITS)]

time: 62.7 us -> 61.5 us (0.981)
  starting transfers between devices: 29.7 us -> 28.6 us
    ppermute x20, starting transfers between devices: 29.7 us -> 28.6 us  [permute(): lax.ppermute(block, BOTH, [(d, route(d)) for d in range(self.devices)])]
  transfers between devices with their start and end apart: 20 -> 20, of which waited for: 9 -> 10; matrix products, arithmetic and copies ran while one was open for 0% -> 0% of each run, Pallas kernels for 8% -> 8%
where the time goes in v13:
time: 61.5 us; the launch traced here: 61.3 us
  starting transfers between devices  28.6 us (47%)
  waiting for transfers between devices  22.6 us (37%)
  Pallas kernels  9.28 us (15%)
  between operations  0.84 us (1%)
    ppermute x20, starting transfers between devices, permute(): lax.ppermute(block, BOTH, [(d, route(d)) for d in range(self.devices)])  28.6 us
    ppermute x20, waiting for transfers between devices, permute(): lax.ppermute(block, BOTH, [(d, route(d)) for d in range(self.devices)])  22.6 us
    pallas_call x21, Pallas kernels, call(): pl.pallas_call(kernel, out_shape=shapes, in_specs=specs or [VMEM] * len(o...  9.28 us
  transfers between devices with their start and end apart: 20, of which 10 were waited for; matrix products, arithmetic and copies ran while one was open for 0% of the time, Pallas kernels for 8%

profile of v13, /device:TPU:1, one launch (start us, length us, event | category | flops | bytes accessed | tf_op | source)
XLA Modules:
  0.0 61.3 jit_solution(17288597785573014418)
XLA Ops:
  0.6 0.0 copy-start
  0.6 2.3 %shard_map.68 = (f32[264,128]{1,0:T(8,128)S(1)}, f32[4,64,256]{2,1,0:T(8,128)S(1)}, f32[4,64,256]{2,1,0:T(8,128)S(1)}, f32[8,128]{1,0:T(8,128)S(1)}) custom-call(f32[1024,128]{1,0:T(8,128)} %vectors_in.1, f32[4,64,256]{2,1,0:T(8,128)} %bitcast.3, f32[7,4,64,128]{3,2,1,0:T(8,128)} %transfer.23, f32[4,64,256]{2,1,0:T(8,128)} %bitcast.4, f32[8,128]{1,0:T(8,128)} %bitcast.5), custom_call_target="tpu_custom_call" | custom-call | flops 16777216 | bytes 524288 | tf_op jit(solution)/shard_map/pallas_call | solution.py:99
  2.9 0.1 collective-permute-start.5
  3.1 2.7 %collective-permute-start = (f32[2,64,256]{2,1,0:T(8,128)S(1)}, f32[2,64,256]{2,1,0:T(8,128)S(1)}, u32[]{:S(2)}, u32[]{:S(2)}) collective-permute-start(f32[2,64,256]{2,1,0:T(8,128)S(1)} %shard_map.69), channel_id=1, source_target_pairs={{0,8},{1,9},{2,10},{3,11},{4,12},{5,13},{6,14},{7,15},{8,0},{9,1},... | collective-permute-start | bytes 393224 | tf_op jit(solution)/shard_map/ppermute | solution.py:36
  5.8 0.0 copy-done
  5.8 0.1 collective-permute-start.3
  5.9 0.0 collective-permute-done.5.partner
  5.9 0.2 shard_map.74.own
  6.2 1.5 %collective-permute-start.6 = (f32[264,128]{1,0:T(8,128)S(1)}, f32[264,128]{1,0:T(8,128)S(1)}, u32[]{:S(2)}, u32[]{:S(2)}) collective-permute-start(f32[264,128]{1,0:T(8,128)S(1)} %shard_map.74.own), channel_id=1, source_target_pairs={{0,2},{1,3},{2,0},{3,1},{4,6},{5,7},{6,4},{7,5},{8,10},{9,11},{10,... | collective-permute-start | bytes 405512 | tf_op jit(solution)/shard_map/ppermute | solution.py:36
  7.7 1.9 %collective-permute-done.first = f32[2,64,256]{2,1,0:T(8,128)S(1)} collective-permute-done((f32[2,64,256]{2,1,0:T(8,128)S(1)}, f32[2,64,256]{2,1,0:T(8,128)S(1)}, u32[]{:S(2)}, u32[]{:S(2)}) %collective-permute-start) | collective-permute-done | bytes 131104 | tf_op jit(solution)/shard_map/ppermute | solution.py:36
  9.7 1.3 %collective-permute-start.1 = (f32[2,64,256]{2,1,0:T(8,128)S(1)}, f32[2,64,256]{2,1,0:T(8,128)S(1)}, u32[]{:S(2)}, u32[]{:S(2)}) collective-permute-start(f32[2,64,256]{2,1,0:T(8,128)S(1)} %shard_map.70), channel_id=1, source_target_pairs={{0,16},{1,17},{2,18},{3,19},{4,20},{5,21},{6,22},{7,23},{8,24},{9,... | collective-permute-start | bytes 393224 | tf_op jit(solution)/shard_map/ppermute | solution.py:36
  10.9 1.5 %collective-permute-done.3.first = f32[2,128,128]{2,1,0:T(8,128)S(1)} collective-permute-done((f32[2,128,128]{2,1,0:T(8,128)S(1)}, f32[2,128,128]{2,1,0:T(8,128)S(1)}, u32[]{:S(2)}, u32[]{:S(2)}) %collective-permute-start.3) | collective-permute-done | bytes 131104 | tf_op jit(solution)/shard_map/ppermute | solution.py:36
  12.5 1.3 %collective-permute-start.4 = (f32[2,128,128]{2,1,0:T(8,128)S(1)}, f32[2,128,128]{2,1,0:T(8,128)S(1)}, u32[]{:S(2)}, u32[]{:S(2)}) collective-permute-start(f32[2,128,128]{2,1,0:T(8,128)S(1)} %shard_map.73), channel_id=1, source_target_pairs={{0,16},{1,17},{2,18},{3,19},{4,20},{5,21},{6,22},{7,23},{8,24},{9,... | collective-permute-start | bytes 393224 | tf_op jit(solution)/shard_map/ppermute | solution.py:36
  13.7 0.0 collective-permute-done.6.partner
  13.7 0.2 shard_map.75
  14.0 2.4 %collective-permute-start.7 = (f32[136,128]{1,0:T(8,128)S(1)}, f32[136,128]{1,0:T(8,128)S(1)}, u32[]{:S(2)}, u32[]{:S(2)}) collective-permute-start(f32[136,128]{1,0:T(8,128)S(1)} %get-tuple-element.31.own), channel_id=1, source_target_pairs={{0,4},{1,5},{2,6},{3,7},{4,0},{5,1},{6,2},{7,3},{8,12},{9,13},{10,... | collective-permute-start | bytes 208904 | tf_op jit(solution)/shard_map/ppermute | solution.py:36
  16.4 0.1 collective-permute-start.8
  16.4 6.3 %collective-permute-done.8.partner = f32[128,128]{1,0:T(8,128)S(1)} collective-permute-done((f32[128,128]{1,0:T(8,128)S(1)}, f32[128,128]{1,0:T(8,128)S(1)}, u32[]{:S(2)}, u32[]{:S(2)}) %collective-permute-start.8) | collective-permute-done | bytes 65568 | tf_op jit(solution)/shard_map/ppermute | solution.py:36
  22.7 0.2 shard_map.78
  22.9 0.2 collective-permute-start.10
  23.2 0.0 collective-permute-done.7.partner
  23.2 0.2 shard_map.79
  23.3 1.2 %collective-permute-start.9 = (f32[64,128]{1,0:T(8,128)S(1)}, f32[64,128]{1,0:T(8,128)S(1)}, u32[]{:S(2)}, u32[]{:S(2)}) collective-permute-start(f32[64,128]{1,0:T(8,128)S(1)} %get-tuple-element.35), channel_id=1, source_target_pairs={{0,8},{1,9},{2,10},{3,11},{4,12},{5,13},{6,14},{7,15},{8,0},{9,1},... | collective-permute-start | bytes 98312 | tf_op jit(solution)/shard_map/ppermute | solution.py:36
  24.6 1.2 %collective-permute-start.11 = (f32[64,128]{1,0:T(8,128)S(1)}, f32[64,128]{1,0:T(8,128)S(1)}, u32[]{:S(2)}, u32[]{:S(2)}) collective-permute-start(f32[64,128]{1,0:T(8,128)S(1)} %get-tuple-element.37), channel_id=1, source_target_pairs={{0,24},{1,25},{2,26},{3,27},{4,28},{5,29},{6,30},{7,31},{8,16},{9,... | collective-permute-start | bytes 98312 | tf_op jit(solution)/shard_map/ppermute | solution.py:36
  25.8 0.0 collective-permute-done.1.second
  25.8 0.0 collective-permute-done.4.second
  25.8 1.2 %shard_map.77 = (f32[256,256]{1,0:T(8,128)S(1)}, f32[256,256]{1,0:T(8,128)S(1)}) custom-call(f32[7,4,64,128]{3,2,1,0:T(8,128)S(1)} %copy-done, f32[2,128,128]{2,1,0:T(8,128)S(1)} %collective-permute-done.3.first, f32[2,128,128]{2,1,0:T(8,128)S(1)} %collective-permute-done.4.second, f32[4,64,256]{2,1,0:T(8,128)S(1)} %shard_map.71.basis, ...), custom_call_target="tpu_custom_call" | custom-call | flops 16777216 | bytes 524288 | tf_op jit(solution)/shard_map/pallas_call | solution.py:99
  27.1 0.0 collective-permute-done.10.refs_2_
  27.1 0.0 collective-permute-done.9.refs_1_
  27.1 1.2 %collective-permute-done.11.refs_3_ = f32[64,128]{1,0:T(8,128)S(1)} collective-permute-done((f32[64,128]{1,0:T(8,128)S(1)}, f32[64,128]{1,0:T(8,128)S(1)}, u32[]{:S(2)}, u32[]{:S(2)}) %collective-permute-start.11) | collective-permute-done | bytes 32800 | tf_op jit(solution)/shard_map/ppermute | solution.py:36
  28.2 0.2 shard_map.82
  28.5 1.3 %collective-permute-start.13 = (f32[64,128]{1,0:T(8,128)S(1)}, f32[64,128]{1,0:T(8,128)S(1)}, u32[]{:S(2)}, u32[]{:S(2)}) collective-permute-start(f32[64,128]{1,0:T(8,128)S(1)} %get-tuple-element.40), channel_id=1, source_target_pairs={{0,24},{1,25},{2,26},{3,27},{4,28},{5,29},{6,30},{7,31},{8,16},{9,... | collective-permute-start | bytes 98312 | tf_op jit(solution)/shard_map/ppermute | solution.py:36
  29.8 1.5 %collective-permute-start.15 = (f32[64,128]{1,0:T(8,128)S(1)}, f32[64,128]{1,0:T(8,128)S(1)}, u32[]{:S(2)}, u32[]{:S(2)}) collective-permute-start(f32[64,128]{1,0:T(8,128)S(1)} %get-tuple-element.43), channel_id=1, source_target_pairs={{0,8},{1,9},{2,10},{3,11},{4,12},{5,13},{6,14},{7,15},{8,0},{9,1},... | collective-permute-start | bytes 98312 | tf_op jit(solution)/shard_map/ppermute | solution.py:36
  31.3 0.0 collective-permute-start.16
  31.3 1.0 %collective-permute-done.13.refs_1_ = f32[64,128]{1,0:T(8,128)S(1)} collective-permute-done((f32[64,128]{1,0:T(8,128)S(1)}, f32[64,128]{1,0:T(8,128)S(1)}, u32[]{:S(2)}, u32[]{:S(2)}) %collective-permute-start.13) | collective-permute-done | bytes 32800 | tf_op jit(solution)/shard_map/ppermute | solution.py:36
  32.2 0.2 shard_map.83
  32.5 0.1 collective-permute-start.14
  32.6 0.4 collective-permute-done.15.refs_0_
  32.9 1.1 %collective-permute-done.16.refs_1_ = f32[64,128]{1,0:T(8,128)S(1)} collective-permute-done((f32[64,128]{1,0:T(8,128)S(1)}, f32[64,128]{1,0:T(8,128)S(1)}, u32[]{:S(2)}, u32[]{:S(2)}) %collective-permute-start.16) | collective-permute-done | bytes 32800 | tf_op jit(solution)/shard_map/ppermute | solution.py:36
  34.0 0.3 shard_map.84
  34.3 1.0 %collective-permute-start.17 = (f32[2,64,128]{2,1,0:T(8,128)S(1)}, f32[2,64,128]{2,1,0:T(8,128)S(1)}, u32[]{:S(2)}, u32[]{:S(2)}) collective-permute-start(f32[2,64,128]{2,1,0:T(8,128)S(1)} %get-tuple-element.46), channel_id=1, source_target_pairs={{0,4},{1,5},{2,6},{3,7},{4,0},{5,1},{6,2},{7,3},{8,12},{9,13},{10,... | collective-permute-start | bytes 196616 | tf_op jit(solution)/shard_map/ppermute | solution.py:36
  35.2 1.3 %collective-permute-done.14.refs_1_ = f32[2,64,128]{2,1,0:T(8,128)S(1)} collective-permute-done((f32[2,64,128]{2,1,0:T(8,128)S(1)}, f32[2,64,128]{2,1,0:T(8,128)S(1)}, u32[]{:S(2)}, u32[]{:S(2)}) %collective-permute-start.14) | collective-permute-done | bytes 65568 | tf_op jit(solution)/shard_map/ppermute | solution.py:36
  36.6 2.3 %collective-permute-done.17.refs_3_ = f32[2,64,128]{2,1,0:T(8,128)S(1)} collective-permute-done((f32[2,64,128]{2,1,0:T(8,128)S(1)}, f32[2,64,128]{2,1,0:T(8,128)S(1)}, u32[]{:S(2)}, u32[]{:S(2)}) %collective-permute-start.17) | collective-permute-done | bytes 65568 | tf_op jit(solution)/shard_map/ppermute | solution.py:36
  38.8 0.3 shard_map.85
  39.1 2.4 %collective-permute-start.18 = (f32[4,64,128]{2,1,0:T(8,128)S(1)}, f32[4,64,128]{2,1,0:T(8,128)S(1)}, u32[]{:S(2)}, u32[]{:S(2)}) collective-permute-start(f32[4,64,128]{2,1,0:T(8,128)S(1)} %get-tuple-element.48), channel_id=1, source_target_pairs={{0,2},{1,3},{2,0},{3,1},{4,6},{5,7},{6,4},{7,5},{8,10},{9,11},{10,... | collective-permute-start | bytes 393224 | tf_op jit(solution)/shard_map/ppermute | solution.py:36
  41.5 8.3 %collective-permute-start.2 = (f32[4,64,256]{2,1,0:T(8,128)S(1)}, f32[4,64,256]{2,1,0:T(8,128)S(1)}, u32[]{:S(2)}, u32[]{:S(2)}) collective-permute-start(f32[4,64,256]{2,1,0:T(8,128)S(1)} %shard_map.71.basis), channel_id=1, source_target_pairs={{0,0},{1,4},{2,2},{3,6},{4,1},{5,5},{6,3},{7,7},{8,8},{9,12},{10,1... | collective-permute-start | bytes 786440 | tf_op jit(solution)/shard_map/ppermute | solution.py:36
  49.8 0.2 shard_map.80
  50.1 1.9 %collective-permute-start.12 = (f32[4,64,128]{2,1,0:T(8,128)S(1)}, f32[4,64,128]{2,1,0:T(8,128)S(1)}, u32[]{:S(2)}, u32[]{:S(2)}) collective-permute-start(f32[4,64,128]{2,1,0:T(8,128)S(1)} %shard_map.80), channel_id=1, source_target_pairs={{0,0},{1,4},{2,2},{3,6},{4,1},{5,5},{6,3},{7,7},{8,8},{9,12},{10,1... | collective-permute-start | bytes 393224 | tf_op jit(solution)/shard_map/ppermute | solution.py:36
  52.0 0.0 collective-permute-done.18.arrived
  52.0 0.3 shard_map.86
  52.3 0.1 collective-permute-start.19
  52.4 0.8 %shard_map.87 = (bf16[4,256,256]{2,1,0:T(8,128)(2,1)S(1)}, bf16[4,256,256]{2,1,0:T(8,128)(2,1)S(1)}) custom-call(f32[7,4,64,128]{3,2,1,0:T(8,128)S(1)} %copy-done, f32[4,64,256]{2,1,0:T(8,128)S(1)} %get-tuple-element.51.basis), custom_call_target="tpu_custom_call" | custom-call | flops 16777216 | bytes 524288 | tf_op jit(solution)/shard_map/pallas_call | solution.py:99
  53.2 5.7 %collective-permute-done.12.coeffs = f32[4,64,128]{2,1,0:T(8,128)S(1)} collective-permute-done((f32[4,64,128]{2,1,0:T(8,128)S(1)}, f32[4,64,128]{2,1,0:T(8,128)S(1)}, u32[]{:S(2)}, u32[]{:S(2)}) %collective-permute-start.12) | collective-permute-done | bytes 131104 | tf_op jit(solution)/shard_map/ppermute | solution.py:36
  58.9 0.0 collective-permute-done.2.basis
  58.9 1.1 %shard_map.81 = f32[1024,128]{1,0:T(8,128)} custom-call(f32[4,64,256]{2,1,0:T(8,128)S(1)} %collective-permute-done.2.basis, f32[4,64,128]{2,1,0:T(8,128)S(1)} %collective-permute-done.12.coeffs), custom_call_target="tpu_custom_call" | custom-call | flops 16777216 | bytes 524288 | tf_op jit(solution)/shard_map/pallas_call | solution.py:99
  60.1 0.0 collective-permute-done.19.arrived
  60.1 1.3 %shard_map.88 = f32[1024,128]{1,0:T(8,128)} custom-call(f32[4,64,128]{2,1,0:T(8,128)S(1)} %get-tuple-element.49.kept, f32[4,64,128]{2,1,0:T(8,128)S(1)} %collective-permute-done.19.arrived, bf16[4,256,256]{2,1,0:T(8,128)(2,1)S(1)} %get-tuple-element.52.high, bf16[4,256,256]{2,1,0:T(8,128)(2,1)S(1)} %get-tuple-element.53.low), custom_call_target="tpu_custom_call" | custom-call | flops 16777216 | bytes 524288 | tf_op jit(solution)/shard_map/pallas_call | solution.py:99
  (6 shorter events, 0.1 us)
Async XLA Ops:
  0.6 5.2 %copy-start = (f32[7,4,64,128]{3,2,1,0:T(8,128)S(1)}, f32[7,4,64,128]{3,2,1,0:T(8,128)}, u32[]{:S(2)}) copy-start(f32[7,4,64,128]{3,2,1,0:T(8,128)} %transfer.23) | copy-start | bytes 2752516
  2.9 3.0 %collective-permute-start.5 = (f32[264,128]{1,0:T(8,128)S(1)}, f32[264,128]{1,0:T(8,128)S(1)}, u32[]{:S(2)}, u32[]{:S(2)}) collective-permute-start(f32[264,128]{1,0:T(8,128)S(1)} %get-tuple-element.30.own), channel_id=1, source_target_pairs={{0,1},{1,0},{2,3},{3,2},{4,5},{5,4},{6,7},{7,6},{8,9},{9,8},{10,11... | collective-permute-start | bytes 405512 | tf_op jit(solution)/shard_map/ppermute | solution.py:36
  3.1 6.6 %collective-permute-start = (f32[2,64,256]{2,1,0:T(8,128)S(1)}, f32[2,64,256]{2,1,0:T(8,128)S(1)}, u32[]{:S(2)}, u32[]{:S(2)}) collective-permute-start(f32[2,64,256]{2,1,0:T(8,128)S(1)} %shard_map.69), channel_id=1, source_target_pairs={{0,8},{1,9},{2,10},{3,11},{4,12},{5,13},{6,14},{7,15},{8,0},{9,1},... | collective-permute-start | bytes 393224 | tf_op jit(solution)/shard_map/ppermute | solution.py:36
  5.8 6.6 %collective-permute-start.3 = (f32[2,128,128]{2,1,0:T(8,128)S(1)}, f32[2,128,128]{2,1,0:T(8,128)S(1)}, u32[]{:S(2)}, u32[]{:S(2)}) collective-permute-start(f32[2,128,128]{2,1,0:T(8,128)S(1)} %shard_map.72), channel_id=1, source_target_pairs={{0,8},{1,9},{2,10},{3,11},{4,12},{5,13},{6,14},{7,15},{8,0},{9,1},... | collective-permute-start | bytes 393224 | tf_op jit(solution)/shard_map/ppermute | solution.py:36
  6.2 7.6 %collective-permute-start.6 = (f32[264,128]{1,0:T(8,128)S(1)}, f32[264,128]{1,0:T(8,128)S(1)}, u32[]{:S(2)}, u32[]{:S(2)}) collective-permute-start(f32[264,128]{1,0:T(8,128)S(1)} %shard_map.74.own), channel_id=1, source_target_pairs={{0,2},{1,3},{2,0},{3,1},{4,6},{5,7},{6,4},{7,5},{8,10},{9,11},{10,... | collective-permute-start | bytes 405512 | tf_op jit(solution)/shard_map/ppermute | solution.py:36
  9.7 16.1 %collective-permute-start.1 = (f32[2,64,256]{2,1,0:T(8,128)S(1)}, f32[2,64,256]{2,1,0:T(8,128)S(1)}, u32[]{:S(2)}, u32[]{:S(2)}) collective-permute-start(f32[2,64,256]{2,1,0:T(8,128)S(1)} %shard_map.70), channel_id=1, source_target_pairs={{0,16},{1,17},{2,18},{3,19},{4,20},{5,21},{6,22},{7,23},{8,24},{9,... | collective-permute-start | bytes 393224 | tf_op jit(solution)/shard_map/ppermute | solution.py:36
  12.5 13.4 %collective-permute-start.4 = (f32[2,128,128]{2,1,0:T(8,128)S(1)}, f32[2,128,128]{2,1,0:T(8,128)S(1)}, u32[]{:S(2)}, u32[]{:S(2)}) collective-permute-start(f32[2,128,128]{2,1,0:T(8,128)S(1)} %shard_map.73), channel_id=1, source_target_pairs={{0,16},{1,17},{2,18},{3,19},{4,20},{5,21},{6,22},{7,23},{8,24},{9,... | collective-permute-start | bytes 393224 | tf_op jit(solution)/shard_map/ppermute | solution.py:36
  14.0 9.2 %collective-permute-start.7 = (f32[136,128]{1,0:T(8,128)S(1)}, f32[136,128]{1,0:T(8,128)S(1)}, u32[]{:S(2)}, u32[]{:S(2)}) collective-permute-start(f32[136,128]{1,0:T(8,128)S(1)} %get-tuple-element.31.own), channel_id=1, source_target_pairs={{0,4},{1,5},{2,6},{3,7},{4,0},{5,1},{6,2},{7,3},{8,12},{9,13},{10,... | collective-permute-start | bytes 208904 | tf_op jit(solution)/shard_map/ppermute | solution.py:36
  16.4 6.4 %collective-permute-start.8 = (f32[128,128]{1,0:T(8,128)S(1)}, f32[128,128]{1,0:T(8,128)S(1)}, u32[]{:S(2)}, u32[]{:S(2)}) collective-permute-start(f32[128,128]{1,0:T(8,128)S(1)} %get-tuple-element.33.own), channel_id=1, source_target_pairs={{0,4},{1,5},{2,6},{3,7},{4,0},{5,1},{6,2},{7,3},{8,12},{9,13},{10,... | collective-permute-start | bytes 196616 | tf_op jit(solution)/shard_map/ppermute | solution.py:36
  22.9 4.1 %collective-permute-start.10 = (f32[64,128]{1,0:T(8,128)S(1)}, f32[64,128]{1,0:T(8,128)S(1)}, u32[]{:S(2)}, u32[]{:S(2)}) collective-permute-start(f32[64,128]{1,0:T(8,128)S(1)} %get-tuple-element.36), channel_id=1, source_target_pairs={{0,16},{1,17},{2,18},{3,19},{4,20},{5,21},{6,22},{7,23},{8,24},{9,... | collective-permute-start | bytes 98312 | tf_op jit(solution)/shard_map/ppermute | solution.py:36
  23.3 3.7 %collective-permute-start.9 = (f32[64,128]{1,0:T(8,128)S(1)}, f32[64,128]{1,0:T(8,128)S(1)}, u32[]{:S(2)}, u32[]{:S(2)}) collective-permute-start(f32[64,128]{1,0:T(8,128)S(1)} %get-tuple-element.35), channel_id=1, source_target_pairs={{0,8},{1,9},{2,10},{3,11},{4,12},{5,13},{6,14},{7,15},{8,0},{9,1},... | collective-permute-start | bytes 98312 | tf_op jit(solution)/shard_map/ppermute | solution.py:36
  24.6 3.7 %collective-permute-start.11 = (f32[64,128]{1,0:T(8,128)S(1)}, f32[64,128]{1,0:T(8,128)S(1)}, u32[]{:S(2)}, u32[]{:S(2)}) collective-permute-start(f32[64,128]{1,0:T(8,128)S(1)} %get-tuple-element.37), channel_id=1, source_target_pairs={{0,24},{1,25},{2,26},{3,27},{4,28},{5,29},{6,30},{7,31},{8,16},{9,... | collective-permute-start | bytes 98312 | tf_op jit(solution)/shard_map/ppermute | solution.py:36
  28.5 3.7 %collective-permute-start.13 = (f32[64,128]{1,0:T(8,128)S(1)}, f32[64,128]{1,0:T(8,128)S(1)}, u32[]{:S(2)}, u32[]{:S(2)}) collective-permute-start(f32[64,128]{1,0:T(8,128)S(1)} %get-tuple-element.40), channel_id=1, source_target_pairs={{0,24},{1,25},{2,26},{3,27},{4,28},{5,29},{6,30},{7,31},{8,16},{9,... | collective-permute-start | bytes 98312 | tf_op jit(solution)/shard_map/ppermute | solution.py:36
  29.8 3.2 %collective-permute-start.15 = (f32[64,128]{1,0:T(8,128)S(1)}, f32[64,128]{1,0:T(8,128)S(1)}, u32[]{:S(2)}, u32[]{:S(2)}) collective-permute-start(f32[64,128]{1,0:T(8,128)S(1)} %get-tuple-element.43), channel_id=1, source_target_pairs={{0,8},{1,9},{2,10},{3,11},{4,12},{5,13},{6,14},{7,15},{8,0},{9,1},... | collective-permute-start | bytes 98312 | tf_op jit(solution)/shard_map/ppermute | solution.py:36
  31.3 2.8 %collective-permute-start.16 = (f32[64,128]{1,0:T(8,128)S(1)}, f32[64,128]{1,0:T(8,128)S(1)}, u32[]{:S(2)}, u32[]{:S(2)}) collective-permute-start(f32[64,128]{1,0:T(8,128)S(1)} %get-tuple-element.44), channel_id=1, source_target_pairs={{0,16},{1,17},{2,18},{3,19},{4,20},{5,21},{6,22},{7,23},{8,24},{9,... | collective-permute-start | bytes 98312 | tf_op jit(solution)/shard_map/ppermute | solution.py:36
  32.5 4.1 %collective-permute-start.14 = (f32[2,64,128]{2,1,0:T(8,128)S(1)}, f32[2,64,128]{2,1,0:T(8,128)S(1)}, u32[]{:S(2)}, u32[]{:S(2)}) collective-permute-start(f32[2,64,128]{2,1,0:T(8,128)S(1)} %get-tuple-element.42), channel_id=1, source_target_pairs={{0,4},{1,5},{2,6},{3,7},{4,0},{5,1},{6,2},{7,3},{8,12},{9,13},{10,... | collective-permute-start | bytes 196616 | tf_op jit(solution)/shard_map/ppermute | solution.py:36
  34.3 4.5 %collective-permute-start.17 = (f32[2,64,128]{2,1,0:T(8,128)S(1)}, f32[2,64,128]{2,1,0:T(8,128)S(1)}, u32[]{:S(2)}, u32[]{:S(2)}) collective-permute-start(f32[2,64,128]{2,1,0:T(8,128)S(1)} %get-tuple-element.46), channel_id=1, source_target_pairs={{0,4},{1,5},{2,6},{3,7},{4,0},{5,1},{6,2},{7,3},{8,12},{9,13},{10,... | collective-permute-start | bytes 196616 | tf_op jit(solution)/shard_map/ppermute | solution.py:36
  39.1 12.9 %collective-permute-start.18 = (f32[4,64,128]{2,1,0:T(8,128)S(1)}, f32[4,64,128]{2,1,0:T(8,128)S(1)}, u32[]{:S(2)}, u32[]{:S(2)}) collective-permute-start(f32[4,64,128]{2,1,0:T(8,128)S(1)} %get-tuple-element.48), channel_id=1, source_target_pairs={{0,2},{1,3},{2,0},{3,1},{4,6},{5,7},{6,4},{7,5},{8,10},{9,11},{10,... | collective-permute-start | bytes 393224 | tf_op jit(solution)/shard_map/ppermute | solution.py:36
  41.5 17.4 %collective-permute-start.2 = (f32[4,64,256]{2,1,0:T(8,128)S(1)}, f32[4,64,256]{2,1,0:T(8,128)S(1)}, u32[]{:S(2)}, u32[]{:S(2)}) collective-permute-start(f32[4,64,256]{2,1,0:T(8,128)S(1)} %shard_map.71.basis), channel_id=1, source_target_pairs={{0,0},{1,4},{2,2},{3,6},{4,1},{5,5},{6,3},{7,7},{8,8},{9,12},{10,1... | collective-permute-start | bytes 786440 | tf_op jit(solution)/shard_map/ppermute | solution.py:36
  50.1 8.9 %collective-permute-start.12 = (f32[4,64,128]{2,1,0:T(8,128)S(1)}, f32[4,64,128]{2,1,0:T(8,128)S(1)}, u32[]{:S(2)}, u32[]{:S(2)}) collective-permute-start(f32[4,64,128]{2,1,0:T(8,128)S(1)} %shard_map.80), channel_id=1, source_target_pairs={{0,0},{1,4},{2,2},{3,6},{4,1},{5,5},{6,3},{7,7},{8,8},{9,12},{10,1... | collective-permute-start | bytes 393224 | tf_op jit(solution)/shard_map/ppermute | solution.py:36
  52.3 7.8 %collective-permute-start.19 = (f32[4,64,128]{2,1,0:T(8,128)S(1)}, f32[4,64,128]{2,1,0:T(8,128)S(1)}, u32[]{:S(2)}, u32[]{:S(2)}) collective-permute-start(f32[4,64,128]{2,1,0:T(8,128)S(1)} %get-tuple-element.50), channel_id=1, source_target_pairs={{0,1},{1,0},{2,3},{3,2},{4,5},{5,4},{6,7},{7,6},{8,9},{9,8},{10,11... | collective-permute-start | bytes 393224 | tf_op jit(solution)/shard_map/ppermute | solution.py:36
